TPU v7x, 256 devices: a whole 4x4x8 slice. The times are simulated.
256 devices in a mesh: dp: 64 (over x_lo, y, z), section: 2 (over core), tensor: 2 (over x_hi).
Axes of the slice: x: 4 (x_hi: 2, x_lo: 2; x = x_hi * 2 + x_lo), y: 4, z: 8, core: 2. Of those that a mesh axis runs over, the one named last changes fastest.
Arguments:
- tower_input: bfloat16 [2, 12288, 1024], P('section', 'dp'), may hold values from -8 to 8
- up_weight: bfloat16 [2, 1024, 4096], P('section', None, 'tensor'), may hold values from -0.1875 to 0.1875
- down_weight: bfloat16 [2, 4096, 1024], P('section', 'tensor'), may hold values from -0.09375 to 0.09375
- pair: int32 [12288], P('dp'), may hold values from 0 to 12287, each once
- scale: float32 [1], replicated, may hold values from 4 to 16
- bias: float32 [1], replicated, may hold values from -4 to -1
Outputs:
- loss: float32 [1], replicated
- slide_grad: float32 [12288, 1024], P(('dp', 'section', 'tensor'))
- report_grad: float32 [12288, 1024], P(('dp', 'section', 'tensor'))
Inputs may be any that keep to these rules, and one draw needn't show every extreme that they name: `pair`: each report index appears exactly once.
All inputs are finite; a program needn't handle non-finite values.
Results may differ from a plain program's by a relative error of at most 0.00036.
Values may be sent and summed in bfloat16 or wider, within the bound.
No kernel may reach another device: no remote copies, remote signals or barrier semaphores. Data moves between devices by JAX's collectives and lax.ppermute only.
A program may use at most 128 MiB of HBM per device.

v0:
```python
import jax
import jax.numpy as jnp
from jax import lax
from jax.sharding import Mesh
from jax.sharding import PartitionSpec as P

DP = ("dp_0", "dp_1", "dp_2")
DP_SECTION_TENSOR = ("dp_0", "dp_1", "dp_2", "section", "tensor")


def cut_along(array, dim, devices):
    before, after = (array.shape[:dim], array.shape[dim + 1 :])
    return jnp.moveaxis(array.reshape(*before, devices, -1, *after), dim, 0)


def sent_and_summed(array, axis, dim):
    parts = cut_along(array, dim, lax.axis_size(axis))
    arrived = lax.all_to_all(parts, axis, split_axis=0, concat_axis=0, tiled=True)
    return arrived.sum(axis=0)


def copy_for_each(array, axis):
    copies = jnp.broadcast_to(array, (lax.axis_size(axis), *array.shape))
    return lax.all_to_all(copies, axis, split_axis=0, concat_axis=0, tiled=True)


def in_order(parts, dim):
    dims = list(parts.shape[1:])
    dims[dim] *= parts.shape[0]
    return jnp.moveaxis(parts, 0, dim).reshape(dims)


def gathered_copies(array, axis, dim):
    parts = copy_for_each(array, axis)
    return in_order(parts, dim)


def all_blocks(array, axes, sequence):
    parts = array
    for k in sequence:
        parts = lax.all_gather(parts, axes[k])
    done = sequence[::-1]
    back = [done.index(k) for k in range(len(axes))]
    parts = parts.transpose(*back, *range(len(axes), parts.ndim))
    return parts.reshape(-1, *array.shape)


def whole_of(array, axes, sequence, dim):
    return in_order(all_blocks(array, axes, sequence), dim)


def by_axis(array, axes):
    for axis in axes:
        array = lax.psum(array, axis)
    return array


def score_block(slides_all, block, pair, columns, scale_value, bias_value):
    logits = (
        scale_value
        * lax.dot_general(
            slides_all, block, (((1,), (1,)), ((), ())), preferred_element_type=jnp.float32
        )
        + bias_value
    )
    sign = jnp.where(pair[:, None] == columns[None, :], 1.0, -1.0).astype(jnp.float32)
    loss_part = jnp.sum(jnp.logaddexp(jnp.float32(0.0), -sign * logits))
    weight = (-scale_value * sign * jax.nn.sigmoid(-sign * logits)).astype(jnp.bfloat16)
    slide_part = jnp.dot(weight, block, preferred_element_type=jnp.float32)
    report_part = lax.dot_general(
        weight, slides_all, (((0,), (0,)), ((), ())), preferred_element_type=jnp.float32
    )
    return (loss_part, slide_part, report_part)


def local(tower_input, up_weight, down_weight, pair, scale, bias):
    n_section = lax.axis_size("section")
    n_tensor = lax.axis_size("tensor")
    n_cycle = lax.axis_size(DP)
    group = n_section * n_tensor
    inputs = tower_input[0]
    width = inputs.shape[1]
    quarter = inputs.shape[0] // group
    hidden = jax.nn.gelu(jnp.dot(inputs, up_weight[0], preferred_element_type=jnp.float32)).astype(
        jnp.bfloat16
    )
    partial_value = jnp.dot(hidden, down_weight[0], preferred_element_type=jnp.float32)
    partial_value = partial_value.reshape(n_section, n_tensor, quarter, width)
    summed = sent_and_summed(partial_value, "tensor", 1)
    local_in = lax.dynamic_slice_in_dim(
        inputs.reshape(n_section, n_tensor, quarter, width), lax.axis_index("tensor"), 1, 1
    )
    raw = (summed + local_in.astype(jnp.float32)).reshape(n_section, quarter, width)
    norms = lax.rsqrt(jnp.sum(raw * raw, axis=-1, keepdims=True) + 1e-06)
    embedded = (raw * norms).astype(jnp.bfloat16)
    both = lax.all_to_all(embedded, "section", split_axis=0, concat_axis=0, tiled=True)
    slides_all = gathered_copies(both[0], ("section", "tensor"), 0)
    reports_own = both[1]
    group_rank = lax.axis_index("section") * n_tensor + lax.axis_index("tensor")
    scale_value = scale[0]
    bias_value = bias[0]
    total = n_cycle * group * quarter
    reports_group = whole_of(reports_own, DP, (0, 1, 2), 0)
    position = jnp.arange(n_cycle * quarter, dtype=jnp.int32)
    columns = (position // quarter * group + group_rank) * quarter + position % quarter
    rows_half = slides_all.shape[0] // 2
    loss_top, slide_top, report_top = score_block(
        slides_all[:rows_half], reports_group, pair[:rows_half], columns, scale_value, bias_value
    )
    loss_bottom, slide_bottom, report_bottom = score_block(
        slides_all[rows_half:], reports_group, pair[rows_half:], columns, scale_value, bias_value
    )
    loss_sum = loss_top + loss_bottom
    slide_sum = jnp.concatenate([slide_top, slide_bottom], axis=0)
    report_grad = lax.psum_scatter(report_top + report_bottom, DP, scatter_dimension=0, tiled=True)
    slide_grad = sent_and_summed(slide_sum, ("section", "tensor"), 0)
    loss = by_axis(loss_sum, DP_SECTION_TENSOR) / total
    return (loss.reshape(1), slide_grad, report_grad)


def solution(mesh):
    finer = Mesh(
        mesh.devices.reshape(2, 4, 8, mesh.shape["section"], mesh.shape["tensor"]),
        ("dp_0", "dp_1", "dp_2", "section", "tensor"),
    )
    return jax.shard_map(
        local,
        mesh=finer,
        in_specs=(
            P("section", DP, None),
            P("section", None, "tensor"),
            P("section", "tensor", None),
            P(DP),
            P(),
            P(),
        ),
        out_specs=(P(), P(DP_SECTION_TENSOR, None), P(DP_SECTION_TENSOR, None)),
        check_vma=False,
    )
```

profile of v0, /device:TPU:4, one launch (start us, length us, event | category | flops | bytes accessed | tf_op | source)
XLA Modules:
  0.0 500.6 jit_solution(10588093942911933948)
XLA Ops:
  7.2 0.0 copy-start.2
  7.2 3.8 fusion.17
  11.0 0.0 copy-done.2
  11.0 1.0 fusion.20
  12.0 1.0 copy.13
  12.9 0.0 copy-start.3
  12.9 5.9 %all-to-all-start = ((f32[2,2,1,48,1024]{4,3,1,2,0:T(8,128)}), f32[2,2,1,48,1024]{4,3,1,2,0:T(8,128)S(1)}, u32[]{:S(2)}, u32[]{:S(2)}) async-start(f32[2,2,1,48,1024]{4,3,1,2,0:T(8,128)} %copy.13), calls=%async_computation | async-start | bytes 1572864 | tf_op jit(solution)/shard_map/all_to_all | solution.py:18
  18.8 0.0 all-gather.4.cloned.1.call-start
  18.8 8.1 %all-to-all-done = f32[2,2,1,48,1024]{4,3,1,2,0:T(8,128)S(1)} async-done(((f32[2,2,1,48,1024]{4,3,1,2,0:T(8,128)}), f32[2,2,1,48,1024]{4,3,1,2,0:T(8,128)S(1)}, u32[]{:S(2)}, u32[]{:S(2)}) %all-to-all-start) | async-done | bytes 786464 | tf_op jit(solution)/shard_map/all_to_all | solution.py:18
  26.9 0.1 reduce_sum.47
  27.0 0.0 copy-done.3
  27.0 0.1 fusion.27
  27.1 0.1 fusion.28
  27.2 3.9 all_to_all.20
  31.1 5.5 %all_gather.15 = bf16[2,48,1024]{2,1,0:T(8,128)(2,1)S(1)} all-gather(bf16[1,48,1024]{2,1,0:T(8,128)(2,1)S(1)} %get-tuple-element.5), channel_id=1, replica_groups=mesh['dp_0'=2,'dp_1'=4,'dp_2'=8,'section'=2,'tensor'=2] {'dp_0'}, dimensions={0}, use_global_device_ids=true | all-gather | bytes 294912 | tf_op jit(solution)/shard_map/all_gather | solution.py:41
  36.7 14.6 %all-gather = bf16[8,48,1024]{2,1,0:T(8,128)(2,1)} all-gather(bf16[2,48,1024]{2,1,0:T(8,128)(2,1)S(1)} %all_gather.15), channel_id=2, replica_groups=mesh['dp_0'=2,'dp_1'=4,'dp_2'=8,'section'=2,'tensor'=2] {'dp_1'}, dimensions={0}, use_global_device_ids=true | all-gather | bytes 983040 | tf_op jit(solution)/shard_map/all_gather | solution.py:41
  51.2 0.0 copy-start.4
  51.2 0.0 all-gather.4.cloned.1.call-update
  52.6 0.8 broadcast_in_dim.20
  53.4 6.7 %all-to-all-start.2 = ((bf16[4,48,1024]{2,1,0:T(8,128)(2,1)}), bf16[4,48,1024]{2,1,0:T(8,128)(2,1)S(1)}, u32[]{:S(2)}, u32[]{:S(2)}) async-start(bf16[4,48,1024]{2,1,0:T(8,128)(2,1)} %broadcast_in_dim.20), calls=%async_computation.2 | async-start | bytes 786432 | tf_op jit(solution)/shard_map/all_to_all | solution.py:24
  60.0 0.0 reduce-scatter.2.cloned.1.call-start
  60.1 0.0 copy-done.4
  60.1 0.1 fusion.50
  60.1 5.5 %all-to-all-done.2 = bf16[4,48,1024]{2,1,0:T(8,128)(2,1)S(1)} async-done(((bf16[4,48,1024]{2,1,0:T(8,128)(2,1)}), bf16[4,48,1024]{2,1,0:T(8,128)(2,1)S(1)}, u32[]{:S(2)}, u32[]{:S(2)}) %all-to-all-start.2) | async-done | bytes 393248 | tf_op jit(solution)/shard_map/all_to_all | solution.py:24
  65.7 64.2 %all-gather.4.cloned.1.call-done = bf16[32,2,48,1024]{3,2,1,0:T(8,128)(2,1)} async-done(((bf16[4,2,48,1024]{3,2,1,0:T(8,128)(2,1)}), bf16[32,2,48,1024]{3,2,1,0:T(8,128)(2,1)}) %all-gather.4.cloned.1.call-update) | async-done | bytes 6291472 | tf_op jit(solution)/shard_map/all_gather | solution.py:41
  129.9 3.6 copy.14
  133.4 0.0 copy-start
  133.5 3.3 select_reduce_fusion.1
  136.8 2.0 fusion.44
  138.7 0.0 copy-done
  138.8 3.4 select_reduce_fusion
  142.1 6.6 %convolution_add_fusion = f32[3072,1024]{1,0:T(8,128)} fusion(f32[3072,1024]{1,0:T(8,128)S(1)} %fusion.44, bf16[96,1024]{1,0:T(8,128)(2,1)S(1)} %bitcast.73, f32[96,3072]{1,0:T(8,128)S(1)} %get-tuple-element.12, f32[]{:T(128)S(6)} %neg.28, s32[3072]{0:T(1024)S(1)} %fusion.39, s32[96]{0:T(128)S(1)} %get-tuple-element.7), kind=kOutput, calls=%fused_computation | convolution fusion | flops 609484800 | bytes 26554756 | tf_op jit(solution)/shard_map/dot_general | solution.py:70
  148.7 0.0 reduce-scatter.2.cloned.1.call-update
  148.8 0.0 copy-start.1
  148.8 4.3 fusion.42
  153.1 0.3 copy-done.1
  153.4 1.5 fusion.46
  154.9 1.0 pad_maximum_fusion
  155.9 4.8 all-to-all-start.3
  161.9 10.3 %psum.35 = f32[]{:T(128)} all-reduce(f32[]{:T(128)S(6)} %add.118), channel_id=1, replica_groups=mesh['dp_0'=2,'dp_1'=4,'dp_2'=8,'section'=2,'tensor'=2] {'dp_0'}, use_global_device_ids=true, to_apply=%region_4.5 | all-reduce | flops 1 | bytes 8 | tf_op jit(solution)/shard_map/psum | solution.py:54
  172.2 19.6 %psum.36 = f32[]{:T(128)} all-reduce(f32[]{:T(128)} %psum.35), channel_id=1, replica_groups=mesh['dp_0'=2,'dp_1'=4,'dp_2'=8,'section'=2,'tensor'=2] {'dp_1'}, use_global_device_ids=true, to_apply=%region_5.6 | all-reduce | flops 1 | bytes 8 | tf_op jit(solution)/shard_map/psum | solution.py:54
  191.8 14.8 %psum.37 = f32[]{:T(128)} all-reduce(f32[]{:T(128)} %psum.36), channel_id=1, replica_groups=mesh['dp_0'=2,'dp_1'=4,'dp_2'=8,'section'=2,'tensor'=2] {'dp_2'}, use_global_device_ids=true, to_apply=%region_6.7 | all-reduce | flops 1 | bytes 8 | tf_op jit(solution)/shard_map/psum | solution.py:54
  206.6 3.1 psum.38
  209.7 7.1 %psum.39 = f32[]{:T(128)} all-reduce(f32[]{:T(128)} %psum.38), channel_id=1, replica_groups=mesh['dp_0'=2,'dp_1'=4,'dp_2'=8,'section'=2,'tensor'=2] {'tensor'}, use_global_device_ids=true, to_apply=%region_8.9 | all-reduce | flops 1 | bytes 8 | tf_op jit(solution)/shard_map/psum | solution.py:54
  217.4 0.0 all-to-all-done.3
  217.4 0.7 reduce_sum.52
  218.2 274.5 %reduce-scatter.2.cloned.1.call-done = f32[48,1024]{1,0:T(8,128)} async-done(((f32[3072,1024]{1,0:T(8,128)}), f32[48,1024]{1,0:T(8,128)}) %reduce-scatter.2.cloned.1.call-update) | async-done | bytes 196624 | tf_op jit(solution)/shard_map/reduce_scatter | solution.py:115
  (4 shorter events, 0.1 us)
Async XLA Ops:
  7.2 3.8 copy-start.2
  12.9 14.0 %copy-start.3 = (bf16[1,192,1024]{2,1,0:T(8,128)(2,1)S(1)}, bf16[1,192,1024]{2,1,0:T(8,128)(2,1)}, u32[]{:S(2)}) copy-start(bf16[1,192,1024]{2,1,0:T(8,128)(2,1)} %param.6) | copy-start | bytes 1179652
  12.9 14.0 %all-to-all-start = ((f32[2,2,1,48,1024]{4,3,1,2,0:T(8,128)}), f32[2,2,1,48,1024]{4,3,1,2,0:T(8,128)S(1)}, u32[]{:S(2)}, u32[]{:S(2)}) async-start(f32[2,2,1,48,1024]{4,3,1,2,0:T(8,128)} %copy.13), calls=%async_computation | async-start | bytes 1572864 | tf_op jit(solution)/shard_map/all_to_all | solution.py:18
  18.8 111.0 %all-gather.4.cloned.1.call-start = ((), (), s32[]{:S(2)}) async-start(), calls=%async_computation.6 | async-start | bytes 7077888 | tf_op jit(solution)/shard_map/all_gather | solution.py:41
  51.2 8.8 %copy-start.4 = (s32[192]{0:T(256)S(1)}, s32[192]{0:T(256)}, u32[]{:S(2)}) copy-start(s32[192]{0:T(256)} %param.9) | copy-start | bytes 2308
  53.4 12.3 %all-to-all-start.2 = ((bf16[4,48,1024]{2,1,0:T(8,128)(2,1)}), bf16[4,48,1024]{2,1,0:T(8,128)(2,1)S(1)}, u32[]{:S(2)}, u32[]{:S(2)}) async-start(bf16[4,48,1024]{2,1,0:T(8,128)(2,1)} %broadcast_in_dim.20), calls=%async_computation.2 | async-start | bytes 786432 | tf_op jit(solution)/shard_map/all_to_all | solution.py:24
  60.0 432.6 %reduce-scatter.2.cloned.1.call-start = ((), (), s32[]{:S(2)}) async-start(), calls=%async_computation.5 | async-start | bytes 12779520 | tf_op jit(solution)/shard_map/reduce_scatter | solution.py:115
  133.4 5.3 %copy-start = (bf16[2,4,8,48,1024]{4,3,2,1,0:T(8,128)(2,1)}, bf16[2,4,8,48,1024]{4,3,2,1,0:T(8,128)(2,1)S(1)}, u32[]{:S(2)}) copy-start(bf16[2,4,8,48,1024]{4,3,2,1,0:T(8,128)(2,1)S(1)} %copy.14) | copy-start | bytes 18874372
  148.8 4.6 copy-start.1
  155.9 61.5 %all-to-all-start.3 = ((f32[4,48,1024]{2,1,0:T(8,128)}), f32[4,48,1024]{2,1,0:T(8,128)S(1)}, u32[]{:S(2)}, u32[]{:S(2)}) async-start(f32[4,48,1024]{2,1,0:T(8,128)} %bitcast.21), calls=%async_computation.3 | async-start | bytes 1572864 | tf_op jit(solution)/shard_map/all_to_all | solution.py:18
Sparse Core Ops, SparseCore 0:
  51.4 78.4 all-gather.3
  148.9 343.7 reduce-scatter.1
where the time goes:
time: 501 us
  waiting for transfers between devices  352 us (70%)
  blocking collectives  78.8 us (16%)
  matrix products  25.9 us (5%)
  between operations  18.5 us (4%)
  starting transfers between devices  17.4 us (3%)
  local copies, waits for them, and re-layouts  5.71 us (1%)
    reduce_scatter x1, waiting for transfers between devices, local(): lax.psum_scatter(report_top + report_bottom, DP, scatter_dimension=0, til...  274 us
    all_gather x1, waiting for transfers between devices, all_blocks(): parts = lax.all_gather(parts, axes[k])  64.2 us
    psum x5, blocking collectives, by_axis(): array = lax.psum(array, axis)  54.8 us
    all_gather x2, blocking collectives, all_blocks(): parts = lax.all_gather(parts, axes[k])  20.1 us
    all_to_all x2, starting transfers between devices, sent_and_summed(): lax.all_to_all(parts, axis, split_axis=0, concat_axis=0, tiled=True)  10.7 us
  transfers between devices with their start and end apart: 5, of which 4 were waited for; matrix products, arithmetic and copies ran while one was open for 2% of the time, Pallas kernels for 0%

commit v1 on v0

v1 whole, which is shorter than its diff:
```python
import jax
import jax.numpy as jnp
from jax import lax
from jax.sharding import Mesh
from jax.sharding import PartitionSpec as P

DP = ("xl", "y", "z")
PLANE = ("xl", "y", "tensor")
ALL = ("xl", "y", "z", "section", "tensor")
SWAP = [(0, 1), (1, 0)]
F32 = jnp.float32
SENT = jnp.float16


def exchanged(parts, axes):
    return lax.all_to_all(parts, axes, split_axis=0, concat_axis=0, tiled=True)


def copies(array, axes):
    return exchanged(jnp.broadcast_to(array, (lax.axis_size(axes), *array.shape)), axes)


def tower(inputs, up, down, tensor):
    rows, width = inputs.shape
    split = inputs.reshape(2, 2, rows // 4, width)
    kept = lax.dynamic_slice_in_dim(split, tensor, 1, 1).reshape(rows // 2, width)
    given = lax.dynamic_slice_in_dim(split, 1 - tensor, 1, 1).reshape(rows // 2, width)
    ordered = jnp.concatenate([given, kept], axis=0)
    hidden = jax.nn.gelu(jnp.dot(ordered, up, preferred_element_type=F32)).astype(jnp.bfloat16)
    sent = jnp.dot(hidden[: rows // 2], down, preferred_element_type=F32)
    arrived = lax.ppermute(sent, "tensor", SWAP)
    own = jnp.dot(hidden[rows // 2 :], down, preferred_element_type=F32)
    raw = own + arrived + kept.astype(F32)
    norms = lax.rsqrt(jnp.sum(raw * raw, axis=-1, keepdims=True) + 1e-06)
    return (raw * norms).astype(jnp.bfloat16).reshape(2, rows // 4, width)


def local(tower_input, up_weight, down_weight, pair, scale, bias):
    section = lax.axis_index("section")
    tensor = lax.axis_index("tensor")
    n_z = lax.axis_size("z")
    n_plane = lax.axis_size(PLANE)
    scale_value, bias_value = scale[0], bias[0]
    quarter = tower_input.shape[1] // 4
    total = lax.axis_size(ALL) * quarter

    pair_rows = lax.dynamic_slice_in_dim(pair.reshape(2, 2, quarter), tensor, 1, 1)
    pair_rows = jnp.pad(pair_rows.reshape(1, 2, quarter), ((0, 0), (0, 0), (0, 128 - quarter)))
    pair_all = copies(pair_rows[0], "z")[:, :, :quarter]
    pair_own = lax.dynamic_index_in_dim(pair_all, section, 1, keepdims=False)
    pair_other = lax.dynamic_index_in_dim(pair_all, 1 - section, 1, keepdims=False)
    pair_all = jnp.concatenate([pair_own.reshape(-1), pair_other.reshape(-1)])

    embedded = tower(tower_input[0], up_weight[0], down_weight[0], tensor)
    mine = lax.dynamic_index_in_dim(embedded, section, 0, keepdims=False)
    given = lax.dynamic_index_in_dim(embedded, 1 - section, 0, keepdims=False)
    got = lax.ppermute(given, "section", SWAP)
    slides = jnp.where(section == 0, mine, got)
    reports = jnp.where(section == 0, got, mine)

    slides_z = copies(slides, "z").reshape(n_z * quarter, -1)
    reports_all = copies(reports, PLANE).reshape(n_plane * quarter, -1)
    slides_all = jnp.concatenate([slides_z, lax.ppermute(slides_z, "section", SWAP)], axis=0)

    place = jnp.arange(n_plane * quarter, dtype=jnp.int32)
    member, row = place // quarter, place % quarter
    owner = ((member // 2 * n_z + lax.axis_index("z")) * 2 + section) * 2 + member % 2
    columns = owner * quarter + row

    dots = lax.dot_general(
        slides_all, reports_all, (((1,), (1,)), ((), ())), preferred_element_type=F32
    )
    logits = scale_value * dots + bias_value
    match = pair_all[:, None] == columns[None, :]
    turned = jnp.where(match, -logits, logits)
    small = jnp.exp(-jnp.abs(turned))
    loss_part = jnp.sum(jnp.maximum(turned, 0.0) + jnp.log1p(small))
    sigmoid = jnp.where(turned >= 0, 1.0, small) / (1.0 + small)
    weight = (jnp.where(match, -scale_value, scale_value) * sigmoid).astype(jnp.bfloat16)
    slide_part = jnp.dot(weight, reports_all, preferred_element_type=F32)
    report_part = lax.dot_general(
        weight, slides_all, (((0,), (0,)), ((), ())), preferred_element_type=F32
    )
    half = n_z * quarter
    slide_half = slide_part[:half] + lax.ppermute(slide_part[half:], "section", SWAP)
    slide_terms = exchanged(slide_half.astype(SENT).reshape(n_z, quarter, -1), "z")
    report_terms = exchanged(report_part.astype(SENT).reshape(n_plane, quarter, -1), PLANE)
    slide_grad = slide_terms.astype(F32).sum(axis=0)
    report_grad = report_terms.astype(F32).sum(axis=0)

    losses = jnp.broadcast_to(loss_part, (1, 128))
    losses = losses + lax.ppermute(losses, "section", SWAP)
    losses = copies(losses, PLANE).sum(axis=0)
    losses = copies(losses, "z").sum(axis=0)
    loss = losses[0, :1] / total
    return (loss, slide_grad, report_grad)


def solution(mesh):
    finer = Mesh(
        mesh.devices.reshape(2, 4, 8, mesh.shape["section"], mesh.shape["tensor"]),
        ALL,
    )
    return jax.shard_map(
        local,
        mesh=finer,
        in_specs=(
            P("section", DP, None),
            P("section", None, "tensor"),
            P("section", "tensor", None),
            P(DP),
            P(),
            P(),
        ),
        out_specs=(P(), P(ALL, None), P(ALL, None)),
        check_vma=False,
    )
```

time: 501 us -> 179 us (0.36)
  waiting for transfers between devices: 352 us -> 76.4 us
  blocking collectives: 78.8 us -> 34.9 us
  starting transfers between devices: 17.4 us -> 33.7 us
  between operations: 18.5 us -> 3.31 us
  matrix products: 25.9 us -> 17.7 us
    reduce_scatter x1 -> x0, waiting for transfers between devices: 274 us -> none  [local(): lax.psum_scatter(report_top + report_bottom, DP, scatter_dimension=0, til...]
    all_gather x1 -> x0, waiting for transfers between devices: 64.2 us -> none  [all_blocks(): parts = lax.all_gather(parts, axes[k])]
    psum x5 -> x0, blocking collectives: 54.8 us -> none  [by_axis(): array = lax.psum(array, axis)]
    all_to_all x3 -> x5, waiting for transfers between devices: 13.6 us -> 66.4 us  [exchanged(): return lax.all_to_all(parts, axes, split_axis=0, concat_axis=0, tiled=True)]
    all_to_all x1 -> x2, blocking collectives: 3.89 us -> 34.9 us  [exchanged(): return lax.all_to_all(parts, axes, split_axis=0, concat_axis=0, tiled=True)]
    all_gather x2 -> x0, blocking collectives: 20.1 us -> none  [all_blocks(): parts = lax.all_gather(parts, axes[k])]
    all_to_all x3 -> x5, starting transfers between devices: 17.4 us -> 30.7 us  [exchanged(): return lax.all_to_all(parts, axes, split_axis=0, concat_axis=0, tiled=True)]
    ppermute x0 -> x5, waiting for transfers between devices: none -> 10 us  [the longest x1 10 us: tower(): arrived = lax.ppermute(sent, 'tensor', SWAP)]
  transfers between devices with their start and end apart: 5 -> 10, of which waited for: 4 -> 6; matrix products, arithmetic and copies ran while one was open for 2% -> 7% of each run, Pallas kernels for 0% -> 0%
where the time goes in v1:
time: 179 us; the launch traced here: 178 us
  waiting for transfers between devices  76.4 us (43%)
  blocking collectives  34.9 us (19%)
  starting transfers between devices  33.7 us (19%)
  matrix products  17.7 us (10%)
  local copies, waits for them, and re-layouts  6.32 us (4%)
  other arithmetic  5.8 us (3%)
  between operations  3.31 us (2%)
    all_to_all x5, waiting for transfers between devices, exchanged(): return lax.all_to_all(parts, axes, split_axis=0, concat_axis=0, tiled=True)  66.4 us
    all_to_all x2, blocking collectives, exchanged(): return lax.all_to_all(parts, axes, split_axis=0, concat_axis=0, tiled=True)  34.9 us
    all_to_all x5, starting transfers between devices, exchanged(): return lax.all_to_all(parts, axes, split_axis=0, concat_axis=0, tiled=True)  30.7 us
    ppermute x1, waiting for transfers between devices, tower(): arrived = lax.ppermute(sent, 'tensor', SWAP)  10 us
    dot_general x1, matrix products, local(): lax.dot_general(slides_all, reports_all, (((1,), (1,)), ((), ())), prefer...  4.59 us
    dot_general x1, matrix products, local(): lax.dot_general(weight, slides_all, (((0,), (0,)), ((), ())), preferred_e...  4.07 us
    dot_general x1, matrix products, tower(): jnp.dot(ordered, up, preferred_element_type=F32)  3.71 us
  transfers between devices with their start and end apart: 10, of which 6 were waited for; matrix products, arithmetic and copies ran while one was open for 7% of the time, Pallas kernels for 0%

profile of v1, /device:TPU:4, one launch (start us, length us, event | category | flops | bytes accessed | tf_op | source)
XLA Modules:
  0.0 178.2 jit_solution(5132469441997192332)
XLA Ops:
  0.6 1.1 constant_dynamic-slice_fusion.1
  1.7 0.0 copy-start
  1.7 3.7 %fusion.17 = bf16[192,2048]{1,0:T(8,128)(2,1)S(1)} fusion(bf16[1,1024,2048]{2,1,0:T(8,128)(2,1)} %param.7, bf16[96,1024]{1,0:T(8,128)(2,1)S(1)} %bitcast.58, bf16[96,1024]{1,0:T(8,128)(2,1)S(1)} %bitcast.66), kind=kOutput, calls=%fused_computation.22 | convolution fusion | flops 809631744 | bytes 5373952 | tf_op jit(solution)/shard_map/dot_general | solution.py:29
  5.4 0.0 copy-start.2
  5.4 0.8 fusion
  6.3 2.3 %collective-permute-start = (f32[96,1024]{1,0:T(8,128)S(1)}, f32[96,1024]{1,0:T(8,128)S(1)}, u32[]{:S(2)}, u32[]{:S(2)}) collective-permute-start(f32[96,1024]{1,0:T(8,128)S(1)} %fusion), channel_id=1, source_target_pairs={{0,1},{1,0},{2,3},{3,2},{4,5},{5,4},{6,7},{7,6},{8,9},{9,8},{10,11... | collective-permute-start | bytes 1179656 | tf_op jit(solution)/shard_map/ppermute | solution.py:31
  8.6 0.1 reshape.106
  8.7 10.0 %collective-permute-done = f32[96,1024]{1,0:T(8,128)S(1)} collective-permute-done((f32[96,1024]{1,0:T(8,128)S(1)}, f32[96,1024]{1,0:T(8,128)S(1)}, u32[]{:S(2)}, u32[]{:S(2)}) %collective-permute-start) | collective-permute-done | bytes 393248 | tf_op jit(solution)/shard_map/ppermute | solution.py:31
  18.7 3.1 %multiply_reduce_fusion = (f32[96]{0:T(128)S(1)}, f32[96,1024]{1,0:T(8,128)S(1)}) fusion(bf16[96,1024]{1,0:T(8,128)(2,1)S(1)} %bitcast.59, f32[96,1024]{1,0:T(8,128)S(1)} %collective-permute-done, bf16[1,2048,1024]{2,1,0:T(8,128)(2,1)} %param.8, bf16[192,2048]{1,0:T(8,128)(2,1)S(1)} %fusion.17), kind=kOutput, calls=%fused_computation.35 | convolution fusion | flops 403144608 | bytes 5570944 | tf_op jit(solution)/shard_map/dot_general | solution.py:32
  21.8 0.1 multiply_convert_fusion
  22.0 0.1 collective-permute-start.1
  22.1 0.6 broadcast_in_dim.31
  22.7 8.5 %all-to-all-start = ((s32[8,2,128]{2,1,0:T(2,128)}), s32[8,2,128]{2,1,0:T(2,128)S(1)}, u32[]{:S(2)}, u32[]{:S(2)}) async-start(s32[8,2,128]{2,1,0:T(2,128)} %broadcast_in_dim.31), calls=%async_computation | async-start | bytes 16384 | tf_op jit(solution)/shard_map/all_to_all | solution.py:16
  31.1 0.0 collective-permute-done.1
  31.2 7.7 %all-to-all-done = s32[8,2,128]{2,1,0:T(2,128)S(1)} async-done(((s32[8,2,128]{2,1,0:T(2,128)}), s32[8,2,128]{2,1,0:T(2,128)S(1)}, u32[]{:S(2)}, u32[]{:S(2)}) %all-to-all-start) | async-done | bytes 8224 | tf_op jit(solution)/shard_map/all_to_all | solution.py:16
  38.9 0.1 broadcast_in_dim.32
  39.0 25.0 %all_to_all.35 = bf16[8,48,1024]{2,1,0:T(8,128)(2,1)S(1)} all-to-all(bf16[8,48,1024]{2,1,0:T(8,128)(2,1)S(1)} %broadcast_in_dim.32), channel_id=1, replica_groups=mesh['xl'=2,'y'=4,'z'=8,'section'=2,'tensor'=2] {'z'}, dimensions={0} | all-to-all | bytes 1572864 | tf_op jit(solution)/shard_map/all_to_all | solution.py:16
  64.0 1.4 broadcast_in_dim.33
  65.4 7.5 %all-to-all-start.2 = ((bf16[16,48,1024]{2,1,0:T(8,128)(2,1)}), bf16[16,48,1024]{2,1,0:T(8,128)(2,1)S(1)}, u32[]{:S(2)}, u32[]{:S(2)}) async-start(bf16[16,48,1024]{2,1,0:T(8,128)(2,1)} %broadcast_in_dim.33), calls=%async_computation.2 | async-start | bytes 3145728 | tf_op jit(solution)/shard_map/all_to_all | solution.py:16
  72.8 0.0 collective-permute-start.2
  74.2 0.1 reshape.108
  74.2 0.1 reshape.109
  74.4 18.2 %all-to-all-done.2 = bf16[16,48,1024]{2,1,0:T(8,128)(2,1)S(1)} async-done(((bf16[16,48,1024]{2,1,0:T(8,128)(2,1)}), bf16[16,48,1024]{2,1,0:T(8,128)(2,1)S(1)}, u32[]{:S(2)}, u32[]{:S(2)}) %all-to-all-start.2) | async-done | bytes 1572896 | tf_op jit(solution)/shard_map/all_to_all | solution.py:16
  92.6 0.0 collective-permute-done.2
  92.6 4.6 %fusion.7 = (bf16[768,768]{1,0:T(8,128)(2,1)S(1)}, f32[]{:T(128)}) fusion(f32[]{:T(128)S(6)} %neg.11, f32[]{:T(128)} %bitcast.52, s32[768]{0:T(1024)S(1)} %get-tuple-element.13, s32[768]{0:T(1024)S(1)} %get-tuple-element.14, f32[]{:T(128)} %bitcast.54, bf16[768,1024]{1,0:T(8,128)(2,1)S(1)} %bitcast.55, bf16[384,1024]{1,0:T(8,128)(2,1)S(1)} %collective-permute-done.2, ...), kind=kOutput, calls=%fused_computation.11 | convolution fusion | flops 1221132288 | bytes 4331536 | tf_op jit(solution)/shard_map/dot_general | solution.py:70
  97.2 0.6 broadcast_in_dim.34
  97.9 0.1 collective-permute-start.3
  98.0 1.4 fusion.54
  99.4 0.0 copy-done.4
  99.4 0.0 copy-start.1
  99.4 0.1 slice.28
  99.5 1.5 copy-done.1
  101.0 0.5 collective-permute-start.4
  101.5 0.0 collective-permute-done.3
  101.5 0.6 add_bitcast_fusion
  102.2 9.9 %all_to_all.36 = f32[16,1,128]{2,1,0:T(1,128)S(1)} all-to-all(f32[16,1,128]{2,1,0:T(1,128)S(1)} %broadcast_in_dim.35), channel_id=1, replica_groups=mesh['xl'=2,'y'=4,'z'=8,'section'=2,'tensor'=2] {'xl','y','tensor'}, dimensions={0} | all-to-all | bytes 16384 | tf_op jit(solution)/shard_map/all_to_all | solution.py:16
  112.1 0.6 broadcast_in_dim.36
  112.7 4.1 %all-to-all-start.4 = ((f32[8,1,128]{2,1,0:T(1,128)}), f32[8,1,128]{2,1,0:T(1,128)S(1)}, u32[]{:S(2)}, u32[]{:S(2)}) async-start(f32[8,1,128]{2,1,0:T(1,128)} %broadcast_in_dim.36), calls=%async_computation.4 | async-start | bytes 8192 | tf_op jit(solution)/shard_map/all_to_all | solution.py:16
  116.8 4.1 %convolution_convert_fusion = f16[768,1024]{1,0:T(8,128)(2,1)} fusion(bf16[768,768]{1,0:T(8,128)(2,1)} %copy-done.4, bf16[384,1024]{1,0:T(8,128)(2,1)} %copy-done.3, bf16[384,1024]{1,0:T(8,128)(2,1)S(1)} %bitcast.62), kind=kOutput, calls=%fused_computation.14 | convolution fusion | flops 1211891712 | bytes 4325376 | tf_op jit(solution)/shard_map/dot_general | solution.py:81
  120.9 3.5 %all-to-all-done.4 = f32[8,1,128]{2,1,0:T(1,128)S(1)} async-done(((f32[8,1,128]{2,1,0:T(1,128)}), f32[8,1,128]{2,1,0:T(1,128)S(1)}, u32[]{:S(2)}, u32[]{:S(2)}) %all-to-all-start.4) | async-done | bytes 4128 | tf_op jit(solution)/shard_map/all_to_all | solution.py:16
  124.4 5.9 %all-to-all-start.6 = ((f16[16,48,1024]{2,1,0:T(8,128)(2,1)}), f16[16,48,1024]{2,1,0:T(8,128)(2,1)S(1)}, u32[]{:S(2)}, u32[]{:S(2)}) async-start(f16[16,48,1024]{2,1,0:T(8,128)(2,1)} %bitcast.57), calls=%async_computation.6 | async-start | bytes 3145728 | tf_op jit(solution)/shard_map/all_to_all | solution.py:16
  130.3 0.0 collective-permute-done.4
  130.3 3.1 %fusion.20 = f16[384,1024]{1,0:T(8,128)(2,1)} fusion(f32[384,1024]{1,0:T(8,128)} %collective-permute-done.4, f32[768,1024]{1,0:T(8,128)} %copy-done.1), kind=kLoop, calls=%fused_computation.24 | loop fusion | flops 786432 | bytes 3932160 | tf_op jit(solution)/shard_map/convert_element_type | solution.py:86
  133.4 16.8 %all-to-all-done.6 = f16[16,48,1024]{2,1,0:T(8,128)(2,1)S(1)} async-done(((f16[16,48,1024]{2,1,0:T(8,128)(2,1)}), f16[16,48,1024]{2,1,0:T(8,128)(2,1)S(1)}, u32[]{:S(2)}, u32[]{:S(2)}) %all-to-all-start.6) | async-done | bytes 1572896 | tf_op jit(solution)/shard_map/all_to_all | solution.py:16
  150.2 4.8 %all-to-all-start.5 = ((f16[8,48,1024]{2,1,0:T(8,128)(2,1)}), f16[8,48,1024]{2,1,0:T(8,128)(2,1)S(1)}, u32[]{:S(2)}, u32[]{:S(2)}) async-start(f16[8,48,1024]{2,1,0:T(8,128)(2,1)} %bitcast.19), calls=%async_computation.5 | async-start | bytes 1572864 | tf_op jit(solution)/shard_map/all_to_all | solution.py:16
  155.1 1.0 convert_reduce_fusion
  156.1 20.1 %all-to-all-done.5 = f16[8,48,1024]{2,1,0:T(8,128)(2,1)S(1)} async-done(((f16[8,48,1024]{2,1,0:T(8,128)(2,1)}), f16[8,48,1024]{2,1,0:T(8,128)(2,1)S(1)}, u32[]{:S(2)}, u32[]{:S(2)}) %all-to-all-start.5) | async-done | bytes 786464 | tf_op jit(solution)/shard_map/all_to_all | solution.py:16
  176.2 0.8 convert_reduce_fusion.1
  (15 shorter events, 0.2 us)
Async XLA Ops:
  1.7 3.7 %copy-start = (bf16[1,2048,1024]{2,1,0:T(8,128)(2,1)S(1)}, bf16[1,2048,1024]{2,1,0:T(8,128)(2,1)}, u32[]{:S(2)}) copy-start(bf16[1,2048,1024]{2,1,0:T(8,128)(2,1)} %param.8) | copy-start | bytes 12582916
  5.4 3.2 %copy-start.2 = (s32[192]{0:T(256)S(1)}, s32[192]{0:T(256)}, u32[]{:S(2)}) copy-start(s32[192]{0:T(256)} %param.9) | copy-start | bytes 2308
  6.3 12.4 %collective-permute-start = (f32[96,1024]{1,0:T(8,128)S(1)}, f32[96,1024]{1,0:T(8,128)S(1)}, u32[]{:S(2)}, u32[]{:S(2)}) collective-permute-start(f32[96,1024]{1,0:T(8,128)S(1)} %fusion), channel_id=1, source_target_pairs={{0,1},{1,0},{2,3},{3,2},{4,5},{5,4},{6,7},{7,6},{8,9},{9,8},{10,11... | collective-permute-start | bytes 1179656 | tf_op jit(solution)/shard_map/ppermute | solution.py:31
  22.0 9.2 %collective-permute-start.1 = (bf16[48,1024]{1,0:T(8,128)(2,1)S(1)}, bf16[48,1024]{1,0:T(8,128)(2,1)S(1)}, u32[]{:S(2)}, u32[]{:S(2)}) collective-permute-start(bf16[48,1024]{1,0:T(8,128)(2,1)S(1)} %dynamic-slice_bitcast_fusion), channel_id=1, source_target_pairs={{0,2},{2,0},{1,3},{3,1},{4,6},{6,4},{5,7},{7,5},{8,10},{10,8},{9,1... | collective-permute-start | bytes 294920 | tf_op jit(solution)/shard_map/ppermute | solution.py:57
  22.7 16.2 %all-to-all-start = ((s32[8,2,128]{2,1,0:T(2,128)}), s32[8,2,128]{2,1,0:T(2,128)S(1)}, u32[]{:S(2)}, u32[]{:S(2)}) async-start(s32[8,2,128]{2,1,0:T(2,128)} %broadcast_in_dim.31), calls=%async_computation | async-start | bytes 16384 | tf_op jit(solution)/shard_map/all_to_all | solution.py:16
  65.4 27.3 %all-to-all-start.2 = ((bf16[16,48,1024]{2,1,0:T(8,128)(2,1)}), bf16[16,48,1024]{2,1,0:T(8,128)(2,1)S(1)}, u32[]{:S(2)}, u32[]{:S(2)}) async-start(bf16[16,48,1024]{2,1,0:T(8,128)(2,1)} %broadcast_in_dim.33), calls=%async_computation.2 | async-start | bytes 3145728 | tf_op jit(solution)/shard_map/all_to_all | solution.py:16
  72.8 19.8 %collective-permute-start.2 = (bf16[384,1024]{1,0:T(8,128)(2,1)S(1)}, bf16[384,1024]{1,0:T(8,128)(2,1)S(1)}, u32[]{:S(2)}, u32[]{:S(2)}) collective-permute-start(bf16[384,1024]{1,0:T(8,128)(2,1)S(1)} %bitcast.60), channel_id=1, source_target_pairs={{0,2},{2,0},{1,3},{3,1},{4,6},{6,4},{5,7},{7,5},{8,10},{10,8},{9,1... | collective-permute-start | bytes 2359304 | tf_op jit(solution)/shard_map/ppermute | solution.py:63
  92.6 4.6 %copy-start.3 = (bf16[384,1024]{1,0:T(8,128)(2,1)}, bf16[384,1024]{1,0:T(8,128)(2,1)S(1)}, u32[]{:S(2)}) copy-start(bf16[384,1024]{1,0:T(8,128)(2,1)S(1)} %collective-permute-done.2) | copy-start | bytes 2359300
  97.2 2.2 %copy-start.4 = (bf16[768,768]{1,0:T(8,128)(2,1)}, bf16[768,768]{1,0:T(8,128)(2,1)S(1)}, u32[]{:S(2)}) copy-start(bf16[768,768]{1,0:T(8,128)(2,1)S(1)} %get-tuple-element.5) | copy-start | bytes 3538948
  97.9 3.7 %collective-permute-start.3 = (f32[1,128]{1,0:T(1,128)S(1)}, f32[1,128]{1,0:T(1,128)S(1)}, u32[]{:S(2)}, u32[]{:S(2)}) collective-permute-start(f32[1,128]{1,0:T(1,128)S(1)} %broadcast_in_dim.34), channel_id=1, source_target_pairs={{0,2},{2,0},{1,3},{3,1},{4,6},{6,4},{5,7},{7,5},{8,10},{10,8},{9,1... | collective-permute-start | bytes 1544 | tf_op jit(solution)/shard_map/ppermute | solution.py:92
  99.4 1.7 copy-start.1
  101.0 29.3 %collective-permute-start.4 = (f32[384,1024]{1,0:T(8,128)S(1)}, f32[384,1024]{1,0:T(8,128)}, u32[]{:S(2)}, u32[]{:S(2)}) collective-permute-start(f32[384,1024]{1,0:T(8,128)S(1)} %slice.28), channel_id=1, source_target_pairs={{0,2},{2,0},{1,3},{3,1},{4,6},{6,4},{5,7},{7,5},{8,10},{10,8},{9,1... | collective-permute-start | bytes 4718600 | tf_op jit(solution)/shard_map/ppermute | solution.py:85
  112.7 11.7 %all-to-all-start.4 = ((f32[8,1,128]{2,1,0:T(1,128)}), f32[8,1,128]{2,1,0:T(1,128)S(1)}, u32[]{:S(2)}, u32[]{:S(2)}) async-start(f32[8,1,128]{2,1,0:T(1,128)} %broadcast_in_dim.36), calls=%async_computation.4 | async-start | bytes 8192 | tf_op jit(solution)/shard_map/all_to_all | solution.py:16
  124.4 25.8 %all-to-all-start.6 = ((f16[16,48,1024]{2,1,0:T(8,128)(2,1)}), f16[16,48,1024]{2,1,0:T(8,128)(2,1)S(1)}, u32[]{:S(2)}, u32[]{:S(2)}) async-start(f16[16,48,1024]{2,1,0:T(8,128)(2,1)} %bitcast.57), calls=%async_computation.6 | async-start | bytes 3145728 | tf_op jit(solution)/shard_map/all_to_all | solution.py:16
  150.2 26.0 %all-to-all-start.5 = ((f16[8,48,1024]{2,1,0:T(8,128)(2,1)}), f16[8,48,1024]{2,1,0:T(8,128)(2,1)S(1)}, u32[]{:S(2)}, u32[]{:S(2)}) async-start(f16[8,48,1024]{2,1,0:T(8,128)(2,1)} %bitcast.19), calls=%async_computation.5 | async-start | bytes 1572864 | tf_op jit(solution)/shard_map/all_to_all | solution.py:16

commit v2 on v1

v2 whole, which is shorter than its diff:
```python
import jax
import jax.numpy as jnp
from jax import lax
from jax.sharding import Mesh
from jax.sharding import PartitionSpec as P

DP = ("xl", "y", "z")
PLANE = ("xl", "y", "tensor")
ALL = ("xl", "y", "z", "section", "tensor")
SWAP = [(0, 1), (1, 0)]
OFFSETS = (0, -1, 1, -2, 2, -3, 3, 4)
F32 = jnp.float32
SENT = jnp.float16


def exchanged(parts, axes):
    return lax.all_to_all(parts, axes, split_axis=0, concat_axis=0, tiled=True)


def copies(array, axes):
    return exchanged(jnp.broadcast_to(array, (lax.axis_size(axes), *array.shape)), axes)


def to_offset(array, offset):
    n = lax.axis_size("z")
    return lax.ppermute(array, "z", [(i, (i + offset) % n) for i in range(n)])


def flipped(array, axis, bit):
    n = lax.axis_size(axis)
    return lax.ppermute(array, axis, [(i, i ^ bit) for i in range(n)])


def ring_gathered(own):
    below, above = to_offset(own, 1), to_offset(own, -1)
    below2, above2 = to_offset(below, 1), to_offset(above, -1)
    below3, above3 = to_offset(below2, 1), to_offset(above2, -1)
    across = to_offset(below2, 2)
    return [own, below, above, below2, above2, below3, above3, across]


def ring_summed(parts):
    own, below, above, below2, above2, below3, above3, across = parts
    up = to_offset(above3.astype(SENT), 1)
    far = to_offset(across.astype(SENT), 2)
    down = to_offset(below3.astype(SENT), -1)
    up = to_offset((above2 + up.astype(F32) + far.astype(F32)).astype(SENT), 1)
    down = to_offset((below2 + down.astype(F32)).astype(SENT), -1)
    up = to_offset((above + up.astype(F32)).astype(SENT), 1)
    down = to_offset((below + down.astype(F32)).astype(SENT), -1)
    return own + up.astype(F32) + down.astype(F32)


def summed_everywhere(value):
    value = value + flipped(value, "section", 1)
    for axis in ("tensor", "xl", "y", "z"):
        bit = 1
        while bit < lax.axis_size(axis):
            value = value + flipped(value, axis, bit)
            bit *= 2
    return value


def tower(inputs, up, down, tensor, pair_rows):
    rows, width = inputs.shape
    split = inputs.reshape(2, 2, rows // 4, width)
    kept = lax.dynamic_slice_in_dim(split, tensor, 1, 1).reshape(rows // 2, width)
    given = lax.dynamic_slice_in_dim(split, 1 - tensor, 1, 1).reshape(rows // 2, width)
    ordered = jnp.concatenate([given, kept], axis=0)
    hidden = jax.nn.gelu(jnp.dot(ordered, up, preferred_element_type=F32)).astype(jnp.bfloat16)
    sent = jnp.dot(hidden[: rows // 2], down, preferred_element_type=F32)
    arrived = lax.ppermute(sent, "tensor", SWAP)
    own = jnp.dot(hidden[rows // 2 :], down, preferred_element_type=F32) + kept.astype(F32)
    own, pair_rows = lax.optimization_barrier((own, pair_rows))
    pairs = jnp.stack(
        [pair_rows] + [to_offset(pair_rows, -offset) for offset in OFFSETS[1:]], axis=1
    )
    raw = own + arrived
    norms = lax.rsqrt(jnp.sum(raw * raw, axis=-1, keepdims=True) + 1e-06)
    return (raw * norms).astype(jnp.bfloat16).reshape(2, rows // 4, width), pairs


def local(tower_input, up_weight, down_weight, pair, scale, bias):
    section = lax.axis_index("section")
    tensor = lax.axis_index("tensor")
    n_z = lax.axis_size("z")
    n_plane = lax.axis_size(PLANE)
    scale_value, bias_value = scale[0], bias[0]
    quarter = tower_input.shape[1] // 4
    total = lax.axis_size(ALL) * quarter
    half = n_z * quarter

    pair_rows = lax.dynamic_slice_in_dim(pair.reshape(2, 2, quarter), tensor, 1, 1)
    embedded, pairs = tower(
        tower_input[0], up_weight[0], down_weight[0], tensor, pair_rows.reshape(2, quarter)
    )
    pair_mine = lax.dynamic_index_in_dim(pairs, section, 0, keepdims=False).reshape(-1)
    pair_other = lax.dynamic_index_in_dim(pairs, 1 - section, 0, keepdims=False).reshape(-1)
    pair_all = jnp.concatenate([pair_mine, pair_other])

    mine = lax.dynamic_index_in_dim(embedded, section, 0, keepdims=False)
    given = lax.dynamic_index_in_dim(embedded, 1 - section, 0, keepdims=False)
    got = lax.ppermute(given, "section", SWAP)
    slides = jnp.where(section == 0, mine, got)
    reports = jnp.where(section == 0, got, mine)

    reports_all = copies(reports, PLANE).reshape(n_plane * quarter, -1)
    slides_z = jnp.concatenate(ring_gathered(slides), axis=0)
    slides_all = jnp.concatenate([slides_z, lax.ppermute(slides_z, "section", SWAP)], axis=0)

    place = jnp.arange(n_plane * quarter, dtype=jnp.int32)
    member, row = place // quarter, place % quarter
    owner = ((member // 2 * n_z + lax.axis_index("z")) * 2 + section) * 2 + member % 2
    columns = owner * quarter + row

    dots = lax.dot_general(
        slides_all, reports_all, (((1,), (1,)), ((), ())), preferred_element_type=F32
    )
    logits = scale_value * dots + bias_value
    match = pair_all[:, None] == columns[None, :]
    turned = jnp.where(match, -logits, logits)
    small = jnp.exp(-jnp.abs(turned))
    loss_part = jnp.sum(jnp.maximum(turned, 0.0) + jnp.log1p(small))
    sigmoid = jnp.where(turned >= 0, 1.0, small) / (1.0 + small)
    weight = (jnp.where(match, -scale_value, scale_value) * sigmoid).astype(jnp.bfloat16)

    report_part = lax.dot_general(
        weight, slides_all, (((0,), (0,)), ((), ())), preferred_element_type=F32
    ).astype(SENT)
    report_part, weight, loss_part = lax.optimization_barrier((report_part, weight, loss_part))
    report_terms = exchanged(report_part.reshape(n_plane, quarter, -1), PLANE)
    slide_other = jnp.dot(weight[half:], reports_all, preferred_element_type=F32)
    slide_back = lax.ppermute(slide_other, "section", SWAP)
    slide_mine = jnp.dot(weight[:half], reports_all, preferred_element_type=F32) + slide_back
    parts = [slide_mine[k * quarter : (k + 1) * quarter] for k in range(n_z)]
    slide_grad = ring_summed(parts)
    loss = summed_everywhere(jnp.broadcast_to(loss_part, (1, 128)))[0, :1] / total
    report_grad = report_terms.astype(F32).sum(axis=0)
    return (loss, slide_grad, report_grad)


def solution(mesh):
    finer = Mesh(
        mesh.devices.reshape(2, 4, 8, mesh.shape["section"], mesh.shape["tensor"]),
        ALL,
    )
    return jax.shard_map(
        local,
        mesh=finer,
        in_specs=(
            P("section", DP, None),
            P("section", None, "tensor"),
            P("section", "tensor", None),
            P(DP),
            P(),
            P(),
        ),
        out_specs=(P(), P(ALL, None), P(ALL, None)),
        check_vma=False,
    )
```

time: 179 us -> 170 us (0.950); the launches traced: 178 us -> 167 us
  blocking collectives: 34.9 us -> 0 us
  starting transfers between devices: 33.7 us -> 53 us
  waiting for transfers between devices: 76.4 us -> 80.4 us
  matrix products: 17.7 us -> 19.8 us
    ppermute x2 -> x30, waiting for transfers between devices: 0.01 us -> 68 us  [the longest x21 39.4 us: to_offset(): return lax.ppermute(array, 'z', [(i, (i + offset) % n) for i in range(n)])]
    all_to_all x5 -> x2, waiting for transfers between devices: 66.4 us -> 0.01 us  [exchanged(): return lax.all_to_all(parts, axes, split_axis=0, concat_axis=0, tiled=True)]
    ppermute x2 -> x30, starting transfers between devices: 0.59 us -> 37.7 us  [the longest x21 33.2 us: to_offset(): return lax.ppermute(array, 'z', [(i, (i + offset) % n) for i in range(n)])]
    all_to_all x2 -> x0, blocking collectives: 34.9 us -> none  [exchanged(): return lax.all_to_all(parts, axes, split_axis=0, concat_axis=0, tiled=True)]
    all_to_all x5 -> x2, starting transfers between devices: 30.7 us -> 14.7 us  [exchanged(): return lax.all_to_all(parts, axes, split_axis=0, concat_axis=0, tiled=True)]
    convert_element_type x2 -> x4, other arithmetic: 3.21 us -> 0.24 us  [the longest x1 0.1 us: tower(): (raw * norms).astype(jnp.bfloat16).reshape(2, rows // 4, width)]
    add x1 -> x9, other arithmetic: 0.65 us -> 2.95 us  [the longest x1 1.64 us: ring_summed(): return own + up.astype(F32) + down.astype(F32)]
    dot_general x1, matrix products: 0.82 us -> 2.99 us  [tower(): sent = jnp.dot(hidden[:rows // 2], down, preferred_element_type=F32)]
  transfers between devices with their start and end apart: 10 -> 35, of which waited for: 6 -> 20; matrix products, arithmetic and copies ran while one was open for 7% -> 7% of each run, Pallas kernels for 0% -> 0%
where the time goes in v2:
time: 170 us; the launch traced here: 167 us
  waiting for transfers between devices  80.4 us (47%)
  starting transfers between devices  53 us (31%)
  matrix products  19.8 us (12%)
  local copies, waits for them, and re-layouts  6.16 us (4%)
  other arithmetic  4.42 us (3%)
  between operations  3.43 us (2%)
    ppermute x21, waiting for transfers between devices, to_offset(): return lax.ppermute(array, 'z', [(i, (i + offset) % n) for i in range(n)])  39.4 us
    ppermute x21, starting transfers between devices, to_offset(): return lax.ppermute(array, 'z', [(i, (i + offset) % n) for i in range(n)])  33.2 us
    ppermute x8, waiting for transfers between devices, flipped(): return lax.ppermute(array, axis, [(i, i ^ bit) for i in range(n)])  28.6 us
    all_to_all x2, starting transfers between devices, exchanged(): return lax.all_to_all(parts, axes, split_axis=0, concat_axis=0, tiled=True)  14.7 us
    ppermute x1, waiting for transfers between devices, tower(): arrived = lax.ppermute(sent, 'tensor', SWAP)  10.1 us
    dot_general x1, matrix products, local(): lax.dot_general(slides_all, reports_all, (((1,), (1,)), ((), ())), prefer...  5.35 us
    ppermute x8, starting transfers between devices, flipped(): return lax.ppermute(array, axis, [(i, i ^ bit) for i in range(n)])  4.35 us
    dot_general x1, matrix products, tower(): jnp.dot(ordered, up, preferred_element_type=F32)  3.69 us
  transfers between devices with their start and end apart: 35, of which 20 were waited for; matrix products, arithmetic and copies ran while one was open for 7% of the time, Pallas kernels for 0%

profile of v2, /device:TPU:4, one launch (start us, length us, event | category | flops | bytes accessed | tf_op | source)
XLA Modules:
  0.0 167.2 jit_solution(10820039373180326242)
XLA Ops:
  1.4 1.1 constant_dynamic-slice_fusion.2
  2.5 3.7 %fusion.17 = bf16[192,2048]{1,0:T(8,128)(2,1)S(1)} fusion(bf16[1,1024,2048]{2,1,0:T(8,128)(2,1)} %param.7, bf16[96,1024]{1,0:T(8,128)(2,1)S(1)} %bitcast.64, bf16[96,1024]{1,0:T(8,128)(2,1)S(1)} %bitcast.69), kind=kOutput, calls=%fused_computation.22 | convolution fusion | flops 809631744 | bytes 5373952 | tf_op jit(solution)/shard_map/dot_general | solution.py:70
  7.0 7.3 %collective-permute-start.6 = (s32[2,48]{1,0:T(2,128)S(1)}, s32[2,48]{1,0:T(2,128)S(1)}, u32[]{:S(2)}, u32[]{:S(2)}) collective-permute-start(s32[2,48]{1,0:T(2,128)S(1)} %bitcast.70), channel_id=1, source_target_pairs={{0,16},{4,20},{8,24},{12,28},{16,0},{20,4},{24,8},{28,12},{1,17},{... | collective-permute-start | bytes 1160 | tf_op jit(solution)/shard_map/ppermute | solution.py:26
  14.3 3.8 %collective-permute-start.4 = (s32[2,48]{1,0:T(2,128)S(1)}, s32[2,48]{1,0:T(2,128)S(1)}, u32[]{:S(2)}, u32[]{:S(2)}) collective-permute-start(s32[2,48]{1,0:T(2,128)S(1)} %bitcast.72), channel_id=1, source_target_pairs={{0,12},{4,16},{8,20},{12,24},{16,28},{20,0},{24,4},{28,8},{1,13},{... | collective-permute-start | bytes 1160 | tf_op jit(solution)/shard_map/ppermute | solution.py:26
  18.1 1.3 collective-permute-start.1
  20.4 3.0 %fusion = f32[96,1024]{1,0:T(8,128)S(1)} fusion(bf16[1,2048,1024]{2,1,0:T(8,128)(2,1)} %param.8, bf16[192,2048]{1,0:T(8,128)(2,1)S(1)} %fusion.17), kind=kOutput, calls=%fused_computation | convolution fusion | flops 402653184 | bytes 4980736 | tf_op jit(solution)/shard_map/dot_general | solution.py:71
  25.9 10.1 %collective-permute-done.7 = f32[96,1024]{1,0:T(8,128)S(1)} collective-permute-done((f32[96,1024]{1,0:T(8,128)S(1)}, f32[96,1024]{1,0:T(8,128)S(1)}, u32[]{:S(2)}, u32[]{:S(2)}) %collective-permute-start.7) | collective-permute-done | bytes 393248 | tf_op jit(solution)/shard_map/ppermute | solution.py:72
  36.0 2.2 %collective-permute-start.2 = (s32[2,48]{1,0:T(2,128)S(1)}, s32[2,48]{1,0:T(2,128)S(1)}, u32[]{:S(2)}, u32[]{:S(2)}) collective-permute-start(s32[2,48]{1,0:T(2,128)S(1)} %bitcast.77), channel_id=1, source_target_pairs={{0,8},{4,12},{8,16},{12,20},{16,24},{20,28},{24,0},{28,4},{1,9},{5... | collective-permute-start | bytes 1160 | tf_op jit(solution)/shard_map/ppermute | solution.py:26
  38.5 3.2 %collective-permute-done.2 = s32[2,48]{1,0:T(2,128)S(1)} collective-permute-done((s32[2,48]{1,0:T(2,128)S(1)}, s32[2,48]{1,0:T(2,128)S(1)}, u32[]{:S(2)}, u32[]{:S(2)}) %collective-permute-start.2) | collective-permute-done | bytes 416 | tf_op jit(solution)/shard_map/ppermute | solution.py:26
  41.7 1.3 collective-permute-done.8
  43.0 1.8 %collective-permute-start.9 = (bf16[48,1024]{1,0:T(8,128)(2,1)S(1)}, bf16[48,1024]{1,0:T(8,128)(2,1)S(1)}, u32[]{:S(2)}, u32[]{:S(2)}) collective-permute-start(bf16[48,1024]{1,0:T(8,128)(2,1)S(1)} %get-tuple-element.16), channel_id=1, source_target_pairs={{0,4},{4,8},{8,12},{12,16},{16,20},{20,24},{24,28},{28,0},{1,5},{5... | collective-permute-start | bytes 294920 | tf_op jit(solution)/shard_map/ppermute | solution.py:26
  44.8 1.4 broadcast_in_dim.23
  46.2 7.5 %all-to-all-start = ((bf16[16,48,1024]{2,1,0:T(8,128)(2,1)}), bf16[16,48,1024]{2,1,0:T(8,128)(2,1)S(1)}, u32[]{:S(2)}, u32[]{:S(2)}) async-start(bf16[16,48,1024]{2,1,0:T(8,128)(2,1)} %broadcast_in_dim.23), calls=%async_computation | async-start | bytes 3145728 | tf_op jit(solution)/shard_map/all_to_all | solution.py:17
  53.7 1.6 collective-permute-start.10
  55.3 3.1 %collective-permute-done.10 = bf16[48,1024]{1,0:T(8,128)(2,1)S(1)} collective-permute-done((bf16[48,1024]{1,0:T(8,128)(2,1)S(1)}, bf16[48,1024]{1,0:T(8,128)(2,1)S(1)}, u32[]{:S(2)}, u32[]{:S(2)}) %collective-permute-start.10) | collective-permute-done | bytes 98336 | tf_op jit(solution)/shard_map/ppermute | solution.py:26
  58.4 5.8 %collective-permute-done.11 = bf16[48,1024]{1,0:T(8,128)(2,1)S(1)} collective-permute-done((bf16[48,1024]{1,0:T(8,128)(2,1)S(1)}, bf16[48,1024]{1,0:T(8,128)(2,1)S(1)}, u32[]{:S(2)}, u32[]{:S(2)}) %collective-permute-start.11) | collective-permute-done | bytes 98336 | tf_op jit(solution)/shard_map/ppermute | solution.py:26
  64.2 1.5 collective-permute-start.12
  65.7 3.1 %collective-permute-done.12 = bf16[48,1024]{1,0:T(8,128)(2,1)S(1)} collective-permute-done((bf16[48,1024]{1,0:T(8,128)(2,1)S(1)}, bf16[48,1024]{1,0:T(8,128)(2,1)S(1)}, u32[]{:S(2)}, u32[]{:S(2)}) %collective-permute-start.12) | collective-permute-done | bytes 98336 | tf_op jit(solution)/shard_map/ppermute | solution.py:26
  68.8 5.8 %collective-permute-done.13 = bf16[48,1024]{1,0:T(8,128)(2,1)S(1)} collective-permute-done((bf16[48,1024]{1,0:T(8,128)(2,1)S(1)}, bf16[48,1024]{1,0:T(8,128)(2,1)S(1)}, u32[]{:S(2)}, u32[]{:S(2)}) %collective-permute-start.13) | collective-permute-done | bytes 98336 | tf_op jit(solution)/shard_map/ppermute | solution.py:26
  74.7 1.5 collective-permute-start.14
  76.2 3.1 %collective-permute-done.14 = bf16[48,1024]{1,0:T(8,128)(2,1)S(1)} collective-permute-done((bf16[48,1024]{1,0:T(8,128)(2,1)S(1)}, bf16[48,1024]{1,0:T(8,128)(2,1)S(1)}, u32[]{:S(2)}, u32[]{:S(2)}) %collective-permute-start.14) | collective-permute-done | bytes 98336 | tf_op jit(solution)/shard_map/ppermute | solution.py:26
  79.3 0.9 collective-permute-start.15
  80.2 6.8 %collective-permute-done.15 = bf16[48,1024]{1,0:T(8,128)(2,1)S(1)} collective-permute-done((bf16[48,1024]{1,0:T(8,128)(2,1)S(1)}, bf16[48,1024]{1,0:T(8,128)(2,1)S(1)}, u32[]{:S(2)}, u32[]{:S(2)}) %collective-permute-start.15) | collective-permute-done | bytes 98336 | tf_op jit(solution)/shard_map/ppermute | solution.py:26
  88.4 1.0 collective-permute-done.16
  89.4 1.0 constant_dynamic-update-slice_fusion.16
  90.4 5.3 %add_reduce_fusion = (f32[]{:T(128)}, bf16[768,768]{1,0:T(8,128)(2,1)S(1)}) fusion(f32[]{:T(128)} %bitcast.58, f32[]{:T(128)S(6)} %neg.9, s32[768]{0:T(1024)S(1)} %get-tuple-element.45, s32[768]{0:T(1024)S(1)} %get-tuple-element.46, f32[]{:T(128)} %bitcast.59, bf16[768,1024]{1,0:T(8,128)(2,1)} %constant_dynamic-update-slice_fusion.16, ...), kind=kOutput, calls=%fused_computation.12 | convolution fusion | flops 1217986560 | bytes 4331536 | tf_op jit(solution)/shard_map/dot_general | solution.py:116
  95.8 2.6 %convolution_convert_fusion = f16[768,1024]{1,0:T(8,128)(2,1)} fusion(bf16[768,768]{1,0:T(8,128)(2,1)S(1)} %get-tuple-element.11, bf16[768,1024]{1,0:T(8,128)(2,1)S(1)} %copy-done.4), kind=kOutput, calls=%fused_computation.14 | convolution fusion | flops 1208745984 | bytes 4325376 | tf_op jit(solution)/shard_map/dot_general | solution.py:127
  98.4 1.9 %fusion.23 = f32[384,1024]{1,0:T(8,128)} fusion(bf16[768,1024]{1,0:T(8,128)(2,1)S(1)} %bitcast.61, bf16[768,768]{1,0:T(8,128)(2,1)S(1)} %get-tuple-element.11), kind=kOutput, calls=%fused_computation.25 | convolution fusion | flops 603979776 | bytes 3735552 | tf_op jit(solution)/shard_map/dot_general | solution.py:132
  100.4 7.2 %all-to-all-start.1 = ((f16[16,48,1024]{2,1,0:T(8,128)(2,1)}), f16[16,48,1024]{2,1,0:T(8,128)(2,1)S(1)}, u32[]{:S(2)}, u32[]{:S(2)}) async-start(f16[16,48,1024]{2,1,0:T(8,128)(2,1)} %bitcast.63), calls=%async_computation.1 | async-start | bytes 3145728 | tf_op jit(solution)/shard_map/all_to_all | solution.py:17
  107.7 2.4 %fusion.58 = (f16[384,1024]{1,0:T(8,128)(2,1)S(1)}, f32[384,1024]{1,0:T(8,128)S(1)}) fusion(f32[384,1024]{1,0:T(8,128)} %collective-permute-done.25, bf16[768,1024]{1,0:T(8,128)(2,1)S(1)} %bitcast.62, bf16[768,768]{1,0:T(8,128)(2,1)} %copy-done.2), kind=kOutput, calls=%fused_computation.113 | convolution fusion | flops 604766208 | bytes 6094848 | tf_op jit(solution)/shard_map/dot_general | solution.py:134
  110.2 1.9 %collective-permute-start.27 = (f16[48,1024]{1,0:T(8,128)(2,1)S(1)}, f16[48,1024]{1,0:T(8,128)(2,1)S(1)}, u32[]{:S(2)}, u32[]{:S(2)}) collective-permute-start(f16[48,1024]{1,0:T(8,128)(2,1)S(1)} %get-tuple-element.25), channel_id=1, source_target_pairs={{0,8},{4,12},{8,16},{12,20},{16,24},{20,28},{24,0},{28,4},{1,9},{5... | collective-permute-start | bytes 294920 | tf_op jit(solution)/shard_map/ppermute | solution.py:26
  112.9 1.4 collective-permute-start.30
  114.3 4.8 %collective-permute-done.26 = f16[48,1024]{1,0:T(8,128)(2,1)S(1)} collective-permute-done((f16[48,1024]{1,0:T(8,128)(2,1)S(1)}, f16[48,1024]{1,0:T(8,128)(2,1)S(1)}, u32[]{:S(2)}, u32[]{:S(2)}) %collective-permute-start.26) | collective-permute-done | bytes 98336 | tf_op jit(solution)/shard_map/ppermute | solution.py:26
  119.2 2.8 %collective-permute-start.28 = (f16[48,1024]{1,0:T(8,128)(2,1)S(1)}, f16[48,1024]{1,0:T(8,128)(2,1)S(1)}, u32[]{:S(2)}, u32[]{:S(2)}) collective-permute-start(f16[48,1024]{1,0:T(8,128)(2,1)S(1)} %fusion.34), channel_id=1, source_target_pairs={{0,4},{4,8},{8,12},{12,16},{16,20},{20,24},{24,28},{28,0},{1,5},{5... | collective-permute-start | bytes 294920 | tf_op jit(solution)/shard_map/ppermute | solution.py:26
  123.1 2.2 %collective-permute-done.28 = f16[48,1024]{1,0:T(8,128)(2,1)S(1)} collective-permute-done((f16[48,1024]{1,0:T(8,128)(2,1)S(1)}, f16[48,1024]{1,0:T(8,128)(2,1)S(1)}, u32[]{:S(2)}, u32[]{:S(2)}) %collective-permute-start.28) | collective-permute-done | bytes 98336 | tf_op jit(solution)/shard_map/ppermute | solution.py:26
  125.4 4.7 %collective-permute-done.18 = f32[1,128]{1,0:T(1,128)S(1)} collective-permute-done((f32[1,128]{1,0:T(1,128)S(1)}, f32[1,128]{1,0:T(1,128)S(1)}, u32[]{:S(2)}, u32[]{:S(2)}) %collective-permute-start.18) | collective-permute-done | bytes 544 | tf_op jit(solution)/shard_map/ppermute | solution.py:31
  131.4 3.1 %collective-permute-done.19 = f32[1,128]{1,0:T(1,128)S(1)} collective-permute-done((f32[1,128]{1,0:T(1,128)S(1)}, f32[1,128]{1,0:T(1,128)S(1)}, u32[]{:S(2)}, u32[]{:S(2)}) %collective-permute-start.19) | collective-permute-done | bytes 544 | tf_op jit(solution)/shard_map/ppermute | solution.py:31
  134.5 3.5 %collective-permute-done.20 = f32[1,128]{1,0:T(1,128)S(1)} collective-permute-done((f32[1,128]{1,0:T(1,128)S(1)}, f32[1,128]{1,0:T(1,128)S(1)}, u32[]{:S(2)}, u32[]{:S(2)}) %collective-permute-start.20) | collective-permute-done | bytes 544 | tf_op jit(solution)/shard_map/ppermute | solution.py:31
  138.0 1.1 collective-permute-start.21
  139.1 3.9 %collective-permute-done.21 = f32[1,128]{1,0:T(1,128)S(1)} collective-permute-done((f32[1,128]{1,0:T(1,128)S(1)}, f32[1,128]{1,0:T(1,128)S(1)}, u32[]{:S(2)}, u32[]{:S(2)}) %collective-permute-start.21) | collective-permute-done | bytes 544 | tf_op jit(solution)/shard_map/ppermute | solution.py:31
  143.1 3.5 %collective-permute-done.22 = f32[1,128]{1,0:T(1,128)S(1)} collective-permute-done((f32[1,128]{1,0:T(1,128)S(1)}, f32[1,128]{1,0:T(1,128)S(1)}, u32[]{:S(2)}, u32[]{:S(2)}) %collective-permute-start.22) | collective-permute-done | bytes 544 | tf_op jit(solution)/shard_map/ppermute | solution.py:31
  146.6 4.4 %collective-permute-done.23 = f32[1,128]{1,0:T(1,128)S(1)} collective-permute-done((f32[1,128]{1,0:T(1,128)S(1)}, f32[1,128]{1,0:T(1,128)S(1)}, u32[]{:S(2)}, u32[]{:S(2)}) %collective-permute-start.23) | collective-permute-done | bytes 544 | tf_op jit(solution)/shard_map/ppermute | solution.py:31
  151.1 2.1 %collective-permute-start.24 = (f32[1,128]{1,0:T(1,128)S(1)}, f32[1,128]{1,0:T(1,128)S(1)}, u32[]{:S(2)}, u32[]{:S(2)}) collective-permute-start(f32[1,128]{1,0:T(1,128)S(1)} %add.197), channel_id=1, source_target_pairs={{0,16},{4,20},{8,24},{12,28},{16,0},{20,4},{24,8},{28,12},{1,17},{... | collective-permute-start | bytes 1544 | tf_op jit(solution)/shard_map/ppermute | solution.py:31
  153.2 5.3 %collective-permute-done.24 = f32[1,128]{1,0:T(1,128)S(1)} collective-permute-done((f32[1,128]{1,0:T(1,128)S(1)}, f32[1,128]{1,0:T(1,128)S(1)}, u32[]{:S(2)}, u32[]{:S(2)}) %collective-permute-start.24) | collective-permute-done | bytes 544 | tf_op jit(solution)/shard_map/ppermute | solution.py:31
  158.7 3.3 %collective-permute-start.32 = (f16[48,1024]{1,0:T(8,128)(2,1)S(1)}, f16[48,1024]{1,0:T(8,128)(2,1)S(1)}, u32[]{:S(2)}, u32[]{:S(2)}) collective-permute-start(f16[48,1024]{1,0:T(8,128)(2,1)S(1)} %fusion.32), channel_id=1, source_target_pairs={{0,28},{4,0},{8,4},{12,8},{16,12},{20,16},{24,20},{28,24},{1,29},{... | collective-permute-start | bytes 294920 | tf_op jit(solution)/shard_map/ppermute | solution.py:26
  162.0 1.0 convert_reduce_fusion
  163.0 1.4 collective-permute-done.29
  164.5 1.6 fusion.36
  (84 shorter events, 9.2 us)
Async XLA Ops:
  2.5 3.7 %copy-start = (bf16[1,2048,1024]{2,1,0:T(8,128)(2,1)S(1)}, bf16[1,2048,1024]{2,1,0:T(8,128)(2,1)}, u32[]{:S(2)}) copy-start(bf16[1,2048,1024]{2,1,0:T(8,128)(2,1)} %param.8) | copy-start | bytes 12582916
  7.0 80.2 %collective-permute-start.6 = (s32[2,48]{1,0:T(2,128)S(1)}, s32[2,48]{1,0:T(2,128)S(1)}, u32[]{:S(2)}, u32[]{:S(2)}) collective-permute-start(s32[2,48]{1,0:T(2,128)S(1)} %bitcast.70), channel_id=1, source_target_pairs={{0,16},{4,20},{8,24},{12,28},{16,0},{20,4},{24,8},{28,12},{1,17},{... | collective-permute-start | bytes 1160 | tf_op jit(solution)/shard_map/ppermute | solution.py:26
  14.3 72.9 %collective-permute-start.5 = (s32[2,48]{1,0:T(2,128)S(1)}, s32[2,48]{1,0:T(2,128)S(1)}, u32[]{:S(2)}, u32[]{:S(2)}) collective-permute-start(s32[2,48]{1,0:T(2,128)S(1)} %bitcast.71), channel_id=1, source_target_pairs={{0,20},{4,24},{8,28},{12,0},{16,4},{20,8},{24,12},{28,16},{1,21},{... | collective-permute-start | bytes 1160 | tf_op jit(solution)/shard_map/ppermute | solution.py:26
  14.3 72.9 %collective-permute-start.4 = (s32[2,48]{1,0:T(2,128)S(1)}, s32[2,48]{1,0:T(2,128)S(1)}, u32[]{:S(2)}, u32[]{:S(2)}) collective-permute-start(s32[2,48]{1,0:T(2,128)S(1)} %bitcast.72), channel_id=1, source_target_pairs={{0,12},{4,16},{8,20},{12,24},{16,28},{20,0},{24,4},{28,8},{1,13},{... | collective-permute-start | bytes 1160 | tf_op jit(solution)/shard_map/ppermute | solution.py:26
  18.1 7.2 %collective-permute-start.1 = (s32[2,48]{1,0:T(2,128)S(1)}, s32[2,48]{1,0:T(2,128)S(1)}, u32[]{:S(2)}, u32[]{:S(2)}) collective-permute-start(s32[2,48]{1,0:T(2,128)S(1)} %bitcast.73), channel_id=1, source_target_pairs={{0,28},{4,0},{8,4},{12,8},{16,12},{20,16},{24,20},{28,24},{1,29},{... | collective-permute-start | bytes 1160 | tf_op jit(solution)/shard_map/ppermute | solution.py:26
  19.4 5.2 %collective-permute-start = (s32[2,48]{1,0:T(2,128)S(1)}, s32[2,48]{1,0:T(2,128)S(1)}, u32[]{:S(2)}, u32[]{:S(2)}) collective-permute-start(s32[2,48]{1,0:T(2,128)S(1)} %bitcast.74), channel_id=1, source_target_pairs={{0,4},{4,8},{8,12},{12,16},{16,20},{20,24},{24,28},{28,0},{1,5},{5... | collective-permute-start | bytes 1160 | tf_op jit(solution)/shard_map/ppermute | solution.py:26
  24.7 11.3 %collective-permute-start.7 = (f32[96,1024]{1,0:T(8,128)S(1)}, f32[96,1024]{1,0:T(8,128)S(1)}, u32[]{:S(2)}, u32[]{:S(2)}) collective-permute-start(f32[96,1024]{1,0:T(8,128)S(1)} %fusion), channel_id=1, source_target_pairs={{0,1},{1,0},{2,3},{3,2},{4,5},{5,4},{6,7},{7,6},{8,9},{9,8},{10,11... | collective-permute-start | bytes 1179656 | tf_op jit(solution)/shard_map/ppermute | solution.py:72
  25.3 61.9 %collective-permute-start.3 = (s32[2,48]{1,0:T(2,128)S(1)}, s32[2,48]{1,0:T(2,128)S(1)}, u32[]{:S(2)}, u32[]{:S(2)}) collective-permute-start(s32[2,48]{1,0:T(2,128)S(1)} %bitcast.76), channel_id=1, source_target_pairs={{0,24},{4,28},{8,0},{12,4},{16,8},{20,12},{24,16},{28,20},{1,25},{... | collective-permute-start | bytes 1160 | tf_op jit(solution)/shard_map/ppermute | solution.py:26
  36.0 5.7 %collective-permute-start.2 = (s32[2,48]{1,0:T(2,128)S(1)}, s32[2,48]{1,0:T(2,128)S(1)}, u32[]{:S(2)}, u32[]{:S(2)}) collective-permute-start(s32[2,48]{1,0:T(2,128)S(1)} %bitcast.77), channel_id=1, source_target_pairs={{0,8},{4,12},{8,16},{12,20},{16,24},{20,28},{24,0},{28,4},{1,9},{5... | collective-permute-start | bytes 1160 | tf_op jit(solution)/shard_map/ppermute | solution.py:26
  41.7 1.3 collective-permute-start.8
  43.0 10.7 %collective-permute-start.9 = (bf16[48,1024]{1,0:T(8,128)(2,1)S(1)}, bf16[48,1024]{1,0:T(8,128)(2,1)S(1)}, u32[]{:S(2)}, u32[]{:S(2)}) collective-permute-start(bf16[48,1024]{1,0:T(8,128)(2,1)S(1)} %get-tuple-element.16), channel_id=1, source_target_pairs={{0,4},{4,8},{8,12},{12,16},{16,20},{20,24},{24,28},{28,0},{1,5},{5... | collective-permute-start | bytes 294920 | tf_op jit(solution)/shard_map/ppermute | solution.py:26
  46.2 44.2 %all-to-all-start = ((bf16[16,48,1024]{2,1,0:T(8,128)(2,1)}), bf16[16,48,1024]{2,1,0:T(8,128)(2,1)S(1)}, u32[]{:S(2)}, u32[]{:S(2)}) async-start(bf16[16,48,1024]{2,1,0:T(8,128)(2,1)} %broadcast_in_dim.23), calls=%async_computation | async-start | bytes 3145728 | tf_op jit(solution)/shard_map/all_to_all | solution.py:17
  53.7 4.7 %collective-permute-start.10 = (bf16[48,1024]{1,0:T(8,128)(2,1)S(1)}, bf16[48,1024]{1,0:T(8,128)(2,1)S(1)}, u32[]{:S(2)}, u32[]{:S(2)}) collective-permute-start(bf16[48,1024]{1,0:T(8,128)(2,1)S(1)} %get-tuple-element.16), channel_id=1, source_target_pairs={{0,28},{4,0},{8,4},{12,8},{16,12},{20,16},{24,20},{28,24},{1,29},{... | collective-permute-start | bytes 294920 | tf_op jit(solution)/shard_map/ppermute | solution.py:26
  58.4 5.8 %collective-permute-start.11 = (bf16[48,1024]{1,0:T(8,128)(2,1)S(1)}, bf16[48,1024]{1,0:T(8,128)(2,1)S(1)}, u32[]{:S(2)}, u32[]{:S(2)}) collective-permute-start(bf16[48,1024]{1,0:T(8,128)(2,1)S(1)} %collective-permute-done.9), channel_id=1, source_target_pairs={{0,4},{4,8},{8,12},{12,16},{16,20},{20,24},{24,28},{28,0},{1,5},{5... | collective-permute-start | bytes 294920 | tf_op jit(solution)/shard_map/ppermute | solution.py:26
  64.2 4.6 %collective-permute-start.12 = (bf16[48,1024]{1,0:T(8,128)(2,1)S(1)}, bf16[48,1024]{1,0:T(8,128)(2,1)S(1)}, u32[]{:S(2)}, u32[]{:S(2)}) collective-permute-start(bf16[48,1024]{1,0:T(8,128)(2,1)S(1)} %collective-permute-done.10), channel_id=1, source_target_pairs={{0,28},{4,0},{8,4},{12,8},{16,12},{20,16},{24,20},{28,24},{1,29},{... | collective-permute-start | bytes 294920 | tf_op jit(solution)/shard_map/ppermute | solution.py:26
  68.8 5.8 %collective-permute-start.13 = (bf16[48,1024]{1,0:T(8,128)(2,1)S(1)}, bf16[48,1024]{1,0:T(8,128)(2,1)S(1)}, u32[]{:S(2)}, u32[]{:S(2)}) collective-permute-start(bf16[48,1024]{1,0:T(8,128)(2,1)S(1)} %collective-permute-done.11), channel_id=1, source_target_pairs={{0,4},{4,8},{8,12},{12,16},{16,20},{20,24},{24,28},{28,0},{1,5},{5... | collective-permute-start | bytes 294920 | tf_op jit(solution)/shard_map/ppermute | solution.py:26
  74.7 4.6 %collective-permute-start.14 = (bf16[48,1024]{1,0:T(8,128)(2,1)S(1)}, bf16[48,1024]{1,0:T(8,128)(2,1)S(1)}, u32[]{:S(2)}, u32[]{:S(2)}) collective-permute-start(bf16[48,1024]{1,0:T(8,128)(2,1)S(1)} %collective-permute-done.12), channel_id=1, source_target_pairs={{0,28},{4,0},{8,4},{12,8},{16,12},{20,16},{24,20},{28,24},{1,29},{... | collective-permute-start | bytes 294920 | tf_op jit(solution)/shard_map/ppermute | solution.py:26
  79.3 7.8 %collective-permute-start.15 = (bf16[48,1024]{1,0:T(8,128)(2,1)S(1)}, bf16[48,1024]{1,0:T(8,128)(2,1)S(1)}, u32[]{:S(2)}, u32[]{:S(2)}) collective-permute-start(bf16[48,1024]{1,0:T(8,128)(2,1)S(1)} %collective-permute-done.11), channel_id=1, source_target_pairs={{0,8},{4,12},{8,16},{12,20},{16,24},{20,28},{24,0},{28,4},{1,9},{5... | collective-permute-start | bytes 294920 | tf_op jit(solution)/shard_map/ppermute | solution.py:26
  87.1 1.2 copy-start.3
  87.1 2.4 %collective-permute-start.16 = (bf16[384,1024]{1,0:T(8,128)(2,1)S(1)}, bf16[384,1024]{1,0:T(8,128)(2,1)S(1)}, u32[]{:S(2)}, u32[]{:S(2)}) collective-permute-start(bf16[384,1024]{1,0:T(8,128)(2,1)S(1)} %get-tuple-element.29), channel_id=1, source_target_pairs={{0,2},{2,0},{1,3},{3,1},{4,6},{6,4},{5,7},{7,5},{8,10},{10,8},{9,1... | collective-permute-start | bytes 2359304 | tf_op jit(solution)/shard_map/ppermute | solution.py:109
  90.4 5.4 %copy-start.4 = (bf16[768,1024]{1,0:T(8,128)(2,1)S(1)}, bf16[768,1024]{1,0:T(8,128)(2,1)}, u32[]{:S(2)}) copy-start(bf16[768,1024]{1,0:T(8,128)(2,1)} %constant_dynamic-update-slice_fusion.16) | copy-start | bytes 4718596
  95.8 2.6 %copy-start.2 = (bf16[768,768]{1,0:T(8,128)(2,1)}, bf16[768,768]{1,0:T(8,128)(2,1)S(1)}, u32[]{:S(2)}) copy-start(bf16[768,768]{1,0:T(8,128)(2,1)S(1)} %get-tuple-element.11) | copy-start | bytes 3538948
  100.3 7.4 %collective-permute-start.25 = (f32[384,1024]{1,0:T(8,128)}, f32[384,1024]{1,0:T(8,128)}, u32[]{:S(2)}, u32[]{:S(2)}) collective-permute-start(f32[384,1024]{1,0:T(8,128)} %fusion.23), channel_id=1, source_target_pairs={{0,2},{2,0},{1,3},{3,1},{4,6},{6,4},{5,7},{7,5},{8,10},{10,8},{9,1... | collective-permute-start | bytes 4718600 | tf_op jit(solution)/shard_map/ppermute | solution.py:133
  100.4 61.6 %all-to-all-start.1 = ((f16[16,48,1024]{2,1,0:T(8,128)(2,1)}), f16[16,48,1024]{2,1,0:T(8,128)(2,1)S(1)}, u32[]{:S(2)}, u32[]{:S(2)}) async-start(f16[16,48,1024]{2,1,0:T(8,128)(2,1)} %bitcast.63), calls=%async_computation.1 | async-start | bytes 3145728 | tf_op jit(solution)/shard_map/all_to_all | solution.py:17
  110.1 48.6 %copy-start.1 = (f32[384,1024]{1,0:T(8,128)}, f32[384,1024]{1,0:T(8,128)S(1)}, u32[]{:S(2)}) copy-start(f32[384,1024]{1,0:T(8,128)S(1)} %get-tuple-element.44) | copy-start | bytes 4718596
  110.2 8.9 %collective-permute-start.26 = (f16[48,1024]{1,0:T(8,128)(2,1)S(1)}, f16[48,1024]{1,0:T(8,128)(2,1)S(1)}, u32[]{:S(2)}, u32[]{:S(2)}) collective-permute-start(f16[48,1024]{1,0:T(8,128)(2,1)S(1)} %get-tuple-element.23), channel_id=1, source_target_pairs={{0,4},{4,8},{8,12},{12,16},{16,20},{20,24},{24,28},{28,0},{1,5},{5... | collective-permute-start | bytes 294920 | tf_op jit(solution)/shard_map/ppermute | solution.py:26
  110.2 8.9 %collective-permute-start.27 = (f16[48,1024]{1,0:T(8,128)(2,1)S(1)}, f16[48,1024]{1,0:T(8,128)(2,1)S(1)}, u32[]{:S(2)}, u32[]{:S(2)}) collective-permute-start(f16[48,1024]{1,0:T(8,128)(2,1)S(1)} %get-tuple-element.25), channel_id=1, source_target_pairs={{0,8},{4,12},{8,16},{12,20},{16,24},{20,28},{24,0},{28,4},{1,9},{5... | collective-permute-start | bytes 294920 | tf_op jit(solution)/shard_map/ppermute | solution.py:26
  112.8 9.2 %collective-permute-start.17 = (f32[1,128]{1,0:T(1,128)S(1)}, f32[1,128]{1,0:T(1,128)S(1)}, u32[]{:S(2)}, u32[]{:S(2)}) collective-permute-start(f32[1,128]{1,0:T(1,128)S(1)} %broadcast_in_dim.25), channel_id=1, source_target_pairs={{0,2},{2,0},{1,3},{3,1},{4,6},{6,4},{5,7},{7,5},{8,10},{10,8},{9,1... | collective-permute-start | bytes 1544 | tf_op jit(solution)/shard_map/ppermute | solution.py:31
  112.9 10.2 %collective-permute-start.30 = (f16[48,1024]{1,0:T(8,128)(2,1)S(1)}, f16[48,1024]{1,0:T(8,128)(2,1)S(1)}, u32[]{:S(2)}, u32[]{:S(2)}) collective-permute-start(f16[48,1024]{1,0:T(8,128)(2,1)S(1)} %get-tuple-element.24), channel_id=1, source_target_pairs={{0,28},{4,0},{8,4},{12,8},{16,12},{20,16},{24,20},{28,24},{1,29},{... | collective-permute-start | bytes 294920 | tf_op jit(solution)/shard_map/ppermute | solution.py:26
  119.2 6.1 %collective-permute-start.28 = (f16[48,1024]{1,0:T(8,128)(2,1)S(1)}, f16[48,1024]{1,0:T(8,128)(2,1)S(1)}, u32[]{:S(2)}, u32[]{:S(2)}) collective-permute-start(f16[48,1024]{1,0:T(8,128)(2,1)S(1)} %fusion.34), channel_id=1, source_target_pairs={{0,4},{4,8},{8,12},{12,16},{16,20},{20,24},{24,28},{28,0},{1,5},{5... | collective-permute-start | bytes 294920 | tf_op jit(solution)/shard_map/ppermute | solution.py:26
  122.6 7.6 %collective-permute-start.18 = (f32[1,128]{1,0:T(1,128)S(1)}, f32[1,128]{1,0:T(1,128)S(1)}, u32[]{:S(2)}, u32[]{:S(2)}) collective-permute-start(f32[1,128]{1,0:T(1,128)S(1)} %broadcast_add_fusion), channel_id=1, source_target_pairs={{0,1},{1,0},{2,3},{3,2},{4,5},{5,4},{6,7},{7,6},{8,9},{9,8},{10,11... | collective-permute-start | bytes 1544 | tf_op jit(solution)/shard_map/ppermute | solution.py:31
  125.3 33.3 %collective-permute-start.31 = (f16[48,1024]{1,0:T(8,128)(2,1)S(1)}, f16[48,1024]{1,0:T(8,128)(2,1)S(1)}, u32[]{:S(2)}, u32[]{:S(2)}) collective-permute-start(f16[48,1024]{1,0:T(8,128)(2,1)S(1)} %get-tuple-element.22), channel_id=1, source_target_pairs={{0,28},{4,0},{8,4},{12,8},{16,12},{20,16},{24,20},{28,24},{1,29},{... | collective-permute-start | bytes 294920 | tf_op jit(solution)/shard_map/ppermute | solution.py:26
  130.8 3.6 %collective-permute-start.19 = (f32[1,128]{1,0:T(1,128)S(1)}, f32[1,128]{1,0:T(1,128)S(1)}, u32[]{:S(2)}, u32[]{:S(2)}) collective-permute-start(f32[1,128]{1,0:T(1,128)S(1)} %fusion.65), channel_id=1, source_target_pairs={{0,128},{128,0},{1,129},{129,1},{2,130},{130,2},{3,131},{131,3},{4... | collective-permute-start | bytes 1544 | tf_op jit(solution)/shard_map/ppermute | solution.py:31
  134.5 3.5 %collective-permute-start.20 = (f32[1,128]{1,0:T(1,128)S(1)}, f32[1,128]{1,0:T(1,128)S(1)}, u32[]{:S(2)}, u32[]{:S(2)}) collective-permute-start(f32[1,128]{1,0:T(1,128)S(1)} %add.193), channel_id=1, source_target_pairs={{0,32},{32,0},{64,96},{96,64},{1,33},{33,1},{65,97},{97,65},{2,34}... | collective-permute-start | bytes 1544 | tf_op jit(solution)/shard_map/ppermute | solution.py:31
  138.0 5.0 %collective-permute-start.21 = (f32[1,128]{1,0:T(1,128)S(1)}, f32[1,128]{1,0:T(1,128)S(1)}, u32[]{:S(2)}, u32[]{:S(2)}) collective-permute-start(f32[1,128]{1,0:T(1,128)S(1)} %add.194), channel_id=1, source_target_pairs={{0,64},{32,96},{64,0},{96,32},{1,65},{33,97},{65,1},{97,33},{2,66}... | collective-permute-start | bytes 1544 | tf_op jit(solution)/shard_map/ppermute | solution.py:31
  143.1 3.5 %collective-permute-start.22 = (f32[1,128]{1,0:T(1,128)S(1)}, f32[1,128]{1,0:T(1,128)S(1)}, u32[]{:S(2)}, u32[]{:S(2)}) collective-permute-start(f32[1,128]{1,0:T(1,128)S(1)} %add.195), channel_id=1, source_target_pairs={{0,4},{4,0},{8,12},{12,8},{16,20},{20,16},{24,28},{28,24},{1,5},{5... | collective-permute-start | bytes 1544 | tf_op jit(solution)/shard_map/ppermute | solution.py:31
  146.6 4.4 %collective-permute-start.23 = (f32[1,128]{1,0:T(1,128)S(1)}, f32[1,128]{1,0:T(1,128)S(1)}, u32[]{:S(2)}, u32[]{:S(2)}) collective-permute-start(f32[1,128]{1,0:T(1,128)S(1)} %add.196), channel_id=1, source_target_pairs={{0,8},{4,12},{8,0},{12,4},{16,24},{20,28},{24,16},{28,20},{1,9},{5... | collective-permute-start | bytes 1544 | tf_op jit(solution)/shard_map/ppermute | solution.py:31
  151.1 7.4 %collective-permute-start.24 = (f32[1,128]{1,0:T(1,128)S(1)}, f32[1,128]{1,0:T(1,128)S(1)}, u32[]{:S(2)}, u32[]{:S(2)}) collective-permute-start(f32[1,128]{1,0:T(1,128)S(1)} %add.197), channel_id=1, source_target_pairs={{0,16},{4,20},{8,24},{12,28},{16,0},{20,4},{24,8},{28,12},{1,17},{... | collective-permute-start | bytes 1544 | tf_op jit(solution)/shard_map/ppermute | solution.py:31
  158.6 5.9 %collective-permute-start.29 = (f16[48,1024]{1,0:T(8,128)(2,1)S(1)}, f16[48,1024]{1,0:T(8,128)(2,1)S(1)}, u32[]{:S(2)}, u32[]{:S(2)}) collective-permute-start(f16[48,1024]{1,0:T(8,128)(2,1)S(1)} %get-tuple-element.21), channel_id=1, source_target_pairs={{0,4},{4,8},{8,12},{12,16},{16,20},{20,24},{24,28},{28,0},{1,5},{5... | collective-permute-start | bytes 294920 | tf_op jit(solution)/shard_map/ppermute | solution.py:26
  158.7 5.8 %collective-permute-start.32 = (f16[48,1024]{1,0:T(8,128)(2,1)S(1)}, f16[48,1024]{1,0:T(8,128)(2,1)S(1)}, u32[]{:S(2)}, u32[]{:S(2)}) collective-permute-start(f16[48,1024]{1,0:T(8,128)(2,1)S(1)} %fusion.32), channel_id=1, source_target_pairs={{0,28},{4,0},{8,4},{12,8},{16,12},{20,16},{24,20},{28,24},{1,29},{... | collective-permute-start | bytes 294920 | tf_op jit(solution)/shard_map/ppermute | solution.py:26

commit v3 on v1

v3 whole, which is shorter than its diff:
```python
import jax
import jax.numpy as jnp
from jax import lax
from jax.sharding import Mesh
from jax.sharding import PartitionSpec as P

DP = ("xl", "y", "z")
PLANE = ("xl", "y", "tensor")
ALL = ("xl", "y", "z", "section", "tensor")
SWAP = [(0, 1), (1, 0)]
LANES = 128
F32 = jnp.float32
SENT = jnp.float16


def exchanged(parts, axes):
    return lax.all_to_all(parts, axes, split_axis=0, concat_axis=0, tiled=True)


def copies(array, axes):
    return exchanged(jnp.broadcast_to(array, (lax.axis_size(axes), *array.shape)), axes)


def to_offset(array, offset):
    n = lax.axis_size("z")
    return lax.ppermute(array, "z", [(i, (i + offset) % n) for i in range(n)])


def flipped(array, axis, bit):
    n = lax.axis_size(axis)
    return lax.ppermute(array, axis, [(i, i ^ bit) for i in range(n)])


def gathered_over_z(own):
    below, above = to_offset(own, 1), to_offset(own, -1)
    below2, above2 = to_offset(own, 2), to_offset(own, -2)
    below, above, below2, above2 = lax.optimization_barrier((below, above, below2, above2))
    cut = own.shape[0] // 2
    below3, above3 = to_offset(below2, 1), to_offset(above2, -1)
    top = to_offset(below2[:cut], 2)
    bottom = to_offset(above2[cut:], -2)
    return [own, below, above, below2, above2, below3, above3, top, bottom]


def tied(*arrays):
    return lax.optimization_barrier(arrays)


def summed_over_z(parts, value):
    own, below, above, below2, above2, below3, above3, across = parts
    cut = own.shape[0] // 2
    halves = across.astype(SENT)
    up3, down3 = to_offset(above3.astype(SENT), 1), to_offset(below3.astype(SENT), -1)
    top, bottom = to_offset(halves[:cut], 2), to_offset(halves[cut:], -2)
    up, down = to_offset(above.astype(SENT), 1), to_offset(below.astype(SENT), -1)
    other = flipped(value, "z", 1)
    up3, down3, top, bottom, up, down, other = tied(up3, down3, top, bottom, up, down, other)
    value = value + other
    up2 = above2 + up3.astype(F32)
    up2 = jnp.concatenate([up2[:cut] + top.astype(F32), up2[cut:]], axis=0)
    down2 = below2 + down3.astype(F32)
    down2 = jnp.concatenate([down2[:cut], down2[cut:] + bottom.astype(F32)], axis=0)
    up2, down2 = to_offset(up2.astype(SENT), 2), to_offset(down2.astype(SENT), -2)
    other = flipped(value, "z", 2)
    up2, down2, other = tied(up2, down2, other)
    value = value + other
    value = value + flipped(value, "z", 4)
    near = own + up.astype(F32) + down.astype(F32)
    return near + up2.astype(F32) + down2.astype(F32), value


def tower(inputs, up, down, tensor):
    rows, width = inputs.shape
    split = inputs.reshape(2, 2, rows // 4, width)
    kept = lax.dynamic_slice_in_dim(split, tensor, 1, 1).reshape(rows // 2, width)
    given = lax.dynamic_slice_in_dim(split, 1 - tensor, 1, 1).reshape(rows // 2, width)
    ordered = jnp.concatenate([given, kept], axis=0)
    hidden = jax.nn.gelu(jnp.dot(ordered, up, preferred_element_type=F32)).astype(jnp.bfloat16)
    sent = jnp.dot(hidden[: rows // 2], down, preferred_element_type=F32)
    arrived = lax.ppermute(sent, "tensor", SWAP)
    later, sent = tied(hidden[rows // 2 :], sent)
    own = jnp.dot(later, down, preferred_element_type=F32) + kept.astype(F32)
    own = lax.optimization_barrier(own)
    raw = own + arrived
    norms = lax.rsqrt(jnp.sum(raw * raw, axis=-1, keepdims=True) + 1e-06)
    return (raw * norms).astype(jnp.bfloat16).reshape(2, rows // 4, width)


def pair_lanes(pair, section, tensor, quarter):
    rows = lax.dynamic_slice_in_dim(pair, (section * 2 + tensor) * quarter, quarter)[:, None]
    lane = lax.broadcasted_iota(jnp.int32, (quarter, LANES), 1)
    digits = jnp.where(lane == 0, rows // LANES, jnp.where(lane == 1, rows % LANES, 0))
    return digits.astype(jnp.bfloat16)


def scored(rows, width, reports, columns, scale_value, bias_value):
    slides = rows[:, :width]
    wanted = rows[:, width].astype(F32) * LANES + rows[:, width + 1].astype(F32)
    dots = lax.dot_general(
        slides, reports, (((1,), (1,)), ((), ())), preferred_element_type=F32
    )
    logits = scale_value * dots + bias_value
    match = wanted[:, None] == columns[None, :]
    turned = jnp.where(match, -logits, logits)
    small = jnp.exp(-jnp.abs(turned))
    loss_part = jnp.sum(jnp.maximum(turned, 0.0) + jnp.log1p(small))
    sigmoid = jnp.where(turned >= 0, 1.0, small) / (1.0 + small)
    weight = jnp.where(match, -scale_value, scale_value) * sigmoid
    return slides, weight.astype(jnp.bfloat16), loss_part


def transposed_dot(weight, slides):
    return lax.dot_general(weight, slides, (((0,), (0,)), ((), ())), preferred_element_type=F32)


def local(tower_input, up_weight, down_weight, pair, scale, bias):
    section = lax.axis_index("section")
    tensor = lax.axis_index("tensor")
    n_z = lax.axis_size("z")
    n_plane = lax.axis_size(PLANE)
    scale_value, bias_value = scale[0], bias[0]
    quarter, width = tower_input.shape[1] // 4, tower_input.shape[2]
    total = lax.axis_size(ALL) * quarter

    lanes = pair_lanes(pair, section, tensor, quarter)
    embedded = tower(tower_input[0], up_weight[0], down_weight[0], tensor)
    mine = lax.dynamic_index_in_dim(embedded, section, 0, keepdims=False)
    given = lax.dynamic_index_in_dim(embedded, 1 - section, 0, keepdims=False)
    got = lax.ppermute(given, "section", SWAP)
    slides = jnp.concatenate([jnp.where(section == 0, mine, got), lanes], axis=1)
    reports = jnp.where(section == 0, got, mine)

    reports_all = copies(reports, PLANE).reshape(n_plane * quarter, -1)
    rows_mine = jnp.concatenate(gathered_over_z(slides), axis=0)
    rows_other = lax.ppermute(rows_mine, "section", SWAP)

    place = jnp.arange(n_plane * quarter, dtype=jnp.int32)
    member, row = place // quarter, place % quarter
    owner = ((member // 2 * n_z + lax.axis_index("z")) * 2 + section) * 2 + member % 2
    columns = (owner * quarter + row).astype(F32)

    slides_mine, weight_mine, loss_mine = scored(
        rows_mine, width, reports_all, columns, scale_value, bias_value
    )
    slides_other, weight_other, loss_other = scored(
        rows_other, width, reports_all, columns, scale_value, bias_value
    )
    loss_value = jnp.broadcast_to(loss_mine + loss_other, (1, 128))
    loss_value = copies(loss_value, PLANE).sum(axis=0)
    report_part = transposed_dot(weight_mine, slides_mine)
    report_part = (report_part + transposed_dot(weight_other, slides_other)).astype(SENT)
    report_part, weight_mine, weight_other = tied(report_part, weight_mine, weight_other)
    report_terms = exchanged(report_part.reshape(n_plane, quarter, -1), PLANE)
    slide_other = jnp.dot(weight_other, reports_all, preferred_element_type=F32)
    slide_back = lax.ppermute(slide_other, "section", SWAP)
    loss_back = lax.ppermute(loss_value, "section", SWAP)
    slide_mine = jnp.dot(weight_mine, reports_all, preferred_element_type=F32) + slide_back
    parts = [slide_mine[k * quarter : (k + 1) * quarter] for k in range(n_z)]
    slide_grad, loss_value = summed_over_z(parts, loss_value + loss_back)
    report_grad = report_terms.astype(F32).sum(axis=0)
    return (loss_value[0, :1] / total, slide_grad, report_grad)


def solution(mesh):
    finer = Mesh(
        mesh.devices.reshape(2, 4, 8, mesh.shape["section"], mesh.shape["tensor"]),
        ALL,
    )
    return jax.shard_map(
        local,
        mesh=finer,
        in_specs=(
            P("section", DP, None),
            P("section", None, "tensor"),
            P("section", "tensor", None),
            P(DP),
            P(),
            P(),
        ),
        out_specs=(P(), P(ALL, None), P(ALL, None)),
        check_vma=False,
    )
```

time: 179 us -> 125 us (0.70)
  waiting for transfers between devices: 76.4 us -> 28.3 us
  blocking collectives: 34.9 us -> 9.91 us
  starting transfers between devices: 33.7 us -> 54.2 us
  local copies, waits for them, and re-layouts: 6.32 us -> 2.71 us
  other arithmetic: 5.8 us -> 3.77 us
    all_to_all x5 -> x2, waiting for transfers between devices: 66.4 us -> 10.6 us  [exchanged(): return lax.all_to_all(parts, axes, split_axis=0, concat_axis=0, tiled=True)]
    ppermute x3 -> x22, starting transfers between devices: 0.59 us -> 38.4 us  [the longest x16 33.4 us: to_offset(): return lax.ppermute(array, 'z', [(i, (i + offset) % n) for i in range(n)])]
    all_to_all x2 -> x1, blocking collectives: 34.9 us -> 9.91 us  [exchanged(): return lax.all_to_all(parts, axes, split_axis=0, concat_axis=0, tiled=True)]
    all_to_all x5 -> x2, starting transfers between devices: 30.7 us -> 13.3 us  [exchanged(): return lax.all_to_all(parts, axes, split_axis=0, concat_axis=0, tiled=True)]
    ppermute x3 -> x22, waiting for transfers between devices: 0.01 us -> 9.5 us  [the longest x16 6.22 us: to_offset(): return lax.ppermute(array, 'z', [(i, (i + offset) % n) for i in range(n)])]
    ppermute x1, waiting for transfers between devices: 10 us -> 6.95 us  [tower(): arrived = lax.ppermute(sent, 'tensor', SWAP)]
    convert_element_type x1 -> x2, other arithmetic: 3.11 us -> 0.11 us  [the longest x1 0.08 us: pair_lanes(): return digits.astype(jnp.bfloat16)]
    dot_general x4 -> x7, matrix products: 13.2 us -> 14.4 us  [the longest x2 3.88 us: scored(): lax.dot_general(slides, reports, (((1,), (1,)), ((), ())), preferred_elem...]
  transfers between devices with their start and end apart: 10 -> 26, of which waited for: 6 -> 11; matrix products, arithmetic and copies ran while one was open for 7% -> 9% of each run, Pallas kernels for 0% -> 0%
where the time goes in v3:
time: 125 us; the launch traced here: 123 us
  starting transfers between devices  54.2 us (43%)
  waiting for transfers between devices  28.3 us (23%)
  matrix products  18.9 us (15%)
  blocking collectives  9.91 us (8%)
  between operations  4.8 us (4%)
  other arithmetic  3.77 us (3%)
  local copies, waits for them, and re-layouts  2.71 us (2%)
    ppermute x16, starting transfers between devices, to_offset(): return lax.ppermute(array, 'z', [(i, (i + offset) % n) for i in range(n)])  33.4 us
    all_to_all x2, starting transfers between devices, exchanged(): return lax.all_to_all(parts, axes, split_axis=0, concat_axis=0, tiled=True)  13.3 us
    all_to_all x2, waiting for transfers between devices, exchanged(): return lax.all_to_all(parts, axes, split_axis=0, concat_axis=0, tiled=True)  10.6 us
    all_to_all x1, blocking collectives, exchanged(): return lax.all_to_all(parts, axes, split_axis=0, concat_axis=0, tiled=True)  9.91 us
    ppermute x1, waiting for transfers between devices, tower(): arrived = lax.ppermute(sent, 'tensor', SWAP)  6.95 us
    ppermute x16, waiting for transfers between devices, to_offset(): return lax.ppermute(array, 'z', [(i, (i + offset) % n) for i in range(n)])  6.22 us
    ppermute x3, starting transfers between devices, flipped(): return lax.ppermute(array, axis, [(i, i ^ bit) for i in range(n)])  4.7 us
    dot_general x2, matrix products, scored(): lax.dot_general(slides, reports, (((1,), (1,)), ((), ())), preferred_elem...  3.88 us
  transfers between devices with their start and end apart: 26, of which 11 were waited for; matrix products, arithmetic and copies ran while one was open for 9% of the time, Pallas kernels for 0%

profile of v3, /device:TPU:4, one launch (start us, length us, event | category | flops | bytes accessed | tf_op | source)
XLA Modules:
  0.0 122.6 jit_solution(15301757808984564787)
XLA Ops:
  0.6 1.1 constant_dynamic-slice_fusion.1
  1.7 3.7 %fusion.15 = bf16[192,2048]{1,0:T(8,128)(2,1)S(1)} fusion(bf16[1,1024,2048]{2,1,0:T(8,128)(2,1)} %param.7, bf16[96,1024]{1,0:T(8,128)(2,1)S(1)} %bitcast.55, bf16[96,1024]{1,0:T(8,128)(2,1)S(1)} %bitcast.60), kind=kOutput, calls=%fused_computation.18 | convolution fusion | flops 809631744 | bytes 5373952 | tf_op jit(solution)/shard_map/dot_general | solution.py:78
  5.4 0.8 fusion.2
  6.2 2.3 %collective-permute-start = (f32[96,1024]{1,0:T(8,128)S(1)}, f32[96,1024]{1,0:T(8,128)S(1)}, u32[]{:S(2)}, u32[]{:S(2)}) collective-permute-start(f32[96,1024]{1,0:T(8,128)S(1)} %fusion.2), channel_id=1, source_target_pairs={{0,1},{1,0},{2,3},{3,2},{4,5},{5,4},{6,7},{7,6},{8,9},{9,8},{10,11... | collective-permute-start | bytes 1179656 | tf_op jit(solution)/shard_map/ppermute | solution.py:80
  8.6 3.0 %fusion.20 = f32[96,1024]{1,0:T(8,128)S(1)} fusion(bf16[96,2048]{1,0:T(8,128)(2,1)S(1)} %slice.106, bf16[1,2048,1024]{2,1,0:T(8,128)(2,1)} %param.8, bf16[96,1024]{1,0:T(8,128)(2,1)S(1)} %bitcast.56), kind=kOutput, calls=%fused_computation.26 | convolution fusion | flops 402849792 | bytes 5177344 | tf_op jit(solution)/shard_map/dot_general | solution.py:82
  11.7 6.9 %collective-permute-done = f32[96,1024]{1,0:T(8,128)S(1)} collective-permute-done((f32[96,1024]{1,0:T(8,128)S(1)}, f32[96,1024]{1,0:T(8,128)S(1)}, u32[]{:S(2)}, u32[]{:S(2)}) %collective-permute-start) | collective-permute-done | bytes 393248 | tf_op jit(solution)/shard_map/ppermute | solution.py:80
  18.7 0.1 multiply_reduce_fusion
  18.8 0.1 multiply_convert_fusion
  19.1 1.2 collective-permute-done.1
  20.4 2.0 %collective-permute-start.2 = (bf16[48,1152]{1,0:T(8,128)(2,1)S(1)}, bf16[48,1152]{1,0:T(8,128)(2,1)S(1)}, u32[]{:S(2)}, u32[]{:S(2)}) collective-permute-start(bf16[48,1152]{1,0:T(8,128)(2,1)S(1)} %get-tuple-element.63), channel_id=1, source_target_pairs={{0,4},{4,8},{8,12},{12,16},{16,20},{20,24},{24,28},{28,0},{1,5},{5... | collective-permute-start | bytes 331784 | tf_op jit(solution)/shard_map/ppermute | solution.py:26
  22.4 4.0 %collective-permute-start.3 = (bf16[48,1152]{1,0:T(8,128)(2,1)S(1)}, bf16[48,1152]{1,0:T(8,128)(2,1)S(1)}, u32[]{:S(2)}, u32[]{:S(2)}) collective-permute-start(bf16[48,1152]{1,0:T(8,128)(2,1)S(1)} %get-tuple-element.63), channel_id=1, source_target_pairs={{0,28},{4,0},{8,4},{12,8},{16,12},{20,16},{24,20},{28,24},{1,29},{... | collective-permute-start | bytes 331784 | tf_op jit(solution)/shard_map/ppermute | solution.py:26
  26.4 4.1 %collective-permute-start.5 = (bf16[48,1152]{1,0:T(8,128)(2,1)S(1)}, bf16[48,1152]{1,0:T(8,128)(2,1)S(1)}, u32[]{:S(2)}, u32[]{:S(2)}) collective-permute-start(bf16[48,1152]{1,0:T(8,128)(2,1)S(1)} %get-tuple-element.63), channel_id=1, source_target_pairs={{0,24},{4,28},{8,0},{12,4},{16,8},{20,12},{24,16},{28,20},{1,25},{... | collective-permute-start | bytes 331784 | tf_op jit(solution)/shard_map/ppermute | solution.py:26
  30.5 1.4 %broadcast_in_dim.42 = bf16[16,48,1024]{2,1,0:T(8,128)(2,1)} broadcast(bf16[48,1024]{1,0:T(8,128)(2,1)S(1)} %get-tuple-element.58), dimensions={1,2} | broadcast | bytes 1671168 | tf_op jit(solution)/shard_map/broadcast_in_dim | solution.py:21
  31.9 7.5 %all-to-all-start = ((bf16[16,48,1024]{2,1,0:T(8,128)(2,1)}), bf16[16,48,1024]{2,1,0:T(8,128)(2,1)S(1)}, u32[]{:S(2)}, u32[]{:S(2)}) async-start(bf16[16,48,1024]{2,1,0:T(8,128)(2,1)} %broadcast_in_dim.42), calls=%async_computation | async-start | bytes 3145728 | tf_op jit(solution)/shard_map/all_to_all | solution.py:17
  39.5 3.3 %collective-permute-start.7 = (bf16[48,1152]{1,0:T(8,128)(2,1)S(1)}, bf16[48,1152]{1,0:T(8,128)(2,1)S(1)}, u32[]{:S(2)}, u32[]{:S(2)}) collective-permute-start(bf16[48,1152]{1,0:T(8,128)(2,1)S(1)} %collective-permute-done.5), channel_id=1, source_target_pairs={{0,28},{4,0},{8,4},{12,8},{16,12},{20,16},{24,20},{28,24},{1,29},{... | collective-permute-start | bytes 331784 | tf_op jit(solution)/shard_map/ppermute | solution.py:26
  43.0 4.1 %collective-permute-start.9 = (bf16[24,1152]{1,0:T(8,128)(2,1)S(1)}, bf16[24,1152]{1,0:T(8,128)(2,1)S(1)}, u32[]{:S(2)}, u32[]{:S(2)}) collective-permute-start(bf16[24,1152]{1,0:T(8,128)(2,1)S(1)} %slice.85), channel_id=1, source_target_pairs={{0,24},{4,28},{8,0},{12,4},{16,8},{20,12},{24,16},{28,20},{1,25},{... | collective-permute-start | bytes 165896 | tf_op jit(solution)/shard_map/ppermute | solution.py:26
  47.1 2.1 %collective-permute-done.8 = bf16[24,1152]{1,0:T(8,128)(2,1)S(1)} collective-permute-done((bf16[24,1152]{1,0:T(8,128)(2,1)S(1)}, bf16[24,1152]{1,0:T(8,128)(2,1)S(1)}, u32[]{:S(2)}, u32[]{:S(2)}) %collective-permute-start.8) | collective-permute-done | bytes 55328 | tf_op jit(solution)/shard_map/ppermute | solution.py:26
  49.2 1.2 collective-permute-done.9
  50.4 0.3 collective-permute-start.10
  52.0 0.2 add_reduce_fusion.3
  52.3 0.9 collective-permute-done.10
  53.1 0.2 add_reduce_fusion.2
  53.3 8.3 %all-to-all-done = bf16[16,48,1024]{2,1,0:T(8,128)(2,1)S(1)} async-done(((bf16[16,48,1024]{2,1,0:T(8,128)(2,1)}), bf16[16,48,1024]{2,1,0:T(8,128)(2,1)S(1)}, u32[]{:S(2)}, u32[]{:S(2)}) %all-to-all-start) | async-done | bytes 1572896 | tf_op jit(solution)/shard_map/all_to_all | solution.py:17
  61.6 0.8 negate_select_fusion
  62.5 3.0 %fusion.24 = (bf16[384,768]{1,0:T(8,128)(2,1)S(1)}, f32[]{:T(128)}, f32[]{:T(128)}, bf16[384,768]{1,0:T(8,128)(2,1)S(1)}) fusion(f32[]{:T(128)S(6)} %neg.20, f32[]{:T(128)} %bitcast.45, f32[768]{0:T(1024)S(1)} %fusion.55, f32[384]{0:T(512)S(1)} %add_reduce_fusion.3, f32[384,768]{1,0:T(8,128)S(1)} %negate_select_fusion, f32[384]{0:T(512)S(1)} %add_reduce_fusion.2, ...), kind=kOutput, calls=%fused_computation.28 | convolution fusion | flops 612827136 | bytes 4726804 | tf_op jit(solution)/shard_map/dot_general | solution.py:99
  65.5 1.0 fusion.27
  66.6 2.2 %add_convert_fusion = f16[768,1024]{1,0:T(8,128)(2,1)} fusion(f32[768,1024]{1,0:T(8,128)S(1)} %fusion.27, bf16[384,768]{1,0:T(8,128)(2,1)S(1)} %get-tuple-element.26, bf16[384,1152]{1,0:T(8,128)(2,1)S(1)} %constant_dynamic-update-slice_fusion), kind=kOutput, calls=%fused_computation.7 | convolution fusion | flops 605552640 | bytes 6094848 | tf_op jit(solution)/shard_map/dot_general | solution.py:113
  68.8 2.0 %fusion.65 = f32[384,1024]{1,0:T(8,128)} fusion(bf16[384,768]{1,0:T(8,128)(2,1)S(1)} %get-tuple-element.27, bf16[768,1024]{1,0:T(8,128)(2,1)S(1)} %bitcast.52), kind=kOutput, calls=%fused_computation.121 | convolution fusion | flops 603979776 | bytes 3735552 | tf_op jit(solution)/shard_map/dot_general | solution.py:154
  72.1 9.9 %all_to_all.15 = f32[16,1,128]{2,1,0:T(1,128)S(1)} all-to-all(f32[16,1,128]{2,1,0:T(1,128)S(1)} %broadcast_in_dim_broadcast_in_dim.3), channel_id=1, replica_groups=mesh['xl'=2,'y'=4,'z'=8,'section'=2,'tensor'=2] {'xl','y','tensor'}, dimensions={0} | all-to-all | bytes 16384 | tf_op jit(solution)/shard_map/all_to_all | solution.py:17
  82.1 5.9 %all-to-all-start.2 = ((f16[16,48,1024]{2,1,0:T(8,128)(2,1)}), f16[16,48,1024]{2,1,0:T(8,128)(2,1)S(1)}, u32[]{:S(2)}, u32[]{:S(2)}) async-start(f16[16,48,1024]{2,1,0:T(8,128)(2,1)} %bitcast.54), calls=%async_computation.2 | async-start | bytes 3145728 | tf_op jit(solution)/shard_map/all_to_all | solution.py:17
  88.1 2.4 %fusion.64 = (f16[384,1024]{1,0:T(8,128)(2,1)S(1)}, f32[384,1024]{1,0:T(8,128)S(1)}) fusion(f32[384,1024]{1,0:T(8,128)} %collective-permute-done.12, bf16[384,768]{1,0:T(8,128)(2,1)} %copy-done.2, bf16[768,1024]{1,0:T(8,128)(2,1)S(1)} %bitcast.53), kind=kOutput, calls=%fused_computation.120 | convolution fusion | flops 604766208 | bytes 6094848 | tf_op jit(solution)/shard_map/dot_general | solution.py:157
  90.6 2.1 %collective-permute-start.13 = (f16[48,1024]{1,0:T(8,128)(2,1)S(1)}, f16[48,1024]{1,0:T(8,128)(2,1)S(1)}, u32[]{:S(2)}, u32[]{:S(2)}) collective-permute-start(f16[48,1024]{1,0:T(8,128)(2,1)S(1)} %get-tuple-element.52), channel_id=1, source_target_pairs={{0,4},{4,8},{8,12},{12,16},{16,20},{20,24},{24,28},{28,0},{1,5},{5... | collective-permute-start | bytes 294920 | tf_op jit(solution)/shard_map/ppermute | solution.py:26
  92.7 0.9 collective-permute-start.15
  93.6 1.8 %collective-permute-start.14 = (f16[48,1024]{1,0:T(8,128)(2,1)S(1)}, f16[48,1024]{1,0:T(8,128)(2,1)S(1)}, u32[]{:S(2)}, u32[]{:S(2)}) collective-permute-start(f16[48,1024]{1,0:T(8,128)(2,1)S(1)} %get-tuple-element.51), channel_id=1, source_target_pairs={{0,28},{4,0},{8,4},{12,8},{16,12},{20,16},{24,20},{28,24},{1,29},{... | collective-permute-start | bytes 294920 | tf_op jit(solution)/shard_map/ppermute | solution.py:26
  95.5 0.4 collective-permute-start.17
  95.8 2.9 %collective-permute-start.18 = (f16[48,1024]{1,0:T(8,128)(2,1)S(1)}, f16[48,1024]{1,0:T(8,128)(2,1)S(1)}, u32[]{:S(2)}, u32[]{:S(2)}) collective-permute-start(f16[48,1024]{1,0:T(8,128)(2,1)S(1)} %get-tuple-element.49), channel_id=1, source_target_pairs={{0,28},{4,0},{8,4},{12,8},{16,12},{20,16},{24,20},{28,24},{1,29},{... | collective-permute-start | bytes 294920 | tf_op jit(solution)/shard_map/ppermute | solution.py:26
  98.7 0.7 collective-permute-done.15
  99.4 3.3 %collective-permute-start.16 = (f16[24,1024]{1,0:T(8,128)(2,1)S(1)}, f16[24,1024]{1,0:T(8,128)(2,1)S(1)}, u32[]{:S(2)}, u32[]{:S(2)}) collective-permute-start(f16[24,1024]{1,0:T(8,128)(2,1)S(1)} %get-tuple-element.53), channel_id=1, source_target_pairs={{0,24},{4,28},{8,0},{12,4},{16,8},{20,12},{24,16},{28,20},{1,25},{... | collective-permute-start | bytes 147464 | tf_op jit(solution)/shard_map/ppermute | solution.py:26
  102.7 2.2 %collective-permute-done.16 = f16[24,1024]{1,0:T(8,128)(2,1)S(1)} collective-permute-done((f16[24,1024]{1,0:T(8,128)(2,1)S(1)}, f16[24,1024]{1,0:T(8,128)(2,1)S(1)}, u32[]{:S(2)}, u32[]{:S(2)}) %collective-permute-start.16) | collective-permute-done | bytes 49184 | tf_op jit(solution)/shard_map/ppermute | solution.py:26
  105.1 1.8 %collective-permute-start.20 = (f16[48,1024]{1,0:T(8,128)(2,1)S(1)}, f16[48,1024]{1,0:T(8,128)(2,1)S(1)}, u32[]{:S(2)}, u32[]{:S(2)}) collective-permute-start(f16[48,1024]{1,0:T(8,128)(2,1)S(1)} %pad_maximum_fusion.1), channel_id=1, source_target_pairs={{0,8},{4,12},{8,16},{12,20},{16,24},{20,28},{24,0},{28,4},{1,9},{5... | collective-permute-start | bytes 294920 | tf_op jit(solution)/shard_map/ppermute | solution.py:26
  106.9 2.5 %collective-permute-start.21 = (f16[48,1024]{1,0:T(8,128)(2,1)S(1)}, f16[48,1024]{1,0:T(8,128)(2,1)S(1)}, u32[]{:S(2)}, u32[]{:S(2)}) collective-permute-start(f16[48,1024]{1,0:T(8,128)(2,1)S(1)} %pad_maximum_fusion.2), channel_id=1, source_target_pairs={{0,24},{4,28},{8,0},{12,4},{16,8},{20,12},{24,16},{28,20},{1,25},{... | collective-permute-start | bytes 294920 | tf_op jit(solution)/shard_map/ppermute | solution.py:26
  109.4 0.6 collective-permute-start.22
  110.0 2.3 %all-to-all-done.2 = f16[16,48,1024]{2,1,0:T(8,128)(2,1)S(1)} async-done(((f16[16,48,1024]{2,1,0:T(8,128)(2,1)}), f16[16,48,1024]{2,1,0:T(8,128)(2,1)S(1)}, u32[]{:S(2)}, u32[]{:S(2)}) %all-to-all-start.2) | async-done | bytes 1572896 | tf_op jit(solution)/shard_map/all_to_all | solution.py:17
  112.3 1.0 convert_reduce_fusion
  113.3 0.6 collective-permute-done.22
  113.9 4.1 %collective-permute-start.23 = (f32[1,128]{1,0:T(1,128)S(1)}, f32[1,128]{1,0:T(1,128)S(1)}, u32[]{:S(2)}, u32[]{:S(2)}) collective-permute-start(f32[1,128]{1,0:T(1,128)S(1)} %add.233), channel_id=1, source_target_pairs={{0,16},{4,20},{8,24},{12,28},{16,0},{20,4},{24,8},{28,12},{1,17},{... | collective-permute-start | bytes 1544 | tf_op jit(solution)/shard_map/ppermute | solution.py:31
  118.0 1.7 %fusion.38 = f32[48,1024]{1,0:T(8,128)} fusion(f32[384,1024]{1,0:T(8,128)} %copy-done.1, f16[48,1024]{1,0:T(8,128)(2,1)S(1)} %collective-permute-done.21, f16[48,1024]{1,0:T(8,128)(2,1)S(1)} %collective-permute-done.20, f16[48,1024]{1,0:T(8,128)(2,1)S(1)} %collective-permute-done.18, f16[48,1024]{1,0:T(8,128)(2,1)S(1)} %collective-permute-done.17), kind=kLoop, calls=%fused_computation.49 | loop fusion | flops 393216 | bytes 786432 | tf_op jit(solution)/shard_map/add | solution.py:69
  119.6 1.8 %collective-permute-done.23 = f32[1,128]{1,0:T(1,128)S(1)} collective-permute-done((f32[1,128]{1,0:T(1,128)S(1)}, f32[1,128]{1,0:T(1,128)S(1)}, u32[]{:S(2)}, u32[]{:S(2)}) %collective-permute-start.23) | collective-permute-done | bytes 544 | tf_op jit(solution)/shard_map/ppermute | solution.py:31
  (63 shorter events, 1.2 us)
Async XLA Ops:
  1.7 3.7 %copy-start = (bf16[1,2048,1024]{2,1,0:T(8,128)(2,1)S(1)}, bf16[1,2048,1024]{2,1,0:T(8,128)(2,1)}, u32[]{:S(2)}) copy-start(bf16[1,2048,1024]{2,1,0:T(8,128)(2,1)} %param.8) | copy-start | bytes 12582916
  6.2 12.4 %collective-permute-start = (f32[96,1024]{1,0:T(8,128)S(1)}, f32[96,1024]{1,0:T(8,128)S(1)}, u32[]{:S(2)}, u32[]{:S(2)}) collective-permute-start(f32[96,1024]{1,0:T(8,128)S(1)} %fusion.2), channel_id=1, source_target_pairs={{0,1},{1,0},{2,3},{3,2},{4,5},{5,4},{6,7},{7,6},{8,9},{9,8},{10,11... | collective-permute-start | bytes 1179656 | tf_op jit(solution)/shard_map/ppermute | solution.py:80
  8.6 3.0 %copy-start.3 = (s32[192]{0:T(256)S(1)}, s32[192]{0:T(256)}, u32[]{:S(2)}) copy-start(s32[192]{0:T(256)} %param.9) | copy-start | bytes 2308
  18.9 1.4 %collective-permute-start.1 = (bf16[48,1024]{1,0:T(8,128)(2,1)S(1)}, bf16[48,1024]{1,0:T(8,128)(2,1)S(1)}, u32[]{:S(2)}, u32[]{:S(2)}) collective-permute-start(bf16[48,1024]{1,0:T(8,128)(2,1)S(1)} %dynamic-slice_bitcast_fusion), channel_id=1, source_target_pairs={{0,2},{2,0},{1,3},{3,1},{4,6},{6,4},{5,7},{7,5},{8,10},{10,8},{9,1... | collective-permute-start | bytes 294920 | tf_op jit(solution)/shard_map/ppermute | solution.py:129
  20.4 19.0 %collective-permute-start.2 = (bf16[48,1152]{1,0:T(8,128)(2,1)S(1)}, bf16[48,1152]{1,0:T(8,128)(2,1)S(1)}, u32[]{:S(2)}, u32[]{:S(2)}) collective-permute-start(bf16[48,1152]{1,0:T(8,128)(2,1)S(1)} %get-tuple-element.63), channel_id=1, source_target_pairs={{0,4},{4,8},{8,12},{12,16},{16,20},{20,24},{24,28},{28,0},{1,5},{5... | collective-permute-start | bytes 331784 | tf_op jit(solution)/shard_map/ppermute | solution.py:26
  22.4 17.0 %collective-permute-start.3 = (bf16[48,1152]{1,0:T(8,128)(2,1)S(1)}, bf16[48,1152]{1,0:T(8,128)(2,1)S(1)}, u32[]{:S(2)}, u32[]{:S(2)}) collective-permute-start(bf16[48,1152]{1,0:T(8,128)(2,1)S(1)} %get-tuple-element.63), channel_id=1, source_target_pairs={{0,28},{4,0},{8,4},{12,8},{16,12},{20,16},{24,20},{28,24},{1,29},{... | collective-permute-start | bytes 331784 | tf_op jit(solution)/shard_map/ppermute | solution.py:26
  26.4 13.0 %collective-permute-start.4 = (bf16[48,1152]{1,0:T(8,128)(2,1)S(1)}, bf16[48,1152]{1,0:T(8,128)(2,1)S(1)}, u32[]{:S(2)}, u32[]{:S(2)}) collective-permute-start(bf16[48,1152]{1,0:T(8,128)(2,1)S(1)} %get-tuple-element.63), channel_id=1, source_target_pairs={{0,8},{4,12},{8,16},{12,20},{16,24},{20,28},{24,0},{28,4},{1,9},{5... | collective-permute-start | bytes 331784 | tf_op jit(solution)/shard_map/ppermute | solution.py:26
  26.4 13.0 %collective-permute-start.5 = (bf16[48,1152]{1,0:T(8,128)(2,1)S(1)}, bf16[48,1152]{1,0:T(8,128)(2,1)S(1)}, u32[]{:S(2)}, u32[]{:S(2)}) collective-permute-start(bf16[48,1152]{1,0:T(8,128)(2,1)S(1)} %get-tuple-element.63), channel_id=1, source_target_pairs={{0,24},{4,28},{8,0},{12,4},{16,8},{20,12},{24,16},{28,20},{1,25},{... | collective-permute-start | bytes 331784 | tf_op jit(solution)/shard_map/ppermute | solution.py:26
  31.9 29.7 %all-to-all-start = ((bf16[16,48,1024]{2,1,0:T(8,128)(2,1)}), bf16[16,48,1024]{2,1,0:T(8,128)(2,1)S(1)}, u32[]{:S(2)}, u32[]{:S(2)}) async-start(bf16[16,48,1024]{2,1,0:T(8,128)(2,1)} %broadcast_in_dim.42), calls=%async_computation | async-start | bytes 3145728 | tf_op jit(solution)/shard_map/all_to_all | solution.py:17
  39.4 7.7 %collective-permute-start.6 = (bf16[48,1152]{1,0:T(8,128)(2,1)S(1)}, bf16[48,1152]{1,0:T(8,128)(2,1)S(1)}, u32[]{:S(2)}, u32[]{:S(2)}) collective-permute-start(bf16[48,1152]{1,0:T(8,128)(2,1)S(1)} %collective-permute-done.4), channel_id=1, source_target_pairs={{0,4},{4,8},{8,12},{12,16},{16,20},{20,24},{24,28},{28,0},{1,5},{5... | collective-permute-start | bytes 331784 | tf_op jit(solution)/shard_map/ppermute | solution.py:26
  39.5 7.6 %collective-permute-start.7 = (bf16[48,1152]{1,0:T(8,128)(2,1)S(1)}, bf16[48,1152]{1,0:T(8,128)(2,1)S(1)}, u32[]{:S(2)}, u32[]{:S(2)}) collective-permute-start(bf16[48,1152]{1,0:T(8,128)(2,1)S(1)} %collective-permute-done.5), channel_id=1, source_target_pairs={{0,28},{4,0},{8,4},{12,8},{16,12},{20,16},{24,20},{28,24},{1,29},{... | collective-permute-start | bytes 331784 | tf_op jit(solution)/shard_map/ppermute | solution.py:26
  42.9 6.3 %collective-permute-start.8 = (bf16[24,1152]{1,0:T(8,128)(2,1)S(1)}, bf16[24,1152]{1,0:T(8,128)(2,1)S(1)}, u32[]{:S(2)}, u32[]{:S(2)}) collective-permute-start(bf16[24,1152]{1,0:T(8,128)(2,1)S(1)} %slice.84), channel_id=1, source_target_pairs={{0,8},{4,12},{8,16},{12,20},{16,24},{20,28},{24,0},{28,4},{1,9},{5... | collective-permute-start | bytes 165896 | tf_op jit(solution)/shard_map/ppermute | solution.py:26
  43.0 7.5 %collective-permute-start.9 = (bf16[24,1152]{1,0:T(8,128)(2,1)S(1)}, bf16[24,1152]{1,0:T(8,128)(2,1)S(1)}, u32[]{:S(2)}, u32[]{:S(2)}) collective-permute-start(bf16[24,1152]{1,0:T(8,128)(2,1)S(1)} %slice.85), channel_id=1, source_target_pairs={{0,24},{4,28},{8,0},{12,4},{16,8},{20,12},{24,16},{28,20},{1,25},{... | collective-permute-start | bytes 165896 | tf_op jit(solution)/shard_map/ppermute | solution.py:26
  50.4 2.7 %collective-permute-start.10 = (bf16[384,1152]{1,0:T(8,128)(2,1)S(1)}, bf16[384,1152]{1,0:T(8,128)(2,1)S(1)}, u32[]{:S(2)}, u32[]{:S(2)}) collective-permute-start(bf16[384,1152]{1,0:T(8,128)(2,1)S(1)} %constant_dynamic-update-slice_fusion), channel_id=1, source_target_pairs={{0,2},{2,0},{1,3},{3,1},{4,6},{6,4},{5,7},{7,5},{8,10},{10,8},{9,1... | collective-permute-start | bytes 2654216 | tf_op jit(solution)/shard_map/ppermute | solution.py:135
  65.5 1.0 copy-start.2
  70.7 17.4 %collective-permute-start.12 = (f32[384,1024]{1,0:T(8,128)}, f32[384,1024]{1,0:T(8,128)}, u32[]{:S(2)}, u32[]{:S(2)}) collective-permute-start(f32[384,1024]{1,0:T(8,128)} %fusion.65), channel_id=1, source_target_pairs={{0,2},{2,0},{1,3},{3,1},{4,6},{6,4},{5,7},{7,5},{8,10},{10,8},{9,1... | collective-permute-start | bytes 4718600 | tf_op jit(solution)/shard_map/ppermute | solution.py:155
  82.0 6.0 %collective-permute-start.11 = (f32[1,128]{1,0:T(1,128)S(1)}, f32[1,128]{1,0:T(1,128)S(1)}, u32[]{:S(2)}, u32[]{:S(2)}) collective-permute-start(f32[1,128]{1,0:T(1,128)S(1)} %bitcast.62), channel_id=1, source_target_pairs={{0,2},{2,0},{1,3},{3,1},{4,6},{6,4},{5,7},{7,5},{8,10},{10,8},{9,1... | collective-permute-start | bytes 1544 | tf_op jit(solution)/shard_map/ppermute | solution.py:156
  82.1 30.2 %all-to-all-start.2 = ((f16[16,48,1024]{2,1,0:T(8,128)(2,1)}), f16[16,48,1024]{2,1,0:T(8,128)(2,1)S(1)}, u32[]{:S(2)}, u32[]{:S(2)}) async-start(f16[16,48,1024]{2,1,0:T(8,128)(2,1)} %bitcast.54), calls=%async_computation.2 | async-start | bytes 3145728 | tf_op jit(solution)/shard_map/all_to_all | solution.py:17
  88.0 7.8 %collective-permute-start.19 = (f32[1,128]{1,0:T(1,128)S(1)}, f32[1,128]{1,0:T(1,128)S(1)}, u32[]{:S(2)}, u32[]{:S(2)}) collective-permute-start(f32[1,128]{1,0:T(1,128)S(1)} %bitcast_add_fusion), channel_id=1, source_target_pairs={{0,4},{4,0},{8,12},{12,8},{16,20},{20,16},{24,28},{28,24},{1,5},{5... | collective-permute-start | bytes 1544 | tf_op jit(solution)/shard_map/ppermute | solution.py:31
  90.5 18.9 %copy-start.1 = (f32[384,1024]{1,0:T(8,128)}, f32[384,1024]{1,0:T(8,128)S(1)}, u32[]{:S(2)}) copy-start(f32[384,1024]{1,0:T(8,128)S(1)} %get-tuple-element.68) | copy-start | bytes 4718596
  90.6 14.3 %collective-permute-start.13 = (f16[48,1024]{1,0:T(8,128)(2,1)S(1)}, f16[48,1024]{1,0:T(8,128)(2,1)S(1)}, u32[]{:S(2)}, u32[]{:S(2)}) collective-permute-start(f16[48,1024]{1,0:T(8,128)(2,1)S(1)} %get-tuple-element.52), channel_id=1, source_target_pairs={{0,4},{4,8},{8,12},{12,16},{16,20},{20,24},{24,28},{28,0},{1,5},{5... | collective-permute-start | bytes 294920 | tf_op jit(solution)/shard_map/ppermute | solution.py:26
  92.7 6.7 %collective-permute-start.15 = (f16[24,1024]{1,0:T(8,128)(2,1)S(1)}, f16[24,1024]{1,0:T(8,128)(2,1)S(1)}, u32[]{:S(2)}, u32[]{:S(2)}) collective-permute-start(f16[24,1024]{1,0:T(8,128)(2,1)S(1)} %get-tuple-element.54), channel_id=1, source_target_pairs={{0,8},{4,12},{8,16},{12,20},{16,24},{20,28},{24,0},{28,4},{1,9},{5... | collective-permute-start | bytes 147464 | tf_op jit(solution)/shard_map/ppermute | solution.py:26
  93.6 11.3 %collective-permute-start.14 = (f16[48,1024]{1,0:T(8,128)(2,1)S(1)}, f16[48,1024]{1,0:T(8,128)(2,1)S(1)}, u32[]{:S(2)}, u32[]{:S(2)}) collective-permute-start(f16[48,1024]{1,0:T(8,128)(2,1)S(1)} %get-tuple-element.51), channel_id=1, source_target_pairs={{0,28},{4,0},{8,4},{12,8},{16,12},{20,16},{24,20},{28,24},{1,29},{... | collective-permute-start | bytes 294920 | tf_op jit(solution)/shard_map/ppermute | solution.py:26
  95.5 9.4 %collective-permute-start.17 = (f16[48,1024]{1,0:T(8,128)(2,1)S(1)}, f16[48,1024]{1,0:T(8,128)(2,1)S(1)}, u32[]{:S(2)}, u32[]{:S(2)}) collective-permute-start(f16[48,1024]{1,0:T(8,128)(2,1)S(1)} %get-tuple-element.50), channel_id=1, source_target_pairs={{0,4},{4,8},{8,12},{12,16},{16,20},{20,24},{24,28},{28,0},{1,5},{5... | collective-permute-start | bytes 294920 | tf_op jit(solution)/shard_map/ppermute | solution.py:26
  95.8 9.1 %collective-permute-start.18 = (f16[48,1024]{1,0:T(8,128)(2,1)S(1)}, f16[48,1024]{1,0:T(8,128)(2,1)S(1)}, u32[]{:S(2)}, u32[]{:S(2)}) collective-permute-start(f16[48,1024]{1,0:T(8,128)(2,1)S(1)} %get-tuple-element.49), channel_id=1, source_target_pairs={{0,28},{4,0},{8,4},{12,8},{16,12},{20,16},{24,20},{28,24},{1,29},{... | collective-permute-start | bytes 294920 | tf_op jit(solution)/shard_map/ppermute | solution.py:26
  99.4 5.5 %collective-permute-start.16 = (f16[24,1024]{1,0:T(8,128)(2,1)S(1)}, f16[24,1024]{1,0:T(8,128)(2,1)S(1)}, u32[]{:S(2)}, u32[]{:S(2)}) collective-permute-start(f16[24,1024]{1,0:T(8,128)(2,1)S(1)} %get-tuple-element.53), channel_id=1, source_target_pairs={{0,24},{4,28},{8,0},{12,4},{16,8},{20,12},{24,16},{28,20},{1,25},{... | collective-permute-start | bytes 147464 | tf_op jit(solution)/shard_map/ppermute | solution.py:26
  105.1 8.9 %collective-permute-start.20 = (f16[48,1024]{1,0:T(8,128)(2,1)S(1)}, f16[48,1024]{1,0:T(8,128)(2,1)S(1)}, u32[]{:S(2)}, u32[]{:S(2)}) collective-permute-start(f16[48,1024]{1,0:T(8,128)(2,1)S(1)} %pad_maximum_fusion.1), channel_id=1, source_target_pairs={{0,8},{4,12},{8,16},{12,20},{16,24},{20,28},{24,0},{28,4},{1,9},{5... | collective-permute-start | bytes 294920 | tf_op jit(solution)/shard_map/ppermute | solution.py:26
  106.9 7.0 %collective-permute-start.21 = (f16[48,1024]{1,0:T(8,128)(2,1)S(1)}, f16[48,1024]{1,0:T(8,128)(2,1)S(1)}, u32[]{:S(2)}, u32[]{:S(2)}) collective-permute-start(f16[48,1024]{1,0:T(8,128)(2,1)S(1)} %pad_maximum_fusion.2), channel_id=1, source_target_pairs={{0,24},{4,28},{8,0},{12,4},{16,8},{20,12},{24,16},{28,20},{1,25},{... | collective-permute-start | bytes 294920 | tf_op jit(solution)/shard_map/ppermute | solution.py:26
  109.4 4.5 %collective-permute-start.22 = (f32[1,128]{1,0:T(1,128)S(1)}, f32[1,128]{1,0:T(1,128)S(1)}, u32[]{:S(2)}, u32[]{:S(2)}) collective-permute-start(f32[1,128]{1,0:T(1,128)S(1)} %add.228), channel_id=1, source_target_pairs={{0,8},{4,12},{8,0},{12,4},{16,24},{20,28},{24,16},{28,20},{1,9},{5... | collective-permute-start | bytes 1544 | tf_op jit(solution)/shard_map/ppermute | solution.py:31
  113.9 7.5 %collective-permute-start.23 = (f32[1,128]{1,0:T(1,128)S(1)}, f32[1,128]{1,0:T(1,128)S(1)}, u32[]{:S(2)}, u32[]{:S(2)}) collective-permute-start(f32[1,128]{1,0:T(1,128)S(1)} %add.233), channel_id=1, source_target_pairs={{0,16},{4,20},{8,24},{12,28},{16,0},{20,4},{24,8},{28,12},{1,17},{... | collective-permute-start | bytes 1544 | tf_op jit(solution)/shard_map/ppermute | solution.py:31

commit v4 on v3

--- a/solution.py
+++ b/solution.py
@@ -32,13 +32,11 @@
 
 
 def gathered_over_z(own):
-    below, above = to_offset(own, 1), to_offset(own, -1)
-    below2, above2 = to_offset(own, 2), to_offset(own, -2)
-    below, above, below2, above2 = lax.optimization_barrier((below, above, below2, above2))
     cut = own.shape[0] // 2
+    below, above = tied(to_offset(own, 1), to_offset(own, -1))
+    below2, above2 = tied(to_offset(below, 1), to_offset(above, -1))
+    top, bottom = to_offset(below2[:cut], 2), to_offset(above2[cut:], -2)
     below3, above3 = to_offset(below2, 1), to_offset(above2, -1)
-    top = to_offset(below2[:cut], 2)
-    bottom = to_offset(above2[cut:], -2)
     return [own, below, above, below2, above2, below3, above3, top, bottom]
 
 
@@ -46,27 +44,39 @@
     return lax.optimization_barrier(arrays)
 
 
-def summed_over_z(parts, value):
+def with_digits(part, value):
+    high = (value / 4096.0).astype(SENT)
+    value = value - high.astype(F32) * 4096.0
+    middle = (value / 4.0).astype(SENT)
+    low = (value - middle.astype(F32) * 4.0).astype(SENT)
+    shape = (*part.shape[:-1], LANES)
+    lane = lax.broadcasted_iota(jnp.int32, shape, len(shape) - 1)
+    lanes = jnp.where(lane == 0, high, jnp.where(lane == 1, middle, low))
+    return jnp.concatenate([part.astype(SENT), lanes], axis=-1)
+
+
+def without_digits(sent):
+    width = sent.shape[-1] - LANES
+    lanes = sent[:, 0, width:].astype(F32).sum(axis=0)
+    value = lanes[0] * 4096.0 + lanes[1] * 4.0 + lanes[2]
+    return sent[..., :width].astype(F32), value
+
+
+def summed_over_z(parts):
     own, below, above, below2, above2, below3, above3, across = parts
     cut = own.shape[0] // 2
     halves = across.astype(SENT)
     up3, down3 = to_offset(above3.astype(SENT), 1), to_offset(below3.astype(SENT), -1)
+    up, down = to_offset(above.astype(SENT), 1), to_offset(below.astype(SENT), -1)
     top, bottom = to_offset(halves[:cut], 2), to_offset(halves[cut:], -2)
-    up, down = to_offset(above.astype(SENT), 1), to_offset(below.astype(SENT), -1)
-    other = flipped(value, "z", 1)
-    up3, down3, top, bottom, up, down, other = tied(up3, down3, top, bottom, up, down, other)
-    value = value + other
+    up3, down3, top, bottom, up, down = tied(up3, down3, top, bottom, up, down)
     up2 = above2 + up3.astype(F32)
     up2 = jnp.concatenate([up2[:cut] + top.astype(F32), up2[cut:]], axis=0)
     down2 = below2 + down3.astype(F32)
     down2 = jnp.concatenate([down2[:cut], down2[cut:] + bottom.astype(F32)], axis=0)
-    up2, down2 = to_offset(up2.astype(SENT), 2), to_offset(down2.astype(SENT), -2)
-    other = flipped(value, "z", 2)
-    up2, down2, other = tied(up2, down2, other)
-    value = value + other
-    value = value + flipped(value, "z", 4)
+    up2, down2 = tied(to_offset(up2.astype(SENT), 2), to_offset(down2.astype(SENT), -2))
     near = own + up.astype(F32) + down.astype(F32)
-    return near + up2.astype(F32) + down2.astype(F32), value
+    return near + up2.astype(F32) + down2.astype(F32)
 
 
 def tower(inputs, up, down, tensor):
@@ -130,7 +140,9 @@
     slides = jnp.concatenate([jnp.where(section == 0, mine, got), lanes], axis=1)
     reports = jnp.where(section == 0, got, mine)
 
-    reports_all = copies(reports, PLANE).reshape(n_plane * quarter, -1)
+    repeated = jnp.broadcast_to(reports, (n_plane, *reports.shape))
+    repeated, slides = tied(repeated, slides)
+    reports_all = exchanged(repeated, PLANE).reshape(n_plane * quarter, -1)
     rows_mine = jnp.concatenate(gathered_over_z(slides), axis=0)
     rows_other = lax.ppermute(rows_mine, "section", SWAP)
 
@@ -145,20 +157,23 @@
     slides_other, weight_other, loss_other = scored(
         rows_other, width, reports_all, columns, scale_value, bias_value
     )
-    loss_value = jnp.broadcast_to(loss_mine + loss_other, (1, 128))
-    loss_value = copies(loss_value, PLANE).sum(axis=0)
     report_part = transposed_dot(weight_mine, slides_mine)
-    report_part = (report_part + transposed_dot(weight_other, slides_other)).astype(SENT)
+    report_part = report_part + transposed_dot(weight_other, slides_other)
+    report_part = with_digits(
+        report_part.reshape(n_plane, quarter, width), loss_mine + loss_other
+    )
     report_part, weight_mine, weight_other = tied(report_part, weight_mine, weight_other)
-    report_terms = exchanged(report_part.reshape(n_plane, quarter, -1), PLANE)
+    report_terms = exchanged(report_part, PLANE)
     slide_other = jnp.dot(weight_other, reports_all, preferred_element_type=F32)
     slide_back = lax.ppermute(slide_other, "section", SWAP)
-    loss_back = lax.ppermute(loss_value, "section", SWAP)
     slide_mine = jnp.dot(weight_mine, reports_all, preferred_element_type=F32) + slide_back
     parts = [slide_mine[k * quarter : (k + 1) * quarter] for k in range(n_z)]
-    slide_grad, loss_value = summed_over_z(parts, loss_value + loss_back)
-    report_grad = report_terms.astype(F32).sum(axis=0)
-    return (loss_value[0, :1] / total, slide_grad, report_grad)
+    slide_grad = summed_over_z(parts)
+    report_terms, slide_grad = tied(report_terms, slide_grad)
+    report_terms, loss_value = without_digits(report_terms)
+    losses = copies(jnp.broadcast_to(loss_value, (1, LANES)), ("z", "section"))
+    loss = jnp.sum(losses, axis=0)[0, :1] / total
+    return (loss, slide_grad, report_terms.sum(axis=0))
 
 
 def solution(mesh):

time: 125 us -> 127 us (1.016)
  the two profiles are of different devices: /device:TPU:4 before, /device:TPU:1 now
where the time goes in v4:
time: 127 us; the launch traced here: 126 us
  starting transfers between devices  57.5 us (45%)
  waiting for transfers between devices  31.2 us (25%)
  matrix products  21.3 us (17%)
  between operations  6.8 us (5%)
  other arithmetic  5.51 us (4%)
  local copies, waits for them, and re-layouts  3.99 us (3%)
    ppermute x16, starting transfers between devices, to_offset(): return lax.ppermute(array, 'z', [(i, (i + offset) % n) for i in range(n)])  27.3 us
    all_to_all x3, starting transfers between devices, exchanged(): return lax.all_to_all(parts, axes, split_axis=0, concat_axis=0, tiled=True)  18.7 us
    ppermute x16, waiting for transfers between devices, to_offset(): return lax.ppermute(array, 'z', [(i, (i + offset) % n) for i in range(n)])  15.7 us
    all_to_all x3, waiting for transfers between devices, exchanged(): return lax.all_to_all(parts, axes, split_axis=0, concat_axis=0, tiled=True)  9.38 us
    dot_general x2, matrix products, scored(): lax.dot_general(slides, reports, (((1,), (1,)), ((), ())), preferred_elem...  6.09 us
    ppermute x1, waiting for transfers between devices, tower(): arrived = lax.ppermute(sent, 'tensor', SWAP)  4.61 us
    dot_general x1, matrix products, tower(): jnp.dot(ordered, up, preferred_element_type=F32)  3.69 us
    ppermute x1, starting transfers between devices, tower(): arrived = lax.ppermute(sent, 'tensor', SWAP)  3.66 us
  transfers between devices with their start and end apart: 23, of which 11 were waited for; matrix products, arithmetic and copies ran while one was open for 7% of the time, Pallas kernels for 0%

profile of v4, /device:TPU:1, one launch (start us, length us, event | category | flops | bytes accessed | tf_op | source)
XLA Modules:
  0.0 126.2 jit_solution(15516429182888385272)
XLA Ops:
  0.6 1.1 constant_dynamic-slice_fusion.1
  1.7 3.7 %fusion.15 = bf16[192,2048]{1,0:T(8,128)(2,1)S(1)} fusion(bf16[1,1024,2048]{2,1,0:T(8,128)(2,1)} %param.7, bf16[96,1024]{1,0:T(8,128)(2,1)S(1)} %bitcast.55, bf16[96,1024]{1,0:T(8,128)(2,1)S(1)} %bitcast.60), kind=kOutput, calls=%fused_computation.19 | convolution fusion | flops 809631744 | bytes 5373952 | tf_op jit(solution)/shard_map/dot_general | solution.py:88
  5.4 0.8 fusion.2
  6.2 3.7 %collective-permute-start = (f32[96,1024]{1,0:T(8,128)S(1)}, f32[96,1024]{1,0:T(8,128)S(1)}, u32[]{:S(2)}, u32[]{:S(2)}) collective-permute-start(f32[96,1024]{1,0:T(8,128)S(1)} %fusion.2), channel_id=1, source_target_pairs={{0,1},{1,0},{2,3},{3,2},{4,5},{5,4},{6,7},{7,6},{8,9},{9,8},{10,11... | collective-permute-start | bytes 1179656 | tf_op jit(solution)/shard_map/ppermute | solution.py:90
  9.9 3.0 %fusion.20 = f32[96,1024]{1,0:T(8,128)S(1)} fusion(bf16[96,2048]{1,0:T(8,128)(2,1)S(1)} %slice.126, bf16[1,2048,1024]{2,1,0:T(8,128)(2,1)} %param.8, bf16[96,1024]{1,0:T(8,128)(2,1)S(1)} %bitcast.56), kind=kOutput, calls=%fused_computation.27 | convolution fusion | flops 402849792 | bytes 5177344 | tf_op jit(solution)/shard_map/dot_general | solution.py:92
  13.1 4.6 %collective-permute-done = f32[96,1024]{1,0:T(8,128)S(1)} collective-permute-done((f32[96,1024]{1,0:T(8,128)S(1)}, f32[96,1024]{1,0:T(8,128)S(1)}, u32[]{:S(2)}, u32[]{:S(2)}) %collective-permute-start) | collective-permute-done | bytes 393248 | tf_op jit(solution)/shard_map/ppermute | solution.py:90
  17.7 0.1 multiply_reduce_fusion
  17.9 2.4 %collective-permute-start.1 = (bf16[48,1024]{1,0:T(8,128)(2,1)S(1)}, bf16[48,1024]{1,0:T(8,128)(2,1)S(1)}, u32[]{:S(2)}, u32[]{:S(2)}) collective-permute-start(bf16[48,1024]{1,0:T(8,128)(2,1)S(1)} %dynamic-slice_bitcast_fusion), channel_id=1, source_target_pairs={{0,2},{2,0},{1,3},{3,1},{4,6},{6,4},{5,7},{7,5},{8,10},{10,8},{9,1... | collective-permute-start | bytes 294920 | tf_op jit(solution)/shard_map/ppermute | solution.py:139
  20.4 0.9 collective-permute-done.1
  21.3 1.4 %broadcast_in_dim.54 = bf16[16,48,1024]{2,1,0:T(8,128)(2,1)} broadcast(bf16[48,1024]{1,0:T(8,128)(2,1)S(1)} %get-tuple-element.62), dimensions={1,2} | broadcast | bytes 1671168 | tf_op jit(solution)/shard_map/broadcast_in_dim | solution.py:143
  22.7 1.9 %collective-permute-start.2 = (bf16[48,1152]{1,0:T(8,128)(2,1)S(1)}, bf16[48,1152]{1,0:T(8,128)(2,1)S(1)}, u32[]{:S(2)}, u32[]{:S(2)}) collective-permute-start(bf16[48,1152]{1,0:T(8,128)(2,1)S(1)} %pad_maximum_fusion.1), channel_id=1, source_target_pairs={{0,4},{4,8},{8,12},{12,16},{16,20},{20,24},{24,28},{28,0},{1,5},{5... | collective-permute-start | bytes 331784 | tf_op jit(solution)/shard_map/ppermute | solution.py:26
  24.5 3.9 %collective-permute-start.3 = (bf16[48,1152]{1,0:T(8,128)(2,1)S(1)}, bf16[48,1152]{1,0:T(8,128)(2,1)S(1)}, u32[]{:S(2)}, u32[]{:S(2)}) collective-permute-start(bf16[48,1152]{1,0:T(8,128)(2,1)S(1)} %pad_maximum_fusion.1), channel_id=1, source_target_pairs={{0,28},{4,0},{8,4},{12,8},{16,12},{20,16},{24,20},{28,24},{1,29},{... | collective-permute-start | bytes 331784 | tf_op jit(solution)/shard_map/ppermute | solution.py:26
  28.5 6.8 %all-to-all-start = ((bf16[16,48,1024]{2,1,0:T(8,128)(2,1)}), bf16[16,48,1024]{2,1,0:T(8,128)(2,1)S(1)}, u32[]{:S(2)}, u32[]{:S(2)}) async-start(bf16[16,48,1024]{2,1,0:T(8,128)(2,1)} %broadcast_in_dim.54), calls=%async_computation | async-start | bytes 3145728 | tf_op jit(solution)/shard_map/all_to_all | solution.py:17
  35.4 2.7 %collective-permute-start.5 = (bf16[48,1152]{1,0:T(8,128)(2,1)S(1)}, bf16[48,1152]{1,0:T(8,128)(2,1)S(1)}, u32[]{:S(2)}, u32[]{:S(2)}) collective-permute-start(bf16[48,1152]{1,0:T(8,128)(2,1)S(1)} %collective-permute-done.3), channel_id=1, source_target_pairs={{0,28},{4,0},{8,4},{12,8},{16,12},{20,16},{24,20},{28,24},{1,29},{... | collective-permute-start | bytes 331784 | tf_op jit(solution)/shard_map/ppermute | solution.py:26
  38.1 2.1 %collective-permute-done.4 = bf16[48,1152]{1,0:T(8,128)(2,1)S(1)} collective-permute-done((bf16[48,1152]{1,0:T(8,128)(2,1)S(1)}, bf16[48,1152]{1,0:T(8,128)(2,1)S(1)}, u32[]{:S(2)}, u32[]{:S(2)}) %collective-permute-start.4) | collective-permute-done | bytes 110624 | tf_op jit(solution)/shard_map/ppermute | solution.py:26
  40.2 3.0 %collective-permute-start.7 = (bf16[48,1152]{1,0:T(8,128)(2,1)S(1)}, bf16[48,1152]{1,0:T(8,128)(2,1)S(1)}, u32[]{:S(2)}, u32[]{:S(2)}) collective-permute-start(bf16[48,1152]{1,0:T(8,128)(2,1)S(1)} %collective-permute-done.5), channel_id=1, source_target_pairs={{0,28},{4,0},{8,4},{12,8},{16,12},{20,16},{24,20},{28,24},{1,29},{... | collective-permute-start | bytes 331784 | tf_op jit(solution)/shard_map/ppermute | solution.py:26
  43.3 2.0 %collective-permute-start.8 = (bf16[24,1152]{1,0:T(8,128)(2,1)S(1)}, bf16[24,1152]{1,0:T(8,128)(2,1)S(1)}, u32[]{:S(2)}, u32[]{:S(2)}) collective-permute-start(bf16[24,1152]{1,0:T(8,128)(2,1)S(1)} %slice.99), channel_id=1, source_target_pairs={{0,8},{4,12},{8,16},{12,20},{16,24},{20,28},{24,0},{28,4},{1,9},{5... | collective-permute-start | bytes 165896 | tf_op jit(solution)/shard_map/ppermute | solution.py:26
  45.3 1.7 %collective-permute-start.9 = (bf16[24,1152]{1,0:T(8,128)(2,1)S(1)}, bf16[24,1152]{1,0:T(8,128)(2,1)S(1)}, u32[]{:S(2)}, u32[]{:S(2)}) collective-permute-start(bf16[24,1152]{1,0:T(8,128)(2,1)S(1)} %slice.100), channel_id=1, source_target_pairs={{0,24},{4,28},{8,0},{12,4},{16,8},{20,12},{24,16},{28,20},{1,25},{... | collective-permute-start | bytes 165896 | tf_op jit(solution)/shard_map/ppermute | solution.py:26
  47.0 2.9 %collective-permute-done.8 = bf16[24,1152]{1,0:T(8,128)(2,1)S(1)} collective-permute-done((bf16[24,1152]{1,0:T(8,128)(2,1)S(1)}, bf16[24,1152]{1,0:T(8,128)(2,1)S(1)}, u32[]{:S(2)}, u32[]{:S(2)}) %collective-permute-start.8) | collective-permute-done | bytes 55328 | tf_op jit(solution)/shard_map/ppermute | solution.py:26
  50.0 3.5 %collective-permute-start.10 = (bf16[384,1152]{1,0:T(8,128)(2,1)S(1)}, bf16[384,1152]{1,0:T(8,128)(2,1)}, u32[]{:S(2)}, u32[]{:S(2)}) collective-permute-start(bf16[384,1152]{1,0:T(8,128)(2,1)S(1)} %constant_dynamic-update-slice_fusion), channel_id=1, source_target_pairs={{0,2},{2,0},{1,3},{3,1},{4,6},{6,4},{5,7},{7,5},{8,10},{10,8},{9,1... | collective-permute-start | bytes 2654216 | tf_op jit(solution)/shard_map/ppermute | solution.py:147
  54.8 0.2 add_reduce_fusion.3
  55.0 0.6 collective-permute-done.10
  55.7 1.2 add_reduce_fusion.2
  56.9 0.7 all-to-all-done
  57.6 2.0 %negate_select_fusion = f32[384,768]{1,0:T(8,128)S(1)} fusion(bf16[768,1024]{1,0:T(8,128)(2,1)S(1)} %bitcast.51, bf16[384,1152]{1,0:T(8,128)(2,1)} %collective-permute-done.10, f32[]{:T(128)} %bitcast.49, f32[]{:T(128)} %bitcast.47, f32[768]{0:T(1024)S(1)} %fusion.55, f32[384]{0:T(512)S(1)} %add_reduce_fusion.2), kind=kOutput, calls=%fused_computation.10 | convolution fusion | flops 605454336 | bytes 3544576 | tf_op jit(solution)/shard_map/dot_general | solution.py:109
  59.6 4.1 %fusion.24 = (bf16[384,768]{1,0:T(8,128)(2,1)S(1)}, f32[]{:T(128)}, f32[]{:T(128)}, bf16[384,768]{1,0:T(8,128)(2,1)}) fusion(f32[]{:T(128)} %bitcast.46, f32[]{:T(128)S(6)} %neg.16, f32[768]{0:T(1024)S(1)} %fusion.55, f32[384]{0:T(512)S(1)} %add_reduce_fusion.3, f32[384,768]{1,0:T(8,128)S(1)} %negate_select_fusion, f32[384]{0:T(512)S(1)} %add_reduce_fusion.2, ...), kind=kOutput, calls=%fused_computation.29 | convolution fusion | flops 612827136 | bytes 4726804 | tf_op jit(solution)/shard_map/dot_general | solution.py:109
  65.1 2.3 %fusion.27 = f32[768,1024]{1,0:T(8,128)S(1)} fusion(bf16[384,768]{1,0:T(8,128)(2,1)} %get-tuple-element.32, bf16[384,1152]{1,0:T(8,128)(2,1)} %collective-permute-done.10), kind=kOutput, calls=%fused_computation.36 | convolution fusion | flops 603979776 | bytes 4521984 | tf_op jit(solution)/shard_map/dot_general | solution.py:123
  67.4 1.0 add_convert_fusion
  68.5 1.8 %pad_maximum_fusion = f16[16,48,1152]{2,1,0:T(8,128)(2,1)} fusion(f16[16,48,128]{2,1,0:T(8,128)(2,1)S(1)} %broadcast_select_fusion, f16[16,48,1024]{2,1,0:T(8,128)(2,1)S(1)} %bitcast.50), kind=kLoop, calls=%fused_computation.9 | loop fusion | flops 884736 | bytes 3538944 | tf_op jit(solution)/shard_map/concatenate | solution.py:55
  70.2 2.0 %fusion.66 = f32[384,1024]{1,0:T(8,128)} fusion(bf16[384,768]{1,0:T(8,128)(2,1)S(1)} %copy-done.2, bf16[768,1024]{1,0:T(8,128)(2,1)S(1)} %bitcast.53), kind=kOutput, calls=%fused_computation.125 | convolution fusion | flops 603979776 | bytes 3735552 | tf_op jit(solution)/shard_map/dot_general | solution.py:167
  72.2 1.8 %collective-permute-start.11 = (f32[384,1024]{1,0:T(8,128)}, f32[384,1024]{1,0:T(8,128)}, u32[]{:S(2)}, u32[]{:S(2)}) collective-permute-start(f32[384,1024]{1,0:T(8,128)} %fusion.66), channel_id=1, source_target_pairs={{0,2},{2,0},{1,3},{3,1},{4,6},{6,4},{5,7},{7,5},{8,10},{10,8},{9,1... | collective-permute-start | bytes 4718600 | tf_op jit(solution)/shard_map/ppermute | solution.py:168
  74.0 4.8 %all-to-all-start.1 = ((f16[16,48,1152]{2,1,0:T(8,128)(2,1)}), f16[16,48,1152]{2,1,0:T(8,128)(2,1)S(1)}, u32[]{:S(2)}, u32[]{:S(2)}) async-start(f16[16,48,1152]{2,1,0:T(8,128)(2,1)} %pad_maximum_fusion), calls=%async_computation.1 | async-start | bytes 3538944 | tf_op jit(solution)/shard_map/all_to_all | solution.py:17
  78.8 2.4 %fusion.65 = (f16[384,1024]{1,0:T(8,128)(2,1)S(1)}, f32[384,1024]{1,0:T(8,128)S(1)}) fusion(f32[384,1024]{1,0:T(8,128)} %collective-permute-done.11, bf16[384,768]{1,0:T(8,128)(2,1)} %copy-done.1, bf16[768,1024]{1,0:T(8,128)(2,1)S(1)} %bitcast.54), kind=kOutput, calls=%fused_computation.124 | convolution fusion | flops 604766208 | bytes 6094848 | tf_op jit(solution)/shard_map/dot_general | solution.py:169
  81.3 1.8 %collective-permute-start.12 = (f16[48,1024]{1,0:T(8,128)(2,1)S(1)}, f16[48,1024]{1,0:T(8,128)(2,1)S(1)}, u32[]{:S(2)}, u32[]{:S(2)}) collective-permute-start(f16[48,1024]{1,0:T(8,128)(2,1)S(1)} %get-tuple-element.56), channel_id=1, source_target_pairs={{0,4},{4,8},{8,12},{12,16},{16,20},{20,24},{24,28},{28,0},{1,5},{5... | collective-permute-start | bytes 294920 | tf_op jit(solution)/shard_map/ppermute | solution.py:26
  83.1 2.0 %collective-permute-start.14 = (f16[24,1024]{1,0:T(8,128)(2,1)S(1)}, f16[24,1024]{1,0:T(8,128)(2,1)S(1)}, u32[]{:S(2)}, u32[]{:S(2)}) collective-permute-start(f16[24,1024]{1,0:T(8,128)(2,1)S(1)} %get-tuple-element.58), channel_id=1, source_target_pairs={{0,8},{4,12},{8,16},{12,20},{16,24},{20,28},{24,0},{28,4},{1,9},{5... | collective-permute-start | bytes 147464 | tf_op jit(solution)/shard_map/ppermute | solution.py:26
  85.1 2.7 %collective-permute-start.13 = (f16[48,1024]{1,0:T(8,128)(2,1)S(1)}, f16[48,1024]{1,0:T(8,128)(2,1)S(1)}, u32[]{:S(2)}, u32[]{:S(2)}) collective-permute-start(f16[48,1024]{1,0:T(8,128)(2,1)S(1)} %get-tuple-element.55), channel_id=1, source_target_pairs={{0,28},{4,0},{8,4},{12,8},{16,12},{20,16},{24,20},{28,24},{1,29},{... | collective-permute-start | bytes 294920 | tf_op jit(solution)/shard_map/ppermute | solution.py:26
  87.8 2.7 %collective-permute-start.17 = (f16[48,1024]{1,0:T(8,128)(2,1)S(1)}, f16[48,1024]{1,0:T(8,128)(2,1)S(1)}, u32[]{:S(2)}, u32[]{:S(2)}) collective-permute-start(f16[48,1024]{1,0:T(8,128)(2,1)S(1)} %get-tuple-element.53), channel_id=1, source_target_pairs={{0,28},{4,0},{8,4},{12,8},{16,12},{20,16},{24,20},{28,24},{1,29},{... | collective-permute-start | bytes 294920 | tf_op jit(solution)/shard_map/ppermute | solution.py:26
  90.4 4.1 %collective-permute-done.15 = f16[24,1024]{1,0:T(8,128)(2,1)S(1)} collective-permute-done((f16[24,1024]{1,0:T(8,128)(2,1)S(1)}, f16[24,1024]{1,0:T(8,128)(2,1)S(1)}, u32[]{:S(2)}, u32[]{:S(2)}) %collective-permute-start.15) | collective-permute-done | bytes 49184 | tf_op jit(solution)/shard_map/ppermute | solution.py:26
  94.7 2.9 %collective-permute-start.19 = (f16[48,1024]{1,0:T(8,128)(2,1)S(1)}, f16[48,1024]{1,0:T(8,128)(2,1)S(1)}, u32[]{:S(2)}, u32[]{:S(2)}) collective-permute-start(f16[48,1024]{1,0:T(8,128)(2,1)S(1)} %pad_maximum_fusion.3), channel_id=1, source_target_pairs={{0,24},{4,28},{8,0},{12,4},{16,8},{20,12},{24,16},{28,20},{1,25},{... | collective-permute-start | bytes 294920 | tf_op jit(solution)/shard_map/ppermute | solution.py:26
  97.8 2.4 %collective-permute-done.19 = f16[48,1024]{1,0:T(8,128)(2,1)S(1)} collective-permute-done((f16[48,1024]{1,0:T(8,128)(2,1)S(1)}, f16[48,1024]{1,0:T(8,128)(2,1)S(1)}, u32[]{:S(2)}, u32[]{:S(2)}) %collective-permute-start.19) | collective-permute-done | bytes 98336 | tf_op jit(solution)/shard_map/ppermute | solution.py:26
  100.2 4.1 %collective-permute-done.18 = f16[48,1024]{1,0:T(8,128)(2,1)S(1)} collective-permute-done((f16[48,1024]{1,0:T(8,128)(2,1)S(1)}, f16[48,1024]{1,0:T(8,128)(2,1)S(1)}, u32[]{:S(2)}, u32[]{:S(2)}) %collective-permute-start.18) | collective-permute-done | bytes 98336 | tf_op jit(solution)/shard_map/ppermute | solution.py:26
  104.3 0.7 fusion.38
  105.0 2.5 %all-to-all-done.1 = f16[16,48,1152]{2,1,0:T(8,128)(2,1)S(1)} async-done(((f16[16,48,1152]{2,1,0:T(8,128)(2,1)}), f16[16,48,1152]{2,1,0:T(8,128)(2,1)S(1)}, u32[]{:S(2)}, u32[]{:S(2)}) %all-to-all-start.1) | async-done | bytes 1769504 | tf_op jit(solution)/shard_map/all_to_all | solution.py:17
  107.6 0.7 fusion.64
  110.2 0.6 broadcast_in_dim_broadcast_in_dim.3
  110.8 7.2 %all-to-all-start.2 = ((f32[16,1,128]{2,1,0:T(1,128)}), f32[16,1,128]{2,1,0:T(1,128)S(1)}, u32[]{:S(2)}, u32[]{:S(2)}) async-start(f32[16,1,128]{2,1,0:T(1,128)} %broadcast_in_dim_broadcast_in_dim.3), calls=%async_computation.2 | async-start | bytes 16384 | tf_op jit(solution)/shard_map/all_to_all | solution.py:17
  118.0 0.9 convert_reduce_fusion
  118.9 6.1 %all-to-all-done.2 = f32[16,1,128]{2,1,0:T(1,128)S(1)} async-done(((f32[16,1,128]{2,1,0:T(1,128)}), f32[16,1,128]{2,1,0:T(1,128)S(1)}, u32[]{:S(2)}, u32[]{:S(2)}) %all-to-all-start.2) | async-done | bytes 8224 | tf_op jit(solution)/shard_map/all_to_all | solution.py:17
  (58 shorter events, 1.1 us)
Async XLA Ops:
  1.7 3.7 %copy-start = (bf16[1,2048,1024]{2,1,0:T(8,128)(2,1)S(1)}, bf16[1,2048,1024]{2,1,0:T(8,128)(2,1)}, u32[]{:S(2)}) copy-start(bf16[1,2048,1024]{2,1,0:T(8,128)(2,1)} %param.8) | copy-start | bytes 12582916
  6.2 11.4 %collective-permute-start = (f32[96,1024]{1,0:T(8,128)S(1)}, f32[96,1024]{1,0:T(8,128)S(1)}, u32[]{:S(2)}, u32[]{:S(2)}) collective-permute-start(f32[96,1024]{1,0:T(8,128)S(1)} %fusion.2), channel_id=1, source_target_pairs={{0,1},{1,0},{2,3},{3,2},{4,5},{5,4},{6,7},{7,6},{8,9},{9,8},{10,11... | collective-permute-start | bytes 1179656 | tf_op jit(solution)/shard_map/ppermute | solution.py:90
  9.9 3.0 %copy-start.3 = (s32[192]{0:T(256)S(1)}, s32[192]{0:T(256)}, u32[]{:S(2)}) copy-start(s32[192]{0:T(256)} %param.9) | copy-start | bytes 2308
  17.9 3.3 %collective-permute-start.1 = (bf16[48,1024]{1,0:T(8,128)(2,1)S(1)}, bf16[48,1024]{1,0:T(8,128)(2,1)S(1)}, u32[]{:S(2)}, u32[]{:S(2)}) collective-permute-start(bf16[48,1024]{1,0:T(8,128)(2,1)S(1)} %dynamic-slice_bitcast_fusion), channel_id=1, source_target_pairs={{0,2},{2,0},{1,3},{3,1},{4,6},{6,4},{5,7},{7,5},{8,10},{10,8},{9,1... | collective-permute-start | bytes 294920 | tf_op jit(solution)/shard_map/ppermute | solution.py:139
  22.7 12.6 %collective-permute-start.2 = (bf16[48,1152]{1,0:T(8,128)(2,1)S(1)}, bf16[48,1152]{1,0:T(8,128)(2,1)S(1)}, u32[]{:S(2)}, u32[]{:S(2)}) collective-permute-start(bf16[48,1152]{1,0:T(8,128)(2,1)S(1)} %pad_maximum_fusion.1), channel_id=1, source_target_pairs={{0,4},{4,8},{8,12},{12,16},{16,20},{20,24},{24,28},{28,0},{1,5},{5... | collective-permute-start | bytes 331784 | tf_op jit(solution)/shard_map/ppermute | solution.py:26
  24.5 10.7 %collective-permute-start.3 = (bf16[48,1152]{1,0:T(8,128)(2,1)S(1)}, bf16[48,1152]{1,0:T(8,128)(2,1)S(1)}, u32[]{:S(2)}, u32[]{:S(2)}) collective-permute-start(bf16[48,1152]{1,0:T(8,128)(2,1)S(1)} %pad_maximum_fusion.1), channel_id=1, source_target_pairs={{0,28},{4,0},{8,4},{12,8},{16,12},{20,16},{24,20},{28,24},{1,29},{... | collective-permute-start | bytes 331784 | tf_op jit(solution)/shard_map/ppermute | solution.py:26
  28.5 29.1 %all-to-all-start = ((bf16[16,48,1024]{2,1,0:T(8,128)(2,1)}), bf16[16,48,1024]{2,1,0:T(8,128)(2,1)S(1)}, u32[]{:S(2)}, u32[]{:S(2)}) async-start(bf16[16,48,1024]{2,1,0:T(8,128)(2,1)} %broadcast_in_dim.54), calls=%async_computation | async-start | bytes 3145728 | tf_op jit(solution)/shard_map/all_to_all | solution.py:17
  35.3 4.9 %collective-permute-start.4 = (bf16[48,1152]{1,0:T(8,128)(2,1)S(1)}, bf16[48,1152]{1,0:T(8,128)(2,1)S(1)}, u32[]{:S(2)}, u32[]{:S(2)}) collective-permute-start(bf16[48,1152]{1,0:T(8,128)(2,1)S(1)} %collective-permute-done.2), channel_id=1, source_target_pairs={{0,4},{4,8},{8,12},{12,16},{16,20},{20,24},{24,28},{28,0},{1,5},{5... | collective-permute-start | bytes 331784 | tf_op jit(solution)/shard_map/ppermute | solution.py:26
  35.4 4.8 %collective-permute-start.5 = (bf16[48,1152]{1,0:T(8,128)(2,1)S(1)}, bf16[48,1152]{1,0:T(8,128)(2,1)S(1)}, u32[]{:S(2)}, u32[]{:S(2)}) collective-permute-start(bf16[48,1152]{1,0:T(8,128)(2,1)S(1)} %collective-permute-done.3), channel_id=1, source_target_pairs={{0,28},{4,0},{8,4},{12,8},{16,12},{20,16},{24,20},{28,24},{1,29},{... | collective-permute-start | bytes 331784 | tf_op jit(solution)/shard_map/ppermute | solution.py:26
  40.2 6.8 %collective-permute-start.6 = (bf16[48,1152]{1,0:T(8,128)(2,1)S(1)}, bf16[48,1152]{1,0:T(8,128)(2,1)S(1)}, u32[]{:S(2)}, u32[]{:S(2)}) collective-permute-start(bf16[48,1152]{1,0:T(8,128)(2,1)S(1)} %collective-permute-done.4), channel_id=1, source_target_pairs={{0,4},{4,8},{8,12},{12,16},{16,20},{20,24},{24,28},{28,0},{1,5},{5... | collective-permute-start | bytes 331784 | tf_op jit(solution)/shard_map/ppermute | solution.py:26
  40.2 6.8 %collective-permute-start.7 = (bf16[48,1152]{1,0:T(8,128)(2,1)S(1)}, bf16[48,1152]{1,0:T(8,128)(2,1)S(1)}, u32[]{:S(2)}, u32[]{:S(2)}) collective-permute-start(bf16[48,1152]{1,0:T(8,128)(2,1)S(1)} %collective-permute-done.5), channel_id=1, source_target_pairs={{0,28},{4,0},{8,4},{12,8},{16,12},{20,16},{24,20},{28,24},{1,29},{... | collective-permute-start | bytes 331784 | tf_op jit(solution)/shard_map/ppermute | solution.py:26
  43.3 6.7 %collective-permute-start.8 = (bf16[24,1152]{1,0:T(8,128)(2,1)S(1)}, bf16[24,1152]{1,0:T(8,128)(2,1)S(1)}, u32[]{:S(2)}, u32[]{:S(2)}) collective-permute-start(bf16[24,1152]{1,0:T(8,128)(2,1)S(1)} %slice.99), channel_id=1, source_target_pairs={{0,8},{4,12},{8,16},{12,20},{16,24},{20,28},{24,0},{28,4},{1,9},{5... | collective-permute-start | bytes 165896 | tf_op jit(solution)/shard_map/ppermute | solution.py:26
  45.3 4.7 %collective-permute-start.9 = (bf16[24,1152]{1,0:T(8,128)(2,1)S(1)}, bf16[24,1152]{1,0:T(8,128)(2,1)S(1)}, u32[]{:S(2)}, u32[]{:S(2)}) collective-permute-start(bf16[24,1152]{1,0:T(8,128)(2,1)S(1)} %slice.100), channel_id=1, source_target_pairs={{0,24},{4,28},{8,0},{12,4},{16,8},{20,12},{24,16},{28,20},{1,25},{... | collective-permute-start | bytes 165896 | tf_op jit(solution)/shard_map/ppermute | solution.py:26
  50.0 5.7 %collective-permute-start.10 = (bf16[384,1152]{1,0:T(8,128)(2,1)S(1)}, bf16[384,1152]{1,0:T(8,128)(2,1)}, u32[]{:S(2)}, u32[]{:S(2)}) collective-permute-start(bf16[384,1152]{1,0:T(8,128)(2,1)S(1)} %constant_dynamic-update-slice_fusion), channel_id=1, source_target_pairs={{0,2},{2,0},{1,3},{3,1},{4,6},{6,4},{5,7},{7,5},{8,10},{10,8},{9,1... | collective-permute-start | bytes 2654216 | tf_op jit(solution)/shard_map/ppermute | solution.py:147
  63.7 3.8 %copy-start.1 = (bf16[384,768]{1,0:T(8,128)(2,1)}, bf16[384,768]{1,0:T(8,128)(2,1)S(1)}, u32[]{:S(2)}) copy-start(bf16[384,768]{1,0:T(8,128)(2,1)S(1)} %get-tuple-element.31) | copy-start | bytes 1769476
  68.5 1.8 %copy-start.2 = (bf16[384,768]{1,0:T(8,128)(2,1)S(1)}, bf16[384,768]{1,0:T(8,128)(2,1)}, u32[]{:S(2)}) copy-start(bf16[384,768]{1,0:T(8,128)(2,1)} %get-tuple-element.32) | copy-start | bytes 1769476
  72.2 6.6 %collective-permute-start.11 = (f32[384,1024]{1,0:T(8,128)}, f32[384,1024]{1,0:T(8,128)}, u32[]{:S(2)}, u32[]{:S(2)}) collective-permute-start(f32[384,1024]{1,0:T(8,128)} %fusion.66), channel_id=1, source_target_pairs={{0,2},{2,0},{1,3},{3,1},{4,6},{6,4},{5,7},{7,5},{8,10},{10,8},{9,1... | collective-permute-start | bytes 4718600 | tf_op jit(solution)/shard_map/ppermute | solution.py:168
  74.0 33.5 %all-to-all-start.1 = ((f16[16,48,1152]{2,1,0:T(8,128)(2,1)}), f16[16,48,1152]{2,1,0:T(8,128)(2,1)S(1)}, u32[]{:S(2)}, u32[]{:S(2)}) async-start(f16[16,48,1152]{2,1,0:T(8,128)(2,1)} %pad_maximum_fusion), calls=%async_computation.1 | async-start | bytes 3538944 | tf_op jit(solution)/shard_map/all_to_all | solution.py:17
  81.3 13.3 %collective-permute-start.12 = (f16[48,1024]{1,0:T(8,128)(2,1)S(1)}, f16[48,1024]{1,0:T(8,128)(2,1)S(1)}, u32[]{:S(2)}, u32[]{:S(2)}) collective-permute-start(f16[48,1024]{1,0:T(8,128)(2,1)S(1)} %get-tuple-element.56), channel_id=1, source_target_pairs={{0,4},{4,8},{8,12},{12,16},{16,20},{20,24},{24,28},{28,0},{1,5},{5... | collective-permute-start | bytes 294920 | tf_op jit(solution)/shard_map/ppermute | solution.py:26
  83.1 7.3 %collective-permute-start.14 = (f16[24,1024]{1,0:T(8,128)(2,1)S(1)}, f16[24,1024]{1,0:T(8,128)(2,1)S(1)}, u32[]{:S(2)}, u32[]{:S(2)}) collective-permute-start(f16[24,1024]{1,0:T(8,128)(2,1)S(1)} %get-tuple-element.58), channel_id=1, source_target_pairs={{0,8},{4,12},{8,16},{12,20},{16,24},{20,28},{24,0},{28,4},{1,9},{5... | collective-permute-start | bytes 147464 | tf_op jit(solution)/shard_map/ppermute | solution.py:26
  85.1 9.5 %collective-permute-start.13 = (f16[48,1024]{1,0:T(8,128)(2,1)S(1)}, f16[48,1024]{1,0:T(8,128)(2,1)S(1)}, u32[]{:S(2)}, u32[]{:S(2)}) collective-permute-start(f16[48,1024]{1,0:T(8,128)(2,1)S(1)} %get-tuple-element.55), channel_id=1, source_target_pairs={{0,28},{4,0},{8,4},{12,8},{16,12},{20,16},{24,20},{28,24},{1,29},{... | collective-permute-start | bytes 294920 | tf_op jit(solution)/shard_map/ppermute | solution.py:26
  87.8 6.8 %collective-permute-start.16 = (f16[48,1024]{1,0:T(8,128)(2,1)S(1)}, f16[48,1024]{1,0:T(8,128)(2,1)S(1)}, u32[]{:S(2)}, u32[]{:S(2)}) collective-permute-start(f16[48,1024]{1,0:T(8,128)(2,1)S(1)} %get-tuple-element.54), channel_id=1, source_target_pairs={{0,4},{4,8},{8,12},{12,16},{16,20},{20,24},{24,28},{28,0},{1,5},{5... | collective-permute-start | bytes 294920 | tf_op jit(solution)/shard_map/ppermute | solution.py:26
  87.8 6.8 %collective-permute-start.17 = (f16[48,1024]{1,0:T(8,128)(2,1)S(1)}, f16[48,1024]{1,0:T(8,128)(2,1)S(1)}, u32[]{:S(2)}, u32[]{:S(2)}) collective-permute-start(f16[48,1024]{1,0:T(8,128)(2,1)S(1)} %get-tuple-element.53), channel_id=1, source_target_pairs={{0,28},{4,0},{8,4},{12,8},{16,12},{20,16},{24,20},{28,24},{1,29},{... | collective-permute-start | bytes 294920 | tf_op jit(solution)/shard_map/ppermute | solution.py:26
  90.4 4.1 %collective-permute-start.15 = (f16[24,1024]{1,0:T(8,128)(2,1)S(1)}, f16[24,1024]{1,0:T(8,128)(2,1)S(1)}, u32[]{:S(2)}, u32[]{:S(2)}) collective-permute-start(f16[24,1024]{1,0:T(8,128)(2,1)S(1)} %get-tuple-element.57), channel_id=1, source_target_pairs={{0,24},{4,28},{8,0},{12,4},{16,8},{20,12},{24,16},{28,20},{1,25},{... | collective-permute-start | bytes 147464 | tf_op jit(solution)/shard_map/ppermute | solution.py:26
  94.7 5.5 %collective-permute-start.19 = (f16[48,1024]{1,0:T(8,128)(2,1)S(1)}, f16[48,1024]{1,0:T(8,128)(2,1)S(1)}, u32[]{:S(2)}, u32[]{:S(2)}) collective-permute-start(f16[48,1024]{1,0:T(8,128)(2,1)S(1)} %pad_maximum_fusion.3), channel_id=1, source_target_pairs={{0,24},{4,28},{8,0},{12,4},{16,8},{20,12},{24,16},{28,20},{1,25},{... | collective-permute-start | bytes 294920 | tf_op jit(solution)/shard_map/ppermute | solution.py:26
  97.7 6.6 %collective-permute-start.18 = (f16[48,1024]{1,0:T(8,128)(2,1)S(1)}, f16[48,1024]{1,0:T(8,128)(2,1)S(1)}, u32[]{:S(2)}, u32[]{:S(2)}) collective-permute-start(f16[48,1024]{1,0:T(8,128)(2,1)S(1)} %pad_maximum_fusion.2), channel_id=1, source_target_pairs={{0,8},{4,12},{8,16},{12,20},{16,24},{20,28},{24,0},{28,4},{1,9},{5... | collective-permute-start | bytes 294920 | tf_op jit(solution)/shard_map/ppermute | solution.py:26
  110.8 14.2 %all-to-all-start.2 = ((f32[16,1,128]{2,1,0:T(1,128)}), f32[16,1,128]{2,1,0:T(1,128)S(1)}, u32[]{:S(2)}, u32[]{:S(2)}) async-start(f32[16,1,128]{2,1,0:T(1,128)} %broadcast_in_dim_broadcast_in_dim.3), calls=%async_computation.2 | async-start | bytes 16384 | tf_op jit(solution)/shard_map/all_to_all | solution.py:17

commit v5 on v4

--- a/solution.py
+++ b/solution.py
@@ -21,23 +21,25 @@
     return exchanged(jnp.broadcast_to(array, (lax.axis_size(axes), *array.shape)), axes)
 
 
-def to_offset(array, offset):
+def along_z(array, chips):
     n = lax.axis_size("z")
-    return lax.ppermute(array, "z", [(i, (i + offset) % n) for i in range(n)])
+    pairs = []
+    for z in range(n):
+        pairs.append((2 * z, 2 * ((z + chips) % n)))
+        pairs.append((2 * z + 1, 2 * ((z - chips) % n) + 1))
+    return lax.ppermute(array, ("z", "section"), pairs)
 
 
-def flipped(array, axis, bit):
-    n = lax.axis_size(axis)
-    return lax.ppermute(array, axis, [(i, i ^ bit) for i in range(n)])
+def row_half(array, which):
+    half = array.shape[0] // 2
+    return lax.dynamic_slice_in_dim(array, which * half, half, 0)
 
 
-def gathered_over_z(own):
-    cut = own.shape[0] // 2
-    below, above = tied(to_offset(own, 1), to_offset(own, -1))
-    below2, above2 = tied(to_offset(below, 1), to_offset(above, -1))
-    top, bottom = to_offset(below2[:cut], 2), to_offset(above2[cut:], -2)
-    below3, above3 = to_offset(below2, 1), to_offset(above2, -1)
-    return [own, below, above, below2, above2, below3, above3, top, bottom]
+def gathered_over_z(own, section):
+    two = along_z(own, 2)
+    one_three = along_z(jnp.concatenate([own, two], axis=0), 1)
+    four = along_z(row_half(two, section), 2)
+    return jnp.concatenate([own, one_three, two, four], axis=0)
 
 
 def tied(*arrays):
@@ -62,21 +64,20 @@
     return sent[..., :width].astype(F32), value
 
 
-def summed_over_z(parts):
-    own, below, above, below2, above2, below3, above3, across = parts
-    cut = own.shape[0] // 2
-    halves = across.astype(SENT)
-    up3, down3 = to_offset(above3.astype(SENT), 1), to_offset(below3.astype(SENT), -1)
-    up, down = to_offset(above.astype(SENT), 1), to_offset(below.astype(SENT), -1)
-    top, bottom = to_offset(halves[:cut], 2), to_offset(halves[cut:], -2)
-    up3, down3, top, bottom, up, down = tied(up3, down3, top, bottom, up, down)
-    up2 = above2 + up3.astype(F32)
-    up2 = jnp.concatenate([up2[:cut] + top.astype(F32), up2[cut:]], axis=0)
-    down2 = below2 + down3.astype(F32)
-    down2 = jnp.concatenate([down2[:cut], down2[cut:] + bottom.astype(F32)], axis=0)
-    up2, down2 = tied(to_offset(up2.astype(SENT), 2), to_offset(down2.astype(SENT), -2))
-    near = own + up.astype(F32) + down.astype(F32)
-    return near + up2.astype(F32) + down2.astype(F32)
+def summed_over_z(kept, section):
+    half = kept.shape[0] // 8
+    one_three = along_z(kept[: 4 * half].astype(SENT), -1)
+    four = along_z(kept[6 * half : 7 * half].astype(SENT), -2)
+    one_three, four = tied(one_three, four)
+    four = four.astype(F32)
+    upper = kept[4 * half : 5 * half] + jnp.where(section == 0, four, 0.0)
+    lower = kept[5 * half : 6 * half] + jnp.where(section == 0, 0.0, four)
+    two = jnp.concatenate([upper, lower], axis=0) + one_three[2 * half :].astype(F32)
+    two = along_z(two.astype(SENT), -2).astype(F32)
+    given = row_half(one_three[: 2 * half], 1 - section).astype(F32) + row_half(two, 1 - section)
+    got = lax.ppermute(given, "section", SWAP)
+    mine = row_half(one_three[: 2 * half], section).astype(F32) + row_half(two, section)
+    return kept[7 * half :] + mine + got
 
 
 def tower(inputs, up, down, tensor):
@@ -93,12 +94,13 @@
     own = lax.optimization_barrier(own)
     raw = own + arrived
     norms = lax.rsqrt(jnp.sum(raw * raw, axis=-1, keepdims=True) + 1e-06)
-    return (raw * norms).astype(jnp.bfloat16).reshape(2, rows // 4, width)
+    return (raw * norms).astype(jnp.bfloat16)
 
 
-def pair_lanes(pair, section, tensor, quarter):
-    rows = lax.dynamic_slice_in_dim(pair, (section * 2 + tensor) * quarter, quarter)[:, None]
-    lane = lax.broadcasted_iota(jnp.int32, (quarter, LANES), 1)
+def pair_lanes(pair, tensor, quarter):
+    rows = lax.dynamic_slice_in_dim(pair.reshape(2, 2, quarter), tensor, 1, 1)
+    rows = rows.reshape(2 * quarter, 1)
+    lane = lax.broadcasted_iota(jnp.int32, (2 * quarter, LANES), 1)
     digits = jnp.where(lane == 0, rows // LANES, jnp.where(lane == 1, rows % LANES, 0))
     return digits.astype(jnp.bfloat16)
 
@@ -132,19 +134,17 @@
     quarter, width = tower_input.shape[1] // 4, tower_input.shape[2]
     total = lax.axis_size(ALL) * quarter
 
-    lanes = pair_lanes(pair, section, tensor, quarter)
+    lanes = pair_lanes(pair, tensor, quarter)
     embedded = tower(tower_input[0], up_weight[0], down_weight[0], tensor)
-    mine = lax.dynamic_index_in_dim(embedded, section, 0, keepdims=False)
-    given = lax.dynamic_index_in_dim(embedded, 1 - section, 0, keepdims=False)
-    got = lax.ppermute(given, "section", SWAP)
-    slides = jnp.concatenate([jnp.where(section == 0, mine, got), lanes], axis=1)
-    reports = jnp.where(section == 0, got, mine)
+    swapped = lax.ppermute(embedded, "section", SWAP)
+    slides = jnp.concatenate([jnp.where(section == 0, embedded, swapped), lanes], axis=1)
+    reports = row_half(jnp.where(section == 0, swapped, embedded), section)
 
     repeated = jnp.broadcast_to(reports, (n_plane, *reports.shape))
     repeated, slides = tied(repeated, slides)
     reports_all = exchanged(repeated, PLANE).reshape(n_plane * quarter, -1)
-    rows_mine = jnp.concatenate(gathered_over_z(slides), axis=0)
-    rows_other = lax.ppermute(rows_mine, "section", SWAP)
+    rows_mine = gathered_over_z(slides, section)
+    rows_other = lax.ppermute(rows_mine[2 * quarter :], "section", SWAP)
 
     place = jnp.arange(n_plane * quarter, dtype=jnp.int32)
     member, row = place // quarter, place % quarter
@@ -157,23 +157,22 @@
     slides_other, weight_other, loss_other = scored(
         rows_other, width, reports_all, columns, scale_value, bias_value
     )
+    loss_value = jnp.broadcast_to(loss_mine + loss_other, (1, LANES))
+    loss_value = copies(loss_value, ("z", "section")).sum(axis=0)[0, 0]
     report_part = transposed_dot(weight_mine, slides_mine)
     report_part = report_part + transposed_dot(weight_other, slides_other)
-    report_part = with_digits(
-        report_part.reshape(n_plane, quarter, width), loss_mine + loss_other
-    )
+    report_part = with_digits(report_part.reshape(n_plane, quarter, width), loss_value)
     report_part, weight_mine, weight_other = tied(report_part, weight_mine, weight_other)
     report_terms = exchanged(report_part, PLANE)
-    slide_other = jnp.dot(weight_other, reports_all, preferred_element_type=F32)
-    slide_back = lax.ppermute(slide_other, "section", SWAP)
-    slide_mine = jnp.dot(weight_mine, reports_all, preferred_element_type=F32) + slide_back
-    parts = [slide_mine[k * quarter : (k + 1) * quarter] for k in range(n_z)]
-    slide_grad = summed_over_z(parts)
-    report_terms, slide_grad = tied(report_terms, slide_grad)
+    weight_own, weight_mine = weight_mine[: 2 * quarter], weight_mine[2 * quarter :]
+    weight_sent = jnp.concatenate([weight_other, row_half(weight_own, 1 - section)], axis=0)
+    weight_kept = jnp.concatenate([weight_mine, row_half(weight_own, section)], axis=0)
+    sent = jnp.dot(weight_sent, reports_all, preferred_element_type=F32)
+    back = lax.ppermute(sent, "section", SWAP)
+    kept = jnp.dot(weight_kept, reports_all, preferred_element_type=F32) + back
+    slide_grad = summed_over_z(kept, section)
     report_terms, loss_value = without_digits(report_terms)
-    losses = copies(jnp.broadcast_to(loss_value, (1, LANES)), ("z", "section"))
-    loss = jnp.sum(losses, axis=0)[0, :1] / total
-    return (loss, slide_grad, report_terms.sum(axis=0))
+    return (jnp.reshape(loss_value / total, (1,)), slide_grad, report_terms.sum(axis=0))
 
 
 def solution(mesh):

time: 127 us -> 130 us (1.024)
  waiting for transfers between devices: 31.2 us -> 54.7 us
  starting transfers between devices: 57.5 us -> 38.4 us
  matrix products: 21.3 us -> 17 us
  local copies, waits for them, and re-layouts: 3.99 us -> 7.38 us
    ppermute x19 -> x10, starting transfers between devices: 35.1 us -> 13.4 us  [the longest x6 8.43 us: along_z(): return lax.ppermute(array, ('z', 'section'), pairs)]
    all_to_all x3, waiting for transfers between devices: 9.38 us -> 27.8 us  [exchanged(): return lax.all_to_all(parts, axes, split_axis=0, concat_axis=0, tiled=True)]
    ppermute x19 -> x10, waiting for transfers between devices: 17.2 us -> 20.2 us  [the longest x6 17.5 us: along_z(): return lax.ppermute(array, ('z', 'section'), pairs)]
    all_to_all x3, starting transfers between devices: 18.7 us -> 21.3 us  [exchanged(): return lax.all_to_all(parts, axes, split_axis=0, concat_axis=0, tiled=True)]
    dot_general x1, matrix products: 3.01 us -> 0.82 us  [tower(): own = jnp.dot(later, down, preferred_element_type=F32) + kept.astype(F32)]
    ppermute x1, waiting for transfers between devices: 4.61 us -> 6.69 us  [tower(): arrived = lax.ppermute(sent, 'tensor', SWAP)]
    slice x4 -> x5, local copies, waits for them, and re-layouts: 0.1 us -> 2.12 us  [the longest x1 1.07 us: local(): weight_mine[2 * quarter:]]
  transfers between devices with their start and end apart: 23 -> 14, of which waited for: 11 -> 10; matrix products, arithmetic and copies ran while one was open for 7% -> 7% of each run, Pallas kernels for 0% -> 0%
where the time goes in v5:
time: 130 us
  waiting for transfers between devices  54.7 us (42%)
  starting transfers between devices  38.4 us (30%)
  matrix products  17 us (13%)
  local copies, waits for them, and re-layouts  7.38 us (6%)
  between operations  6.76 us (5%)
  other arithmetic  5.59 us (4%)
    all_to_all x3, waiting for transfers between devices, exchanged(): return lax.all_to_all(parts, axes, split_axis=0, concat_axis=0, tiled=True)  27.8 us
    all_to_all x3, starting transfers between devices, exchanged(): return lax.all_to_all(parts, axes, split_axis=0, concat_axis=0, tiled=True)  21.3 us
    ppermute x6, waiting for transfers between devices, along_z(): return lax.ppermute(array, ('z', 'section'), pairs)  17.5 us
    ppermute x6, starting transfers between devices, along_z(): return lax.ppermute(array, ('z', 'section'), pairs)  8.43 us
    ppermute x1, waiting for transfers between devices, tower(): arrived = lax.ppermute(sent, 'tensor', SWAP)  6.69 us
    dot_general x2, matrix products, scored(): lax.dot_general(slides, reports, (((1,), (1,)), ((), ())), preferred_elem...  5.49 us
    dot_general x1, matrix products, tower(): jnp.dot(ordered, up, preferred_element_type=F32)  3.69 us
    ppermute x1, starting transfers between devices, tower(): arrived = lax.ppermute(sent, 'tensor', SWAP)  3.66 us
  transfers between devices with their start and end apart: 14, of which 10 were waited for; matrix products, arithmetic and copies ran while one was open for 7% of the time, Pallas kernels for 0%

profile of v5, /device:TPU:1, one launch (start us, length us, event | category | flops | bytes accessed | tf_op | source)
XLA Modules:
  0.0 129.8 jit_solution(17775738435415237543)
XLA Ops:
  0.6 1.1 constant_dynamic-slice_fusion.5
  1.7 3.7 %fusion.15 = bf16[192,2048]{1,0:T(8,128)(2,1)S(1)} fusion(bf16[1,1024,2048]{2,1,0:T(8,128)(2,1)} %param.7, bf16[96,1024]{1,0:T(8,128)(2,1)S(1)} %bitcast.46, bf16[96,1024]{1,0:T(8,128)(2,1)S(1)} %bitcast.49), kind=kOutput, calls=%fused_computation.19 | convolution fusion | flops 809631744 | bytes 5373952 | tf_op jit(solution)/shard_map/dot_general | solution.py:89
  5.4 0.8 fusion.2
  6.2 3.7 %collective-permute-start = (f32[96,1024]{1,0:T(8,128)S(1)}, f32[96,1024]{1,0:T(8,128)S(1)}, u32[]{:S(2)}, u32[]{:S(2)}) collective-permute-start(f32[96,1024]{1,0:T(8,128)S(1)} %fusion.2), channel_id=1, source_target_pairs={{0,1},{1,0},{2,3},{3,2},{4,5},{5,4},{6,7},{7,6},{8,9},{9,8},{10,11... | collective-permute-start | bytes 1179656 | tf_op jit(solution)/shard_map/ppermute | solution.py:91
  9.9 0.8 fusion.22
  11.0 6.7 %collective-permute-done = f32[96,1024]{1,0:T(8,128)S(1)} collective-permute-done((f32[96,1024]{1,0:T(8,128)S(1)}, f32[96,1024]{1,0:T(8,128)S(1)}, u32[]{:S(2)}, u32[]{:S(2)}) %collective-permute-start) | collective-permute-done | bytes 393248 | tf_op jit(solution)/shard_map/ppermute | solution.py:91
  17.7 0.1 multiply_reduce_fusion
  17.8 0.1 multiply_convert_fusion
  17.9 2.4 %collective-permute-start.1 = (bf16[96,1024]{1,0:T(8,128)(2,1)S(1)}, bf16[96,1024]{1,0:T(8,128)(2,1)S(1)}, u32[]{:S(2)}, u32[]{:S(2)}) collective-permute-start(bf16[96,1024]{1,0:T(8,128)(2,1)S(1)} %multiply_convert_fusion), channel_id=1, source_target_pairs={{0,2},{2,0},{1,3},{3,1},{4,6},{6,4},{5,7},{7,5},{8,10},{10,8},{9,1... | collective-permute-start | bytes 589832 | tf_op jit(solution)/shard_map/ppermute | solution.py:139
  20.4 1.0 collective-permute-done.1
  21.4 0.1 broadcast_select_fusion.1
  21.6 1.3 %broadcast_in_dim.68 = bf16[16,48,1024]{2,1,0:T(8,128)(2,1)} broadcast(bf16[48,1024]{1,0:T(8,128)(2,1)S(1)} %dynamic-slice_select_fusion), dimensions={1,2} | broadcast | bytes 1671168 | tf_op jit(solution)/shard_map/broadcast_in_dim | solution.py:143
  22.9 6.2 %collective-permute-start.2 = (bf16[96,1152]{1,0:T(8,128)(2,1)S(1)}, bf16[96,1152]{1,0:T(8,128)(2,1)S(1)}, u32[]{:S(2)}, u32[]{:S(2)}) collective-permute-start(bf16[96,1152]{1,0:T(8,128)(2,1)S(1)} %pad_maximum_fusion.3), channel_id=1, source_target_pairs={{0,8},{2,26},{4,12},{6,30},{8,16},{10,2},{12,20},{14,6},{16,24},{1... | collective-permute-start | bytes 663560 | tf_op jit(solution)/shard_map/ppermute | solution.py:30
  30.5 6.8 %all-to-all-start = ((bf16[16,48,1024]{2,1,0:T(8,128)(2,1)}), bf16[16,48,1024]{2,1,0:T(8,128)(2,1)S(1)}, u32[]{:S(2)}, u32[]{:S(2)}) async-start(bf16[16,48,1024]{2,1,0:T(8,128)(2,1)} %broadcast_in_dim.68), calls=%async_computation | async-start | bytes 3145728 | tf_op jit(solution)/shard_map/all_to_all | solution.py:17
  37.3 0.8 collective-permute-start.3
  38.1 0.5 collective-permute-start.4
  38.7 9.0 %collective-permute-done.4 = bf16[48,1152]{1,0:T(8,128)(2,1)S(1)} collective-permute-done((bf16[48,1152]{1,0:T(8,128)(2,1)S(1)}, bf16[48,1152]{1,0:T(8,128)(2,1)S(1)}, u32[]{:S(2)}, u32[]{:S(2)}) %collective-permute-start.4) | collective-permute-done | bytes 110624 | tf_op jit(solution)/shard_map/ppermute | solution.py:30
  47.7 0.8 collective-permute-start.5
  48.6 0.2 add_reduce_fusion.2
  48.8 1.6 %collective-permute-done.5 = bf16[336,1152]{1,0:T(8,128)(2,1)S(1)} collective-permute-done((bf16[336,1152]{1,0:T(8,128)(2,1)S(1)}, bf16[336,1152]{1,0:T(8,128)(2,1)S(1)}, u32[]{:S(2)}, u32[]{:S(2)}) %collective-permute-start.5) | collective-permute-done | bytes 774176 | tf_op jit(solution)/shard_map/ppermute | solution.py:147
  50.4 0.9 copy-done.7
  51.3 0.2 add_reduce_fusion.3
  51.5 7.1 %all-to-all-done = bf16[16,48,1024]{2,1,0:T(8,128)(2,1)S(1)} async-done(((bf16[16,48,1024]{2,1,0:T(8,128)(2,1)}), bf16[16,48,1024]{2,1,0:T(8,128)(2,1)S(1)}, u32[]{:S(2)}, u32[]{:S(2)}) %all-to-all-start) | async-done | bytes 1572896 | tf_op jit(solution)/shard_map/all_to_all | solution.py:17
  58.6 3.3 %fusion.21 = (bf16[432,768]{1,0:T(8,128)(2,1)}, f32[]{:T(128)}) fusion(f32[]{:T(128)} %bitcast.37, f32[]{:T(128)S(6)} %neg.16, f32[768]{0:T(1024)S(1)} %fusion.62, f32[432]{0:T(512)S(1)} %add_reduce_fusion.2, f32[]{:T(128)} %bitcast.39, bf16[768,1024]{1,0:T(8,128)(2,1)S(1)} %bitcast.41, bf16[432,1152]{1,0:T(8,128)(2,1)S(1)} %constant_dynamic-update-slice_fusion), kind=kOutput, calls=%fused_computation.27 | convolution fusion | flops 685117440 | bytes 3127312 | tf_op jit(solution)/shard_map/dot_general | solution.py:111
  61.9 2.2 %fusion.26 = (bf16[336,768]{1,0:T(8,128)(2,1)S(1)}, f32[]{:T(128)}) fusion(f32[]{:T(128)} %bitcast.38, f32[]{:T(128)S(6)} %neg.16, f32[768]{0:T(1024)S(1)} %fusion.62, f32[336]{0:T(512)S(1)} %add_reduce_fusion.3, f32[]{:T(128)} %bitcast.40, bf16[768,1024]{1,0:T(8,128)(2,1)S(1)} %bitcast.42, bf16[336,1152]{1,0:T(8,128)(2,1)S(1)} %copy-done.8), kind=kOutput, calls=%fused_computation.33 | convolution fusion | flops 532869120 | bytes 2783248 | tf_op jit(solution)/shard_map/dot_general | solution.py:111
  65.4 0.6 broadcast_in_dim_broadcast_in_dim.3
  66.0 8.5 %all-to-all-start.1 = ((f32[16,1,128]{2,1,0:T(1,128)}), f32[16,1,128]{2,1,0:T(1,128)S(1)}, u32[]{:S(2)}, u32[]{:S(2)}) async-start(f32[16,1,128]{2,1,0:T(1,128)} %broadcast_in_dim_broadcast_in_dim.3), calls=%async_computation.1 | async-start | bytes 16384 | tf_op jit(solution)/shard_map/all_to_all | solution.py:17
  74.4 1.0 fusion.29
  75.5 0.3 copy-done.6
  75.8 1.0 add_convert_fusion
  76.9 4.5 %all-to-all-done.1 = f32[16,1,128]{2,1,0:T(1,128)S(1)} async-done(((f32[16,1,128]{2,1,0:T(1,128)}), f32[16,1,128]{2,1,0:T(1,128)S(1)}, u32[]{:S(2)}, u32[]{:S(2)}) %all-to-all-start.1) | async-done | bytes 8224 | tf_op jit(solution)/shard_map/all_to_all | solution.py:17
  81.6 1.7 %pad_maximum_fusion = f16[16,48,1152]{2,1,0:T(8,128)(2,1)} fusion(f16[16,48,128]{2,1,0:T(8,128)(2,1)S(1)} %broadcast_select_fusion, f16[16,48,1024]{2,1,0:T(8,128)(2,1)S(1)} %bitcast.45), kind=kLoop, calls=%fused_computation.10 | loop fusion | flops 884736 | bytes 3538944 | tf_op jit(solution)/shard_map/concatenate | solution.py:57
  83.3 0.9 slice.88
  84.2 1.9 %fusion.35 = f32[384,1024]{1,0:T(8,128)} fusion(bf16[768,1024]{1,0:T(8,128)(2,1)S(1)} %bitcast.43, bf16[48,768]{1,0:T(8,128)(2,1)S(1)} %get-tuple-element.30, bf16[336,768]{1,0:T(8,128)(2,1)S(1)} %copy-done.4), kind=kOutput, calls=%fused_computation.45 | convolution fusion | flops 605159424 | bytes 3735552 | tf_op jit(solution)/shard_map/dot_general | solution.py:170
  86.2 0.7 collective-permute-start.6
  86.8 6.1 %all-to-all-start.2 = ((f16[16,48,1152]{2,1,0:T(8,128)(2,1)}), f16[16,48,1152]{2,1,0:T(8,128)(2,1)S(1)}, u32[]{:S(2)}, u32[]{:S(2)}) async-start(f16[16,48,1152]{2,1,0:T(8,128)(2,1)} %pad_maximum_fusion), calls=%async_computation.2 | async-start | bytes 3538944 | tf_op jit(solution)/shard_map/all_to_all | solution.py:17
  92.9 1.1 slice.87
  94.0 2.2 %fusion.73 = (f16[384,1024]{1,0:T(8,128)(2,1)S(1)}, f32[384,1024]{1,0:T(8,128)S(1)}) fusion(f32[384,1024]{1,0:T(8,128)} %collective-permute-done.6, bf16[768,1024]{1,0:T(8,128)(2,1)S(1)} %bitcast.44, bf16[48,768]{1,0:T(8,128)(2,1)S(1)} %get-tuple-element.29, bf16[336,768]{1,0:T(8,128)(2,1)S(1)} %slice.87), kind=kOutput, calls=%fused_computation.128 | convolution fusion | flops 605945856 | bytes 6094848 | tf_op jit(solution)/shard_map/dot_general | solution.py:172
  96.3 0.3 collective-permute-start.7
  96.7 0.4 collective-permute-start.8
  97.1 7.4 %collective-permute-done.8 = f16[48,1024]{1,0:T(8,128)(2,1)S(1)} collective-permute-done((f16[48,1024]{1,0:T(8,128)(2,1)S(1)}, f16[48,1024]{1,0:T(8,128)(2,1)S(1)}, u32[]{:S(2)}, u32[]{:S(2)}) %collective-permute-start.8) | collective-permute-done | bytes 98336 | tf_op jit(solution)/shard_map/ppermute | solution.py:30
  104.5 1.1 collective-permute-done.7
  105.8 16.3 %all-to-all-done.2 = f16[16,48,1152]{2,1,0:T(8,128)(2,1)S(1)} async-done(((f16[16,48,1152]{2,1,0:T(8,128)(2,1)}), f16[16,48,1152]{2,1,0:T(8,128)(2,1)S(1)}, u32[]{:S(2)}, u32[]{:S(2)}) %all-to-all-start.2) | async-done | bytes 1769504 | tf_op jit(solution)/shard_map/all_to_all | solution.py:17
  122.1 0.6 fusion.72
  124.8 1.2 collective-permute-start.10
  126.0 0.9 convert_reduce_fusion
  126.9 0.2 collective-permute-done.10
  127.1 1.7 %fusion.46 = f32[48,1024]{1,0:T(8,128)} fusion(f32[48,1024]{1,0:T(8,128)S(1)} %collective-permute-done.10, f32[384,1024]{1,0:T(8,128)} %copy-done.1, f32[96,1024]{1,0:T(8,128)S(1)} %convert_element_type.112, s32[]{:T(128)S(6)} %select_n.148, f16[96,1024]{1,0:T(8,128)(2,1)S(1)} %slice.92), kind=kLoop, calls=%fused_computation.65 | loop fusion | flops 196608 | bytes 884740 | tf_op jit(solution)/shard_map/add | solution.py:80
  (55 shorter events, 1.2 us)
Async XLA Ops:
  1.7 3.7 %copy-start = (bf16[1,2048,1024]{2,1,0:T(8,128)(2,1)S(1)}, bf16[1,2048,1024]{2,1,0:T(8,128)(2,1)}, u32[]{:S(2)}) copy-start(bf16[1,2048,1024]{2,1,0:T(8,128)(2,1)} %param.8) | copy-start | bytes 12582916
  6.2 11.4 %collective-permute-start = (f32[96,1024]{1,0:T(8,128)S(1)}, f32[96,1024]{1,0:T(8,128)S(1)}, u32[]{:S(2)}, u32[]{:S(2)}) collective-permute-start(f32[96,1024]{1,0:T(8,128)S(1)} %fusion.2), channel_id=1, source_target_pairs={{0,1},{1,0},{2,3},{3,2},{4,5},{5,4},{6,7},{7,6},{8,9},{9,8},{10,11... | collective-permute-start | bytes 1179656 | tf_op jit(solution)/shard_map/ppermute | solution.py:91
  9.9 0.8 copy-start.10
  17.9 3.4 %collective-permute-start.1 = (bf16[96,1024]{1,0:T(8,128)(2,1)S(1)}, bf16[96,1024]{1,0:T(8,128)(2,1)S(1)}, u32[]{:S(2)}, u32[]{:S(2)}) collective-permute-start(bf16[96,1024]{1,0:T(8,128)(2,1)S(1)} %multiply_convert_fusion), channel_id=1, source_target_pairs={{0,2},{2,0},{1,3},{3,1},{4,6},{6,4},{5,7},{7,5},{8,10},{10,8},{9,1... | collective-permute-start | bytes 589832 | tf_op jit(solution)/shard_map/ppermute | solution.py:139
  22.9 14.3 %collective-permute-start.2 = (bf16[96,1152]{1,0:T(8,128)(2,1)S(1)}, bf16[96,1152]{1,0:T(8,128)(2,1)S(1)}, u32[]{:S(2)}, u32[]{:S(2)}) collective-permute-start(bf16[96,1152]{1,0:T(8,128)(2,1)S(1)} %pad_maximum_fusion.3), channel_id=1, source_target_pairs={{0,8},{2,26},{4,12},{6,30},{8,16},{10,2},{12,20},{14,6},{16,24},{1... | collective-permute-start | bytes 663560 | tf_op jit(solution)/shard_map/ppermute | solution.py:30
  30.5 28.1 %all-to-all-start = ((bf16[16,48,1024]{2,1,0:T(8,128)(2,1)}), bf16[16,48,1024]{2,1,0:T(8,128)(2,1)S(1)}, u32[]{:S(2)}, u32[]{:S(2)}) async-start(bf16[16,48,1024]{2,1,0:T(8,128)(2,1)} %broadcast_in_dim.68), calls=%async_computation | async-start | bytes 3145728 | tf_op jit(solution)/shard_map/all_to_all | solution.py:17
  37.3 10.3 %collective-permute-start.3 = (bf16[192,1152]{1,0:T(8,128)(2,1)S(1)}, bf16[192,1152]{1,0:T(8,128)(2,1)S(1)}, u32[]{:S(2)}, u32[]{:S(2)}) collective-permute-start(bf16[192,1152]{1,0:T(8,128)(2,1)S(1)} %pad_maximum_fusion.2), channel_id=1, source_target_pairs={{0,4},{2,30},{4,8},{6,2},{8,12},{10,6},{12,16},{14,10},{16,20},{18... | collective-permute-start | bytes 1327112 | tf_op jit(solution)/shard_map/ppermute | solution.py:30
  38.1 9.5 %collective-permute-start.4 = (bf16[48,1152]{1,0:T(8,128)(2,1)S(1)}, bf16[48,1152]{1,0:T(8,128)(2,1)S(1)}, u32[]{:S(2)}, u32[]{:S(2)}) collective-permute-start(bf16[48,1152]{1,0:T(8,128)(2,1)S(1)} %constant_dynamic-slice_fusion.2), channel_id=1, source_target_pairs={{0,8},{2,26},{4,12},{6,30},{8,16},{10,2},{12,20},{14,6},{16,24},{1... | collective-permute-start | bytes 331784 | tf_op jit(solution)/shard_map/ppermute | solution.py:30
  47.7 2.6 %collective-permute-start.5 = (bf16[336,1152]{1,0:T(8,128)(2,1)S(1)}, bf16[336,1152]{1,0:T(8,128)(2,1)S(1)}, u32[]{:S(2)}, u32[]{:S(2)}) collective-permute-start(bf16[336,1152]{1,0:T(8,128)(2,1)S(1)} %pad_maximum_fusion.1), channel_id=1, source_target_pairs={{0,2},{2,0},{1,3},{3,1},{4,6},{6,4},{5,7},{7,5},{8,10},{10,8},{9,1... | collective-permute-start | bytes 2322440 | tf_op jit(solution)/shard_map/ppermute | solution.py:147
  48.6 13.3 %copy-start.5 = (bf16[432,1152]{1,0:T(8,128)(2,1)}, bf16[432,1152]{1,0:T(8,128)(2,1)S(1)}, u32[]{:S(2)}) copy-start(bf16[432,1152]{1,0:T(8,128)(2,1)S(1)} %constant_dynamic-update-slice_fusion) | copy-start | bytes 2985988
  50.4 0.9 copy-start.7
  58.6 3.3 %copy-start.8 = (bf16[336,1152]{1,0:T(8,128)(2,1)S(1)}, bf16[336,1152]{1,0:T(8,128)(2,1)}, u32[]{:S(2)}) copy-start(bf16[336,1152]{1,0:T(8,128)(2,1)} %copy-done.7) | copy-start | bytes 2322436
  61.9 12.5 %copy-start.9 = (bf16[336,1152]{1,0:T(8,128)(2,1)S(1)}, bf16[336,1152]{1,0:T(8,128)(2,1)}, u32[]{:S(2)}) copy-start(bf16[336,1152]{1,0:T(8,128)(2,1)} %copy-done.7) | copy-start | bytes 2322436
  64.1 11.4 %copy-start.3 = (bf16[336,768]{1,0:T(8,128)(2,1)}, bf16[336,768]{1,0:T(8,128)(2,1)S(1)}, u32[]{:S(2)}) copy-start(bf16[336,768]{1,0:T(8,128)(2,1)S(1)} %get-tuple-element.16) | copy-start | bytes 1548292
  66.0 15.4 %all-to-all-start.1 = ((f32[16,1,128]{2,1,0:T(1,128)}), f32[16,1,128]{2,1,0:T(1,128)S(1)}, u32[]{:S(2)}, u32[]{:S(2)}) async-start(f32[16,1,128]{2,1,0:T(1,128)} %broadcast_in_dim_broadcast_in_dim.3), calls=%async_computation.1 | async-start | bytes 16384 | tf_op jit(solution)/shard_map/all_to_all | solution.py:17
  74.4 1.1 copy-start.2
  74.4 1.4 %copy-start.6 = (bf16[432,1152]{1,0:T(8,128)(2,1)S(1)}, bf16[432,1152]{1,0:T(8,128)(2,1)}, u32[]{:S(2)}) copy-start(bf16[432,1152]{1,0:T(8,128)(2,1)} %copy-done.5) | copy-start | bytes 2985988
  81.5 2.7 %copy-start.4 = (bf16[336,768]{1,0:T(8,128)(2,1)S(1)}, bf16[336,768]{1,0:T(8,128)(2,1)}, u32[]{:S(2)}) copy-start(bf16[336,768]{1,0:T(8,128)(2,1)} %copy-done.3) | copy-start | bytes 1548292
  86.2 7.8 %collective-permute-start.6 = (f32[384,1024]{1,0:T(8,128)}, f32[384,1024]{1,0:T(8,128)}, u32[]{:S(2)}, u32[]{:S(2)}) collective-permute-start(f32[384,1024]{1,0:T(8,128)} %fusion.35), channel_id=1, source_target_pairs={{0,2},{2,0},{1,3},{3,1},{4,6},{6,4},{5,7},{7,5},{8,10},{10,8},{9,1... | collective-permute-start | bytes 4718600 | tf_op jit(solution)/shard_map/ppermute | solution.py:171
  86.8 35.3 %all-to-all-start.2 = ((f16[16,48,1152]{2,1,0:T(8,128)(2,1)}), f16[16,48,1152]{2,1,0:T(8,128)(2,1)S(1)}, u32[]{:S(2)}, u32[]{:S(2)}) async-start(f16[16,48,1152]{2,1,0:T(8,128)(2,1)} %pad_maximum_fusion), calls=%async_computation.2 | async-start | bytes 3538944 | tf_op jit(solution)/shard_map/all_to_all | solution.py:17
  96.3 9.5 %copy-start.1 = (f32[384,1024]{1,0:T(8,128)}, f32[384,1024]{1,0:T(8,128)S(1)}, u32[]{:S(2)}) copy-start(f32[384,1024]{1,0:T(8,128)S(1)} %get-tuple-element.37) | copy-start | bytes 4718596
  96.3 9.3 %collective-permute-start.7 = (f16[192,1024]{1,0:T(8,128)(2,1)S(1)}, f16[192,1024]{1,0:T(8,128)(2,1)S(1)}, u32[]{:S(2)}, u32[]{:S(2)}) collective-permute-start(f16[192,1024]{1,0:T(8,128)(2,1)S(1)} %slice.107), channel_id=1, source_target_pairs={{0,28},{2,6},{4,0},{6,10},{8,4},{10,14},{12,8},{14,18},{16,12},{18... | collective-permute-start | bytes 1179656 | tf_op jit(solution)/shard_map/ppermute | solution.py:30
  96.7 7.8 %collective-permute-start.8 = (f16[48,1024]{1,0:T(8,128)(2,1)S(1)}, f16[48,1024]{1,0:T(8,128)(2,1)S(1)}, u32[]{:S(2)}, u32[]{:S(2)}) collective-permute-start(f16[48,1024]{1,0:T(8,128)(2,1)S(1)} %slice.108), channel_id=1, source_target_pairs={{0,24},{2,10},{4,28},{6,14},{8,0},{10,18},{12,4},{14,22},{16,8},{1... | collective-permute-start | bytes 294920 | tf_op jit(solution)/shard_map/ppermute | solution.py:30
  105.7 19.0 %collective-permute-start.9 = (f16[96,1024]{1,0:T(8,128)(2,1)S(1)}, f16[96,1024]{1,0:T(8,128)(2,1)S(1)}, u32[]{:S(2)}, u32[]{:S(2)}) collective-permute-start(f16[96,1024]{1,0:T(8,128)(2,1)S(1)} %fusion.43), channel_id=1, source_target_pairs={{0,24},{2,10},{4,28},{6,14},{8,0},{10,18},{12,4},{14,22},{16,8},{1... | collective-permute-start | bytes 589832 | tf_op jit(solution)/shard_map/ppermute | solution.py:30
  124.8 2.3 %collective-permute-start.10 = (f32[48,1024]{1,0:T(8,128)S(1)}, f32[48,1024]{1,0:T(8,128)S(1)}, u32[]{:S(2)}, u32[]{:S(2)}) collective-permute-start(f32[48,1024]{1,0:T(8,128)S(1)} %dynamic-slice_add_fusion), channel_id=1, source_target_pairs={{0,2},{2,0},{1,3},{3,1},{4,6},{6,4},{5,7},{7,5},{8,10},{10,8},{9,1... | collective-permute-start | bytes 589832 | tf_op jit(solution)/shard_map/ppermute | solution.py:78

commit v6 on v5

--- a/solution.py
+++ b/solution.py
@@ -46,38 +46,30 @@
     return lax.optimization_barrier(arrays)
 
 
-def with_digits(part, value):
-    high = (value / 4096.0).astype(SENT)
-    value = value - high.astype(F32) * 4096.0
-    middle = (value / 4.0).astype(SENT)
-    low = (value - middle.astype(F32) * 4.0).astype(SENT)
-    shape = (*part.shape[:-1], LANES)
-    lane = lax.broadcasted_iota(jnp.int32, shape, len(shape) - 1)
-    lanes = jnp.where(lane == 0, high, jnp.where(lane == 1, middle, low))
-    return jnp.concatenate([part.astype(SENT), lanes], axis=-1)
+def with_partner(value, axis, bit):
+    pairs = [(i, i ^ bit) for i in range(lax.axis_size(axis))]
+    return value + lax.ppermute(value, axis, pairs)
 
 
-def without_digits(sent):
-    width = sent.shape[-1] - LANES
-    lanes = sent[:, 0, width:].astype(F32).sum(axis=0)
-    value = lanes[0] * 4096.0 + lanes[1] * 4.0 + lanes[2]
-    return sent[..., :width].astype(F32), value
-
-
-def summed_over_z(kept, section):
+def summed_over_z(kept, section, loss):
     half = kept.shape[0] // 8
     one_three = along_z(kept[: 4 * half].astype(SENT), -1)
     four = along_z(kept[6 * half : 7 * half].astype(SENT), -2)
-    one_three, four = tied(one_three, four)
+    loss = with_partner(with_partner(loss, "y", 1), "y", 2)
+    one_three, four, loss = tied(one_three, four, loss)
     four = four.astype(F32)
     upper = kept[4 * half : 5 * half] + jnp.where(section == 0, four, 0.0)
     lower = kept[5 * half : 6 * half] + jnp.where(section == 0, 0.0, four)
     two = jnp.concatenate([upper, lower], axis=0) + one_three[2 * half :].astype(F32)
-    two = along_z(two.astype(SENT), -2).astype(F32)
+    two = along_z(two.astype(SENT), -2)
+    loss = with_partner(loss, "z", 1)
+    two, loss = tied(two, loss)
+    two = two.astype(F32)
     given = row_half(one_three[: 2 * half], 1 - section).astype(F32) + row_half(two, 1 - section)
     got = lax.ppermute(given, "section", SWAP)
+    loss = with_partner(with_partner(loss, "z", 2), "z", 4)
     mine = row_half(one_three[: 2 * half], section).astype(F32) + row_half(two, section)
-    return kept[7 * half :] + mine + got
+    return kept[7 * half :] + mine + got, loss
 
 
 def tower(inputs, up, down, tensor):
@@ -157,22 +149,27 @@
     slides_other, weight_other, loss_other = scored(
         rows_other, width, reports_all, columns, scale_value, bias_value
     )
-    loss_value = jnp.broadcast_to(loss_mine + loss_other, (1, LANES))
-    loss_value = copies(loss_value, ("z", "section")).sum(axis=0)[0, 0]
+    loss = with_partner(jnp.broadcast_to(loss_mine + loss_other, (1, LANES)), "section", 1)
     report_part = transposed_dot(weight_mine, slides_mine)
     report_part = report_part + transposed_dot(weight_other, slides_other)
-    report_part = with_digits(report_part.reshape(n_plane, quarter, width), loss_value)
-    report_part, weight_mine, weight_other = tied(report_part, weight_mine, weight_other)
+    report_part = report_part.astype(SENT).reshape(n_plane, quarter, width)
+    report_part, weight_mine, weight_other, loss = tied(
+        report_part, weight_mine, weight_other, loss
+    )
     report_terms = exchanged(report_part, PLANE)
+    loss = with_partner(loss, "tensor", 1)
     weight_own, weight_mine = weight_mine[: 2 * quarter], weight_mine[2 * quarter :]
     weight_sent = jnp.concatenate([weight_other, row_half(weight_own, 1 - section)], axis=0)
     weight_kept = jnp.concatenate([weight_mine, row_half(weight_own, section)], axis=0)
     sent = jnp.dot(weight_sent, reports_all, preferred_element_type=F32)
+    sent, loss = tied(sent, loss)
     back = lax.ppermute(sent, "section", SWAP)
+    loss = with_partner(loss, "xl", 1)
     kept = jnp.dot(weight_kept, reports_all, preferred_element_type=F32) + back
-    slide_grad = summed_over_z(kept, section)
-    report_terms, loss_value = without_digits(report_terms)
-    return (jnp.reshape(loss_value / total, (1,)), slide_grad, report_terms.sum(axis=0))
+    kept, loss = tied(kept, loss)
+    slide_grad, loss = summed_over_z(kept, section, loss)
+    report_grad = report_terms.astype(F32).sum(axis=0)
+    return (loss[0, :1] / total, slide_grad, report_grad)
 
 
 def solution(mesh):

time: 130 us -> 147 us (1.13)
  the two profiles are of different devices: /device:TPU:1 before, /device:TPU:4 now
where the time goes in v6:
time: 147 us; the launch traced here: 146 us
  waiting for transfers between devices  69.1 us (47%)
  starting transfers between devices  43.6 us (30%)
  matrix products  17.1 us (12%)
  other arithmetic  6.4 us (4%)
  local copies, waits for them, and re-layouts  4.86 us (3%)
  between operations  4.76 us (3%)
    ppermute x8, waiting for transfers between devices, with_partner(): return value + lax.ppermute(value, axis, pairs)  41.4 us
    ppermute x6, starting transfers between devices, along_z(): return lax.ppermute(array, ('z', 'section'), pairs)  19.5 us
    all_to_all x2, starting transfers between devices, exchanged(): return lax.all_to_all(parts, axes, split_axis=0, concat_axis=0, tiled=True)  12.3 us
    ppermute x8, starting transfers between devices, with_partner(): return value + lax.ppermute(value, axis, pairs)  9.18 us
    ppermute x1, waiting for transfers between devices, tower(): arrived = lax.ppermute(sent, 'tensor', SWAP)  9.01 us
    ppermute x6, waiting for transfers between devices, along_z(): return lax.ppermute(array, ('z', 'section'), pairs)  7.93 us
    all_to_all x2, waiting for transfers between devices, exchanged(): return lax.all_to_all(parts, axes, split_axis=0, concat_axis=0, tiled=True)  7.55 us
    dot_general x2, matrix products, scored(): lax.dot_general(slides, reports, (((1,), (1,)), ((), ())), preferred_elem...  4.75 us
  transfers between devices with their start and end apart: 21, of which 13 were waited for; matrix products, arithmetic and copies ran while one was open for 9% of the time, Pallas kernels for 0%

profile of v6, /device:TPU:4, one launch (start us, length us, event | category | flops | bytes accessed | tf_op | source)
XLA Modules:
  0.0 145.8 jit_solution(14122254091339026921)
XLA Ops:
  0.6 1.1 constant_dynamic-slice_fusion.5
  1.7 3.7 %fusion.15 = bf16[192,2048]{1,0:T(8,128)(2,1)S(1)} fusion(bf16[1,1024,2048]{2,1,0:T(8,128)(2,1)} %param.7, bf16[96,1024]{1,0:T(8,128)(2,1)S(1)} %bitcast.44, bf16[96,1024]{1,0:T(8,128)(2,1)S(1)} %bitcast.47), kind=kOutput, calls=%fused_computation.18 | convolution fusion | flops 809631744 | bytes 5373952 | tf_op jit(solution)/shard_map/dot_general | solution.py:81
  5.4 0.8 fusion.2
  6.2 2.3 %collective-permute-start = (f32[96,1024]{1,0:T(8,128)S(1)}, f32[96,1024]{1,0:T(8,128)S(1)}, u32[]{:S(2)}, u32[]{:S(2)}) collective-permute-start(f32[96,1024]{1,0:T(8,128)S(1)} %fusion.2), channel_id=1, source_target_pairs={{0,1},{1,0},{2,3},{3,2},{4,5},{5,4},{6,7},{7,6},{8,9},{9,8},{10,11... | collective-permute-start | bytes 1179656 | tf_op jit(solution)/shard_map/ppermute | solution.py:83
  8.6 0.8 fusion.22
  9.7 9.0 %collective-permute-done = f32[96,1024]{1,0:T(8,128)S(1)} collective-permute-done((f32[96,1024]{1,0:T(8,128)S(1)}, f32[96,1024]{1,0:T(8,128)S(1)}, u32[]{:S(2)}, u32[]{:S(2)}) %collective-permute-start) | collective-permute-done | bytes 393248 | tf_op jit(solution)/shard_map/ppermute | solution.py:83
  18.7 0.1 multiply_reduce_fusion
  19.1 1.3 collective-permute-done.1
  20.6 1.4 broadcast_in_dim.59
  22.0 3.3 %collective-permute-start.2 = (bf16[96,1152]{1,0:T(8,128)(2,1)S(1)}, bf16[96,1152]{1,0:T(8,128)(2,1)S(1)}, u32[]{:S(2)}, u32[]{:S(2)}) collective-permute-start(bf16[96,1152]{1,0:T(8,128)(2,1)S(1)} %pad_maximum_fusion.2), channel_id=1, source_target_pairs={{0,8},{2,26},{4,12},{6,30},{8,16},{10,2},{12,20},{14,6},{16,24},{1... | collective-permute-start | bytes 663560 | tf_op jit(solution)/shard_map/ppermute | solution.py:30
  26.6 7.5 %all-to-all-start = ((bf16[16,48,1024]{2,1,0:T(8,128)(2,1)}), bf16[16,48,1024]{2,1,0:T(8,128)(2,1)S(1)}, u32[]{:S(2)}, u32[]{:S(2)}) async-start(bf16[16,48,1024]{2,1,0:T(8,128)(2,1)} %broadcast_in_dim.59), calls=%async_computation | async-start | bytes 3145728 | tf_op jit(solution)/shard_map/all_to_all | solution.py:17
  34.1 2.0 %collective-permute-start.3 = (bf16[192,1152]{1,0:T(8,128)(2,1)S(1)}, bf16[192,1152]{1,0:T(8,128)(2,1)S(1)}, u32[]{:S(2)}, u32[]{:S(2)}) collective-permute-start(bf16[192,1152]{1,0:T(8,128)(2,1)S(1)} %pad_maximum_fusion.1), channel_id=1, source_target_pairs={{0,4},{2,30},{4,8},{6,2},{8,12},{10,6},{12,16},{14,10},{16,20},{18... | collective-permute-start | bytes 1327112 | tf_op jit(solution)/shard_map/ppermute | solution.py:30
  36.1 3.7 %collective-permute-start.4 = (bf16[48,1152]{1,0:T(8,128)(2,1)S(1)}, bf16[48,1152]{1,0:T(8,128)(2,1)S(1)}, u32[]{:S(2)}, u32[]{:S(2)}) collective-permute-start(bf16[48,1152]{1,0:T(8,128)(2,1)S(1)} %constant_dynamic-slice_fusion.2), channel_id=1, source_target_pairs={{0,8},{2,26},{4,12},{6,30},{8,16},{10,2},{12,20},{14,6},{16,24},{1... | collective-permute-start | bytes 331784 | tf_op jit(solution)/shard_map/ppermute | solution.py:30
  39.8 7.1 %collective-permute-done.4 = bf16[48,1152]{1,0:T(8,128)(2,1)S(1)} collective-permute-done((bf16[48,1152]{1,0:T(8,128)(2,1)S(1)}, bf16[48,1152]{1,0:T(8,128)(2,1)S(1)}, u32[]{:S(2)}, u32[]{:S(2)}) %collective-permute-start.4) | collective-permute-done | bytes 110624 | tf_op jit(solution)/shard_map/ppermute | solution.py:30
  47.2 0.2 add_reduce_fusion.2
  47.4 1.9 %collective-permute-done.5 = bf16[336,1152]{1,0:T(8,128)(2,1)S(1)} collective-permute-done((bf16[336,1152]{1,0:T(8,128)(2,1)S(1)}, bf16[336,1152]{1,0:T(8,128)(2,1)S(1)}, u32[]{:S(2)}, u32[]{:S(2)}) %collective-permute-start.5) | collective-permute-done | bytes 774176 | tf_op jit(solution)/shard_map/ppermute | solution.py:139
  49.3 0.9 copy-done.3
  50.2 0.2 add_reduce_fusion.3
  50.4 7.5 %all-to-all-done = bf16[16,48,1024]{2,1,0:T(8,128)(2,1)S(1)} async-done(((bf16[16,48,1024]{2,1,0:T(8,128)(2,1)}), bf16[16,48,1024]{2,1,0:T(8,128)(2,1)S(1)}, u32[]{:S(2)}, u32[]{:S(2)}) %all-to-all-start) | async-done | bytes 1572896 | tf_op jit(solution)/shard_map/all_to_all | solution.py:17
  58.0 2.5 %add_reduce_fusion = (f32[]{:T(128)}, bf16[432,768]{1,0:T(8,128)(2,1)S(1)}) fusion(f32[]{:T(128)} %bitcast.35, f32[]{:T(128)S(6)} %neg.16, f32[768]{0:T(1024)S(1)} %fusion.61, f32[432]{0:T(512)S(1)} %add_reduce_fusion.2, f32[]{:T(128)} %bitcast.37, bf16[768,1024]{1,0:T(8,128)(2,1)S(1)} %bitcast.39, bf16[432,1152]{1,0:T(8,128)(2,1)S(1)} %constant_dynamic-update-slice_fusion), kind=kOutput, calls=%fused_computation.26 | convolution fusion | flops 685117440 | bytes 3127312 | tf_op jit(solution)/shard_map/dot_general | solution.py:103
  60.5 2.2 %add_reduce_fusion.1 = (f32[]{:T(128)}, bf16[336,768]{1,0:T(8,128)(2,1)S(1)}) fusion(f32[]{:T(128)} %bitcast.36, f32[]{:T(128)S(6)} %neg.16, f32[768]{0:T(1024)S(1)} %fusion.61, f32[336]{0:T(512)S(1)} %add_reduce_fusion.3, f32[]{:T(128)} %bitcast.38, bf16[768,1024]{1,0:T(8,128)(2,1)S(1)} %bitcast.40, bf16[336,1152]{1,0:T(8,128)(2,1)S(1)} %copy-done.4), kind=kOutput, calls=%fused_computation.32 | convolution fusion | flops 532869120 | bytes 2783248 | tf_op jit(solution)/shard_map/dot_general | solution.py:103
  64.1 1.1 collective-permute-start.6
  65.2 1.0 fusion.29
  66.2 0.2 copy-done.2
  66.4 2.2 %add_convert_fusion = f16[768,1024]{1,0:T(8,128)(2,1)} fusion(f32[768,1024]{1,0:T(8,128)S(1)} %fusion.29, bf16[432,768]{1,0:T(8,128)(2,1)S(1)} %get-tuple-element.22, bf16[432,1152]{1,0:T(8,128)(2,1)S(1)} %copy-done.2), kind=kOutput, calls=%fused_computation.7 | convolution fusion | flops 681050112 | bytes 6266880 | tf_op jit(solution)/shard_map/dot_general | solution.py:117
  68.7 1.9 %fusion.36 = f32[384,1024]{1,0:T(8,128)} fusion(bf16[768,1024]{1,0:T(8,128)(2,1)S(1)} %bitcast.41, bf16[48,768]{1,0:T(8,128)(2,1)S(1)} %get-tuple-element.45, bf16[336,768]{1,0:T(8,128)(2,1)S(1)} %get-tuple-element.23), kind=kOutput, calls=%fused_computation.44 | convolution fusion | flops 605159424 | bytes 3735552 | tf_op jit(solution)/shard_map/dot_general | solution.py:164
  70.6 3.1 %collective-permute-done.7 = f32[1,128]{1,0:T(1,128)S(1)} collective-permute-done((f32[1,128]{1,0:T(1,128)S(1)}, f32[1,128]{1,0:T(1,128)S(1)}, u32[]{:S(2)}, u32[]{:S(2)}) %collective-permute-start.7) | collective-permute-done | bytes 544 | tf_op jit(solution)/shard_map/ppermute | solution.py:51
  73.7 0.8 slice.67
  74.5 4.9 %all-to-all-start.1 = ((f16[16,48,1024]{2,1,0:T(8,128)(2,1)}), f16[16,48,1024]{2,1,0:T(8,128)(2,1)S(1)}, u32[]{:S(2)}, u32[]{:S(2)}) async-start(f16[16,48,1024]{2,1,0:T(8,128)(2,1)} %bitcast.43), calls=%async_computation.1 | async-start | bytes 3145728 | tf_op jit(solution)/shard_map/all_to_all | solution.py:17
  79.4 1.2 collective-permute-start.9
  80.6 1.8 %fusion.32 = f32[384,1024]{1,0:T(8,128)S(1)} fusion(bf16[768,1024]{1,0:T(8,128)(2,1)S(1)} %bitcast.42, bf16[48,768]{1,0:T(8,128)(2,1)S(1)} %get-tuple-element.46, bf16[336,768]{1,0:T(8,128)(2,1)} %slice.67), kind=kOutput, calls=%fused_computation.40 | convolution fusion | flops 605159424 | bytes 3735552 | tf_op jit(solution)/shard_map/dot_general | solution.py:168
  82.4 21.1 %collective-permute-done.9 = f32[1,128]{1,0:T(1,128)S(1)} collective-permute-done((f32[1,128]{1,0:T(1,128)S(1)}, f32[1,128]{1,0:T(1,128)S(1)}, u32[]{:S(2)}, u32[]{:S(2)}) %collective-permute-start.9) | collective-permute-done | bytes 544 | tf_op jit(solution)/shard_map/ppermute | solution.py:51
  103.5 1.7 %add.247 = f32[384,1024]{1,0:T(8,128)S(1)} add(f32[384,1024]{1,0:T(8,128)S(1)} %fusion.32, f32[384,1024]{1,0:T(8,128)} %collective-permute-done.8) | non-fusion elementwise | flops 393216 | bytes 4718592 | tf_op jit(solution)/shard_map/add | solution.py:168
  105.4 7.2 %collective-permute-start.10 = (f16[192,1024]{1,0:T(8,128)(2,1)S(1)}, f16[192,1024]{1,0:T(8,128)(2,1)S(1)}, u32[]{:S(2)}, u32[]{:S(2)}) collective-permute-start(f16[192,1024]{1,0:T(8,128)(2,1)S(1)} %slice.85), channel_id=1, source_target_pairs={{0,28},{2,6},{4,0},{6,10},{8,4},{10,14},{12,8},{14,18},{16,12},{18... | collective-permute-start | bytes 1179656 | tf_op jit(solution)/shard_map/ppermute | solution.py:30
  112.6 0.5 collective-permute-start.11
  113.1 3.5 %collective-permute-done.12 = f32[1,128]{1,0:T(1,128)S(1)} collective-permute-done((f32[1,128]{1,0:T(1,128)S(1)}, f32[1,128]{1,0:T(1,128)S(1)}, u32[]{:S(2)}, u32[]{:S(2)}) %collective-permute-start.12) | collective-permute-done | bytes 544 | tf_op jit(solution)/shard_map/ppermute | solution.py:51
  116.7 1.4 collective-permute-start.13
  118.1 3.6 %collective-permute-done.13 = f32[1,128]{1,0:T(1,128)S(1)} collective-permute-done((f32[1,128]{1,0:T(1,128)S(1)}, f32[1,128]{1,0:T(1,128)S(1)}, u32[]{:S(2)}, u32[]{:S(2)}) %collective-permute-start.13) | collective-permute-done | bytes 544 | tf_op jit(solution)/shard_map/ppermute | solution.py:51
  121.9 2.9 %collective-permute-start.14 = (f16[96,1024]{1,0:T(8,128)(2,1)S(1)}, f16[96,1024]{1,0:T(8,128)(2,1)S(1)}, u32[]{:S(2)}, u32[]{:S(2)}) collective-permute-start(f16[96,1024]{1,0:T(8,128)(2,1)S(1)} %fusion.44), channel_id=1, source_target_pairs={{0,24},{2,10},{4,28},{6,14},{8,0},{10,18},{12,4},{14,22},{16,8},{1... | collective-permute-start | bytes 589832 | tf_op jit(solution)/shard_map/ppermute | solution.py:30
  124.8 4.6 %collective-permute-done.15 = f32[1,128]{1,0:T(1,128)S(1)} collective-permute-done((f32[1,128]{1,0:T(1,128)S(1)}, f32[1,128]{1,0:T(1,128)S(1)}, u32[]{:S(2)}, u32[]{:S(2)}) %collective-permute-start.15) | collective-permute-done | bytes 544 | tf_op jit(solution)/shard_map/ppermute | solution.py:51
  129.5 0.8 collective-permute-done.14
  130.3 0.7 dynamic-slice_add_fusion
  131.0 2.4 %collective-permute-start.16 = (f32[1,128]{1,0:T(1,128)S(1)}, f32[1,128]{1,0:T(1,128)S(1)}, u32[]{:S(2)}, u32[]{:S(2)}) collective-permute-start(f32[1,128]{1,0:T(1,128)S(1)} %add.254), channel_id=1, source_target_pairs={{0,8},{4,12},{8,0},{12,4},{16,24},{20,28},{24,16},{28,20},{1,9},{5... | collective-permute-start | bytes 1544 | tf_op jit(solution)/shard_map/ppermute | solution.py:51
  133.4 2.1 %collective-permute-done.16 = f32[1,128]{1,0:T(1,128)S(1)} collective-permute-done((f32[1,128]{1,0:T(1,128)S(1)}, f32[1,128]{1,0:T(1,128)S(1)}, u32[]{:S(2)}, u32[]{:S(2)}) %collective-permute-start.16) | collective-permute-done | bytes 544 | tf_op jit(solution)/shard_map/ppermute | solution.py:51
  135.5 3.1 %collective-permute-start.17 = (f32[1,128]{1,0:T(1,128)S(1)}, f32[1,128]{1,0:T(1,128)S(1)}, u32[]{:S(2)}, u32[]{:S(2)}) collective-permute-start(f32[1,128]{1,0:T(1,128)S(1)} %add.255), channel_id=1, source_target_pairs={{0,16},{4,20},{8,24},{12,28},{16,0},{20,4},{24,8},{28,12},{1,17},{... | collective-permute-start | bytes 1544 | tf_op jit(solution)/shard_map/ppermute | solution.py:51
  138.6 1.0 convert_reduce_fusion
  139.6 3.3 %collective-permute-done.17 = f32[1,128]{1,0:T(1,128)S(1)} collective-permute-done((f32[1,128]{1,0:T(1,128)S(1)}, f32[1,128]{1,0:T(1,128)S(1)}, u32[]{:S(2)}, u32[]{:S(2)}) %collective-permute-start.17) | collective-permute-done | bytes 544 | tf_op jit(solution)/shard_map/ppermute | solution.py:51
  143.0 1.7 %add_add_fusion = f32[48,1024]{1,0:T(8,128)} fusion(f32[48,1024]{1,0:T(8,128)} %collective-permute-done.18, f32[96,1024]{1,0:T(8,128)S(1)} %convert_element_type.83, s32[]{:T(128)S(6)} %select_n.139, f32[384,1024]{1,0:T(8,128)S(1)} %add.247, f16[96,1024]{1,0:T(8,128)(2,1)S(1)} %copy-done.7), kind=kLoop, calls=%fused_computation.64 | loop fusion | flops 196608 | bytes 884740 | tf_op jit(solution)/shard_map/add | solution.py:72
  (69 shorter events, 1.5 us)
Async XLA Ops:
  1.7 3.7 %copy-start = (bf16[1,2048,1024]{2,1,0:T(8,128)(2,1)S(1)}, bf16[1,2048,1024]{2,1,0:T(8,128)(2,1)}, u32[]{:S(2)}) copy-start(bf16[1,2048,1024]{2,1,0:T(8,128)(2,1)} %param.8) | copy-start | bytes 12582916
  6.2 12.4 %collective-permute-start = (f32[96,1024]{1,0:T(8,128)S(1)}, f32[96,1024]{1,0:T(8,128)S(1)}, u32[]{:S(2)}, u32[]{:S(2)}) collective-permute-start(f32[96,1024]{1,0:T(8,128)S(1)} %fusion.2), channel_id=1, source_target_pairs={{0,1},{1,0},{2,3},{3,2},{4,5},{5,4},{6,7},{7,6},{8,9},{9,8},{10,11... | collective-permute-start | bytes 1179656 | tf_op jit(solution)/shard_map/ppermute | solution.py:83
  8.6 0.9 copy-start.8
  18.9 1.5 %collective-permute-start.1 = (bf16[96,1024]{1,0:T(8,128)(2,1)S(1)}, bf16[96,1024]{1,0:T(8,128)(2,1)S(1)}, u32[]{:S(2)}, u32[]{:S(2)}) collective-permute-start(bf16[96,1024]{1,0:T(8,128)(2,1)S(1)} %multiply_convert_fusion), channel_id=1, source_target_pairs={{0,2},{2,0},{1,3},{3,1},{4,6},{6,4},{5,7},{7,5},{8,10},{10,8},{9,1... | collective-permute-start | bytes 589832 | tf_op jit(solution)/shard_map/ppermute | solution.py:131
  22.0 12.1 %collective-permute-start.2 = (bf16[96,1152]{1,0:T(8,128)(2,1)S(1)}, bf16[96,1152]{1,0:T(8,128)(2,1)S(1)}, u32[]{:S(2)}, u32[]{:S(2)}) collective-permute-start(bf16[96,1152]{1,0:T(8,128)(2,1)S(1)} %pad_maximum_fusion.2), channel_id=1, source_target_pairs={{0,8},{2,26},{4,12},{6,30},{8,16},{10,2},{12,20},{14,6},{16,24},{1... | collective-permute-start | bytes 663560 | tf_op jit(solution)/shard_map/ppermute | solution.py:30
  26.6 31.3 %all-to-all-start = ((bf16[16,48,1024]{2,1,0:T(8,128)(2,1)}), bf16[16,48,1024]{2,1,0:T(8,128)(2,1)S(1)}, u32[]{:S(2)}, u32[]{:S(2)}) async-start(bf16[16,48,1024]{2,1,0:T(8,128)(2,1)} %broadcast_in_dim.59), calls=%async_computation | async-start | bytes 3145728 | tf_op jit(solution)/shard_map/all_to_all | solution.py:17
  34.1 12.8 %collective-permute-start.3 = (bf16[192,1152]{1,0:T(8,128)(2,1)S(1)}, bf16[192,1152]{1,0:T(8,128)(2,1)S(1)}, u32[]{:S(2)}, u32[]{:S(2)}) collective-permute-start(bf16[192,1152]{1,0:T(8,128)(2,1)S(1)} %pad_maximum_fusion.1), channel_id=1, source_target_pairs={{0,4},{2,30},{4,8},{6,2},{8,12},{10,6},{12,16},{14,10},{16,20},{18... | collective-permute-start | bytes 1327112 | tf_op jit(solution)/shard_map/ppermute | solution.py:30
  36.1 10.8 %collective-permute-start.4 = (bf16[48,1152]{1,0:T(8,128)(2,1)S(1)}, bf16[48,1152]{1,0:T(8,128)(2,1)S(1)}, u32[]{:S(2)}, u32[]{:S(2)}) collective-permute-start(bf16[48,1152]{1,0:T(8,128)(2,1)S(1)} %constant_dynamic-slice_fusion.2), channel_id=1, source_target_pairs={{0,8},{2,26},{4,12},{6,30},{8,16},{10,2},{12,20},{14,6},{16,24},{1... | collective-permute-start | bytes 331784 | tf_op jit(solution)/shard_map/ppermute | solution.py:30
  47.0 2.4 %collective-permute-start.5 = (bf16[336,1152]{1,0:T(8,128)(2,1)S(1)}, bf16[336,1152]{1,0:T(8,128)(2,1)S(1)}, u32[]{:S(2)}, u32[]{:S(2)}) collective-permute-start(bf16[336,1152]{1,0:T(8,128)(2,1)S(1)} %pad_maximum_fusion), channel_id=1, source_target_pairs={{0,2},{2,0},{1,3},{3,1},{4,6},{6,4},{5,7},{7,5},{8,10},{10,8},{9,1... | collective-permute-start | bytes 2322440 | tf_op jit(solution)/shard_map/ppermute | solution.py:139
  47.2 13.3 %copy-start.1 = (bf16[432,1152]{1,0:T(8,128)(2,1)}, bf16[432,1152]{1,0:T(8,128)(2,1)S(1)}, u32[]{:S(2)}) copy-start(bf16[432,1152]{1,0:T(8,128)(2,1)S(1)} %constant_dynamic-update-slice_fusion) | copy-start | bytes 2985988
  49.3 0.9 copy-start.3
  58.0 2.5 %copy-start.4 = (bf16[336,1152]{1,0:T(8,128)(2,1)S(1)}, bf16[336,1152]{1,0:T(8,128)(2,1)}, u32[]{:S(2)}) copy-start(bf16[336,1152]{1,0:T(8,128)(2,1)} %copy-done.3) | copy-start | bytes 2322436
  60.5 4.7 %copy-start.5 = (bf16[336,1152]{1,0:T(8,128)(2,1)S(1)}, bf16[336,1152]{1,0:T(8,128)(2,1)}, u32[]{:S(2)}) copy-start(bf16[336,1152]{1,0:T(8,128)(2,1)} %copy-done.3) | copy-start | bytes 2322436
  64.1 4.6 %collective-permute-start.6 = (f32[1,128]{1,0:T(1,128)S(1)}, f32[1,128]{1,0:T(1,128)S(1)}, u32[]{:S(2)}, u32[]{:S(2)}) collective-permute-start(f32[1,128]{1,0:T(1,128)S(1)} %broadcast_in_dim.68), channel_id=1, source_target_pairs={{0,2},{2,0},{1,3},{3,1},{4,6},{6,4},{5,7},{7,5},{8,10},{10,8},{9,1... | collective-permute-start | bytes 1544 | tf_op jit(solution)/shard_map/ppermute | solution.py:51
  65.2 1.2 copy-start.2
  68.6 5.0 %collective-permute-start.7 = (f32[1,128]{1,0:T(1,128)S(1)}, f32[1,128]{1,0:T(1,128)S(1)}, u32[]{:S(2)}, u32[]{:S(2)}) collective-permute-start(f32[1,128]{1,0:T(1,128)S(1)} %broadcast_add_fusion), channel_id=1, source_target_pairs={{0,1},{1,0},{2,3},{3,2},{4,5},{5,4},{6,7},{7,6},{8,9},{9,8},{10,11... | collective-permute-start | bytes 1544 | tf_op jit(solution)/shard_map/ppermute | solution.py:51
  73.7 29.9 %collective-permute-start.8 = (f32[384,1024]{1,0:T(8,128)}, f32[384,1024]{1,0:T(8,128)}, u32[]{:S(2)}, u32[]{:S(2)}) collective-permute-start(f32[384,1024]{1,0:T(8,128)} %fusion.36), channel_id=1, source_target_pairs={{0,2},{2,0},{1,3},{3,1},{4,6},{6,4},{5,7},{7,5},{8,10},{10,8},{9,1... | collective-permute-start | bytes 4718600 | tf_op jit(solution)/shard_map/ppermute | solution.py:166
  74.5 64.1 %all-to-all-start.1 = ((f16[16,48,1024]{2,1,0:T(8,128)(2,1)}), f16[16,48,1024]{2,1,0:T(8,128)(2,1)S(1)}, u32[]{:S(2)}, u32[]{:S(2)}) async-start(f16[16,48,1024]{2,1,0:T(8,128)(2,1)} %bitcast.43), calls=%async_computation.1 | async-start | bytes 3145728 | tf_op jit(solution)/shard_map/all_to_all | solution.py:17
  79.4 24.1 %collective-permute-start.9 = (f32[1,128]{1,0:T(1,128)S(1)}, f32[1,128]{1,0:T(1,128)S(1)}, u32[]{:S(2)}, u32[]{:S(2)}) collective-permute-start(f32[1,128]{1,0:T(1,128)S(1)} %add.246), channel_id=1, source_target_pairs={{0,128},{128,0},{1,129},{129,1},{2,130},{130,2},{3,131},{131,3},{4... | collective-permute-start | bytes 1544 | tf_op jit(solution)/shard_map/ppermute | solution.py:51
  105.4 16.3 %collective-permute-start.10 = (f16[192,1024]{1,0:T(8,128)(2,1)S(1)}, f16[192,1024]{1,0:T(8,128)(2,1)S(1)}, u32[]{:S(2)}, u32[]{:S(2)}) collective-permute-start(f16[192,1024]{1,0:T(8,128)(2,1)S(1)} %slice.85), channel_id=1, source_target_pairs={{0,28},{2,6},{4,0},{6,10},{8,4},{10,14},{12,8},{14,18},{16,12},{18... | collective-permute-start | bytes 1179656 | tf_op jit(solution)/shard_map/ppermute | solution.py:30
  112.6 9.1 %collective-permute-start.11 = (f16[48,1024]{1,0:T(8,128)(2,1)S(1)}, f16[48,1024]{1,0:T(8,128)(2,1)S(1)}, u32[]{:S(2)}, u32[]{:S(2)}) collective-permute-start(f16[48,1024]{1,0:T(8,128)(2,1)S(1)} %slice.86), channel_id=1, source_target_pairs={{0,24},{2,10},{4,28},{6,14},{8,0},{10,18},{12,4},{14,22},{16,8},{1... | collective-permute-start | bytes 294920 | tf_op jit(solution)/shard_map/ppermute | solution.py:30
  113.1 3.5 %collective-permute-start.12 = (f32[1,128]{1,0:T(1,128)S(1)}, f32[1,128]{1,0:T(1,128)S(1)}, u32[]{:S(2)}, u32[]{:S(2)}) collective-permute-start(f32[1,128]{1,0:T(1,128)S(1)} %add.248), channel_id=1, source_target_pairs={{0,32},{32,0},{64,96},{96,64},{1,33},{33,1},{65,97},{97,65},{2,34}... | collective-permute-start | bytes 1544 | tf_op jit(solution)/shard_map/ppermute | solution.py:51
  116.7 5.0 %collective-permute-start.13 = (f32[1,128]{1,0:T(1,128)S(1)}, f32[1,128]{1,0:T(1,128)S(1)}, u32[]{:S(2)}, u32[]{:S(2)}) collective-permute-start(f32[1,128]{1,0:T(1,128)S(1)} %add.249), channel_id=1, source_target_pairs={{0,64},{32,96},{64,0},{96,32},{1,65},{33,97},{65,1},{97,33},{2,66}... | collective-permute-start | bytes 1544 | tf_op jit(solution)/shard_map/ppermute | solution.py:51
  121.9 8.4 %collective-permute-start.14 = (f16[96,1024]{1,0:T(8,128)(2,1)S(1)}, f16[96,1024]{1,0:T(8,128)(2,1)S(1)}, u32[]{:S(2)}, u32[]{:S(2)}) collective-permute-start(f16[96,1024]{1,0:T(8,128)(2,1)S(1)} %fusion.44), channel_id=1, source_target_pairs={{0,24},{2,10},{4,28},{6,14},{8,0},{10,18},{12,4},{14,22},{16,8},{1... | collective-permute-start | bytes 589832 | tf_op jit(solution)/shard_map/ppermute | solution.py:30
  124.8 4.7 %collective-permute-start.15 = (f32[1,128]{1,0:T(1,128)S(1)}, f32[1,128]{1,0:T(1,128)S(1)}, u32[]{:S(2)}, u32[]{:S(2)}) collective-permute-start(f32[1,128]{1,0:T(1,128)S(1)} %add.250), channel_id=1, source_target_pairs={{0,4},{4,0},{8,12},{12,8},{16,20},{20,16},{24,28},{28,24},{1,5},{5... | collective-permute-start | bytes 1544 | tf_op jit(solution)/shard_map/ppermute | solution.py:51
  124.8 10.7 %copy-start.6 = (f16[96,1024]{1,0:T(8,128)(2,1)}, f16[96,1024]{1,0:T(8,128)(2,1)S(1)}, u32[]{:S(2)}) copy-start(f16[96,1024]{1,0:T(8,128)(2,1)S(1)} %slice.76) | copy-start | bytes 589828
  131.0 12.0 %collective-permute-start.18 = (f32[48,1024]{1,0:T(8,128)}, f32[48,1024]{1,0:T(8,128)}, u32[]{:S(2)}, u32[]{:S(2)}) collective-permute-start(f32[48,1024]{1,0:T(8,128)} %dynamic-slice_add_fusion), channel_id=1, source_target_pairs={{0,2},{2,0},{1,3},{3,1},{4,6},{6,4},{5,7},{7,5},{8,10},{10,8},{9,1... | collective-permute-start | bytes 589832 | tf_op jit(solution)/shard_map/ppermute | solution.py:69
  131.0 4.4 %collective-permute-start.16 = (f32[1,128]{1,0:T(1,128)S(1)}, f32[1,128]{1,0:T(1,128)S(1)}, u32[]{:S(2)}, u32[]{:S(2)}) collective-permute-start(f32[1,128]{1,0:T(1,128)S(1)} %add.254), channel_id=1, source_target_pairs={{0,8},{4,12},{8,0},{12,4},{16,24},{20,28},{24,16},{28,20},{1,9},{5... | collective-permute-start | bytes 1544 | tf_op jit(solution)/shard_map/ppermute | solution.py:51
  135.5 7.5 %collective-permute-start.17 = (f32[1,128]{1,0:T(1,128)S(1)}, f32[1,128]{1,0:T(1,128)S(1)}, u32[]{:S(2)}, u32[]{:S(2)}) collective-permute-start(f32[1,128]{1,0:T(1,128)S(1)} %add.255), channel_id=1, source_target_pairs={{0,16},{4,20},{8,24},{12,28},{16,0},{20,4},{24,8},{28,12},{1,17},{... | collective-permute-start | bytes 1544 | tf_op jit(solution)/shard_map/ppermute | solution.py:51
  138.6 4.4 %copy-start.7 = (f16[96,1024]{1,0:T(8,128)(2,1)S(1)}, f16[96,1024]{1,0:T(8,128)(2,1)}, u32[]{:S(2)}) copy-start(f16[96,1024]{1,0:T(8,128)(2,1)} %copy-done.6) | copy-start | bytes 589828

commit v7 on v6

--- a/solution.py
+++ b/solution.py
@@ -55,19 +55,19 @@
     half = kept.shape[0] // 8
     one_three = along_z(kept[: 4 * half].astype(SENT), -1)
     four = along_z(kept[6 * half : 7 * half].astype(SENT), -2)
-    loss = with_partner(with_partner(loss, "y", 1), "y", 2)
+    loss = with_partner(with_partner(loss, "z", 1), "z", 2)
     one_three, four, loss = tied(one_three, four, loss)
     four = four.astype(F32)
     upper = kept[4 * half : 5 * half] + jnp.where(section == 0, four, 0.0)
     lower = kept[5 * half : 6 * half] + jnp.where(section == 0, 0.0, four)
     two = jnp.concatenate([upper, lower], axis=0) + one_three[2 * half :].astype(F32)
     two = along_z(two.astype(SENT), -2)
-    loss = with_partner(loss, "z", 1)
+    loss = with_partner(loss, "z", 4)
     two, loss = tied(two, loss)
     two = two.astype(F32)
     given = row_half(one_three[: 2 * half], 1 - section).astype(F32) + row_half(two, 1 - section)
     got = lax.ppermute(given, "section", SWAP)
-    loss = with_partner(with_partner(loss, "z", 2), "z", 4)
+    loss = with_partner(with_partner(loss, "y", 1), "y", 2)
     mine = row_half(one_three[: 2 * half], section).astype(F32) + row_half(two, section)
     return kept[7 * half :] + mine + got, loss
 
@@ -149,7 +149,7 @@
     slides_other, weight_other, loss_other = scored(
         rows_other, width, reports_all, columns, scale_value, bias_value
     )
-    loss = with_partner(jnp.broadcast_to(loss_mine + loss_other, (1, LANES)), "section", 1)
+    loss = with_partner(jnp.broadcast_to(loss_mine + loss_other, (1, LANES)), "tensor", 1)
     report_part = transposed_dot(weight_mine, slides_mine)
     report_part = report_part + transposed_dot(weight_other, slides_other)
     report_part = report_part.astype(SENT).reshape(n_plane, quarter, width)
@@ -157,16 +157,16 @@
         report_part, weight_mine, weight_other, loss
     )
     report_terms = exchanged(report_part, PLANE)
-    loss = with_partner(loss, "tensor", 1)
+    loss = with_partner(loss, "xl", 1)
     weight_own, weight_mine = weight_mine[: 2 * quarter], weight_mine[2 * quarter :]
     weight_sent = jnp.concatenate([weight_other, row_half(weight_own, 1 - section)], axis=0)
     weight_kept = jnp.concatenate([weight_mine, row_half(weight_own, section)], axis=0)
     sent = jnp.dot(weight_sent, reports_all, preferred_element_type=F32)
     sent, loss = tied(sent, loss)
     back = lax.ppermute(sent, "section", SWAP)
-    loss = with_partner(loss, "xl", 1)
+    loss = with_partner(loss, "section", 1)
+    back, loss = tied(back, loss)
     kept = jnp.dot(weight_kept, reports_all, preferred_element_type=F32) + back
-    kept, loss = tied(kept, loss)
     slide_grad, loss = summed_over_z(kept, section, loss)
     report_grad = report_terms.astype(F32).sum(axis=0)
     return (loss[0, :1] / total, slide_grad, report_grad)

time: 147 us -> 124 us (0.84)
  waiting for transfers between devices: 69.1 us -> 46.5 us
    ppermute x8, waiting for transfers between devices: 41.4 us -> 19.6 us  [with_partner(): return value + lax.ppermute(value, axis, pairs)]
    add x1 -> x0, other arithmetic: 1.67 us -> none  [local(): kept = jnp.dot(weight_kept, reports_all, preferred_element_type=F32) + back]
    another operation x1, other arithmetic: 0.12 us -> 1.75 us
  transfers between devices with their start and end apart: 21 -> 21, of which waited for: 13 -> 12; matrix products, arithmetic and copies ran while one was open for 9% -> 11% of each run, Pallas kernels for 0% -> 0%
where the time goes in v7:
time: 124 us
  waiting for transfers between devices  46.5 us (38%)
  starting transfers between devices  44.2 us (36%)
  matrix products  17 us (14%)
  other arithmetic  6.37 us (5%)
  local copies, waits for them, and re-layouts  4.84 us (4%)
  between operations  4.66 us (4%)
    ppermute x6, starting transfers between devices, along_z(): return lax.ppermute(array, ('z', 'section'), pairs)  19.7 us
    ppermute x8, waiting for transfers between devices, with_partner(): return value + lax.ppermute(value, axis, pairs)  19.6 us
    all_to_all x2, starting transfers between devices, exchanged(): return lax.all_to_all(parts, axes, split_axis=0, concat_axis=0, tiled=True)  12.9 us
    ppermute x8, starting transfers between devices, with_partner(): return value + lax.ppermute(value, axis, pairs)  9.07 us
    ppermute x1, waiting for transfers between devices, tower(): arrived = lax.ppermute(sent, 'tensor', SWAP)  9.01 us
    all_to_all x2, waiting for transfers between devices, exchanged(): return lax.all_to_all(parts, axes, split_axis=0, concat_axis=0, tiled=True)  7.55 us
    ppermute x6, waiting for transfers between devices, along_z(): return lax.ppermute(array, ('z', 'section'), pairs)  7.1 us
    dot_general x2, matrix products, scored(): lax.dot_general(slides, reports, (((1,), (1,)), ((), ())), preferred_elem...  4.68 us
  transfers between devices with their start and end apart: 21, of which 12 were waited for; matrix products, arithmetic and copies ran while one was open for 11% of the time, Pallas kernels for 0%

profile of v7, /device:TPU:4, one launch (start us, length us, event | category | flops | bytes accessed | tf_op | source)
XLA Modules:
  0.0 123.6 jit_solution(2961867468465913806)
XLA Ops:
  0.6 1.1 constant_dynamic-slice_fusion.5
  1.7 3.7 %fusion.15 = bf16[192,2048]{1,0:T(8,128)(2,1)S(1)} fusion(bf16[1,1024,2048]{2,1,0:T(8,128)(2,1)} %param.7, bf16[96,1024]{1,0:T(8,128)(2,1)S(1)} %bitcast.44, bf16[96,1024]{1,0:T(8,128)(2,1)S(1)} %bitcast.47), kind=kOutput, calls=%fused_computation.18 | convolution fusion | flops 809631744 | bytes 5373952 | tf_op jit(solution)/shard_map/dot_general | solution.py:81
  5.4 0.8 fusion.2
  6.2 2.3 %collective-permute-start = (f32[96,1024]{1,0:T(8,128)S(1)}, f32[96,1024]{1,0:T(8,128)S(1)}, u32[]{:S(2)}, u32[]{:S(2)}) collective-permute-start(f32[96,1024]{1,0:T(8,128)S(1)} %fusion.2), channel_id=1, source_target_pairs={{0,1},{1,0},{2,3},{3,2},{4,5},{5,4},{6,7},{7,6},{8,9},{9,8},{10,11... | collective-permute-start | bytes 1179656 | tf_op jit(solution)/shard_map/ppermute | solution.py:83
  8.6 0.8 fusion.22
  9.7 9.0 %collective-permute-done = f32[96,1024]{1,0:T(8,128)S(1)} collective-permute-done((f32[96,1024]{1,0:T(8,128)S(1)}, f32[96,1024]{1,0:T(8,128)S(1)}, u32[]{:S(2)}, u32[]{:S(2)}) %collective-permute-start) | collective-permute-done | bytes 393248 | tf_op jit(solution)/shard_map/ppermute | solution.py:83
  19.1 1.3 %collective-permute-done.1 = bf16[96,1024]{1,0:T(8,128)(2,1)S(1)} collective-permute-done((bf16[96,1024]{1,0:T(8,128)(2,1)S(1)}, bf16[96,1024]{1,0:T(8,128)(2,1)S(1)}, u32[]{:S(2)}, u32[]{:S(2)}) %collective-permute-start.1) | collective-permute-done | bytes 196640 | tf_op jit(solution)/shard_map/ppermute | solution.py:131
  20.6 1.4 %broadcast_in_dim.59 = bf16[16,48,1024]{2,1,0:T(8,128)(2,1)} broadcast(bf16[48,1024]{1,0:T(8,128)(2,1)S(1)} %dynamic-slice_select_fusion), dimensions={1,2} | broadcast | bytes 1671168 | tf_op jit(solution)/shard_map/broadcast_in_dim | solution.py:135
  22.0 3.3 %collective-permute-start.2 = (bf16[96,1152]{1,0:T(8,128)(2,1)S(1)}, bf16[96,1152]{1,0:T(8,128)(2,1)S(1)}, u32[]{:S(2)}, u32[]{:S(2)}) collective-permute-start(bf16[96,1152]{1,0:T(8,128)(2,1)S(1)} %pad_maximum_fusion.2), channel_id=1, source_target_pairs={{0,8},{2,26},{4,12},{6,30},{8,16},{10,2},{12,20},{14,6},{16,24},{1... | collective-permute-start | bytes 663560 | tf_op jit(solution)/shard_map/ppermute | solution.py:30
  26.6 7.5 %all-to-all-start = ((bf16[16,48,1024]{2,1,0:T(8,128)(2,1)}), bf16[16,48,1024]{2,1,0:T(8,128)(2,1)S(1)}, u32[]{:S(2)}, u32[]{:S(2)}) async-start(bf16[16,48,1024]{2,1,0:T(8,128)(2,1)} %broadcast_in_dim.59), calls=%async_computation | async-start | bytes 3145728 | tf_op jit(solution)/shard_map/all_to_all | solution.py:17
  34.1 2.0 %collective-permute-start.3 = (bf16[192,1152]{1,0:T(8,128)(2,1)S(1)}, bf16[192,1152]{1,0:T(8,128)(2,1)S(1)}, u32[]{:S(2)}, u32[]{:S(2)}) collective-permute-start(bf16[192,1152]{1,0:T(8,128)(2,1)S(1)} %pad_maximum_fusion.1), channel_id=1, source_target_pairs={{0,4},{2,30},{4,8},{6,2},{8,12},{10,6},{12,16},{14,10},{16,20},{18... | collective-permute-start | bytes 1327112 | tf_op jit(solution)/shard_map/ppermute | solution.py:30
  36.1 3.7 %collective-permute-start.4 = (bf16[48,1152]{1,0:T(8,128)(2,1)S(1)}, bf16[48,1152]{1,0:T(8,128)(2,1)S(1)}, u32[]{:S(2)}, u32[]{:S(2)}) collective-permute-start(bf16[48,1152]{1,0:T(8,128)(2,1)S(1)} %constant_dynamic-slice_fusion.2), channel_id=1, source_target_pairs={{0,8},{2,26},{4,12},{6,30},{8,16},{10,2},{12,20},{14,6},{16,24},{1... | collective-permute-start | bytes 331784 | tf_op jit(solution)/shard_map/ppermute | solution.py:30
  39.8 7.1 %collective-permute-done.4 = bf16[48,1152]{1,0:T(8,128)(2,1)S(1)} collective-permute-done((bf16[48,1152]{1,0:T(8,128)(2,1)S(1)}, bf16[48,1152]{1,0:T(8,128)(2,1)S(1)}, u32[]{:S(2)}, u32[]{:S(2)}) %collective-permute-start.4) | collective-permute-done | bytes 110624 | tf_op jit(solution)/shard_map/ppermute | solution.py:30
  47.2 0.2 add_reduce_fusion.2
  47.4 1.9 %collective-permute-done.5 = bf16[336,1152]{1,0:T(8,128)(2,1)S(1)} collective-permute-done((bf16[336,1152]{1,0:T(8,128)(2,1)S(1)}, bf16[336,1152]{1,0:T(8,128)(2,1)S(1)}, u32[]{:S(2)}, u32[]{:S(2)}) %collective-permute-start.5) | collective-permute-done | bytes 774176 | tf_op jit(solution)/shard_map/ppermute | solution.py:139
  49.3 0.9 copy-done.3
  50.2 0.2 add_reduce_fusion.3
  50.4 7.5 %all-to-all-done = bf16[16,48,1024]{2,1,0:T(8,128)(2,1)S(1)} async-done(((bf16[16,48,1024]{2,1,0:T(8,128)(2,1)}), bf16[16,48,1024]{2,1,0:T(8,128)(2,1)S(1)}, u32[]{:S(2)}, u32[]{:S(2)}) %all-to-all-start) | async-done | bytes 1572896 | tf_op jit(solution)/shard_map/all_to_all | solution.py:17
  58.0 2.5 %add_reduce_fusion = (f32[]{:T(128)}, bf16[432,768]{1,0:T(8,128)(2,1)S(1)}) fusion(f32[]{:T(128)} %bitcast.35, f32[]{:T(128)S(6)} %neg.16, f32[768]{0:T(1024)S(1)} %fusion.62, f32[432]{0:T(512)S(1)} %add_reduce_fusion.2, f32[]{:T(128)} %bitcast.37, bf16[768,1024]{1,0:T(8,128)(2,1)S(1)} %bitcast.39, bf16[432,1152]{1,0:T(8,128)(2,1)S(1)} %constant_dynamic-update-slice_fusion), kind=kOutput, calls=%fused_computation.26 | convolution fusion | flops 685117440 | bytes 3127312 | tf_op jit(solution)/shard_map/dot_general | solution.py:103
  60.5 2.1 %add_reduce_fusion.1 = (f32[]{:T(128)}, bf16[336,768]{1,0:T(8,128)(2,1)S(1)}) fusion(f32[]{:T(128)} %bitcast.36, f32[]{:T(128)S(6)} %neg.16, f32[768]{0:T(1024)S(1)} %fusion.62, f32[336]{0:T(512)S(1)} %add_reduce_fusion.3, f32[]{:T(128)} %bitcast.38, bf16[768,1024]{1,0:T(8,128)(2,1)S(1)} %bitcast.40, bf16[336,1152]{1,0:T(8,128)(2,1)S(1)} %copy-done.4), kind=kOutput, calls=%fused_computation.32 | convolution fusion | flops 532869120 | bytes 2783248 | tf_op jit(solution)/shard_map/dot_general | solution.py:103
  63.9 0.3 collective-permute-start.6
  64.2 1.0 fusion.29
  65.4 2.2 %add_convert_fusion = f16[768,1024]{1,0:T(8,128)(2,1)} fusion(f32[768,1024]{1,0:T(8,128)S(1)} %fusion.29, bf16[432,768]{1,0:T(8,128)(2,1)S(1)} %get-tuple-element.22, bf16[432,1152]{1,0:T(8,128)(2,1)S(1)} %copy-done.2), kind=kOutput, calls=%fused_computation.7 | convolution fusion | flops 681050112 | bytes 6266880 | tf_op jit(solution)/shard_map/dot_general | solution.py:117
  67.6 1.6 %collective-permute-done.6 = f32[1,128]{1,0:T(1,128)S(1)} collective-permute-done((f32[1,128]{1,0:T(1,128)S(1)}, f32[1,128]{1,0:T(1,128)S(1)}, u32[]{:S(2)}, u32[]{:S(2)}) %collective-permute-start.6) | collective-permute-done | bytes 544 | tf_op jit(solution)/shard_map/ppermute | solution.py:51
  69.2 0.9 collective-permute-start.7
  70.1 1.9 %fusion.36 = f32[384,1024]{1,0:T(8,128)} fusion(bf16[768,1024]{1,0:T(8,128)(2,1)S(1)} %bitcast.41, bf16[48,768]{1,0:T(8,128)(2,1)S(1)} %get-tuple-element.47, bf16[336,768]{1,0:T(8,128)(2,1)S(1)} %get-tuple-element.23), kind=kOutput, calls=%fused_computation.44 | convolution fusion | flops 605159424 | bytes 3735552 | tf_op jit(solution)/shard_map/dot_general | solution.py:164
  72.1 0.6 collective-permute-done.7
  72.7 0.8 slice.67
  73.6 5.4 %all-to-all-start.1 = ((f16[16,48,1024]{2,1,0:T(8,128)(2,1)}), f16[16,48,1024]{2,1,0:T(8,128)(2,1)S(1)}, u32[]{:S(2)}, u32[]{:S(2)}) async-start(f16[16,48,1024]{2,1,0:T(8,128)(2,1)} %bitcast.43), calls=%async_computation.1 | async-start | bytes 3145728 | tf_op jit(solution)/shard_map/all_to_all | solution.py:17
  79.0 0.2 collective-permute-start.9
  79.2 1.8 %fusion.32 = f32[384,1024]{1,0:T(8,128)S(1)} fusion(bf16[768,1024]{1,0:T(8,128)(2,1)S(1)} %bitcast.42, bf16[48,768]{1,0:T(8,128)(2,1)S(1)} %get-tuple-element.48, bf16[336,768]{1,0:T(8,128)(2,1)} %slice.67), kind=kOutput, calls=%fused_computation.40 | convolution fusion | flops 605159424 | bytes 3735552 | tf_op jit(solution)/shard_map/dot_general | solution.py:169
  81.1 1.8 %fusion.72 = (f16[384,1024]{1,0:T(8,128)(2,1)S(1)}, f32[384,1024]{1,0:T(8,128)S(1)}) fusion(f32[384,1024]{1,0:T(8,128)S(1)} %fusion.32, f32[384,1024]{1,0:T(8,128)} %collective-permute-done.8), kind=kLoop, calls=%fused_computation.123 | loop fusion | flops 786432 | bytes 5505024 | tf_op jit(solution)/shard_map/convert.1
  82.9 7.1 %collective-permute-start.10 = (f16[192,1024]{1,0:T(8,128)(2,1)S(1)}, f16[192,1024]{1,0:T(8,128)(2,1)S(1)}, u32[]{:S(2)}, u32[]{:S(2)}) collective-permute-start(f16[192,1024]{1,0:T(8,128)(2,1)S(1)} %slice.86), channel_id=1, source_target_pairs={{0,28},{2,6},{4,0},{6,10},{8,4},{10,14},{12,8},{14,18},{16,12},{18... | collective-permute-start | bytes 1179656 | tf_op jit(solution)/shard_map/ppermute | solution.py:30
  90.0 0.6 collective-permute-start.11
  90.6 2.0 %collective-permute-start.12 = (f32[1,128]{1,0:T(1,128)S(1)}, f32[1,128]{1,0:T(1,128)S(1)}, u32[]{:S(2)}, u32[]{:S(2)}) collective-permute-start(f32[1,128]{1,0:T(1,128)S(1)} %add.247), channel_id=1, source_target_pairs={{0,4},{4,0},{8,12},{12,8},{16,20},{20,16},{24,28},{28,24},{1,5},{5... | collective-permute-start | bytes 1544 | tf_op jit(solution)/shard_map/ppermute | solution.py:51
  92.6 3.6 %collective-permute-done.12 = f32[1,128]{1,0:T(1,128)S(1)} collective-permute-done((f32[1,128]{1,0:T(1,128)S(1)}, f32[1,128]{1,0:T(1,128)S(1)}, u32[]{:S(2)}, u32[]{:S(2)}) %collective-permute-start.12) | collective-permute-done | bytes 544 | tf_op jit(solution)/shard_map/ppermute | solution.py:51
  96.2 0.4 collective-permute-start.13
  96.5 4.1 %collective-permute-done.13 = f32[1,128]{1,0:T(1,128)S(1)} collective-permute-done((f32[1,128]{1,0:T(1,128)S(1)}, f32[1,128]{1,0:T(1,128)S(1)}, u32[]{:S(2)}, u32[]{:S(2)}) %collective-permute-start.13) | collective-permute-done | bytes 544 | tf_op jit(solution)/shard_map/ppermute | solution.py:51
  100.8 3.1 %collective-permute-start.14 = (f16[96,1024]{1,0:T(8,128)(2,1)S(1)}, f16[96,1024]{1,0:T(8,128)(2,1)S(1)}, u32[]{:S(2)}, u32[]{:S(2)}) collective-permute-start(f16[96,1024]{1,0:T(8,128)(2,1)S(1)} %fusion.44), channel_id=1, source_target_pairs={{0,24},{2,10},{4,28},{6,14},{8,0},{10,18},{12,4},{14,22},{16,8},{1... | collective-permute-start | bytes 589832 | tf_op jit(solution)/shard_map/ppermute | solution.py:30
  103.9 0.9 collective-permute-start.15
  104.8 6.5 %collective-permute-done.15 = f32[1,128]{1,0:T(1,128)S(1)} collective-permute-done((f32[1,128]{1,0:T(1,128)S(1)}, f32[1,128]{1,0:T(1,128)S(1)}, u32[]{:S(2)}, u32[]{:S(2)}) %collective-permute-start.15) | collective-permute-done | bytes 544 | tf_op jit(solution)/shard_map/ppermute | solution.py:51
  111.4 0.7 dynamic-slice_add_fusion
  112.1 1.5 %collective-permute-start.16 = (f32[1,128]{1,0:T(1,128)S(1)}, f32[1,128]{1,0:T(1,128)S(1)}, u32[]{:S(2)}, u32[]{:S(2)}) collective-permute-start(f32[1,128]{1,0:T(1,128)S(1)} %add.254), channel_id=1, source_target_pairs={{0,32},{32,0},{64,96},{96,64},{1,33},{33,1},{65,97},{97,65},{2,34}... | collective-permute-start | bytes 1544 | tf_op jit(solution)/shard_map/ppermute | solution.py:51
  113.6 2.1 %collective-permute-done.16 = f32[1,128]{1,0:T(1,128)S(1)} collective-permute-done((f32[1,128]{1,0:T(1,128)S(1)}, f32[1,128]{1,0:T(1,128)S(1)}, u32[]{:S(2)}, u32[]{:S(2)}) %collective-permute-start.16) | collective-permute-done | bytes 544 | tf_op jit(solution)/shard_map/ppermute | solution.py:51
  115.7 3.0 %collective-permute-start.17 = (f32[1,128]{1,0:T(1,128)S(1)}, f32[1,128]{1,0:T(1,128)S(1)}, u32[]{:S(2)}, u32[]{:S(2)}) collective-permute-start(f32[1,128]{1,0:T(1,128)S(1)} %add.255), channel_id=1, source_target_pairs={{0,64},{32,96},{64,0},{96,32},{1,65},{33,97},{65,1},{97,33},{2,66}... | collective-permute-start | bytes 1544 | tf_op jit(solution)/shard_map/ppermute | solution.py:51
  118.6 1.0 convert_reduce_fusion
  119.6 1.1 collective-permute-done.17
  120.8 1.7 %fusion.47 = f32[48,1024]{1,0:T(8,128)} fusion(f32[48,1024]{1,0:T(8,128)} %collective-permute-done.18, f32[384,1024]{1,0:T(8,128)S(1)} %get-tuple-element.36, f32[96,1024]{1,0:T(8,128)S(1)} %convert_element_type.83, s32[]{:T(128)S(6)} %select_n.139, f16[96,1024]{1,0:T(8,128)(2,1)S(1)} %copy-done.7), kind=kLoop, calls=%fused_computation.64 | loop fusion | flops 196608 | bytes 884740 | tf_op jit(solution)/shard_map/add | solution.py:72
  (68 shorter events, 1.7 us)
Async XLA Ops:
  1.7 3.7 %copy-start = (bf16[1,2048,1024]{2,1,0:T(8,128)(2,1)S(1)}, bf16[1,2048,1024]{2,1,0:T(8,128)(2,1)}, u32[]{:S(2)}) copy-start(bf16[1,2048,1024]{2,1,0:T(8,128)(2,1)} %param.8) | copy-start | bytes 12582916
  6.2 12.4 %collective-permute-start = (f32[96,1024]{1,0:T(8,128)S(1)}, f32[96,1024]{1,0:T(8,128)S(1)}, u32[]{:S(2)}, u32[]{:S(2)}) collective-permute-start(f32[96,1024]{1,0:T(8,128)S(1)} %fusion.2), channel_id=1, source_target_pairs={{0,1},{1,0},{2,3},{3,2},{4,5},{5,4},{6,7},{7,6},{8,9},{9,8},{10,11... | collective-permute-start | bytes 1179656 | tf_op jit(solution)/shard_map/ppermute | solution.py:83
  8.6 0.9 copy-start.8
  18.9 1.5 %collective-permute-start.1 = (bf16[96,1024]{1,0:T(8,128)(2,1)S(1)}, bf16[96,1024]{1,0:T(8,128)(2,1)S(1)}, u32[]{:S(2)}, u32[]{:S(2)}) collective-permute-start(bf16[96,1024]{1,0:T(8,128)(2,1)S(1)} %multiply_convert_fusion), channel_id=1, source_target_pairs={{0,2},{2,0},{1,3},{3,1},{4,6},{6,4},{5,7},{7,5},{8,10},{10,8},{9,1... | collective-permute-start | bytes 589832 | tf_op jit(solution)/shard_map/ppermute | solution.py:131
  22.0 12.1 %collective-permute-start.2 = (bf16[96,1152]{1,0:T(8,128)(2,1)S(1)}, bf16[96,1152]{1,0:T(8,128)(2,1)S(1)}, u32[]{:S(2)}, u32[]{:S(2)}) collective-permute-start(bf16[96,1152]{1,0:T(8,128)(2,1)S(1)} %pad_maximum_fusion.2), channel_id=1, source_target_pairs={{0,8},{2,26},{4,12},{6,30},{8,16},{10,2},{12,20},{14,6},{16,24},{1... | collective-permute-start | bytes 663560 | tf_op jit(solution)/shard_map/ppermute | solution.py:30
  26.6 31.3 %all-to-all-start = ((bf16[16,48,1024]{2,1,0:T(8,128)(2,1)}), bf16[16,48,1024]{2,1,0:T(8,128)(2,1)S(1)}, u32[]{:S(2)}, u32[]{:S(2)}) async-start(bf16[16,48,1024]{2,1,0:T(8,128)(2,1)} %broadcast_in_dim.59), calls=%async_computation | async-start | bytes 3145728 | tf_op jit(solution)/shard_map/all_to_all | solution.py:17
  34.1 12.8 %collective-permute-start.3 = (bf16[192,1152]{1,0:T(8,128)(2,1)S(1)}, bf16[192,1152]{1,0:T(8,128)(2,1)S(1)}, u32[]{:S(2)}, u32[]{:S(2)}) collective-permute-start(bf16[192,1152]{1,0:T(8,128)(2,1)S(1)} %pad_maximum_fusion.1), channel_id=1, source_target_pairs={{0,4},{2,30},{4,8},{6,2},{8,12},{10,6},{12,16},{14,10},{16,20},{18... | collective-permute-start | bytes 1327112 | tf_op jit(solution)/shard_map/ppermute | solution.py:30
  36.1 10.8 %collective-permute-start.4 = (bf16[48,1152]{1,0:T(8,128)(2,1)S(1)}, bf16[48,1152]{1,0:T(8,128)(2,1)S(1)}, u32[]{:S(2)}, u32[]{:S(2)}) collective-permute-start(bf16[48,1152]{1,0:T(8,128)(2,1)S(1)} %constant_dynamic-slice_fusion.2), channel_id=1, source_target_pairs={{0,8},{2,26},{4,12},{6,30},{8,16},{10,2},{12,20},{14,6},{16,24},{1... | collective-permute-start | bytes 331784 | tf_op jit(solution)/shard_map/ppermute | solution.py:30
  47.0 2.4 %collective-permute-start.5 = (bf16[336,1152]{1,0:T(8,128)(2,1)S(1)}, bf16[336,1152]{1,0:T(8,128)(2,1)S(1)}, u32[]{:S(2)}, u32[]{:S(2)}) collective-permute-start(bf16[336,1152]{1,0:T(8,128)(2,1)S(1)} %pad_maximum_fusion), channel_id=1, source_target_pairs={{0,2},{2,0},{1,3},{3,1},{4,6},{6,4},{5,7},{7,5},{8,10},{10,8},{9,1... | collective-permute-start | bytes 2322440 | tf_op jit(solution)/shard_map/ppermute | solution.py:139
  47.2 13.3 %copy-start.1 = (bf16[432,1152]{1,0:T(8,128)(2,1)}, bf16[432,1152]{1,0:T(8,128)(2,1)S(1)}, u32[]{:S(2)}) copy-start(bf16[432,1152]{1,0:T(8,128)(2,1)S(1)} %constant_dynamic-update-slice_fusion) | copy-start | bytes 2985988
  49.3 0.9 copy-start.3
  58.0 2.5 %copy-start.4 = (bf16[336,1152]{1,0:T(8,128)(2,1)S(1)}, bf16[336,1152]{1,0:T(8,128)(2,1)}, u32[]{:S(2)}) copy-start(bf16[336,1152]{1,0:T(8,128)(2,1)} %copy-done.3) | copy-start | bytes 2322436
  60.5 3.7 %copy-start.5 = (bf16[336,1152]{1,0:T(8,128)(2,1)S(1)}, bf16[336,1152]{1,0:T(8,128)(2,1)}, u32[]{:S(2)}) copy-start(bf16[336,1152]{1,0:T(8,128)(2,1)} %copy-done.3) | copy-start | bytes 2322436
  63.9 5.3 %collective-permute-start.6 = (f32[1,128]{1,0:T(1,128)S(1)}, f32[1,128]{1,0:T(1,128)S(1)}, u32[]{:S(2)}, u32[]{:S(2)}) collective-permute-start(f32[1,128]{1,0:T(1,128)S(1)} %broadcast_in_dim.68), channel_id=1, source_target_pairs={{0,1},{1,0},{2,3},{3,2},{4,5},{5,4},{6,7},{7,6},{8,9},{9,8},{10,11... | collective-permute-start | bytes 1544 | tf_op jit(solution)/shard_map/ppermute | solution.py:51
  64.2 1.2 copy-start.2
  69.2 3.5 %collective-permute-start.7 = (f32[1,128]{1,0:T(1,128)S(1)}, f32[1,128]{1,0:T(1,128)S(1)}, u32[]{:S(2)}, u32[]{:S(2)}) collective-permute-start(f32[1,128]{1,0:T(1,128)S(1)} %broadcast_add_fusion), channel_id=1, source_target_pairs={{0,128},{128,0},{1,129},{129,1},{2,130},{130,2},{3,131},{131,3},{4... | collective-permute-start | bytes 1544 | tf_op jit(solution)/shard_map/ppermute | solution.py:51
  72.7 8.3 %collective-permute-start.8 = (f32[384,1024]{1,0:T(8,128)}, f32[384,1024]{1,0:T(8,128)}, u32[]{:S(2)}, u32[]{:S(2)}) collective-permute-start(f32[384,1024]{1,0:T(8,128)} %fusion.36), channel_id=1, source_target_pairs={{0,2},{2,0},{1,3},{3,1},{4,6},{6,4},{5,7},{7,5},{8,10},{10,8},{9,1... | collective-permute-start | bytes 4718600 | tf_op jit(solution)/shard_map/ppermute | solution.py:166
  73.6 45.1 %all-to-all-start.1 = ((f16[16,48,1024]{2,1,0:T(8,128)(2,1)}), f16[16,48,1024]{2,1,0:T(8,128)(2,1)S(1)}, u32[]{:S(2)}, u32[]{:S(2)}) async-start(f16[16,48,1024]{2,1,0:T(8,128)(2,1)} %bitcast.43), calls=%async_computation.1 | async-start | bytes 3145728 | tf_op jit(solution)/shard_map/all_to_all | solution.py:17
  79.0 2.0 %collective-permute-start.9 = (f32[1,128]{1,0:T(1,128)S(1)}, f32[1,128]{1,0:T(1,128)S(1)}, u32[]{:S(2)}, u32[]{:S(2)}) collective-permute-start(f32[1,128]{1,0:T(1,128)S(1)} %add.246), channel_id=1, source_target_pairs={{0,2},{2,0},{1,3},{3,1},{4,6},{6,4},{5,7},{7,5},{8,10},{10,8},{9,1... | collective-permute-start | bytes 1544 | tf_op jit(solution)/shard_map/ppermute | solution.py:51
  82.9 17.7 %collective-permute-start.10 = (f16[192,1024]{1,0:T(8,128)(2,1)S(1)}, f16[192,1024]{1,0:T(8,128)(2,1)S(1)}, u32[]{:S(2)}, u32[]{:S(2)}) collective-permute-start(f16[192,1024]{1,0:T(8,128)(2,1)S(1)} %slice.86), channel_id=1, source_target_pairs={{0,28},{2,6},{4,0},{6,10},{8,4},{10,14},{12,8},{14,18},{16,12},{18... | collective-permute-start | bytes 1179656 | tf_op jit(solution)/shard_map/ppermute | solution.py:30
  90.0 10.6 %collective-permute-start.11 = (f16[48,1024]{1,0:T(8,128)(2,1)S(1)}, f16[48,1024]{1,0:T(8,128)(2,1)S(1)}, u32[]{:S(2)}, u32[]{:S(2)}) collective-permute-start(f16[48,1024]{1,0:T(8,128)(2,1)S(1)} %slice.87), channel_id=1, source_target_pairs={{0,24},{2,10},{4,28},{6,14},{8,0},{10,18},{12,4},{14,22},{16,8},{1... | collective-permute-start | bytes 294920 | tf_op jit(solution)/shard_map/ppermute | solution.py:30
  90.6 5.6 %collective-permute-start.12 = (f32[1,128]{1,0:T(1,128)S(1)}, f32[1,128]{1,0:T(1,128)S(1)}, u32[]{:S(2)}, u32[]{:S(2)}) collective-permute-start(f32[1,128]{1,0:T(1,128)S(1)} %add.247), channel_id=1, source_target_pairs={{0,4},{4,0},{8,12},{12,8},{16,20},{20,16},{24,28},{28,24},{1,5},{5... | collective-permute-start | bytes 1544 | tf_op jit(solution)/shard_map/ppermute | solution.py:51
  96.2 4.4 %collective-permute-start.13 = (f32[1,128]{1,0:T(1,128)S(1)}, f32[1,128]{1,0:T(1,128)S(1)}, u32[]{:S(2)}, u32[]{:S(2)}) collective-permute-start(f32[1,128]{1,0:T(1,128)S(1)} %add.249), channel_id=1, source_target_pairs={{0,8},{4,12},{8,0},{12,4},{16,24},{20,28},{24,16},{28,20},{1,9},{5... | collective-permute-start | bytes 1544 | tf_op jit(solution)/shard_map/ppermute | solution.py:51
  100.8 10.6 %collective-permute-start.14 = (f16[96,1024]{1,0:T(8,128)(2,1)S(1)}, f16[96,1024]{1,0:T(8,128)(2,1)S(1)}, u32[]{:S(2)}, u32[]{:S(2)}) collective-permute-start(f16[96,1024]{1,0:T(8,128)(2,1)S(1)} %fusion.44), channel_id=1, source_target_pairs={{0,24},{2,10},{4,28},{6,14},{8,0},{10,18},{12,4},{14,22},{16,8},{1... | collective-permute-start | bytes 589832 | tf_op jit(solution)/shard_map/ppermute | solution.py:30
  103.9 7.4 %collective-permute-start.15 = (f32[1,128]{1,0:T(1,128)S(1)}, f32[1,128]{1,0:T(1,128)S(1)}, u32[]{:S(2)}, u32[]{:S(2)}) collective-permute-start(f32[1,128]{1,0:T(1,128)S(1)} %add.250), channel_id=1, source_target_pairs={{0,16},{4,20},{8,24},{12,28},{16,0},{20,4},{24,8},{28,12},{1,17},{... | collective-permute-start | bytes 1544 | tf_op jit(solution)/shard_map/ppermute | solution.py:51
  104.8 10.8 %copy-start.6 = (f16[96,1024]{1,0:T(8,128)(2,1)}, f16[96,1024]{1,0:T(8,128)(2,1)S(1)}, u32[]{:S(2)}) copy-start(f16[96,1024]{1,0:T(8,128)(2,1)S(1)} %slice.76) | copy-start | bytes 589828
  112.1 8.6 %collective-permute-start.18 = (f32[48,1024]{1,0:T(8,128)}, f32[48,1024]{1,0:T(8,128)}, u32[]{:S(2)}, u32[]{:S(2)}) collective-permute-start(f32[48,1024]{1,0:T(8,128)} %dynamic-slice_add_fusion), channel_id=1, source_target_pairs={{0,2},{2,0},{1,3},{3,1},{4,6},{6,4},{5,7},{7,5},{8,10},{10,8},{9,1... | collective-permute-start | bytes 589832 | tf_op jit(solution)/shard_map/ppermute | solution.py:69
  112.1 3.5 %collective-permute-start.16 = (f32[1,128]{1,0:T(1,128)S(1)}, f32[1,128]{1,0:T(1,128)S(1)}, u32[]{:S(2)}, u32[]{:S(2)}) collective-permute-start(f32[1,128]{1,0:T(1,128)S(1)} %add.254), channel_id=1, source_target_pairs={{0,32},{32,0},{64,96},{96,64},{1,33},{33,1},{65,97},{97,65},{2,34}... | collective-permute-start | bytes 1544 | tf_op jit(solution)/shard_map/ppermute | solution.py:51
  115.7 5.0 %collective-permute-start.17 = (f32[1,128]{1,0:T(1,128)S(1)}, f32[1,128]{1,0:T(1,128)S(1)}, u32[]{:S(2)}, u32[]{:S(2)}) collective-permute-start(f32[1,128]{1,0:T(1,128)S(1)} %add.255), channel_id=1, source_target_pairs={{0,64},{32,96},{64,0},{96,32},{1,65},{33,97},{65,1},{97,33},{2,66}... | collective-permute-start | bytes 1544 | tf_op jit(solution)/shard_map/ppermute | solution.py:51
  118.6 2.1 %copy-start.7 = (f16[96,1024]{1,0:T(8,128)(2,1)S(1)}, f16[96,1024]{1,0:T(8,128)(2,1)}, u32[]{:S(2)}) copy-start(f16[96,1024]{1,0:T(8,128)(2,1)} %copy-done.6) | copy-start | bytes 589828

commit v8 on v7

--- a/solution.py
+++ b/solution.py
@@ -3,6 +3,8 @@
 from jax import lax
 from jax.sharding import Mesh
 from jax.sharding import PartitionSpec as P
+from jax.experimental import pallas as pl
+from jax.experimental.pallas import tpu as pltpu
 
 DP = ("xl", "y", "z")
 PLANE = ("xl", "y", "tensor")
@@ -49,27 +51,6 @@
 def with_partner(value, axis, bit):
     pairs = [(i, i ^ bit) for i in range(lax.axis_size(axis))]
     return value + lax.ppermute(value, axis, pairs)
-
-
-def summed_over_z(kept, section, loss):
-    half = kept.shape[0] // 8
-    one_three = along_z(kept[: 4 * half].astype(SENT), -1)
-    four = along_z(kept[6 * half : 7 * half].astype(SENT), -2)
-    loss = with_partner(with_partner(loss, "z", 1), "z", 2)
-    one_three, four, loss = tied(one_three, four, loss)
-    four = four.astype(F32)
-    upper = kept[4 * half : 5 * half] + jnp.where(section == 0, four, 0.0)
-    lower = kept[5 * half : 6 * half] + jnp.where(section == 0, 0.0, four)
-    two = jnp.concatenate([upper, lower], axis=0) + one_three[2 * half :].astype(F32)
-    two = along_z(two.astype(SENT), -2)
-    loss = with_partner(loss, "z", 4)
-    two, loss = tied(two, loss)
-    two = two.astype(F32)
-    given = row_half(one_three[: 2 * half], 1 - section).astype(F32) + row_half(two, 1 - section)
-    got = lax.ppermute(given, "section", SWAP)
-    loss = with_partner(with_partner(loss, "y", 1), "y", 2)
-    mine = row_half(one_three[: 2 * half], section).astype(F32) + row_half(two, section)
-    return kept[7 * half :] + mine + got, loss
 
 
 def tower(inputs, up, down, tensor):
@@ -97,20 +78,79 @@
     return digits.astype(jnp.bfloat16)
 
 
-def scored(rows, width, reports, columns, scale_value, bias_value):
-    slides = rows[:, :width]
-    wanted = rows[:, width].astype(F32) * LANES + rows[:, width + 1].astype(F32)
-    dots = lax.dot_general(
-        slides, reports, (((1,), (1,)), ((), ())), preferred_element_type=F32
-    )
-    logits = scale_value * dots + bias_value
-    match = wanted[:, None] == columns[None, :]
-    turned = jnp.where(match, -logits, logits)
-    small = jnp.exp(-jnp.abs(turned))
-    loss_part = jnp.sum(jnp.maximum(turned, 0.0) + jnp.log1p(small))
-    sigmoid = jnp.where(turned >= 0, 1.0, small) / (1.0 + small)
-    weight = jnp.where(match, -scale_value, scale_value) * sigmoid
-    return slides, weight.astype(jnp.bfloat16), loss_part
+def score_kernel(
+    spot, scale, bias, mine, other, reports, columns, weight, moved, sent, loss
+):
+    count, width = reports.shape
+    scale_value, bias_value = scale[0], bias[0]
+    z, section = spot[0], spot[1]
+    toward = 2 * section - 1
+    quarter = mine.shape[0] // 9
+    half = 8 * quarter
+
+    def place(step, own):
+        row = lax.rem(z + toward * step + 8, 8) * quarter
+        return pl.multiple_of(row + (1 - own) * half, 16)
+
+    blocks = []
+    for step in (0, 1, 3, 2):
+        blocks += [(step, 1 - section), (step, section)]
+    blocks.append((4, 1))
+    for step in (-1, -3, -2):
+        blocks += [(step, 1 - section), (step, section)]
+    blocks.append((4, 0))
+
+    total = jnp.zeros((1, count), F32)
+    block = 0
+    for rows, sizes in ((mine, (4, 5)), (other, (4, 3))):
+        start = 0
+        for size in sizes:
+            stop = start + size * quarter
+            marks = rows[start:stop, width : width + 2].astype(F32)
+            wanted = marks[:, 0:1] * LANES + marks[:, 1:2]
+            dots = lax.dot_general(
+                rows[start:stop, :width],
+                reports[...],
+                (((1,), (1,)), ((), ())),
+                preferred_element_type=F32,
+            )
+            logits = scale_value * dots + bias_value
+            match = wanted == columns[...]
+            turned = jnp.where(match, -logits, logits)
+            small = jnp.exp(-jnp.abs(turned))
+            losses = jnp.maximum(turned, 0.0) + jnp.log1p(small)
+            total = total + jnp.sum(losses, axis=0, keepdims=True)
+            sigmoid = jnp.where(turned >= 0, 1.0, small) / (1.0 + small)
+            signed = jnp.where(match, -scale_value, scale_value) * sigmoid
+            signed = signed.astype(jnp.bfloat16)
+            weight[block * quarter : (block + size) * quarter, :] = signed
+            for k in range(size):
+                part = signed[k * quarter : (k + 1) * quarter]
+                moved[pl.ds(place(*blocks[block + k]), quarter), :] = part
+            start, block = stop, block + size
+    sent[...] = jnp.dot(moved[half:, :], reports[...], preferred_element_type=F32)
+    loss[...] = jnp.broadcast_to(jnp.sum(total, axis=1, keepdims=True), loss.shape)
+
+
+def scored(scale, bias, mine, other, reports, columns):
+    count, width = reports.shape
+    rows = mine.shape[0] + other.shape[0]
+    spot = jnp.stack([lax.axis_index("z"), lax.axis_index("section")]).astype(jnp.int32)
+    scalar = pl.BlockSpec(memory_space=pltpu.SMEM)
+    whole = pl.BlockSpec(memory_space=pltpu.VMEM)
+    return pl.pallas_call(
+        score_kernel,
+        in_specs=[scalar, scalar, scalar, whole, whole, whole, whole],
+        out_specs=[whole, whole, whole, whole],
+        out_shape=[
+            jax.ShapeDtypeStruct((rows, count), jnp.bfloat16),
+            jax.ShapeDtypeStruct((rows, count), jnp.bfloat16),
+            jax.ShapeDtypeStruct((rows // 2, width), F32),
+            jax.ShapeDtypeStruct((1, LANES), F32),
+        ],
+        compiler_params=pltpu.CompilerParams(vmem_limit_bytes=48 * 1024 * 1024),
+        name="scores",
+    )(spot, scale, bias, mine, other, reports, columns)
 
 
 def transposed_dot(weight, slides):
@@ -122,7 +162,6 @@
     tensor = lax.axis_index("tensor")
     n_z = lax.axis_size("z")
     n_plane = lax.axis_size(PLANE)
-    scale_value, bias_value = scale[0], bias[0]
     quarter, width = tower_input.shape[1] // 4, tower_input.shape[2]
     total = lax.axis_size(ALL) * quarter
 
@@ -143,31 +182,26 @@
     owner = ((member // 2 * n_z + lax.axis_index("z")) * 2 + section) * 2 + member % 2
     columns = (owner * quarter + row).astype(F32)
 
-    slides_mine, weight_mine, loss_mine = scored(
-        rows_mine, width, reports_all, columns, scale_value, bias_value
+    weight, moved, sent, loss = scored(
+        scale, bias, rows_mine, rows_other, reports_all, columns[None, :]
     )
-    slides_other, weight_other, loss_other = scored(
-        rows_other, width, reports_all, columns, scale_value, bias_value
-    )
-    loss = with_partner(jnp.broadcast_to(loss_mine + loss_other, (1, LANES)), "tensor", 1)
-    report_part = transposed_dot(weight_mine, slides_mine)
-    report_part = report_part + transposed_dot(weight_other, slides_other)
+    back = lax.ppermute(sent, "section", SWAP)
+    loss = with_partner(loss, "tensor", 1)
+    kept = jnp.dot(moved[: sent.shape[0]], reports_all, preferred_element_type=F32)
+    kept, weight = tied(kept, weight)
+    slide_grad = lax.psum_scatter(kept + back, "z", tiled=True)
+    loss = with_partner(loss, "xl", 1)
+    cut = rows_mine.shape[0]
+    report_part = transposed_dot(weight[:cut], rows_mine[:, :width])
+    report_part = report_part + transposed_dot(weight[cut:], rows_other[:, :width])
     report_part = report_part.astype(SENT).reshape(n_plane, quarter, width)
-    report_part, weight_mine, weight_other, loss = tied(
-        report_part, weight_mine, weight_other, loss
-    )
+    report_part, loss = tied(report_part, loss)
     report_terms = exchanged(report_part, PLANE)
-    loss = with_partner(loss, "xl", 1)
-    weight_own, weight_mine = weight_mine[: 2 * quarter], weight_mine[2 * quarter :]
-    weight_sent = jnp.concatenate([weight_other, row_half(weight_own, 1 - section)], axis=0)
-    weight_kept = jnp.concatenate([weight_mine, row_half(weight_own, section)], axis=0)
-    sent = jnp.dot(weight_sent, reports_all, preferred_element_type=F32)
-    sent, loss = tied(sent, loss)
-    back = lax.ppermute(sent, "section", SWAP)
     loss = with_partner(loss, "section", 1)
-    back, loss = tied(back, loss)
-    kept = jnp.dot(weight_kept, reports_all, preferred_element_type=F32) + back
-    slide_grad, loss = summed_over_z(kept, section, loss)
+    for bit in (1, 2, 4):
+        loss = with_partner(loss, "z", bit)
+    report_terms, loss = tied(report_terms, loss)
+    loss = with_partner(with_partner(loss, "y", 1), "y", 2)
     report_grad = report_terms.astype(F32).sum(axis=0)
     return (loss[0, :1] / total, slide_grad, report_grad)
 

time: 124 us -> 137 us (1.10)
  waiting for transfers between devices: 46.5 us -> 67.1 us
  starting transfers between devices: 44.2 us -> 29.6 us
  between operations: 4.66 us -> 16.7 us
  matrix products: 17 us -> 10.7 us
  Pallas kernels: 0 us -> 6.07 us
  other arithmetic: 6.37 us -> 3.3 us
  local copies, waits for them, and re-layouts: 4.84 us -> 2.75 us
    ppermute x6 -> x3, starting transfers between devices: 19.7 us -> 6.55 us  [along_z(): return lax.ppermute(array, ('z', 'section'), pairs)]
    all_to_all x2, waiting for transfers between devices: 7.55 us -> 18.3 us  [exchanged(): return lax.all_to_all(parts, axes, split_axis=0, concat_axis=0, tiled=True)]
    dot_general x4 -> x1, matrix products: 8.43 us -> 2.18 us  [local(): jnp.dot(moved[:sent.shape[0]], reports_all, preferred_element_type=F32)]
    ppermute x6 -> x3, waiting for transfers between devices: 7.1 us -> 13.2 us  [along_z(): return lax.ppermute(array, ('z', 'section'), pairs)]
    pallas_call x0 -> x1, Pallas kernels: none -> 6.07 us  [scored(): pl.pallas_call(score_kernel, in_specs=[scalar, scalar, scalar, whole, who...]
    ppermute x8, waiting for transfers between devices: 19.6 us -> 21.9 us  [with_partner(): return value + lax.ppermute(value, axis, pairs)]
    another operation x1, other arithmetic: 1.75 us -> 0.07 us  [scored(): jnp.stack([lax.axis_index('z'), lax.axis_index('section')])]
    add x5 -> x1, other arithmetic: 2.86 us -> 1.53 us  [local(): slide_grad = lax.psum_scatter(kept + back, 'z', tiled=True)]
  transfers between devices with their start and end apart: 21 -> 18, of which waited for: 12 -> 15; matrix products, arithmetic and copies ran while one was open for 11% -> 6% of each run, Pallas kernels for 0% -> 0%
where the time goes in v8:
time: 137 us; the launch traced here: 136 us
  waiting for transfers between devices  67.1 us (49%)
  starting transfers between devices  29.6 us (22%)
  between operations  16.7 us (12%)
  matrix products  10.7 us (8%)
  Pallas kernels  6.07 us (4%)
  other arithmetic  3.3 us (2%)
  local copies, waits for them, and re-layouts  2.75 us (2%)
    ppermute x8, waiting for transfers between devices, with_partner(): return value + lax.ppermute(value, axis, pairs)  21.9 us
    all_to_all x2, waiting for transfers between devices, exchanged(): return lax.all_to_all(parts, axes, split_axis=0, concat_axis=0, tiled=True)  18.3 us
    ppermute x3, waiting for transfers between devices, along_z(): return lax.ppermute(array, ('z', 'section'), pairs)  13.2 us
    all_to_all x2, starting transfers between devices, exchanged(): return lax.all_to_all(parts, axes, split_axis=0, concat_axis=0, tiled=True)  12.3 us
    ppermute x1, waiting for transfers between devices, tower(): arrived = lax.ppermute(sent, 'tensor', SWAP)  9.02 us
    ppermute x8, starting transfers between devices, with_partner(): return value + lax.ppermute(value, axis, pairs)  7.93 us
    ppermute x3, starting transfers between devices, along_z(): return lax.ppermute(array, ('z', 'section'), pairs)  6.55 us
    pallas_call x1, Pallas kernels, scored(): pl.pallas_call(score_kernel, in_specs=[scalar, scalar, scalar, whole, who...  6.07 us
  transfers between devices with their start and end apart: 18, of which 15 were waited for; matrix products, arithmetic and copies ran while one was open for 6% of the time, Pallas kernels for 0%

profile of v8, /device:TPU:4, one launch (start us, length us, event | category | flops | bytes accessed | tf_op | source)
XLA Modules:
  0.0 136.2 jit_solution(9797406121611621825)
XLA Ops:
  7.2 1.1 constant_dynamic-slice_fusion.3
  8.2 3.7 %fusion.15 = bf16[192,2048]{1,0:T(8,128)(2,1)S(1)} fusion(bf16[1,1024,2048]{2,1,0:T(8,128)(2,1)} %param.7, bf16[96,1024]{1,0:T(8,128)(2,1)S(1)} %bitcast.30, bf16[96,1024]{1,0:T(8,128)(2,1)S(1)} %bitcast.33), kind=kOutput, calls=%fused_computation.16 | convolution fusion | flops 809631744 | bytes 5373952 | tf_op jit(solution)/shard_map/dot_general | solution.py:62
  11.9 0.8 fusion.2
  12.8 2.3 %collective-permute-start = (f32[96,1024]{1,0:T(8,128)S(1)}, f32[96,1024]{1,0:T(8,128)S(1)}, u32[]{:S(2)}, u32[]{:S(2)}) collective-permute-start(f32[96,1024]{1,0:T(8,128)S(1)} %fusion.2), channel_id=1, source_target_pairs={{0,1},{1,0},{2,3},{3,2},{4,5},{5,4},{6,7},{7,6},{8,9},{9,8},{10,11... | collective-permute-start | bytes 1179656 | tf_op jit(solution)/shard_map/ppermute | solution.py:64
  15.1 0.8 fusion.18
  16.0 0.1 reshape.258
  16.1 0.1 reshape.259
  16.2 9.0 %collective-permute-done = f32[96,1024]{1,0:T(8,128)S(1)} collective-permute-done((f32[96,1024]{1,0:T(8,128)S(1)}, f32[96,1024]{1,0:T(8,128)S(1)}, u32[]{:S(2)}, u32[]{:S(2)}) %collective-permute-start) | collective-permute-done | bytes 393248 | tf_op jit(solution)/shard_map/ppermute | solution.py:64
  25.2 0.1 multiply_reduce_fusion
  25.4 0.1 multiply_convert_fusion
  25.5 0.1 collective-permute-start.1
  25.6 0.1 select_convert_fusion
  25.7 1.3 collective-permute-done.1
  27.0 0.1 broadcast_select_fusion
  27.2 1.3 broadcast_in_dim.23
  28.5 3.3 %collective-permute-start.2 = (bf16[96,1152]{1,0:T(8,128)(2,1)S(1)}, bf16[96,1152]{1,0:T(8,128)(2,1)S(1)}, u32[]{:S(2)}, u32[]{:S(2)}) collective-permute-start(bf16[96,1152]{1,0:T(8,128)(2,1)S(1)} %pad_maximum_fusion.2), channel_id=1, source_target_pairs={{0,8},{2,26},{4,12},{6,30},{8,16},{10,2},{12,20},{14,6},{16,24},{1... | collective-permute-start | bytes 663560 | tf_op jit(solution)/shard_map/ppermute | solution.py:32
  33.1 6.2 %collective-permute-done.2 = bf16[96,1152]{1,0:T(8,128)(2,1)S(1)} collective-permute-done((bf16[96,1152]{1,0:T(8,128)(2,1)S(1)}, bf16[96,1152]{1,0:T(8,128)(2,1)S(1)}, u32[]{:S(2)}, u32[]{:S(2)}) %collective-permute-start.2) | collective-permute-done | bytes 221216 | tf_op jit(solution)/shard_map/ppermute | solution.py:32
  39.4 2.9 %collective-permute-start.3 = (bf16[192,1152]{1,0:T(8,128)(2,1)S(1)}, bf16[192,1152]{1,0:T(8,128)(2,1)S(1)}, u32[]{:S(2)}, u32[]{:S(2)}) collective-permute-start(bf16[192,1152]{1,0:T(8,128)(2,1)S(1)} %pad_maximum_fusion.1), channel_id=1, source_target_pairs={{0,4},{2,30},{4,8},{6,2},{8,12},{10,6},{12,16},{14,10},{16,20},{18... | collective-permute-start | bytes 1327112 | tf_op jit(solution)/shard_map/ppermute | solution.py:32
  42.3 7.5 %all-to-all-start = ((bf16[16,48,1024]{2,1,0:T(8,128)(2,1)}), bf16[16,48,1024]{2,1,0:T(8,128)(2,1)}, u32[]{:S(2)}, u32[]{:S(2)}) async-start(bf16[16,48,1024]{2,1,0:T(8,128)(2,1)} %broadcast_in_dim.23), calls=%async_computation | async-start | bytes 3145728 | tf_op jit(solution)/shard_map/all_to_all | solution.py:19
  49.7 0.0 reduce-scatter.2.cloned.1.call-start
  49.8 0.4 collective-permute-start.4
  50.2 0.1 pad_add_fusion.spot
  50.3 6.9 %collective-permute-done.4 = bf16[48,1152]{1,0:T(8,128)(2,1)S(1)} collective-permute-done((bf16[48,1152]{1,0:T(8,128)(2,1)S(1)}, bf16[48,1152]{1,0:T(8,128)(2,1)S(1)}, u32[]{:S(2)}, u32[]{:S(2)}) %collective-permute-start.4) | collective-permute-done | bytes 110624 | tf_op jit(solution)/shard_map/ppermute | solution.py:32
  57.2 0.1 pad_maximum_fusion
  57.3 0.1 collective-permute-start.5
  57.5 2.1 %collective-permute-done.5.other = bf16[336,1152]{1,0:T(8,128)(2,1)S(1)} collective-permute-done((bf16[336,1152]{1,0:T(8,128)(2,1)S(1)}, bf16[336,1152]{1,0:T(8,128)(2,1)S(1)}, u32[]{:S(2)}, u32[]{:S(2)}) %collective-permute-start.5) | collective-permute-done | bytes 774176 | tf_op jit(solution)/shard_map/ppermute | solution.py:178
  59.7 13.5 %all-to-all-done = bf16[16,48,1024]{2,1,0:T(8,128)(2,1)} async-done(((bf16[16,48,1024]{2,1,0:T(8,128)(2,1)}), bf16[16,48,1024]{2,1,0:T(8,128)(2,1)}, u32[]{:S(2)}, u32[]{:S(2)}) %all-to-all-start) | async-done | bytes 1572896 | tf_op jit(solution)/shard_map/all_to_all | solution.py:19
  73.2 6.1 %scores.1 = (bf16[768,768]{1,0:T(8,128)(2,1)S(1)}, bf16[768,768]{1,0:T(8,128)(2,1)S(1)}, f32[384,1024]{1,0:T(8,128)S(1)}, f32[1,128]{1,0:T(1,128)S(1)}) custom-call(s32[2]{0:T(128)S(1)} %pad_add_fusion.spot, f32[1]{0:T(128)S(6)} %copy.18.scale, f32[1]{0:T(128)S(6)} %copy.19.bias, bf16[432,1152]{1,0:T(8,128)(2,1)S(1)} %constant_dynamic-update-slice_fusion.mine, ...), custom_call_target="tpu_custom_call" | custom-call | tf_op jit(solution)/shard_map/scores/pallas_call | solution.py:141
  79.2 0.3 collective-permute-start.14
  79.5 2.2 %fusion.25 = f32[384,1024]{1,0:T(8,128)S(1)} fusion(bf16[768,1024]{1,0:T(8,128)(2,1)} %bitcast.7.reports, bf16[768,768]{1,0:T(8,128)(2,1)S(1)} %get-tuple-element.19), kind=kOutput, calls=%fused_computation.23 | convolution fusion | flops 603979776 | bytes 3735552 | tf_op jit(solution)/shard_map/dot_general | solution.py:190
  81.7 1.2 collective-permute-done.14
  82.9 1.5 %add.201 = f32[384,1024]{1,0:T(8,128)} add(f32[384,1024]{1,0:T(8,128)S(1)} %fusion.25, f32[384,1024]{1,0:T(8,128)S(1)} %collective-permute-done.14) | non-fusion elementwise | flops 393216 | bytes 4718592 | tf_op jit(solution)/shard_map/add | solution.py:192
  84.5 0.7 collective-permute-start.6
  85.1 1.0 fusion.22
  86.1 3.5 %collective-permute-done.6 = f32[1,128]{1,0:T(1,128)S(1)} collective-permute-done((f32[1,128]{1,0:T(1,128)S(1)}, f32[1,128]{1,0:T(1,128)S(1)}, u32[]{:S(2)}, u32[]{:S(2)}) %collective-permute-start.6) | collective-permute-done | bytes 544 | tf_op jit(solution)/shard_map/ppermute | solution.py:53
  89.6 1.6 %collective-permute-start.7 = (f32[1,128]{1,0:T(1,128)S(1)}, f32[1,128]{1,0:T(1,128)S(1)}, u32[]{:S(2)}, u32[]{:S(2)}) collective-permute-start(f32[1,128]{1,0:T(1,128)S(1)} %add.193), channel_id=1, source_target_pairs={{0,128},{128,0},{1,129},{129,1},{2,130},{130,2},{3,131},{131,3},{4... | collective-permute-start | bytes 1544 | tf_op jit(solution)/shard_map/ppermute | solution.py:53
  91.2 2.2 %add_convert_fusion = f16[768,1024]{1,0:T(8,128)(2,1)} fusion(f32[768,1024]{1,0:T(8,128)S(1)} %fusion.22, bf16[432,1152]{1,0:T(8,128)(2,1)S(1)} %constant_dynamic-update-slice_fusion.mine, bf16[768,768]{1,0:T(8,128)(2,1)S(1)} %get-tuple-element.21), kind=kOutput, calls=%fused_computation.7 | convolution fusion | flops 681050112 | bytes 6266880 | tf_op jit(solution)/shard_map/dot_general | solution.py:157
  93.4 4.8 %all-to-all-start.1 = ((f16[16,48,1024]{2,1,0:T(8,128)(2,1)}), f16[16,48,1024]{2,1,0:T(8,128)(2,1)S(1)}, u32[]{:S(2)}, u32[]{:S(2)}) async-start(f16[16,48,1024]{2,1,0:T(8,128)(2,1)} %bitcast.29), calls=%async_computation.1 | async-start | bytes 3145728 | tf_op jit(solution)/shard_map/all_to_all | solution.py:19
  98.2 1.1 collective-permute-done.8
  99.3 3.5 %collective-permute-done.9 = f32[1,128]{1,0:T(1,128)S(1)} collective-permute-done((f32[1,128]{1,0:T(1,128)S(1)}, f32[1,128]{1,0:T(1,128)S(1)}, u32[]{:S(2)}, u32[]{:S(2)}) %collective-permute-start.9) | collective-permute-done | bytes 544 | tf_op jit(solution)/shard_map/ppermute | solution.py:53
  102.9 4.4 %collective-permute-done.10 = f32[1,128]{1,0:T(1,128)S(1)} collective-permute-done((f32[1,128]{1,0:T(1,128)S(1)}, f32[1,128]{1,0:T(1,128)S(1)}, u32[]{:S(2)}, u32[]{:S(2)}) %collective-permute-start.10) | collective-permute-done | bytes 544 | tf_op jit(solution)/shard_map/ppermute | solution.py:53
  107.3 5.7 %collective-permute-start.11 = (f32[1,128]{1,0:T(1,128)S(1)}, f32[1,128]{1,0:T(1,128)S(1)}, u32[]{:S(2)}, u32[]{:S(2)}) collective-permute-start(f32[1,128]{1,0:T(1,128)S(1)} %add.197), channel_id=1, source_target_pairs={{0,16},{4,20},{8,24},{12,28},{16,0},{20,4},{24,8},{28,12},{1,17},{... | collective-permute-start | bytes 1544 | tf_op jit(solution)/shard_map/ppermute | solution.py:53
  113.0 1.8 %collective-permute-done.11 = f32[1,128]{1,0:T(1,128)S(1)} collective-permute-done((f32[1,128]{1,0:T(1,128)S(1)}, f32[1,128]{1,0:T(1,128)S(1)}, u32[]{:S(2)}, u32[]{:S(2)}) %collective-permute-start.11) | collective-permute-done | bytes 544 | tf_op jit(solution)/shard_map/ppermute | solution.py:53
  114.8 4.8 %all-to-all-done.1 = f16[16,48,1024]{2,1,0:T(8,128)(2,1)S(1)} async-done(((f16[16,48,1024]{2,1,0:T(8,128)(2,1)}), f16[16,48,1024]{2,1,0:T(8,128)(2,1)S(1)}, u32[]{:S(2)}, u32[]{:S(2)}) %all-to-all-start.1) | async-done | bytes 1572896 | tf_op jit(solution)/shard_map/all_to_all | solution.py:19
  119.6 3.5 %collective-permute-done.12 = f32[1,128]{1,0:T(1,128)S(1)} collective-permute-done((f32[1,128]{1,0:T(1,128)S(1)}, f32[1,128]{1,0:T(1,128)S(1)}, u32[]{:S(2)}, u32[]{:S(2)}) %collective-permute-start.12) | collective-permute-done | bytes 544 | tf_op jit(solution)/shard_map/ppermute | solution.py:53
  123.1 1.0 convert_reduce_fusion
  124.1 4.0 %collective-permute-done.13 = f32[1,128]{1,0:T(1,128)S(1)} collective-permute-done((f32[1,128]{1,0:T(1,128)S(1)}, f32[1,128]{1,0:T(1,128)S(1)}, u32[]{:S(2)}, u32[]{:S(2)}) %collective-permute-start.13) | collective-permute-done | bytes 544 | tf_op jit(solution)/shard_map/ppermute | solution.py:53
  128.2 0.0 reduce-scatter.2.cloned.1.call-done
  (34 shorter events, 0.4 us)
Async XLA Ops:
  8.2 3.7 %copy-start = (bf16[1,2048,1024]{2,1,0:T(8,128)(2,1)S(1)}, bf16[1,2048,1024]{2,1,0:T(8,128)(2,1)}, u32[]{:S(2)}) copy-start(bf16[1,2048,1024]{2,1,0:T(8,128)(2,1)} %param.8) | copy-start | bytes 12582916
  12.8 12.4 %collective-permute-start = (f32[96,1024]{1,0:T(8,128)S(1)}, f32[96,1024]{1,0:T(8,128)S(1)}, u32[]{:S(2)}, u32[]{:S(2)}) collective-permute-start(f32[96,1024]{1,0:T(8,128)S(1)} %fusion.2), channel_id=1, source_target_pairs={{0,1},{1,0},{2,3},{3,2},{4,5},{5,4},{6,7},{7,6},{8,9},{9,8},{10,11... | collective-permute-start | bytes 1179656 | tf_op jit(solution)/shard_map/ppermute | solution.py:64
  15.1 0.8 copy-start.1
  25.5 1.5 %collective-permute-start.1 = (bf16[96,1024]{1,0:T(8,128)(2,1)S(1)}, bf16[96,1024]{1,0:T(8,128)(2,1)S(1)}, u32[]{:S(2)}, u32[]{:S(2)}) collective-permute-start(bf16[96,1024]{1,0:T(8,128)(2,1)S(1)} %multiply_convert_fusion), channel_id=1, source_target_pairs={{0,2},{2,0},{1,3},{3,1},{4,6},{6,4},{5,7},{7,5},{8,10},{10,8},{9,1... | collective-permute-start | bytes 589832 | tf_op jit(solution)/shard_map/ppermute | solution.py:170
  28.5 10.8 %collective-permute-start.2 = (bf16[96,1152]{1,0:T(8,128)(2,1)S(1)}, bf16[96,1152]{1,0:T(8,128)(2,1)S(1)}, u32[]{:S(2)}, u32[]{:S(2)}) collective-permute-start(bf16[96,1152]{1,0:T(8,128)(2,1)S(1)} %pad_maximum_fusion.2), channel_id=1, source_target_pairs={{0,8},{2,26},{4,12},{6,30},{8,16},{10,2},{12,20},{14,6},{16,24},{1... | collective-permute-start | bytes 663560 | tf_op jit(solution)/shard_map/ppermute | solution.py:32
  39.4 17.9 %collective-permute-start.3 = (bf16[192,1152]{1,0:T(8,128)(2,1)S(1)}, bf16[192,1152]{1,0:T(8,128)(2,1)S(1)}, u32[]{:S(2)}, u32[]{:S(2)}) collective-permute-start(bf16[192,1152]{1,0:T(8,128)(2,1)S(1)} %pad_maximum_fusion.1), channel_id=1, source_target_pairs={{0,4},{2,30},{4,8},{6,2},{8,12},{10,6},{12,16},{14,10},{16,20},{18... | collective-permute-start | bytes 1327112 | tf_op jit(solution)/shard_map/ppermute | solution.py:32
  42.3 30.9 %all-to-all-start = ((bf16[16,48,1024]{2,1,0:T(8,128)(2,1)}), bf16[16,48,1024]{2,1,0:T(8,128)(2,1)}, u32[]{:S(2)}, u32[]{:S(2)}) async-start(bf16[16,48,1024]{2,1,0:T(8,128)(2,1)} %broadcast_in_dim.23), calls=%async_computation | async-start | bytes 3145728 | tf_op jit(solution)/shard_map/all_to_all | solution.py:19
  49.7 78.5 %reduce-scatter.2.cloned.1.call-start = ((), (), s32[]{:S(2)}) async-start(), calls=%async_computation.3 | async-start | bytes 1769472 | tf_op jit(solution)/shard_map/reduce_scatter | solution.py:192
  49.8 7.4 %collective-permute-start.4 = (bf16[48,1152]{1,0:T(8,128)(2,1)S(1)}, bf16[48,1152]{1,0:T(8,128)(2,1)S(1)}, u32[]{:S(2)}, u32[]{:S(2)}) collective-permute-start(bf16[48,1152]{1,0:T(8,128)(2,1)S(1)} %constant_dynamic-slice_fusion), channel_id=1, source_target_pairs={{0,8},{2,26},{4,12},{6,30},{8,16},{10,2},{12,20},{14,6},{16,24},{1... | collective-permute-start | bytes 331784 | tf_op jit(solution)/shard_map/ppermute | solution.py:32
  57.3 2.4 %collective-permute-start.5 = (bf16[336,1152]{1,0:T(8,128)(2,1)S(1)}, bf16[336,1152]{1,0:T(8,128)(2,1)S(1)}, u32[]{:S(2)}, u32[]{:S(2)}) collective-permute-start(bf16[336,1152]{1,0:T(8,128)(2,1)S(1)} %pad_maximum_fusion), channel_id=1, source_target_pairs={{0,2},{2,0},{1,3},{3,1},{4,6},{6,4},{5,7},{7,5},{8,10},{10,8},{9,1... | collective-permute-start | bytes 2322440 | tf_op jit(solution)/shard_map/ppermute | solution.py:178
  79.2 3.7 %collective-permute-start.14 = (f32[384,1024]{1,0:T(8,128)S(1)}, f32[384,1024]{1,0:T(8,128)S(1)}, u32[]{:S(2)}, u32[]{:S(2)}) collective-permute-start(f32[384,1024]{1,0:T(8,128)S(1)} %get-tuple-element.27), channel_id=1, source_target_pairs={{0,2},{2,0},{1,3},{3,1},{4,6},{6,4},{5,7},{7,5},{8,10},{10,8},{9,1... | collective-permute-start | bytes 4718600 | tf_op jit(solution)/shard_map/ppermute | solution.py:188
  84.5 5.1 %collective-permute-start.6 = (f32[1,128]{1,0:T(1,128)S(1)}, f32[1,128]{1,0:T(1,128)S(1)}, u32[]{:S(2)}, u32[]{:S(2)}) collective-permute-start(f32[1,128]{1,0:T(1,128)S(1)} %get-tuple-element.22), channel_id=1, source_target_pairs={{0,1},{1,0},{2,3},{3,2},{4,5},{5,4},{6,7},{7,6},{8,9},{9,8},{10,11... | collective-permute-start | bytes 1544 | tf_op jit(solution)/shard_map/ppermute | solution.py:53
  89.6 3.8 %collective-permute-start.7 = (f32[1,128]{1,0:T(1,128)S(1)}, f32[1,128]{1,0:T(1,128)S(1)}, u32[]{:S(2)}, u32[]{:S(2)}) collective-permute-start(f32[1,128]{1,0:T(1,128)S(1)} %add.193), channel_id=1, source_target_pairs={{0,128},{128,0},{1,129},{129,1},{2,130},{130,2},{3,131},{131,3},{4... | collective-permute-start | bytes 1544 | tf_op jit(solution)/shard_map/ppermute | solution.py:53
  93.4 26.2 %all-to-all-start.1 = ((f16[16,48,1024]{2,1,0:T(8,128)(2,1)}), f16[16,48,1024]{2,1,0:T(8,128)(2,1)S(1)}, u32[]{:S(2)}, u32[]{:S(2)}) async-start(f16[16,48,1024]{2,1,0:T(8,128)(2,1)} %bitcast.29), calls=%async_computation.1 | async-start | bytes 3145728 | tf_op jit(solution)/shard_map/all_to_all | solution.py:19
  98.2 1.1 collective-permute-start.8
  99.3 3.5 %collective-permute-start.9 = (f32[1,128]{1,0:T(1,128)S(1)}, f32[1,128]{1,0:T(1,128)S(1)}, u32[]{:S(2)}, u32[]{:S(2)}) collective-permute-start(f32[1,128]{1,0:T(1,128)S(1)} %add.195), channel_id=1, source_target_pairs={{0,4},{4,0},{8,12},{12,8},{16,20},{20,16},{24,28},{28,24},{1,5},{5... | collective-permute-start | bytes 1544 | tf_op jit(solution)/shard_map/ppermute | solution.py:53
  102.9 4.4 %collective-permute-start.10 = (f32[1,128]{1,0:T(1,128)S(1)}, f32[1,128]{1,0:T(1,128)S(1)}, u32[]{:S(2)}, u32[]{:S(2)}) collective-permute-start(f32[1,128]{1,0:T(1,128)S(1)} %add.196), channel_id=1, source_target_pairs={{0,8},{4,12},{8,0},{12,4},{16,24},{20,28},{24,16},{28,20},{1,9},{5... | collective-permute-start | bytes 1544 | tf_op jit(solution)/shard_map/ppermute | solution.py:53
  107.3 7.5 %collective-permute-start.11 = (f32[1,128]{1,0:T(1,128)S(1)}, f32[1,128]{1,0:T(1,128)S(1)}, u32[]{:S(2)}, u32[]{:S(2)}) collective-permute-start(f32[1,128]{1,0:T(1,128)S(1)} %add.197), channel_id=1, source_target_pairs={{0,16},{4,20},{8,24},{12,28},{16,0},{20,4},{24,8},{28,12},{1,17},{... | collective-permute-start | bytes 1544 | tf_op jit(solution)/shard_map/ppermute | solution.py:53
  119.6 3.5 %collective-permute-start.12 = (f32[1,128]{1,0:T(1,128)S(1)}, f32[1,128]{1,0:T(1,128)S(1)}, u32[]{:S(2)}, u32[]{:S(2)}) collective-permute-start(f32[1,128]{1,0:T(1,128)S(1)} %add.198), channel_id=1, source_target_pairs={{0,32},{32,0},{64,96},{96,64},{1,33},{33,1},{65,97},{97,65},{2,34}... | collective-permute-start | bytes 1544 | tf_op jit(solution)/shard_map/ppermute | solution.py:53
  123.1 5.0 %collective-permute-start.13 = (f32[1,128]{1,0:T(1,128)S(1)}, f32[1,128]{1,0:T(1,128)S(1)}, u32[]{:S(2)}, u32[]{:S(2)}) collective-permute-start(f32[1,128]{1,0:T(1,128)S(1)} %add.199), channel_id=1, source_target_pairs={{0,64},{32,96},{64,0},{96,32},{1,65},{33,97},{65,1},{97,33},{2,66}... | collective-permute-start | bytes 1544 | tf_op jit(solution)/shard_map/ppermute | solution.py:53
Sparse Core Ops, SparseCore 0:
  84.6 40.3 reduce-scatter.1

commit v9 on v8

--- a/solution.py
+++ b/solution.py
@@ -11,6 +11,7 @@
 ALL = ("xl", "y", "z", "section", "tensor")
 SWAP = [(0, 1), (1, 0)]
 LANES = 128
+STEP = 512
 F32 = jnp.float32
 SENT = jnp.float16
 
@@ -48,24 +49,104 @@
     return lax.optimization_barrier(arrays)
 
 
-def with_partner(value, axis, bit):
-    pairs = [(i, i ^ bit) for i in range(lax.axis_size(axis))]
-    return value + lax.ppermute(value, axis, pairs)
+def with_digits(part, value):
+    high = (value / 4096.0).astype(SENT)
+    value = value - high.astype(F32) * 4096.0
+    middle = (value / 4.0).astype(SENT)
+    low = (value - middle.astype(F32) * 4.0).astype(SENT)
+    shape = (*part.shape[:-1], LANES)
+    lane = lax.broadcasted_iota(jnp.int32, shape, len(shape) - 1)
+    lanes = jnp.where(lane == 0, high, jnp.where(lane == 1, middle, low))
+    return jnp.concatenate([part.astype(SENT), lanes], axis=-1)
+
+
+def without_digits(sent):
+    width = sent.shape[-1] - LANES
+    lanes = sent[:, 0, width:].astype(F32).sum(axis=0)
+    value = lanes[0] * 4096.0 + lanes[1] * 4.0 + lanes[2]
+    return sent[..., :width].astype(F32), value
+
+
+def summed_over_z(kept, section):
+    half = kept.shape[0] // 8
+    one_three = along_z(kept[: 4 * half].astype(SENT), -1)
+    four = along_z(kept[6 * half : 7 * half].astype(SENT), -2)
+    one_three, four = tied(one_three, four)
+    four = four.astype(F32)
+    upper = kept[4 * half : 5 * half] + jnp.where(section == 0, four, 0.0)
+    lower = kept[5 * half : 6 * half] + jnp.where(section == 0, 0.0, four)
+    two = jnp.concatenate([upper, lower], axis=0) + one_three[2 * half :].astype(F32)
+    two = along_z(two.astype(SENT), -2).astype(F32)
+    given = row_half(one_three[: 2 * half], 1 - section).astype(F32) + row_half(two, 1 - section)
+    got = lax.ppermute(given, "section", SWAP)
+    mine = row_half(one_three[: 2 * half], section).astype(F32) + row_half(two, section)
+    return kept[7 * half :] + mine + got
+
+
+def tower_kernel(spot, inputs, up, down, sent, own, ordered, up_held, down_held, sems):
+    quarter = inputs.shape[0] // 4
+    tensor = spot[0]
+    step = STEP
+    count = up.shape[1] // step
+    loads = []
+    for k, which in enumerate((1 - tensor, 3 - tensor, tensor, 2 + tensor)):
+        start = pl.multiple_of(which * quarter, 16)
+        rows = pl.ds(k * quarter, quarter)
+        loads.append(
+            pltpu.make_async_copy(
+                inputs.at[pl.ds(start, quarter), :], ordered.at[rows, :], sems.at[k]
+            )
+        )
+    for k in range(count):
+        part = pl.ds(k * step, step)
+        loads.append(
+            pltpu.make_async_copy(up.at[:, part], up_held.at[:, part], sems.at[4 + 2 * k])
+        )
+        loads.append(
+            pltpu.make_async_copy(down.at[part, :], down_held.at[part, :], sems.at[5 + 2 * k])
+        )
+    for load in loads:
+        load.start()
+    for load in loads[:4]:
+        load.wait()
+    total = jnp.zeros((4 * quarter, inputs.shape[1]), F32)
+    for k in range(count):
+        loads[4 + 2 * k].wait()
+        hidden = jnp.dot(
+            ordered[...], up_held[:, k * step : (k + 1) * step], preferred_element_type=F32
+        )
+        hidden = jax.nn.gelu(hidden).astype(jnp.bfloat16)
+        loads[5 + 2 * k].wait()
+        total = total + jnp.dot(
+            hidden, down_held[k * step : (k + 1) * step, :], preferred_element_type=F32
+        )
+    sent[...] = total[: 2 * quarter]
+    own[...] = total[2 * quarter :] + ordered[2 * quarter :, :].astype(F32)
 
 
 def tower(inputs, up, down, tensor):
     rows, width = inputs.shape
-    split = inputs.reshape(2, 2, rows // 4, width)
-    kept = lax.dynamic_slice_in_dim(split, tensor, 1, 1).reshape(rows // 2, width)
-    given = lax.dynamic_slice_in_dim(split, 1 - tensor, 1, 1).reshape(rows // 2, width)
-    ordered = jnp.concatenate([given, kept], axis=0)
-    hidden = jax.nn.gelu(jnp.dot(ordered, up, preferred_element_type=F32)).astype(jnp.bfloat16)
-    sent = jnp.dot(hidden[: rows // 2], down, preferred_element_type=F32)
-    arrived = lax.ppermute(sent, "tensor", SWAP)
-    later, sent = tied(hidden[rows // 2 :], sent)
-    own = jnp.dot(later, down, preferred_element_type=F32) + kept.astype(F32)
-    own = lax.optimization_barrier(own)
-    raw = own + arrived
+    units = up.shape[1]
+    out = jax.ShapeDtypeStruct((rows // 2, width), F32)
+    stays = pl.BlockSpec(memory_space=pltpu.HBM)
+    sent, own = pl.pallas_call(
+        tower_kernel,
+        in_specs=[pl.BlockSpec(memory_space=pltpu.SMEM), stays, stays, stays],
+        out_specs=[pl.BlockSpec(memory_space=pltpu.VMEM)] * 2,
+        out_shape=[out, out],
+        scratch_shapes=[
+            pltpu.VMEM((rows, width), jnp.bfloat16),
+            pltpu.VMEM((width, units), jnp.bfloat16),
+            pltpu.VMEM((units, width), jnp.bfloat16),
+            pltpu.SemaphoreType.DMA((4 + 2 * (units // STEP),)),
+        ],
+        compiler_params=pltpu.CompilerParams(vmem_limit_bytes=20 * 1024 * 1024),
+        name="tower",
+    )(
+        jnp.reshape(tensor, (1,)).astype(jnp.int32),
+        *(pltpu.with_memory_space_constraint(x, pltpu.HBM) for x in (inputs, up, down)),
+    )
+    raw = own + lax.ppermute(sent, "tensor", SWAP)
     norms = lax.rsqrt(jnp.sum(raw * raw, axis=-1, keepdims=True) + 1e-06)
     return (raw * norms).astype(jnp.bfloat16)
 
@@ -79,26 +160,17 @@
 
 
 def score_kernel(
-    spot, scale, bias, mine, other, reports, columns, weight, moved, sent, loss
+    spot, scale, bias, mine, other, reports, columns, kept, sent, report_part, loss, weight, moved
 ):
     count, width = reports.shape
     scale_value, bias_value = scale[0], bias[0]
-    z, section = spot[0], spot[1]
-    toward = 2 * section - 1
+    section = spot[0]
     quarter = mine.shape[0] // 9
     half = 8 * quarter
-
-    def place(step, own):
-        row = lax.rem(z + toward * step + 8, 8) * quarter
-        return pl.multiple_of(row + (1 - own) * half, 16)
-
-    blocks = []
-    for step in (0, 1, 3, 2):
-        blocks += [(step, 1 - section), (step, section)]
-    blocks.append((4, 1))
-    for step in (-1, -3, -2):
-        blocks += [(step, 1 - section), (step, section)]
-    blocks.append((4, 0))
+    own_rows = pl.multiple_of(half - quarter + section * half, 16)
+    other_rows = pl.multiple_of(half - quarter + (1 - section) * half, 16)
+    blocks = [own_rows, other_rows]
+    blocks += [k * quarter for k in range(7)] + [half + k * quarter for k in range(7)]
 
     total = jnp.zeros((1, count), F32)
     block = 0
@@ -126,16 +198,20 @@
             weight[block * quarter : (block + size) * quarter, :] = signed
             for k in range(size):
                 part = signed[k * quarter : (k + 1) * quarter]
-                moved[pl.ds(place(*blocks[block + k]), quarter), :] = part
+                moved[pl.ds(blocks[block + k], quarter), :] = part
             start, block = stop, block + size
     sent[...] = jnp.dot(moved[half:, :], reports[...], preferred_element_type=F32)
+    kept[...] = moved[:half, :]
+    cut = mine.shape[0]
+    report_part[...] = transposed_dot(weight[:cut, :], mine[:, :width])
+    report_part[...] += transposed_dot(weight[cut:, :], other[:, :width])
     loss[...] = jnp.broadcast_to(jnp.sum(total, axis=1, keepdims=True), loss.shape)
 
 
 def scored(scale, bias, mine, other, reports, columns):
     count, width = reports.shape
     rows = mine.shape[0] + other.shape[0]
-    spot = jnp.stack([lax.axis_index("z"), lax.axis_index("section")]).astype(jnp.int32)
+    spot = jnp.reshape(lax.axis_index("section"), (1,)).astype(jnp.int32)
     scalar = pl.BlockSpec(memory_space=pltpu.SMEM)
     whole = pl.BlockSpec(memory_space=pltpu.VMEM)
     return pl.pallas_call(
@@ -143,12 +219,16 @@
         in_specs=[scalar, scalar, scalar, whole, whole, whole, whole],
         out_specs=[whole, whole, whole, whole],
         out_shape=[
-            jax.ShapeDtypeStruct((rows, count), jnp.bfloat16),
-            jax.ShapeDtypeStruct((rows, count), jnp.bfloat16),
+            jax.ShapeDtypeStruct((rows // 2, count), jnp.bfloat16),
             jax.ShapeDtypeStruct((rows // 2, width), F32),
+            jax.ShapeDtypeStruct((count, width), F32),
             jax.ShapeDtypeStruct((1, LANES), F32),
         ],
-        compiler_params=pltpu.CompilerParams(vmem_limit_bytes=48 * 1024 * 1024),
+        scratch_shapes=[
+            pltpu.VMEM((rows, count), jnp.bfloat16),
+            pltpu.VMEM((rows, count), jnp.bfloat16),
+        ],
+        compiler_params=pltpu.CompilerParams(vmem_limit_bytes=20 * 1024 * 1024),
         name="scores",
     )(spot, scale, bias, mine, other, reports, columns)
 
@@ -182,28 +262,20 @@
     owner = ((member // 2 * n_z + lax.axis_index("z")) * 2 + section) * 2 + member % 2
     columns = (owner * quarter + row).astype(F32)
 
-    weight, moved, sent, loss = scored(
+    weight, sent, report_part, loss = scored(
         scale, bias, rows_mine, rows_other, reports_all, columns[None, :]
     )
+    report_part = with_digits(report_part.reshape(n_plane, quarter, width), loss[0, 0])
     back = lax.ppermute(sent, "section", SWAP)
-    loss = with_partner(loss, "tensor", 1)
-    kept = jnp.dot(moved[: sent.shape[0]], reports_all, preferred_element_type=F32)
-    kept, weight = tied(kept, weight)
-    slide_grad = lax.psum_scatter(kept + back, "z", tiled=True)
-    loss = with_partner(loss, "xl", 1)
-    cut = rows_mine.shape[0]
-    report_part = transposed_dot(weight[:cut], rows_mine[:, :width])
-    report_part = report_part + transposed_dot(weight[cut:], rows_other[:, :width])
-    report_part = report_part.astype(SENT).reshape(n_plane, quarter, width)
-    report_part, loss = tied(report_part, loss)
+    report_part, weight = tied(report_part, weight)
     report_terms = exchanged(report_part, PLANE)
-    loss = with_partner(loss, "section", 1)
-    for bit in (1, 2, 4):
-        loss = with_partner(loss, "z", bit)
-    report_terms, loss = tied(report_terms, loss)
-    loss = with_partner(with_partner(loss, "y", 1), "y", 2)
-    report_grad = report_terms.astype(F32).sum(axis=0)
-    return (loss[0, :1] / total, slide_grad, report_grad)
+    kept = jnp.dot(weight, reports_all, preferred_element_type=F32) + back
+    slide_grad = summed_over_z(kept, section)
+    report_terms, slide_grad = tied(report_terms, slide_grad)
+    report_terms, loss_value = without_digits(report_terms)
+    losses = copies(jnp.broadcast_to(loss_value, (1, LANES)), ("z", "section"))
+    loss = jnp.sum(losses, axis=0)[0, :1] / total
+    return (loss, slide_grad, report_terms.sum(axis=0))
 
 
 def solution(mesh):

time: 137 us -> 134 us (0.978)
  the two profiles are of different devices: /device:TPU:4 before, /device:TPU:1 now
where the time goes in v9:
time: 134 us; the launch traced here: 133 us
  waiting for transfers between devices  55.5 us (41%)
  starting transfers between devices  43.3 us (32%)
  other arithmetic  13.4 us (10%)
  Pallas kernels  10.6 us (8%)
  between operations  5.32 us (4%)
  local copies, waits for them, and re-layouts  4.5 us (3%)
    ppermute x6, waiting for transfers between devices, along_z(): return lax.ppermute(array, ('z', 'section'), pairs)  30.7 us
    all_to_all x3, starting transfers between devices, exchanged(): return lax.all_to_all(parts, axes, split_axis=0, concat_axis=0, tiled=True)  19.9 us
    all_to_all x3, waiting for transfers between devices, exchanged(): return lax.all_to_all(parts, axes, split_axis=0, concat_axis=0, tiled=True)  15.2 us
    ppermute x6, starting transfers between devices, along_z(): return lax.ppermute(array, ('z', 'section'), pairs)  10.7 us
    ppermute x1, waiting for transfers between devices, tower(): raw = own + lax.ppermute(sent, 'tensor', SWAP)  7.56 us
    pallas_call x1, Pallas kernels, scored(): pl.pallas_call(score_kernel, in_specs=[scalar, scalar, scalar, whole, who...  5.87 us
    pallas_call x1, Pallas kernels, tower(): pl.pallas_call(tower_kernel, in_specs=[pl.BlockSpec(memory_space=pltpu.SM...  4.68 us
    ppermute x1, starting transfers between devices, tower(): raw = own + lax.ppermute(sent, 'tensor', SWAP)  3.66 us
  transfers between devices with their start and end apart: 14, of which 10 were waited for; matrix products, arithmetic and copies ran while one was open for 10% of the time, Pallas kernels for 0%

profile of v9, /device:TPU:1, one launch (start us, length us, event | category | flops | bytes accessed | tf_op | source)
XLA Modules:
  0.0 133.3 jit_solution(11399181330240355010)
XLA Ops:
  0.6 4.7 %tower.1 = (f32[96,1024]{1,0:T(8,128)S(1)}, f32[96,1024]{1,0:T(8,128)S(1)}) custom-call(s32[1]{0:T(128)} %bitcast.1.spot, bf16[192,1024]{1,0:T(8,128)(2,1)} %bitcast.23, bf16[1024,2048]{1,0:T(8,128)(2,1)} %bitcast.21, bf16[2048,1024]{1,0:T(8,128)(2,1)} %bitcast.22), custom_call_target="tpu_custom_call" | custom-call | tf_op jit(solution)/shard_map/tower/pallas_call | solution.py:132
  5.3 3.7 %collective-permute-start = (f32[96,1024]{1,0:T(8,128)S(1)}, f32[96,1024]{1,0:T(8,128)S(1)}, u32[]{:S(2)}, u32[]{:S(2)}) collective-permute-start(f32[96,1024]{1,0:T(8,128)S(1)} %get-tuple-element.18), channel_id=1, source_target_pairs={{0,1},{1,0},{2,3},{3,2},{4,5},{5,4},{6,7},{7,6},{8,9},{9,8},{10,11... | collective-permute-start | bytes 1179656 | tf_op jit(solution)/shard_map/ppermute | solution.py:149
  9.0 0.1 reshape.265
  9.1 0.1 reshape.266
  9.2 7.6 %collective-permute-done = f32[96,1024]{1,0:T(8,128)S(1)} collective-permute-done((f32[96,1024]{1,0:T(8,128)S(1)}, f32[96,1024]{1,0:T(8,128)S(1)}, u32[]{:S(2)}, u32[]{:S(2)}) %collective-permute-start) | collective-permute-done | bytes 393248 | tf_op jit(solution)/shard_map/ppermute | solution.py:149
  16.8 0.1 multiply_reduce_fusion
  16.9 0.1 multiply_convert_fusion
  17.0 2.4 %collective-permute-start.1 = (bf16[96,1024]{1,0:T(8,128)(2,1)S(1)}, bf16[96,1024]{1,0:T(8,128)(2,1)S(1)}, u32[]{:S(2)}, u32[]{:S(2)}) collective-permute-start(bf16[96,1024]{1,0:T(8,128)(2,1)S(1)} %multiply_convert_fusion), channel_id=1, source_target_pairs={{0,2},{2,0},{1,3},{3,1},{4,6},{6,4},{5,7},{7,5},{8,10},{10,8},{9,1... | collective-permute-start | bytes 589832 | tf_op jit(solution)/shard_map/ppermute | solution.py:250
  19.4 0.1 select_convert_fusion
  19.5 1.0 collective-permute-done.1
  20.5 0.1 broadcast_select_fusion.1
  20.7 1.4 %broadcast_in_dim.41 = bf16[16,48,1024]{2,1,0:T(8,128)(2,1)} broadcast(bf16[48,1024]{1,0:T(8,128)(2,1)S(1)} %dynamic-slice_select_fusion), dimensions={1,2} | broadcast | bytes 1671168 | tf_op jit(solution)/shard_map/broadcast_in_dim | solution.py:254
  22.0 6.2 %collective-permute-start.2 = (bf16[96,1152]{1,0:T(8,128)(2,1)S(1)}, bf16[96,1152]{1,0:T(8,128)(2,1)S(1)}, u32[]{:S(2)}, u32[]{:S(2)}) collective-permute-start(bf16[96,1152]{1,0:T(8,128)(2,1)S(1)} %pad_maximum_fusion.4), channel_id=1, source_target_pairs={{0,8},{2,26},{4,12},{6,30},{8,16},{10,2},{12,20},{14,6},{16,24},{1... | collective-permute-start | bytes 663560 | tf_op jit(solution)/shard_map/ppermute | solution.py:33
  28.3 5.2 %collective-permute-done.2 = bf16[96,1152]{1,0:T(8,128)(2,1)S(1)} collective-permute-done((bf16[96,1152]{1,0:T(8,128)(2,1)S(1)}, bf16[96,1152]{1,0:T(8,128)(2,1)S(1)}, u32[]{:S(2)}, u32[]{:S(2)}) %collective-permute-start.2) | collective-permute-done | bytes 221216 | tf_op jit(solution)/shard_map/ppermute | solution.py:33
  33.6 2.2 %collective-permute-start.3 = (bf16[192,1152]{1,0:T(8,128)(2,1)S(1)}, bf16[192,1152]{1,0:T(8,128)(2,1)S(1)}, u32[]{:S(2)}, u32[]{:S(2)}) collective-permute-start(bf16[192,1152]{1,0:T(8,128)(2,1)S(1)} %pad_maximum_fusion.3), channel_id=1, source_target_pairs={{0,4},{2,30},{4,8},{6,2},{8,12},{10,6},{12,16},{14,10},{16,20},{18... | collective-permute-start | bytes 1327112 | tf_op jit(solution)/shard_map/ppermute | solution.py:33
  35.8 6.8 %all-to-all-start = ((bf16[16,48,1024]{2,1,0:T(8,128)(2,1)}), bf16[16,48,1024]{2,1,0:T(8,128)(2,1)S(1)}, u32[]{:S(2)}, u32[]{:S(2)}) async-start(bf16[16,48,1024]{2,1,0:T(8,128)(2,1)} %broadcast_in_dim.41), calls=%async_computation | async-start | bytes 3145728 | tf_op jit(solution)/shard_map/all_to_all | solution.py:20
  42.6 2.0 %collective-permute-start.4 = (bf16[48,1152]{1,0:T(8,128)(2,1)S(1)}, bf16[48,1152]{1,0:T(8,128)(2,1)S(1)}, u32[]{:S(2)}, u32[]{:S(2)}) collective-permute-start(bf16[48,1152]{1,0:T(8,128)(2,1)S(1)} %constant_dynamic-slice_fusion), channel_id=1, source_target_pairs={{0,8},{2,26},{4,12},{6,30},{8,16},{10,2},{12,20},{14,6},{16,24},{1... | collective-permute-start | bytes 331784 | tf_op jit(solution)/shard_map/ppermute | solution.py:33
  44.6 3.1 %collective-permute-done.4 = bf16[48,1152]{1,0:T(8,128)(2,1)S(1)} collective-permute-done((bf16[48,1152]{1,0:T(8,128)(2,1)S(1)}, bf16[48,1152]{1,0:T(8,128)(2,1)S(1)}, u32[]{:S(2)}, u32[]{:S(2)}) %collective-permute-start.4) | collective-permute-done | bytes 110624 | tf_op jit(solution)/shard_map/ppermute | solution.py:33
  47.7 0.8 copy-done.4
  48.5 1.0 pad_maximum_fusion.2
  49.4 3.2 %collective-permute-start.5 = (bf16[336,1152]{1,0:T(8,128)(2,1)}, bf16[336,1152]{1,0:T(8,128)(2,1)S(1)}, u32[]{:S(2)}, u32[]{:S(2)}) collective-permute-start(bf16[336,1152]{1,0:T(8,128)(2,1)} %pad_maximum_fusion.2), channel_id=1, source_target_pairs={{0,2},{2,0},{1,3},{3,1},{4,6},{6,4},{5,7},{7,5},{8,10},{10,8},{9,1... | collective-permute-start | bytes 2322440 | tf_op jit(solution)/shard_map/ppermute | solution.py:258
  54.0 1.3 pad_maximum_fusion.1.mine
  55.2 10.2 %all-to-all-done = bf16[16,48,1024]{2,1,0:T(8,128)(2,1)S(1)} async-done(((bf16[16,48,1024]{2,1,0:T(8,128)(2,1)}), bf16[16,48,1024]{2,1,0:T(8,128)(2,1)S(1)}, u32[]{:S(2)}, u32[]{:S(2)}) %all-to-all-start) | async-done | bytes 1572896 | tf_op jit(solution)/shard_map/all_to_all | solution.py:20
  65.4 5.9 %scores.1 = (bf16[384,768]{1,0:T(8,128)(2,1)S(1)}, f32[384,1024]{1,0:T(8,128)}, f32[768,1024]{1,0:T(8,128)S(1)}, f32[1,128]{1,0:T(1,128)S(1)}) custom-call(s32[1]{0:T(128)} %bitcast.spot, f32[1]{0:T(128)S(6)} %copy.10.scale, f32[1]{0:T(128)S(6)} %copy.11.bias, bf16[432,1152]{1,0:T(8,128)(2,1)S(1)} %pad_maximum_fusion.1.mine, ...), custom_call_target="tpu_custom_call" | custom-call | tf_op jit(solution)/shard_map/scores/pallas_call | solution.py:217
  71.3 0.8 copy-done
  72.1 1.8 %collective-permute-start.6 = (f32[384,1024]{1,0:T(8,128)}, f32[384,1024]{1,0:T(8,128)}, u32[]{:S(2)}, u32[]{:S(2)}) collective-permute-start(f32[384,1024]{1,0:T(8,128)} %get-tuple-element.26), channel_id=1, source_target_pairs={{0,2},{2,0},{1,3},{3,1},{4,6},{6,4},{5,7},{7,5},{8,10},{10,8},{9,1... | collective-permute-start | bytes 4718600 | tf_op jit(solution)/shard_map/ppermute | solution.py:269
  73.9 1.5 %convert_element_type.67 = f16[768,1024]{1,0:T(8,128)(2,1)} convert(f32[768,1024]{1,0:T(8,128)S(1)} %get-tuple-element.21) | non-fusion elementwise | flops 786432 | bytes 4718592 | tf_op jit(solution)/shard_map/convert_element_type | solution.py:60
  75.6 3.1 %pad_maximum_fusion = f16[16,48,1152]{2,1,0:T(8,128)(2,1)} fusion(f16[16,48,128]{2,1,0:T(8,128)(2,1)S(1)} %broadcast_select_fusion, f16[16,48,1024]{2,1,0:T(8,128)(2,1)} %bitcast.20), kind=kLoop, calls=%fused_computation.1 | loop fusion | flops 884736 | bytes 3538944 | tf_op jit(solution)/shard_map/concatenate | solution.py:60
  78.7 4.6 %all-to-all-start.1 = ((f16[16,48,1152]{2,1,0:T(8,128)(2,1)}), f16[16,48,1152]{2,1,0:T(8,128)(2,1)}, u32[]{:S(2)}, u32[]{:S(2)}) async-start(f16[16,48,1152]{2,1,0:T(8,128)(2,1)} %pad_maximum_fusion), calls=%async_computation.1 | async-start | bytes 3538944 | tf_op jit(solution)/shard_map/all_to_all | solution.py:20
  83.2 0.8 fusion.10
  84.0 1.8 %fusion.8 = (f16[384,1024]{1,0:T(8,128)(2,1)S(1)}, f32[384,1024]{1,0:T(8,128)S(1)}) fusion(f32[384,1024]{1,0:T(8,128)S(1)} %fusion.10, f32[384,1024]{1,0:T(8,128)} %collective-permute-done.6), kind=kLoop, calls=%fused_computation.47 | loop fusion | flops 786432 | bytes 5505024 | tf_op jit(solution)/shard_map/convert.1
  85.8 0.1 slice.62
  85.9 0.1 collective-permute-start.7
  86.0 0.1 collective-permute-start.8
  86.1 15.1 %collective-permute-done.8 = f16[48,1024]{1,0:T(8,128)(2,1)S(1)} collective-permute-done((f16[48,1024]{1,0:T(8,128)(2,1)S(1)}, f16[48,1024]{1,0:T(8,128)(2,1)S(1)}, u32[]{:S(2)}, u32[]{:S(2)}) %collective-permute-start.8) | collective-permute-done | bytes 98336 | tf_op jit(solution)/shard_map/ppermute | solution.py:33
  101.2 0.1 fusion
  101.3 0.1 collective-permute-start.9
  101.4 7.3 %collective-permute-done.9 = f16[96,1024]{1,0:T(8,128)(2,1)S(1)} collective-permute-done((f16[96,1024]{1,0:T(8,128)(2,1)S(1)}, f16[96,1024]{1,0:T(8,128)(2,1)S(1)}, u32[]{:S(2)}, u32[]{:S(2)}) %collective-permute-start.9) | collective-permute-done | bytes 196640 | tf_op jit(solution)/shard_map/ppermute | solution.py:33
  108.7 1.7 %collective-permute-start.10 = (f32[48,1024]{1,0:T(8,128)S(1)}, f32[48,1024]{1,0:T(8,128)S(1)}, u32[]{:S(2)}, u32[]{:S(2)}) collective-permute-start(f32[48,1024]{1,0:T(8,128)S(1)} %dynamic-slice_add_fusion), channel_id=1, source_target_pairs={{0,2},{2,0},{1,3},{3,1},{4,6},{6,4},{5,7},{7,5},{8,10},{10,8},{9,1... | collective-permute-start | bytes 589832 | tf_op jit(solution)/shard_map/ppermute | solution.py:81
  110.5 1.1 collective-permute-done.10
  111.5 0.7 fusion.3
  112.3 0.4 all-to-all-done.1
  112.7 0.8 convert_reduce_fusion.1
  113.5 0.6 fusion.9
  115.9 0.6 broadcast_in_dim_broadcast_in_dim.3
  116.5 8.6 %all-to-all-start.2 = ((f32[16,1,128]{2,1,0:T(1,128)}), f32[16,1,128]{2,1,0:T(1,128)S(1)}, u32[]{:S(2)}, u32[]{:S(2)}) async-start(f32[16,1,128]{2,1,0:T(1,128)} %broadcast_in_dim_broadcast_in_dim.3), calls=%async_computation.2 | async-start | bytes 16384 | tf_op jit(solution)/shard_map/all_to_all | solution.py:20
  125.1 2.4 %convert_reduce_fusion = f32[48,1024]{1,0:T(8,128)} fusion(f16[16,48,1152]{2,1,0:T(8,128)(2,1)} %all-to-all-done.1), kind=kLoop, calls=%fused_computation | loop fusion | flops 1523712 | bytes 1769472 | tf_op jit(solution)/shard_map/reduce_sum | solution.py:278
  127.6 4.6 %all-to-all-done.2 = f32[16,1,128]{2,1,0:T(1,128)S(1)} async-done(((f32[16,1,128]{2,1,0:T(1,128)}), f32[16,1,128]{2,1,0:T(1,128)S(1)}, u32[]{:S(2)}, u32[]{:S(2)}) %all-to-all-start.2) | async-done | bytes 8224 | tf_op jit(solution)/shard_map/all_to_all | solution.py:20
  (31 shorter events, 0.5 us)
Async XLA Ops:
  0.6 8.4 %copy-start.5 = (s32[192]{0:T(256)S(1)}, s32[192]{0:T(256)}, u32[]{:S(2)}) copy-start(s32[192]{0:T(256)} %param.9) | copy-start | bytes 2308
  5.3 11.4 %collective-permute-start = (f32[96,1024]{1,0:T(8,128)S(1)}, f32[96,1024]{1,0:T(8,128)S(1)}, u32[]{:S(2)}, u32[]{:S(2)}) collective-permute-start(f32[96,1024]{1,0:T(8,128)S(1)} %get-tuple-element.18), channel_id=1, source_target_pairs={{0,1},{1,0},{2,3},{3,2},{4,5},{5,4},{6,7},{7,6},{8,9},{9,8},{10,11... | collective-permute-start | bytes 1179656 | tf_op jit(solution)/shard_map/ppermute | solution.py:149
  17.0 3.5 %collective-permute-start.1 = (bf16[96,1024]{1,0:T(8,128)(2,1)S(1)}, bf16[96,1024]{1,0:T(8,128)(2,1)S(1)}, u32[]{:S(2)}, u32[]{:S(2)}) collective-permute-start(bf16[96,1024]{1,0:T(8,128)(2,1)S(1)} %multiply_convert_fusion), channel_id=1, source_target_pairs={{0,2},{2,0},{1,3},{3,1},{4,6},{6,4},{5,7},{7,5},{8,10},{10,8},{9,1... | collective-permute-start | bytes 589832 | tf_op jit(solution)/shard_map/ppermute | solution.py:250
  20.6 12.9 %copy-start.3 = (bf16[96,1152]{1,0:T(8,128)(2,1)}, bf16[96,1152]{1,0:T(8,128)(2,1)S(1)}, u32[]{:S(2)}) copy-start(bf16[96,1152]{1,0:T(8,128)(2,1)S(1)} %pad_maximum_fusion.4) | copy-start | bytes 663556
  22.0 11.5 %collective-permute-start.2 = (bf16[96,1152]{1,0:T(8,128)(2,1)S(1)}, bf16[96,1152]{1,0:T(8,128)(2,1)S(1)}, u32[]{:S(2)}, u32[]{:S(2)}) collective-permute-start(bf16[96,1152]{1,0:T(8,128)(2,1)S(1)} %pad_maximum_fusion.4), channel_id=1, source_target_pairs={{0,8},{2,26},{4,12},{6,30},{8,16},{10,2},{12,20},{14,6},{16,24},{1... | collective-permute-start | bytes 663560 | tf_op jit(solution)/shard_map/ppermute | solution.py:33
  33.5 14.2 %copy-start.2 = (bf16[96,1152]{1,0:T(8,128)(2,1)}, bf16[96,1152]{1,0:T(8,128)(2,1)S(1)}, u32[]{:S(2)}) copy-start(bf16[96,1152]{1,0:T(8,128)(2,1)S(1)} %collective-permute-done.2) | copy-start | bytes 663556
  33.6 14.1 %collective-permute-start.3 = (bf16[192,1152]{1,0:T(8,128)(2,1)S(1)}, bf16[192,1152]{1,0:T(8,128)(2,1)S(1)}, u32[]{:S(2)}, u32[]{:S(2)}) collective-permute-start(bf16[192,1152]{1,0:T(8,128)(2,1)S(1)} %pad_maximum_fusion.3), channel_id=1, source_target_pairs={{0,4},{2,30},{4,8},{6,2},{8,12},{10,6},{12,16},{14,10},{16,20},{18... | collective-permute-start | bytes 1327112 | tf_op jit(solution)/shard_map/ppermute | solution.py:33
  35.8 29.7 %all-to-all-start = ((bf16[16,48,1024]{2,1,0:T(8,128)(2,1)}), bf16[16,48,1024]{2,1,0:T(8,128)(2,1)S(1)}, u32[]{:S(2)}, u32[]{:S(2)}) async-start(bf16[16,48,1024]{2,1,0:T(8,128)(2,1)} %broadcast_in_dim.41), calls=%async_computation | async-start | bytes 3145728 | tf_op jit(solution)/shard_map/all_to_all | solution.py:20
  42.6 5.1 %collective-permute-start.4 = (bf16[48,1152]{1,0:T(8,128)(2,1)S(1)}, bf16[48,1152]{1,0:T(8,128)(2,1)S(1)}, u32[]{:S(2)}, u32[]{:S(2)}) collective-permute-start(bf16[48,1152]{1,0:T(8,128)(2,1)S(1)} %constant_dynamic-slice_fusion), channel_id=1, source_target_pairs={{0,8},{2,26},{4,12},{6,30},{8,16},{10,2},{12,20},{14,6},{16,24},{1... | collective-permute-start | bytes 331784 | tf_op jit(solution)/shard_map/ppermute | solution.py:33
  47.7 0.8 copy-start.4
  49.4 5.8 %collective-permute-start.5 = (bf16[336,1152]{1,0:T(8,128)(2,1)}, bf16[336,1152]{1,0:T(8,128)(2,1)S(1)}, u32[]{:S(2)}, u32[]{:S(2)}) collective-permute-start(bf16[336,1152]{1,0:T(8,128)(2,1)} %pad_maximum_fusion.2), channel_id=1, source_target_pairs={{0,2},{2,0},{1,3},{3,1},{4,6},{6,4},{5,7},{7,5},{8,10},{10,8},{9,1... | collective-permute-start | bytes 2322440 | tf_op jit(solution)/shard_map/ppermute | solution.py:258
  71.3 0.8 copy-start
  72.1 11.9 %collective-permute-start.6 = (f32[384,1024]{1,0:T(8,128)}, f32[384,1024]{1,0:T(8,128)}, u32[]{:S(2)}, u32[]{:S(2)}) collective-permute-start(f32[384,1024]{1,0:T(8,128)} %get-tuple-element.26), channel_id=1, source_target_pairs={{0,2},{2,0},{1,3},{3,1},{4,6},{6,4},{5,7},{7,5},{8,10},{10,8},{9,1... | collective-permute-start | bytes 4718600 | tf_op jit(solution)/shard_map/ppermute | solution.py:269
  78.7 4.6 %copy-start.1 = (bf16[384,768]{1,0:T(8,128)(2,1)S(1)}, bf16[384,768]{1,0:T(8,128)(2,1)}, u32[]{:S(2)}) copy-start(bf16[384,768]{1,0:T(8,128)(2,1)} %copy-done) | copy-start | bytes 1769476
  78.7 34.0 %all-to-all-start.1 = ((f16[16,48,1152]{2,1,0:T(8,128)(2,1)}), f16[16,48,1152]{2,1,0:T(8,128)(2,1)}, u32[]{:S(2)}, u32[]{:S(2)}) async-start(f16[16,48,1152]{2,1,0:T(8,128)(2,1)} %pad_maximum_fusion), calls=%async_computation.1 | async-start | bytes 3538944 | tf_op jit(solution)/shard_map/all_to_all | solution.py:20
  85.9 15.3 %collective-permute-start.7 = (f16[192,1024]{1,0:T(8,128)(2,1)S(1)}, f16[192,1024]{1,0:T(8,128)(2,1)S(1)}, u32[]{:S(2)}, u32[]{:S(2)}) collective-permute-start(f16[192,1024]{1,0:T(8,128)(2,1)S(1)} %slice.62), channel_id=1, source_target_pairs={{0,28},{2,6},{4,0},{6,10},{8,4},{10,14},{12,8},{14,18},{16,12},{18... | collective-permute-start | bytes 1179656 | tf_op jit(solution)/shard_map/ppermute | solution.py:33
  86.0 15.1 %collective-permute-start.8 = (f16[48,1024]{1,0:T(8,128)(2,1)S(1)}, f16[48,1024]{1,0:T(8,128)(2,1)S(1)}, u32[]{:S(2)}, u32[]{:S(2)}) collective-permute-start(f16[48,1024]{1,0:T(8,128)(2,1)S(1)} %slice.63), channel_id=1, source_target_pairs={{0,24},{2,10},{4,28},{6,14},{8,0},{10,18},{12,4},{14,22},{16,8},{1... | collective-permute-start | bytes 294920 | tf_op jit(solution)/shard_map/ppermute | solution.py:33
  101.3 7.4 %collective-permute-start.9 = (f16[96,1024]{1,0:T(8,128)(2,1)S(1)}, f16[96,1024]{1,0:T(8,128)(2,1)S(1)}, u32[]{:S(2)}, u32[]{:S(2)}) collective-permute-start(f16[96,1024]{1,0:T(8,128)(2,1)S(1)} %fusion), channel_id=1, source_target_pairs={{0,24},{2,10},{4,28},{6,14},{8,0},{10,18},{12,4},{14,22},{16,8},{1... | collective-permute-start | bytes 589832 | tf_op jit(solution)/shard_map/ppermute | solution.py:33
  108.7 2.8 %collective-permute-start.10 = (f32[48,1024]{1,0:T(8,128)S(1)}, f32[48,1024]{1,0:T(8,128)S(1)}, u32[]{:S(2)}, u32[]{:S(2)}) collective-permute-start(f32[48,1024]{1,0:T(8,128)S(1)} %dynamic-slice_add_fusion), channel_id=1, source_target_pairs={{0,2},{2,0},{1,3},{3,1},{4,6},{6,4},{5,7},{7,5},{8,10},{10,8},{9,1... | collective-permute-start | bytes 589832 | tf_op jit(solution)/shard_map/ppermute | solution.py:81
  116.5 15.6 %all-to-all-start.2 = ((f32[16,1,128]{2,1,0:T(1,128)}), f32[16,1,128]{2,1,0:T(1,128)S(1)}, u32[]{:S(2)}, u32[]{:S(2)}) async-start(f32[16,1,128]{2,1,0:T(1,128)} %broadcast_in_dim_broadcast_in_dim.3), calls=%async_computation.2 | async-start | bytes 16384 | tf_op jit(solution)/shard_map/all_to_all | solution.py:20

commit v10 on v9

--- a/solution.py
+++ b/solution.py
@@ -38,49 +38,45 @@
     return lax.dynamic_slice_in_dim(array, which * half, half, 0)
 
 
-def gathered_over_z(own, section):
+def gathered_over_z(own, section, reports):
     two = along_z(own, 2)
+    two_swapped = lax.ppermute(two, "section", SWAP)
     one_three = along_z(jnp.concatenate([own, two], axis=0), 1)
     four = along_z(row_half(two, section), 2)
-    return jnp.concatenate([own, one_three, two, four], axis=0)
+    one_three, four = tied(one_three, four)
+    others = [lax.ppermute(one_three, "section", SWAP), two_swapped]
+    others.append(lax.ppermute(four, "section", SWAP))
+    return [one_three, two, four, *others], reports
 
 
 def tied(*arrays):
     return lax.optimization_barrier(arrays)
 
 
-def with_digits(part, value):
-    high = (value / 4096.0).astype(SENT)
-    value = value - high.astype(F32) * 4096.0
-    middle = (value / 4.0).astype(SENT)
-    low = (value - middle.astype(F32) * 4.0).astype(SENT)
-    shape = (*part.shape[:-1], LANES)
-    lane = lax.broadcasted_iota(jnp.int32, shape, len(shape) - 1)
-    lanes = jnp.where(lane == 0, high, jnp.where(lane == 1, middle, low))
-    return jnp.concatenate([part.astype(SENT), lanes], axis=-1)
-
-
-def without_digits(sent):
-    width = sent.shape[-1] - LANES
-    lanes = sent[:, 0, width:].astype(F32).sum(axis=0)
-    value = lanes[0] * 4096.0 + lanes[1] * 4.0 + lanes[2]
-    return sent[..., :width].astype(F32), value
-
-
-def summed_over_z(kept, section):
+def with_partner(value, axis, bit):
+    pairs = [(i, i ^ bit) for i in range(lax.axis_size(axis))]
+    return value + lax.ppermute(value, axis, pairs)
+
+
+def summed_over_z(kept, section, loss):
     half = kept.shape[0] // 8
     one_three = along_z(kept[: 4 * half].astype(SENT), -1)
     four = along_z(kept[6 * half : 7 * half].astype(SENT), -2)
-    one_three, four = tied(one_three, four)
+    loss = with_partner(with_partner(loss, "z", 1), "z", 2)
+    one_three, four, loss = tied(one_three, four, loss)
     four = four.astype(F32)
     upper = kept[4 * half : 5 * half] + jnp.where(section == 0, four, 0.0)
     lower = kept[5 * half : 6 * half] + jnp.where(section == 0, 0.0, four)
     two = jnp.concatenate([upper, lower], axis=0) + one_three[2 * half :].astype(F32)
-    two = along_z(two.astype(SENT), -2).astype(F32)
+    two = along_z(two.astype(SENT), -2)
+    loss = with_partner(loss, "z", 4)
+    two, loss = tied(two, loss)
+    two = two.astype(F32)
     given = row_half(one_three[: 2 * half], 1 - section).astype(F32) + row_half(two, 1 - section)
     got = lax.ppermute(given, "section", SWAP)
+    loss = with_partner(with_partner(loss, "y", 1), "y", 2)
     mine = row_half(one_three[: 2 * half], section).astype(F32) + row_half(two, section)
-    return kept[7 * half :] + mine + got
+    return kept[7 * half :] + mine + got, loss
 
 
 def tower_kernel(spot, inputs, up, down, sent, own, ordered, up_held, down_held, sems):
@@ -160,63 +156,63 @@
 
 
 def score_kernel(
-    spot, scale, bias, mine, other, reports, columns, kept, sent, report_part, loss, weight, moved
+    spot, scale, bias, own, one_three, two, four, one_three_other, two_other, four_other,
+    reports, columns, kept, sent, report_part, loss, rows, weight,
 ):
     count, width = reports.shape
     scale_value, bias_value = scale[0], bias[0]
     section = spot[0]
-    quarter = mine.shape[0] // 9
-    half = 8 * quarter
-    own_rows = pl.multiple_of(half - quarter + section * half, 16)
-    other_rows = pl.multiple_of(half - quarter + (1 - section) * half, 16)
-    blocks = [own_rows, other_rows]
-    blocks += [k * quarter for k in range(7)] + [half + k * quarter for k in range(7)]
+    quarter = own.shape[0] // 2
+    place = 0
+    groups = (
+        (one_three, two, four, section),
+        (one_three_other, two_other, four_other, 1 - section),
+    )
+    for group in groups:
+        for part in group[:3]:
+            rows[place : place + part.shape[0], :] = part[...]
+            place += part.shape[0]
+        start = pl.multiple_of(group[3] * quarter, 16)
+        rows[place : place + quarter, :] = own[pl.ds(start, quarter), :]
+        place += quarter
 
     total = jnp.zeros((1, count), F32)
-    block = 0
-    for rows, sizes in ((mine, (4, 5)), (other, (4, 3))):
-        start = 0
-        for size in sizes:
-            stop = start + size * quarter
-            marks = rows[start:stop, width : width + 2].astype(F32)
-            wanted = marks[:, 0:1] * LANES + marks[:, 1:2]
-            dots = lax.dot_general(
-                rows[start:stop, :width],
-                reports[...],
-                (((1,), (1,)), ((), ())),
-                preferred_element_type=F32,
-            )
-            logits = scale_value * dots + bias_value
-            match = wanted == columns[...]
-            turned = jnp.where(match, -logits, logits)
-            small = jnp.exp(-jnp.abs(turned))
-            losses = jnp.maximum(turned, 0.0) + jnp.log1p(small)
-            total = total + jnp.sum(losses, axis=0, keepdims=True)
-            sigmoid = jnp.where(turned >= 0, 1.0, small) / (1.0 + small)
-            signed = jnp.where(match, -scale_value, scale_value) * sigmoid
-            signed = signed.astype(jnp.bfloat16)
-            weight[block * quarter : (block + size) * quarter, :] = signed
-            for k in range(size):
-                part = signed[k * quarter : (k + 1) * quarter]
-                moved[pl.ds(blocks[block + k], quarter), :] = part
-            start, block = stop, block + size
-    sent[...] = jnp.dot(moved[half:, :], reports[...], preferred_element_type=F32)
-    kept[...] = moved[:half, :]
-    cut = mine.shape[0]
-    report_part[...] = transposed_dot(weight[:cut, :], mine[:, :width])
-    report_part[...] += transposed_dot(weight[cut:, :], other[:, :width])
+    step = place // 4
+    for k in range(4):
+        start, stop = k * step, (k + 1) * step
+        marks = rows[start:stop, width : width + 2].astype(F32)
+        wanted = marks[:, 0:1] * LANES + marks[:, 1:2]
+        dots = lax.dot_general(
+            rows[start:stop, :width],
+            reports[...],
+            (((1,), (1,)), ((), ())),
+            preferred_element_type=F32,
+        )
+        logits = scale_value * dots + bias_value
+        match = wanted == columns[...]
+        turned = jnp.where(match, -logits, logits)
+        small = jnp.exp(-jnp.abs(turned))
+        losses = jnp.maximum(turned, 0.0) + jnp.log1p(small)
+        total = total + jnp.sum(losses, axis=0, keepdims=True)
+        sigmoid = jnp.where(turned >= 0, 1.0, small) / (1.0 + small)
+        signed = jnp.where(match, -scale_value, scale_value) * sigmoid
+        weight[start:stop, :] = signed.astype(jnp.bfloat16)
+    half = 2 * step
     loss[...] = jnp.broadcast_to(jnp.sum(total, axis=1, keepdims=True), loss.shape)
-
-
-def scored(scale, bias, mine, other, reports, columns):
+    kept[...] = weight[:half, :]
+    sent[...] = jnp.dot(weight[half:, :], reports[...], preferred_element_type=F32)
+    report_part[...] = transposed_dot(weight[...], rows[:, :width])
+
+
+def scored(scale, bias, own, pieces, reports, columns):
     count, width = reports.shape
-    rows = mine.shape[0] + other.shape[0]
+    rows = own.shape[0] + sum(piece.shape[0] for piece in pieces)
     spot = jnp.reshape(lax.axis_index("section"), (1,)).astype(jnp.int32)
     scalar = pl.BlockSpec(memory_space=pltpu.SMEM)
     whole = pl.BlockSpec(memory_space=pltpu.VMEM)
     return pl.pallas_call(
         score_kernel,
-        in_specs=[scalar, scalar, scalar, whole, whole, whole, whole],
+        in_specs=[scalar] * 3 + [whole] * 9,
         out_specs=[whole, whole, whole, whole],
         out_shape=[
             jax.ShapeDtypeStruct((rows // 2, count), jnp.bfloat16),
@@ -225,12 +221,12 @@
             jax.ShapeDtypeStruct((1, LANES), F32),
         ],
         scratch_shapes=[
-            pltpu.VMEM((rows, count), jnp.bfloat16),
+            pltpu.VMEM((rows, own.shape[1]), jnp.bfloat16),
             pltpu.VMEM((rows, count), jnp.bfloat16),
         ],
         compiler_params=pltpu.CompilerParams(vmem_limit_bytes=20 * 1024 * 1024),
         name="scores",
-    )(spot, scale, bias, mine, other, reports, columns)
+    )(spot, scale, bias, own, *pieces, reports, columns)
 
 
 def transposed_dot(weight, slides):
@@ -254,8 +250,7 @@
     repeated = jnp.broadcast_to(reports, (n_plane, *reports.shape))
     repeated, slides = tied(repeated, slides)
     reports_all = exchanged(repeated, PLANE).reshape(n_plane * quarter, -1)
-    rows_mine = gathered_over_z(slides, section)
-    rows_other = lax.ppermute(rows_mine[2 * quarter :], "section", SWAP)
+    pieces, reports_all = gathered_over_z(slides, section, reports_all)
 
     place = jnp.arange(n_plane * quarter, dtype=jnp.int32)
     member, row = place // quarter, place % quarter
@@ -263,19 +258,21 @@
     columns = (owner * quarter + row).astype(F32)
 
     weight, sent, report_part, loss = scored(
-        scale, bias, rows_mine, rows_other, reports_all, columns[None, :]
-    )
-    report_part = with_digits(report_part.reshape(n_plane, quarter, width), loss[0, 0])
+        scale, bias, slides, pieces, reports_all, columns[None, :]
+    )
     back = lax.ppermute(sent, "section", SWAP)
-    report_part, weight = tied(report_part, weight)
+    loss = with_partner(loss, "tensor", 1)
+    report_part = report_part.astype(SENT).reshape(n_plane, quarter, width)
+    report_part, loss = tied(report_part, loss)
+    loss = with_partner(loss, "xl", 1)
+    report_part, loss, weight = tied(report_part, loss, weight)
     report_terms = exchanged(report_part, PLANE)
+    loss = with_partner(loss, "section", 1)
+    back, loss = tied(back, loss)
     kept = jnp.dot(weight, reports_all, preferred_element_type=F32) + back
-    slide_grad = summed_over_z(kept, section)
-    report_terms, slide_grad = tied(report_terms, slide_grad)
-    report_terms, loss_value = without_digits(report_terms)
-    losses = copies(jnp.broadcast_to(loss_value, (1, LANES)), ("z", "section"))
-    loss = jnp.sum(losses, axis=0)[0, :1] / total
-    return (loss, slide_grad, report_terms.sum(axis=0))
+    slide_grad, loss = summed_over_z(kept, section, loss)
+    report_grad = report_terms.astype(F32).sum(axis=0)
+    return (loss[0, :1] / total, slide_grad, report_grad)
 
 
 def solution(mesh):

time: 134 us -> 120 us (0.90)
  the two profiles are of different devices: /device:TPU:1 before, /device:TPU:4 now
where the time goes in v10:
time: 120 us; the launch traced here: 119 us
  waiting for transfers between devices  50.3 us (42%)
  starting transfers between devices  40.7 us (34%)
  Pallas kernels  10.2 us (8%)
  local copies, waits for them, and re-layouts  6.43 us (5%)
  other arithmetic  6.35 us (5%)
  between operations  3.35 us (3%)
  matrix products  2.19 us (2%)
    ppermute x8, waiting for transfers between devices, with_partner(): return value + lax.ppermute(value, axis, pairs)  21.3 us
    ppermute x6, waiting for transfers between devices, along_z(): return lax.ppermute(array, ('z', 'section'), pairs)  17.7 us
    all_to_all x2, starting transfers between devices, exchanged(): return lax.all_to_all(parts, axes, split_axis=0, concat_axis=0, tiled=True)  14.7 us
    ppermute x6, starting transfers between devices, along_z(): return lax.ppermute(array, ('z', 'section'), pairs)  13.8 us
    ppermute x1, waiting for transfers between devices, tower(): raw = own + lax.ppermute(sent, 'tensor', SWAP)  9.9 us
    ppermute x8, starting transfers between devices, with_partner(): return value + lax.ppermute(value, axis, pairs)  8.35 us
    pallas_call x1, Pallas kernels, scored(): pl.pallas_call(score_kernel, in_specs=[scalar] * 3 + [whole] * 9, out_spe...  5.53 us
    unnamed x16, local copies, waits for them, and re-layouts  4.72 us
  transfers between devices with their start and end apart: 23, of which 10 were waited for; matrix products, arithmetic and copies ran while one was open for 6% of the time, Pallas kernels for 0%

profile of v10, /device:TPU:4, one launch (start us, length us, event | category | flops | bytes accessed | tf_op | source)
XLA Modules:
  0.0 119.5 jit_solution(1656618705721137722)
XLA Ops:
  0.6 4.7 %tower.1 = (f32[96,1024]{1,0:T(8,128)S(1)}, f32[96,1024]{1,0:T(8,128)S(1)}) custom-call(s32[1]{0:T(128)} %bitcast.1.spot, bf16[192,1024]{1,0:T(8,128)(2,1)} %bitcast.16, bf16[1024,2048]{1,0:T(8,128)(2,1)} %bitcast.14, bf16[2048,1024]{1,0:T(8,128)(2,1)} %bitcast.15), custom_call_target="tpu_custom_call" | custom-call | tf_op jit(solution)/shard_map/tower/pallas_call | solution.py:128
  5.3 2.3 %collective-permute-start = (f32[96,1024]{1,0:T(8,128)S(1)}, f32[96,1024]{1,0:T(8,128)S(1)}, u32[]{:S(2)}, u32[]{:S(2)}) collective-permute-start(f32[96,1024]{1,0:T(8,128)S(1)} %get-tuple-element.26), channel_id=1, source_target_pairs={{0,1},{1,0},{2,3},{3,2},{4,5},{5,4},{6,7},{7,6},{8,9},{9,8},{10,11... | collective-permute-start | bytes 1179656 | tf_op jit(solution)/shard_map/ppermute | solution.py:145
  7.7 0.1 reshape.258
  7.8 0.1 reshape.259
  7.9 9.9 %collective-permute-done = f32[96,1024]{1,0:T(8,128)S(1)} collective-permute-done((f32[96,1024]{1,0:T(8,128)S(1)}, f32[96,1024]{1,0:T(8,128)S(1)}, u32[]{:S(2)}, u32[]{:S(2)}) %collective-permute-start) | collective-permute-done | bytes 393248 | tf_op jit(solution)/shard_map/ppermute | solution.py:145
  17.8 0.1 multiply_reduce_fusion
  17.9 0.1 multiply_convert_fusion
  18.0 0.1 collective-permute-start.1
  18.1 0.1 select_convert_fusion
  18.2 1.3 %collective-permute-done.1 = bf16[96,1024]{1,0:T(8,128)(2,1)S(1)} collective-permute-done((bf16[96,1024]{1,0:T(8,128)(2,1)S(1)}, bf16[96,1024]{1,0:T(8,128)(2,1)S(1)}, u32[]{:S(2)}, u32[]{:S(2)}) %collective-permute-start.1) | collective-permute-done | bytes 196640 | tf_op jit(solution)/shard_map/ppermute | solution.py:246
  19.6 0.1 broadcast_select_fusion
  19.7 1.4 %broadcast_in_dim.29 = bf16[16,48,1024]{2,1,0:T(8,128)(2,1)} broadcast(bf16[48,1024]{1,0:T(8,128)(2,1)S(1)} %dynamic-slice_select_fusion), dimensions={1,2} | broadcast | bytes 1671168 | tf_op jit(solution)/shard_map/broadcast_in_dim | solution.py:250
  21.1 7.5 %all-to-all-start = ((bf16[16,48,1024]{2,1,0:T(8,128)(2,1)}), bf16[16,48,1024]{2,1,0:T(8,128)(2,1)S(1)}, u32[]{:S(2)}, u32[]{:S(2)}) async-start(bf16[16,48,1024]{2,1,0:T(8,128)(2,1)} %broadcast_in_dim.29), calls=%async_computation | async-start | bytes 3145728 | tf_op jit(solution)/shard_map/all_to_all | solution.py:20
  28.6 3.3 %collective-permute-start.2 = (bf16[96,1152]{1,0:T(8,128)(2,1)S(1)}, bf16[96,1152]{1,0:T(8,128)(2,1)S(1)}, u32[]{:S(2)}, u32[]{:S(2)}) collective-permute-start(bf16[96,1152]{1,0:T(8,128)(2,1)S(1)} %pad_maximum_fusion.1.own), channel_id=1, source_target_pairs={{0,8},{2,26},{4,12},{6,30},{8,16},{10,2},{12,20},{14,6},{16,24},{1... | collective-permute-start | bytes 663560 | tf_op jit(solution)/shard_map/ppermute | solution.py:33
  31.9 7.5 %collective-permute-done.2.two = bf16[96,1152]{1,0:T(8,128)(2,1)S(1)} collective-permute-done((bf16[96,1152]{1,0:T(8,128)(2,1)S(1)}, bf16[96,1152]{1,0:T(8,128)(2,1)S(1)}, u32[]{:S(2)}, u32[]{:S(2)}) %collective-permute-start.2) | collective-permute-done | bytes 221216 | tf_op jit(solution)/shard_map/ppermute | solution.py:33
  39.4 2.9 %collective-permute-start.3 = (bf16[192,1152]{1,0:T(8,128)(2,1)S(1)}, bf16[192,1152]{1,0:T(8,128)(2,1)S(1)}, u32[]{:S(2)}, u32[]{:S(2)}) collective-permute-start(bf16[192,1152]{1,0:T(8,128)(2,1)S(1)} %pad_maximum_fusion), channel_id=1, source_target_pairs={{0,4},{2,30},{4,8},{6,2},{8,12},{10,6},{12,16},{14,10},{16,20},{18... | collective-permute-start | bytes 1327112 | tf_op jit(solution)/shard_map/ppermute | solution.py:33
  42.3 0.4 collective-permute-start.4
  42.7 10.1 %collective-permute-done.4.four = bf16[48,1152]{1,0:T(8,128)(2,1)S(1)} collective-permute-done((bf16[48,1152]{1,0:T(8,128)(2,1)S(1)}, bf16[48,1152]{1,0:T(8,128)(2,1)S(1)}, u32[]{:S(2)}, u32[]{:S(2)}) %collective-permute-start.4) | collective-permute-done | bytes 110624 | tf_op jit(solution)/shard_map/ppermute | solution.py:33
  52.9 0.5 collective-permute-start.6
  54.7 0.3 collective-permute-start.7
  55.0 0.6 copy-done.2
  55.7 0.7 copy-done
  56.4 0.6 copy-done.4
  57.0 0.9 copy-done.1
  58.0 0.9 copy-done.3
  58.9 0.9 copy-done.5
  59.8 5.5 %scores.1 = (bf16[384,768]{1,0:T(8,128)(2,1)S(1)}, f32[384,1024]{1,0:T(8,128)}, f32[768,1024]{1,0:T(8,128)S(1)}, f32[1,128]{1,0:T(1,128)S(1)}) custom-call(s32[1]{0:T(128)} %bitcast.spot, f32[1]{0:T(128)S(6)} %copy.9.scale, f32[1]{0:T(128)S(6)} %copy.10.bias, bf16[96,1152]{1,0:T(8,128)(2,1)S(1)} %pad_maximum_fusion.1.own, ...), custom_call_target="tpu_custom_call" | custom-call | tf_op jit(solution)/shard_map/scores/pallas_call | solution.py:213
  65.3 0.6 collective-permute-start.10
  65.9 0.2 collective-permute-start.8
  66.1 1.5 %convert_element_type.45 = f16[768,1024]{1,0:T(8,128)(2,1)} convert(f32[768,1024]{1,0:T(8,128)S(1)} %get-tuple-element.31) | non-fusion elementwise | flops 786432 | bytes 4718592 | tf_op jit(solution)/shard_map/convert_element_type | solution.py:265
  67.5 3.4 %collective-permute-done.8 = f32[1,128]{1,0:T(1,128)S(1)} collective-permute-done((f32[1,128]{1,0:T(1,128)S(1)}, f32[1,128]{1,0:T(1,128)S(1)}, u32[]{:S(2)}, u32[]{:S(2)}) %collective-permute-start.8) | collective-permute-done | bytes 544 | tf_op jit(solution)/shard_map/ppermute | solution.py:58
  70.9 1.2 collective-permute-start.9
  72.1 2.4 %collective-permute-done.9 = f32[1,128]{1,0:T(1,128)S(1)} collective-permute-done((f32[1,128]{1,0:T(1,128)S(1)}, f32[1,128]{1,0:T(1,128)S(1)}, u32[]{:S(2)}, u32[]{:S(2)}) %collective-permute-start.9) | collective-permute-done | bytes 544 | tf_op jit(solution)/shard_map/ppermute | solution.py:58
  74.5 7.2 %all-to-all-start.1 = ((f16[16,48,1024]{2,1,0:T(8,128)(2,1)}), f16[16,48,1024]{2,1,0:T(8,128)(2,1)}, u32[]{:S(2)}, u32[]{:S(2)}) async-start(f16[16,48,1024]{2,1,0:T(8,128)(2,1)} %bitcast.13), calls=%async_computation.1 | async-start | bytes 3145728 | tf_op jit(solution)/shard_map/all_to_all | solution.py:20
  81.7 2.2 %fusion.8 = (f16[384,1024]{1,0:T(8,128)(2,1)S(1)}, f32[384,1024]{1,0:T(8,128)S(1)}) fusion(f32[384,1024]{1,0:T(8,128)} %collective-permute-done.10, bf16[384,768]{1,0:T(8,128)(2,1)S(1)} %get-tuple-element.36, bf16[768,1024]{1,0:T(8,128)(2,1)S(1)} %bitcast.12), kind=kOutput, calls=%fused_computation.42 | convolution fusion | flops 604766208 | bytes 6094848 | tf_op jit(solution)/shard_map/dot_general | solution.py:272
  84.0 2.1 %collective-permute-start.12 = (f16[192,1024]{1,0:T(8,128)(2,1)S(1)}, f16[192,1024]{1,0:T(8,128)(2,1)S(1)}, u32[]{:S(2)}, u32[]{:S(2)}) collective-permute-start(f16[192,1024]{1,0:T(8,128)(2,1)S(1)} %slice.36), channel_id=1, source_target_pairs={{0,28},{2,6},{4,0},{6,10},{8,4},{10,14},{12,8},{14,18},{16,12},{18... | collective-permute-start | bytes 1179656 | tf_op jit(solution)/shard_map/ppermute | solution.py:33
  86.2 3.8 %collective-permute-start.13 = (f16[48,1024]{1,0:T(8,128)(2,1)S(1)}, f16[48,1024]{1,0:T(8,128)(2,1)S(1)}, u32[]{:S(2)}, u32[]{:S(2)}) collective-permute-start(f16[48,1024]{1,0:T(8,128)(2,1)S(1)} %slice.37), channel_id=1, source_target_pairs={{0,24},{2,10},{4,28},{6,14},{8,0},{10,18},{12,4},{14,22},{16,8},{1... | collective-permute-start | bytes 294920 | tf_op jit(solution)/shard_map/ppermute | solution.py:33
  90.0 4.0 %collective-permute-done.14 = f32[1,128]{1,0:T(1,128)S(1)} collective-permute-done((f32[1,128]{1,0:T(1,128)S(1)}, f32[1,128]{1,0:T(1,128)S(1)}, u32[]{:S(2)}, u32[]{:S(2)}) %collective-permute-start.14) | collective-permute-done | bytes 544 | tf_op jit(solution)/shard_map/ppermute | solution.py:58
  94.0 4.4 %collective-permute-done.15 = f32[1,128]{1,0:T(1,128)S(1)} collective-permute-done((f32[1,128]{1,0:T(1,128)S(1)}, f32[1,128]{1,0:T(1,128)S(1)}, u32[]{:S(2)}, u32[]{:S(2)}) %collective-permute-start.15) | collective-permute-done | bytes 544 | tf_op jit(solution)/shard_map/ppermute | solution.py:58
  98.6 1.3 %collective-permute-start.16 = (f16[96,1024]{1,0:T(8,128)(2,1)S(1)}, f16[96,1024]{1,0:T(8,128)(2,1)S(1)}, u32[]{:S(2)}, u32[]{:S(2)}) collective-permute-start(f16[96,1024]{1,0:T(8,128)(2,1)S(1)} %fusion), channel_id=1, source_target_pairs={{0,24},{2,10},{4,28},{6,14},{8,0},{10,18},{12,4},{14,22},{16,8},{1... | collective-permute-start | bytes 589832 | tf_op jit(solution)/shard_map/ppermute | solution.py:33
  99.9 2.5 %collective-permute-start.17 = (f32[1,128]{1,0:T(1,128)S(1)}, f32[1,128]{1,0:T(1,128)S(1)}, u32[]{:S(2)}, u32[]{:S(2)}) collective-permute-start(f32[1,128]{1,0:T(1,128)S(1)} %add.197), channel_id=1, source_target_pairs={{0,16},{4,20},{8,24},{12,28},{16,0},{20,4},{24,8},{28,12},{1,17},{... | collective-permute-start | bytes 1544 | tf_op jit(solution)/shard_map/ppermute | solution.py:58
  102.4 5.0 %collective-permute-done.17 = f32[1,128]{1,0:T(1,128)S(1)} collective-permute-done((f32[1,128]{1,0:T(1,128)S(1)}, f32[1,128]{1,0:T(1,128)S(1)}, u32[]{:S(2)}, u32[]{:S(2)}) %collective-permute-start.17) | collective-permute-done | bytes 544 | tf_op jit(solution)/shard_map/ppermute | solution.py:58
  107.5 0.1 collective-permute-start.20
  107.6 1.6 %collective-permute-start.18 = (f32[1,128]{1,0:T(1,128)S(1)}, f32[1,128]{1,0:T(1,128)S(1)}, u32[]{:S(2)}, u32[]{:S(2)}) collective-permute-start(f32[1,128]{1,0:T(1,128)S(1)} %add.201), channel_id=1, source_target_pairs={{0,32},{32,0},{64,96},{96,64},{1,33},{33,1},{65,97},{97,65},{2,34}... | collective-permute-start | bytes 1544 | tf_op jit(solution)/shard_map/ppermute | solution.py:58
  109.1 2.1 %collective-permute-done.18 = f32[1,128]{1,0:T(1,128)S(1)} collective-permute-done((f32[1,128]{1,0:T(1,128)S(1)}, f32[1,128]{1,0:T(1,128)S(1)}, u32[]{:S(2)}, u32[]{:S(2)}) %collective-permute-start.18) | collective-permute-done | bytes 544 | tf_op jit(solution)/shard_map/ppermute | solution.py:58
  111.2 3.0 %collective-permute-start.19 = (f32[1,128]{1,0:T(1,128)S(1)}, f32[1,128]{1,0:T(1,128)S(1)}, u32[]{:S(2)}, u32[]{:S(2)}) collective-permute-start(f32[1,128]{1,0:T(1,128)S(1)} %add.202), channel_id=1, source_target_pairs={{0,64},{32,96},{64,0},{96,32},{1,65},{33,97},{65,1},{97,33},{2,66}... | collective-permute-start | bytes 1544 | tf_op jit(solution)/shard_map/ppermute | solution.py:58
  114.2 2.4 %convert_reduce_fusion = f32[48,1024]{1,0:T(8,128)} fusion(f16[16,48,1024]{2,1,0:T(8,128)(2,1)} %all-to-all-done.1), kind=kLoop, calls=%fused_computation | loop fusion | flops 1523712 | bytes 1769472 | tf_op jit(solution)/shard_map/reduce_sum | solution.py:274
  116.7 1.7 %fusion.3 = f32[48,1024]{1,0:T(8,128)} fusion(f32[48,1024]{1,0:T(8,128)S(1)} %collective-permute-done.20, f32[384,1024]{1,0:T(8,128)} %copy-done.6, f32[96,1024]{1,0:T(8,128)S(1)} %convert_element_type.50, s32[]{:T(128)S(6)} %select_n.119, f16[96,1024]{1,0:T(8,128)(2,1)S(1)} %slice.34), kind=kLoop, calls=%fused_computation.13 | loop fusion | flops 196608 | bytes 884740 | tf_op jit(solution)/shard_map/add | solution.py:79
  (51 shorter events, 0.6 us)
Async XLA Ops:
  0.6 7.0 %copy-start.7 = (s32[192]{0:T(256)S(1)}, s32[192]{0:T(256)}, u32[]{:S(2)}) copy-start(s32[192]{0:T(256)} %param.9) | copy-start | bytes 2308
  5.3 12.5 %collective-permute-start = (f32[96,1024]{1,0:T(8,128)S(1)}, f32[96,1024]{1,0:T(8,128)S(1)}, u32[]{:S(2)}, u32[]{:S(2)}) collective-permute-start(f32[96,1024]{1,0:T(8,128)S(1)} %get-tuple-element.26), channel_id=1, source_target_pairs={{0,1},{1,0},{2,3},{3,2},{4,5},{5,4},{6,7},{7,6},{8,9},{9,8},{10,11... | collective-permute-start | bytes 1179656 | tf_op jit(solution)/shard_map/ppermute | solution.py:145
  18.0 1.5 %collective-permute-start.1 = (bf16[96,1024]{1,0:T(8,128)(2,1)S(1)}, bf16[96,1024]{1,0:T(8,128)(2,1)S(1)}, u32[]{:S(2)}, u32[]{:S(2)}) collective-permute-start(bf16[96,1024]{1,0:T(8,128)(2,1)S(1)} %multiply_convert_fusion), channel_id=1, source_target_pairs={{0,2},{2,0},{1,3},{3,1},{4,6},{6,4},{5,7},{7,5},{8,10},{10,8},{9,1... | collective-permute-start | bytes 589832 | tf_op jit(solution)/shard_map/ppermute | solution.py:246
  21.1 35.9 %all-to-all-start = ((bf16[16,48,1024]{2,1,0:T(8,128)(2,1)}), bf16[16,48,1024]{2,1,0:T(8,128)(2,1)S(1)}, u32[]{:S(2)}, u32[]{:S(2)}) async-start(bf16[16,48,1024]{2,1,0:T(8,128)(2,1)} %broadcast_in_dim.29), calls=%async_computation | async-start | bytes 3145728 | tf_op jit(solution)/shard_map/all_to_all | solution.py:20
  28.6 10.8 %collective-permute-start.2 = (bf16[96,1152]{1,0:T(8,128)(2,1)S(1)}, bf16[96,1152]{1,0:T(8,128)(2,1)S(1)}, u32[]{:S(2)}, u32[]{:S(2)}) collective-permute-start(bf16[96,1152]{1,0:T(8,128)(2,1)S(1)} %pad_maximum_fusion.1.own), channel_id=1, source_target_pairs={{0,8},{2,26},{4,12},{6,30},{8,16},{10,2},{12,20},{14,6},{16,24},{1... | collective-permute-start | bytes 663560 | tf_op jit(solution)/shard_map/ppermute | solution.py:33
  39.4 13.4 %collective-permute-start.3 = (bf16[192,1152]{1,0:T(8,128)(2,1)S(1)}, bf16[192,1152]{1,0:T(8,128)(2,1)S(1)}, u32[]{:S(2)}, u32[]{:S(2)}) collective-permute-start(bf16[192,1152]{1,0:T(8,128)(2,1)S(1)} %pad_maximum_fusion), channel_id=1, source_target_pairs={{0,4},{2,30},{4,8},{6,2},{8,12},{10,6},{12,16},{14,10},{16,20},{18... | collective-permute-start | bytes 1327112 | tf_op jit(solution)/shard_map/ppermute | solution.py:33
  42.3 10.6 %collective-permute-start.4 = (bf16[48,1152]{1,0:T(8,128)(2,1)S(1)}, bf16[48,1152]{1,0:T(8,128)(2,1)S(1)}, u32[]{:S(2)}, u32[]{:S(2)}) collective-permute-start(bf16[48,1152]{1,0:T(8,128)(2,1)S(1)} %constant_dynamic-slice_fusion), channel_id=1, source_target_pairs={{0,8},{2,26},{4,12},{6,30},{8,16},{10,2},{12,20},{14,6},{16,24},{1... | collective-permute-start | bytes 331784 | tf_op jit(solution)/shard_map/ppermute | solution.py:33
  52.9 4.2 %collective-permute-start.5 = (bf16[192,1152]{1,0:T(8,128)(2,1)S(1)}, bf16[192,1152]{1,0:T(8,128)(2,1)S(1)}, u32[]{:S(2)}, u32[]{:S(2)}) collective-permute-start(bf16[192,1152]{1,0:T(8,128)(2,1)S(1)} %collective-permute-done.3.one_three), channel_id=1, source_target_pairs={{0,2},{2,0},{1,3},{3,1},{4,6},{6,4},{5,7},{7,5},{8,10},{10,8},{9,1... | collective-permute-start | bytes 1327112 | tf_op jit(solution)/shard_map/ppermute | solution.py:47
  52.9 2.8 %collective-permute-start.6 = (bf16[96,1152]{1,0:T(8,128)(2,1)S(1)}, bf16[96,1152]{1,0:T(8,128)(2,1)S(1)}, u32[]{:S(2)}, u32[]{:S(2)}) collective-permute-start(bf16[96,1152]{1,0:T(8,128)(2,1)S(1)} %collective-permute-done.2.two), channel_id=1, source_target_pairs={{0,2},{2,0},{1,3},{3,1},{4,6},{6,4},{5,7},{7,5},{8,10},{10,8},{9,1... | collective-permute-start | bytes 663560 | tf_op jit(solution)/shard_map/ppermute | solution.py:43
  54.7 1.7 %collective-permute-start.7 = (bf16[48,1152]{1,0:T(8,128)(2,1)S(1)}, bf16[48,1152]{1,0:T(8,128)(2,1)S(1)}, u32[]{:S(2)}, u32[]{:S(2)}) collective-permute-start(bf16[48,1152]{1,0:T(8,128)(2,1)S(1)} %collective-permute-done.4.four), channel_id=1, source_target_pairs={{0,2},{2,0},{1,3},{3,1},{4,6},{6,4},{5,7},{7,5},{8,10},{10,8},{9,1... | collective-permute-start | bytes 331784 | tf_op jit(solution)/shard_map/ppermute | solution.py:48
  55.0 0.6 copy-start.2
  55.7 0.7 copy-start
  56.4 0.6 copy-start.4
  57.0 0.9 copy-start.1
  58.0 0.9 copy-start.3
  58.9 0.9 copy-start.5
  65.3 16.4 %collective-permute-start.10 = (f32[384,1024]{1,0:T(8,128)}, f32[384,1024]{1,0:T(8,128)}, u32[]{:S(2)}, u32[]{:S(2)}) collective-permute-start(f32[384,1024]{1,0:T(8,128)} %get-tuple-element.37), channel_id=1, source_target_pairs={{0,2},{2,0},{1,3},{3,1},{4,6},{6,4},{5,7},{7,5},{8,10},{10,8},{9,1... | collective-permute-start | bytes 4718600 | tf_op jit(solution)/shard_map/ppermute | solution.py:263
  65.9 5.0 %collective-permute-start.8 = (f32[1,128]{1,0:T(1,128)S(1)}, f32[1,128]{1,0:T(1,128)S(1)}, u32[]{:S(2)}, u32[]{:S(2)}) collective-permute-start(f32[1,128]{1,0:T(1,128)S(1)} %get-tuple-element.32), channel_id=1, source_target_pairs={{0,1},{1,0},{2,3},{3,2},{4,5},{5,4},{6,7},{7,6},{8,9},{9,8},{10,11... | collective-permute-start | bytes 1544 | tf_op jit(solution)/shard_map/ppermute | solution.py:58
  70.9 3.5 %collective-permute-start.9 = (f32[1,128]{1,0:T(1,128)S(1)}, f32[1,128]{1,0:T(1,128)S(1)}, u32[]{:S(2)}, u32[]{:S(2)}) collective-permute-start(f32[1,128]{1,0:T(1,128)S(1)} %add.192), channel_id=1, source_target_pairs={{0,128},{128,0},{1,129},{129,1},{2,130},{130,2},{3,131},{131,3},{4... | collective-permute-start | bytes 1544 | tf_op jit(solution)/shard_map/ppermute | solution.py:58
  74.5 7.2 %collective-permute-start.11 = (f32[1,128]{1,0:T(1,128)S(1)}, f32[1,128]{1,0:T(1,128)S(1)}, u32[]{:S(2)}, u32[]{:S(2)}) collective-permute-start(f32[1,128]{1,0:T(1,128)S(1)} %add.193), channel_id=1, source_target_pairs={{0,2},{2,0},{1,3},{3,1},{4,6},{6,4},{5,7},{7,5},{8,10},{10,8},{9,1... | collective-permute-start | bytes 1544 | tf_op jit(solution)/shard_map/ppermute | solution.py:58
  74.5 39.7 %all-to-all-start.1 = ((f16[16,48,1024]{2,1,0:T(8,128)(2,1)}), f16[16,48,1024]{2,1,0:T(8,128)(2,1)}, u32[]{:S(2)}, u32[]{:S(2)}) async-start(f16[16,48,1024]{2,1,0:T(8,128)(2,1)} %bitcast.13), calls=%async_computation.1 | async-start | bytes 3145728 | tf_op jit(solution)/shard_map/all_to_all | solution.py:20
  83.9 14.5 %copy-start.6 = (f32[384,1024]{1,0:T(8,128)}, f32[384,1024]{1,0:T(8,128)S(1)}, u32[]{:S(2)}) copy-start(f32[384,1024]{1,0:T(8,128)S(1)} %get-tuple-element.54) | copy-start | bytes 4718596
  84.0 14.4 %collective-permute-start.12 = (f16[192,1024]{1,0:T(8,128)(2,1)S(1)}, f16[192,1024]{1,0:T(8,128)(2,1)S(1)}, u32[]{:S(2)}, u32[]{:S(2)}) collective-permute-start(f16[192,1024]{1,0:T(8,128)(2,1)S(1)} %slice.36), channel_id=1, source_target_pairs={{0,28},{2,6},{4,0},{6,10},{8,4},{10,14},{12,8},{14,18},{16,12},{18... | collective-permute-start | bytes 1179656 | tf_op jit(solution)/shard_map/ppermute | solution.py:33
  86.2 12.3 %collective-permute-start.13 = (f16[48,1024]{1,0:T(8,128)(2,1)S(1)}, f16[48,1024]{1,0:T(8,128)(2,1)S(1)}, u32[]{:S(2)}, u32[]{:S(2)}) collective-permute-start(f16[48,1024]{1,0:T(8,128)(2,1)S(1)} %slice.37), channel_id=1, source_target_pairs={{0,24},{2,10},{4,28},{6,14},{8,0},{10,18},{12,4},{14,22},{16,8},{1... | collective-permute-start | bytes 294920 | tf_op jit(solution)/shard_map/ppermute | solution.py:33
  90.0 4.0 %collective-permute-start.14 = (f32[1,128]{1,0:T(1,128)S(1)}, f32[1,128]{1,0:T(1,128)S(1)}, u32[]{:S(2)}, u32[]{:S(2)}) collective-permute-start(f32[1,128]{1,0:T(1,128)S(1)} %add.194), channel_id=1, source_target_pairs={{0,4},{4,0},{8,12},{12,8},{16,20},{20,16},{24,28},{28,24},{1,5},{5... | collective-permute-start | bytes 1544 | tf_op jit(solution)/shard_map/ppermute | solution.py:58
  94.0 4.4 %collective-permute-start.15 = (f32[1,128]{1,0:T(1,128)S(1)}, f32[1,128]{1,0:T(1,128)S(1)}, u32[]{:S(2)}, u32[]{:S(2)}) collective-permute-start(f32[1,128]{1,0:T(1,128)S(1)} %add.196), channel_id=1, source_target_pairs={{0,8},{4,12},{8,0},{12,4},{16,24},{20,28},{24,16},{28,20},{1,9},{5... | collective-permute-start | bytes 1544 | tf_op jit(solution)/shard_map/ppermute | solution.py:58
  98.6 8.8 %collective-permute-start.16 = (f16[96,1024]{1,0:T(8,128)(2,1)S(1)}, f16[96,1024]{1,0:T(8,128)(2,1)S(1)}, u32[]{:S(2)}, u32[]{:S(2)}) collective-permute-start(f16[96,1024]{1,0:T(8,128)(2,1)S(1)} %fusion), channel_id=1, source_target_pairs={{0,24},{2,10},{4,28},{6,14},{8,0},{10,18},{12,4},{14,22},{16,8},{1... | collective-permute-start | bytes 589832 | tf_op jit(solution)/shard_map/ppermute | solution.py:33
  99.9 7.5 %collective-permute-start.17 = (f32[1,128]{1,0:T(1,128)S(1)}, f32[1,128]{1,0:T(1,128)S(1)}, u32[]{:S(2)}, u32[]{:S(2)}) collective-permute-start(f32[1,128]{1,0:T(1,128)S(1)} %add.197), channel_id=1, source_target_pairs={{0,16},{4,20},{8,24},{12,28},{16,0},{20,4},{24,8},{28,12},{1,17},{... | collective-permute-start | bytes 1544 | tf_op jit(solution)/shard_map/ppermute | solution.py:58
  107.5 9.2 %collective-permute-start.20 = (f32[48,1024]{1,0:T(8,128)S(1)}, f32[48,1024]{1,0:T(8,128)S(1)}, u32[]{:S(2)}, u32[]{:S(2)}) collective-permute-start(f32[48,1024]{1,0:T(8,128)S(1)} %dynamic-slice_add_fusion), channel_id=1, source_target_pairs={{0,2},{2,0},{1,3},{3,1},{4,6},{6,4},{5,7},{7,5},{8,10},{10,8},{9,1... | collective-permute-start | bytes 589832 | tf_op jit(solution)/shard_map/ppermute | solution.py:76
  107.6 3.6 %collective-permute-start.18 = (f32[1,128]{1,0:T(1,128)S(1)}, f32[1,128]{1,0:T(1,128)S(1)}, u32[]{:S(2)}, u32[]{:S(2)}) collective-permute-start(f32[1,128]{1,0:T(1,128)S(1)} %add.201), channel_id=1, source_target_pairs={{0,32},{32,0},{64,96},{96,64},{1,33},{33,1},{65,97},{97,65},{2,34}... | collective-permute-start | bytes 1544 | tf_op jit(solution)/shard_map/ppermute | solution.py:58
  111.2 5.4 %collective-permute-start.19 = (f32[1,128]{1,0:T(1,128)S(1)}, f32[1,128]{1,0:T(1,128)S(1)}, u32[]{:S(2)}, u32[]{:S(2)}) collective-permute-start(f32[1,128]{1,0:T(1,128)S(1)} %add.202), channel_id=1, source_target_pairs={{0,64},{32,96},{64,0},{96,32},{1,65},{33,97},{65,1},{97,33},{2,66}... | collective-permute-start | bytes 1544 | tf_op jit(solution)/shard_map/ppermute | solution.py:58

commit v11 on v10

--- a/solution.py
+++ b/solution.py
@@ -106,16 +106,20 @@
     for load in loads[:4]:
         load.wait()
     total = jnp.zeros((4 * quarter, inputs.shape[1]), F32)
-    for k in range(count):
-        loads[4 + 2 * k].wait()
-        hidden = jnp.dot(
-            ordered[...], up_held[:, k * step : (k + 1) * step], preferred_element_type=F32
-        )
-        hidden = jax.nn.gelu(hidden).astype(jnp.bfloat16)
-        loads[5 + 2 * k].wait()
-        total = total + jnp.dot(
-            hidden, down_held[k * step : (k + 1) * step, :], preferred_element_type=F32
-        )
+    hidden = None
+    for k in range(count + 1):
+        if k < count:
+            loads[4 + 2 * k].wait()
+        if k > 0:
+            loads[3 + 2 * k].wait()
+        if k < count:
+            part = up_held[:, k * step : (k + 1) * step]
+            coming = jnp.dot(ordered[...], part, preferred_element_type=F32)
+        if k > 0:
+            part = down_held[(k - 1) * step : k * step, :]
+            total = total + jnp.dot(hidden, part, preferred_element_type=F32)
+        if k < count:
+            hidden = jax.nn.gelu(coming).astype(jnp.bfloat16)
     sent[...] = total[: 2 * quarter]
     own[...] = total[2 * quarter :] + ordered[2 * quarter :, :].astype(F32)
 
@@ -157,7 +161,7 @@
 
 def score_kernel(
     spot, scale, bias, own, one_three, two, four, one_three_other, two_other, four_other,
-    reports, columns, kept, sent, report_part, loss, rows, weight,
+    reports, columns, kept, sent, report_part, loss, rows, weight, sems,
 ):
     count, width = reports.shape
     scale_value, bias_value = scale[0], bias[0]
@@ -168,13 +172,18 @@
         (one_three, two, four, section),
         (one_three_other, two_other, four_other, 1 - section),
     )
+    loads = []
     for group in groups:
-        for part in group[:3]:
-            rows[place : place + part.shape[0], :] = part[...]
-            place += part.shape[0]
         start = pl.multiple_of(group[3] * quarter, 16)
-        rows[place : place + quarter, :] = own[pl.ds(start, quarter), :]
-        place += quarter
+        for part in (*group[:3], own.at[pl.ds(start, quarter), :]):
+            size = part.shape[0]
+            held = rows.at[pl.ds(place, size), :]
+            loads.append(pltpu.make_async_copy(part, held, sems.at[len(loads)]))
+            place += size
+    for load in loads:
+        load.start()
+    for load in loads:
+        load.wait()
 
     total = jnp.zeros((1, count), F32)
     step = place // 4
@@ -212,7 +221,7 @@
     whole = pl.BlockSpec(memory_space=pltpu.VMEM)
     return pl.pallas_call(
         score_kernel,
-        in_specs=[scalar] * 3 + [whole] * 9,
+        in_specs=[scalar] * 3 + [pl.BlockSpec(memory_space=pltpu.HBM)] * 7 + [whole] * 2,
         out_specs=[whole, whole, whole, whole],
         out_shape=[
             jax.ShapeDtypeStruct((rows // 2, count), jnp.bfloat16),
@@ -223,10 +232,18 @@
         scratch_shapes=[
             pltpu.VMEM((rows, own.shape[1]), jnp.bfloat16),
             pltpu.VMEM((rows, count), jnp.bfloat16),
+            pltpu.SemaphoreType.DMA((8,)),
         ],
-        compiler_params=pltpu.CompilerParams(vmem_limit_bytes=20 * 1024 * 1024),
+        compiler_params=pltpu.CompilerParams(vmem_limit_bytes=12 * 1024 * 1024),
         name="scores",
-    )(spot, scale, bias, own, *pieces, reports, columns)
+    )(
+        spot,
+        scale,
+        bias,
+        *(pltpu.with_memory_space_constraint(x, pltpu.HBM) for x in (own, *pieces)),
+        reports,
+        columns,
+    )
 
 
 def transposed_dot(weight, slides):

time: 120 us -> 118 us (0.983)
  local copies, waits for them, and re-layouts: 6.43 us -> 2.51 us
  Pallas kernels: 10.2 us -> 11.6 us
    unnamed x16 -> x18, local copies, waits for them, and re-layouts: 4.72 us -> 0.8 us
    pallas_call x1, Pallas kernels: 5.53 us -> 7.03 us  [scored(): pl.pallas_call(score_kernel, in_specs=[scalar] * 3 + [pl.BlockSpec(memory...]
  transfers between devices with their start and end apart: 23 -> 23, of which waited for: 10 -> 11; matrix products, arithmetic and copies ran while one was open for 6% -> 6% of each run, Pallas kernels for 0% -> 0%
where the time goes in v11:
time: 118 us
  waiting for transfers between devices  51.4 us (44%)
  starting transfers between devices  40.5 us (34%)
  Pallas kernels  11.6 us (10%)
  other arithmetic  6.36 us (5%)
  between operations  3.36 us (3%)
  local copies, waits for them, and re-layouts  2.51 us (2%)
  matrix products  2.23 us (2%)
    ppermute x8, waiting for transfers between devices, with_partner(): return value + lax.ppermute(value, axis, pairs)  21.3 us
    ppermute x6, waiting for transfers between devices, along_z(): return lax.ppermute(array, ('z', 'section'), pairs)  17.7 us
    all_to_all x2, starting transfers between devices, exchanged(): return lax.all_to_all(parts, axes, split_axis=0, concat_axis=0, tiled=True)  14.7 us
    ppermute x6, starting transfers between devices, along_z(): return lax.ppermute(array, ('z', 'section'), pairs)  13.8 us
    ppermute x1, waiting for transfers between devices, tower(): raw = own + lax.ppermute(sent, 'tensor', SWAP)  9.91 us
    ppermute x8, starting transfers between devices, with_partner(): return value + lax.ppermute(value, axis, pairs)  8.33 us
    pallas_call x1, Pallas kernels, scored(): pl.pallas_call(score_kernel, in_specs=[scalar] * 3 + [pl.BlockSpec(memory...  7.03 us
    pallas_call x1, Pallas kernels, tower(): pl.pallas_call(tower_kernel, in_specs=[pl.BlockSpec(memory_space=pltpu.SM...  4.54 us
  transfers between devices with their start and end apart: 23, of which 11 were waited for; matrix products, arithmetic and copies ran while one was open for 6% of the time, Pallas kernels for 0%

profile of v11, /device:TPU:4, one launch (start us, length us, event | category | flops | bytes accessed | tf_op | source)
XLA Modules:
  0.0 117.9 jit_solution(3028940845890277328)
XLA Ops:
  0.6 4.5 %tower.1 = (f32[96,1024]{1,0:T(8,128)S(1)}, f32[96,1024]{1,0:T(8,128)S(1)}) custom-call(s32[1]{0:T(128)} %bitcast.1.spot, bf16[192,1024]{1,0:T(8,128)(2,1)} %bitcast.16, bf16[1024,2048]{1,0:T(8,128)(2,1)} %bitcast.14, bf16[2048,1024]{1,0:T(8,128)(2,1)} %bitcast.15), custom_call_target="tpu_custom_call" | custom-call | tf_op jit(solution)/shard_map/tower/pallas_call | solution.py:132
  5.2 2.3 %collective-permute-start = (f32[96,1024]{1,0:T(8,128)S(1)}, f32[96,1024]{1,0:T(8,128)S(1)}, u32[]{:S(2)}, u32[]{:S(2)}) collective-permute-start(f32[96,1024]{1,0:T(8,128)S(1)} %get-tuple-element.26), channel_id=1, source_target_pairs={{0,1},{1,0},{2,3},{3,2},{4,5},{5,4},{6,7},{7,6},{8,9},{9,8},{10,11... | collective-permute-start | bytes 1179656 | tf_op jit(solution)/shard_map/ppermute | solution.py:149
  7.5 0.1 reshape.258
  7.6 0.1 reshape.259
  7.7 9.9 %collective-permute-done = f32[96,1024]{1,0:T(8,128)S(1)} collective-permute-done((f32[96,1024]{1,0:T(8,128)S(1)}, f32[96,1024]{1,0:T(8,128)S(1)}, u32[]{:S(2)}, u32[]{:S(2)}) %collective-permute-start) | collective-permute-done | bytes 393248 | tf_op jit(solution)/shard_map/ppermute | solution.py:149
  17.6 0.1 multiply_reduce_fusion
  17.8 0.1 multiply_convert_fusion
  17.9 0.1 collective-permute-start.1
  18.0 0.1 select_convert_fusion
  18.1 1.3 %collective-permute-done.1 = bf16[96,1024]{1,0:T(8,128)(2,1)S(1)} collective-permute-done((bf16[96,1024]{1,0:T(8,128)(2,1)S(1)}, bf16[96,1024]{1,0:T(8,128)(2,1)S(1)}, u32[]{:S(2)}, u32[]{:S(2)}) %collective-permute-start.1) | collective-permute-done | bytes 196640 | tf_op jit(solution)/shard_map/ppermute | solution.py:263
  19.4 0.1 broadcast_select_fusion
  19.6 1.4 %broadcast_in_dim.29 = bf16[16,48,1024]{2,1,0:T(8,128)(2,1)} broadcast(bf16[48,1024]{1,0:T(8,128)(2,1)S(1)} %dynamic-slice_select_fusion), dimensions={1,2} | broadcast | bytes 1671168 | tf_op jit(solution)/shard_map/broadcast_in_dim | solution.py:267
  21.0 7.5 %all-to-all-start = ((bf16[16,48,1024]{2,1,0:T(8,128)(2,1)}), bf16[16,48,1024]{2,1,0:T(8,128)(2,1)S(1)}, u32[]{:S(2)}, u32[]{:S(2)}) async-start(bf16[16,48,1024]{2,1,0:T(8,128)(2,1)} %broadcast_in_dim.29), calls=%async_computation | async-start | bytes 3145728 | tf_op jit(solution)/shard_map/all_to_all | solution.py:20
  28.4 3.3 %collective-permute-start.2 = (bf16[96,1152]{1,0:T(8,128)(2,1)S(1)}, bf16[96,1152]{1,0:T(8,128)(2,1)S(1)}, u32[]{:S(2)}, u32[]{:S(2)}) collective-permute-start(bf16[96,1152]{1,0:T(8,128)(2,1)S(1)} %pad_maximum_fusion.1.own), channel_id=1, source_target_pairs={{0,8},{2,26},{4,12},{6,30},{8,16},{10,2},{12,20},{14,6},{16,24},{1... | collective-permute-start | bytes 663560 | tf_op jit(solution)/shard_map/ppermute | solution.py:33
  31.7 7.6 %collective-permute-done.2.two = bf16[96,1152]{1,0:T(8,128)(2,1)S(1)} collective-permute-done((bf16[96,1152]{1,0:T(8,128)(2,1)S(1)}, bf16[96,1152]{1,0:T(8,128)(2,1)S(1)}, u32[]{:S(2)}, u32[]{:S(2)}) %collective-permute-start.2) | collective-permute-done | bytes 221216 | tf_op jit(solution)/shard_map/ppermute | solution.py:33
  39.3 2.8 %collective-permute-start.3 = (bf16[192,1152]{1,0:T(8,128)(2,1)S(1)}, bf16[192,1152]{1,0:T(8,128)(2,1)S(1)}, u32[]{:S(2)}, u32[]{:S(2)}) collective-permute-start(bf16[192,1152]{1,0:T(8,128)(2,1)S(1)} %pad_maximum_fusion), channel_id=1, source_target_pairs={{0,4},{2,30},{4,8},{6,2},{8,12},{10,6},{12,16},{14,10},{16,20},{18... | collective-permute-start | bytes 1327112 | tf_op jit(solution)/shard_map/ppermute | solution.py:33
  42.2 0.4 collective-permute-start.4
  42.6 10.1 %collective-permute-done.4.four = bf16[48,1152]{1,0:T(8,128)(2,1)S(1)} collective-permute-done((bf16[48,1152]{1,0:T(8,128)(2,1)S(1)}, bf16[48,1152]{1,0:T(8,128)(2,1)S(1)}, u32[]{:S(2)}, u32[]{:S(2)}) %collective-permute-start.4) | collective-permute-done | bytes 110624 | tf_op jit(solution)/shard_map/ppermute | solution.py:33
  52.7 0.1 collective-permute-start.5
  52.8 0.5 collective-permute-start.6
  54.6 0.4 collective-permute-start.7
  55.0 1.2 collective-permute-done.7.four_other
  56.2 0.6 copy-done.7
  56.9 0.1 copy-done.4
  57.0 7.0 %scores.1 = (bf16[384,768]{1,0:T(8,128)(2,1)S(1)}, f32[384,1024]{1,0:T(8,128)}, f32[768,1024]{1,0:T(8,128)S(1)}, f32[1,128]{1,0:T(1,128)S(1)}) custom-call(s32[1]{0:T(128)} %bitcast.spot, f32[1]{0:T(128)S(6)} %copy.9.scale, f32[1]{0:T(128)S(6)} %copy.10.bias, bf16[96,1152]{1,0:T(8,128)(2,1)} %copy-done.1, bf16[192,1152]{1,0:T(8,128)(2,1)} %copy-done.3, ...), custom_call_target="tpu_custom_call" | custom-call | tf_op jit(solution)/shard_map/scores/pallas_call | solution.py:222
  64.0 0.2 collective-permute-start.10
  64.3 0.2 collective-permute-start.8
  64.5 1.5 %convert_element_type.45 = f16[768,1024]{1,0:T(8,128)(2,1)} convert(f32[768,1024]{1,0:T(8,128)S(1)} %get-tuple-element.31) | non-fusion elementwise | flops 786432 | bytes 4718592 | tf_op jit(solution)/shard_map/convert_element_type | solution.py:282
  65.9 3.4 %collective-permute-done.8 = f32[1,128]{1,0:T(1,128)S(1)} collective-permute-done((f32[1,128]{1,0:T(1,128)S(1)}, f32[1,128]{1,0:T(1,128)S(1)}, u32[]{:S(2)}, u32[]{:S(2)}) %collective-permute-start.8) | collective-permute-done | bytes 544 | tf_op jit(solution)/shard_map/ppermute | solution.py:58
  69.3 1.2 collective-permute-start.9
  70.5 2.4 %collective-permute-done.9 = f32[1,128]{1,0:T(1,128)S(1)} collective-permute-done((f32[1,128]{1,0:T(1,128)S(1)}, f32[1,128]{1,0:T(1,128)S(1)}, u32[]{:S(2)}, u32[]{:S(2)}) %collective-permute-start.9) | collective-permute-done | bytes 544 | tf_op jit(solution)/shard_map/ppermute | solution.py:58
  72.9 7.2 %all-to-all-start.1 = ((f16[16,48,1024]{2,1,0:T(8,128)(2,1)}), f16[16,48,1024]{2,1,0:T(8,128)(2,1)}, u32[]{:S(2)}, u32[]{:S(2)}) async-start(f16[16,48,1024]{2,1,0:T(8,128)(2,1)} %bitcast.13), calls=%async_computation.1 | async-start | bytes 3145728 | tf_op jit(solution)/shard_map/all_to_all | solution.py:20
  80.1 2.2 %fusion.8 = (f16[384,1024]{1,0:T(8,128)(2,1)S(1)}, f32[384,1024]{1,0:T(8,128)S(1)}) fusion(f32[384,1024]{1,0:T(8,128)} %collective-permute-done.10, bf16[384,768]{1,0:T(8,128)(2,1)S(1)} %get-tuple-element.36, bf16[768,1024]{1,0:T(8,128)(2,1)S(1)} %bitcast.12), kind=kOutput, calls=%fused_computation.42 | convolution fusion | flops 604766208 | bytes 6094848 | tf_op jit(solution)/shard_map/dot_general | solution.py:289
  82.4 0.1 slice.36
  82.5 2.2 %collective-permute-start.12 = (f16[192,1024]{1,0:T(8,128)(2,1)S(1)}, f16[192,1024]{1,0:T(8,128)(2,1)S(1)}, u32[]{:S(2)}, u32[]{:S(2)}) collective-permute-start(f16[192,1024]{1,0:T(8,128)(2,1)S(1)} %slice.36), channel_id=1, source_target_pairs={{0,28},{2,6},{4,0},{6,10},{8,4},{10,14},{12,8},{14,18},{16,12},{18... | collective-permute-start | bytes 1179656 | tf_op jit(solution)/shard_map/ppermute | solution.py:33
  84.6 3.8 %collective-permute-start.13 = (f16[48,1024]{1,0:T(8,128)(2,1)S(1)}, f16[48,1024]{1,0:T(8,128)(2,1)S(1)}, u32[]{:S(2)}, u32[]{:S(2)}) collective-permute-start(f16[48,1024]{1,0:T(8,128)(2,1)S(1)} %slice.37), channel_id=1, source_target_pairs={{0,24},{2,10},{4,28},{6,14},{8,0},{10,18},{12,4},{14,22},{16,8},{1... | collective-permute-start | bytes 294920 | tf_op jit(solution)/shard_map/ppermute | solution.py:33
  88.4 4.0 %collective-permute-done.14 = f32[1,128]{1,0:T(1,128)S(1)} collective-permute-done((f32[1,128]{1,0:T(1,128)S(1)}, f32[1,128]{1,0:T(1,128)S(1)}, u32[]{:S(2)}, u32[]{:S(2)}) %collective-permute-start.14) | collective-permute-done | bytes 544 | tf_op jit(solution)/shard_map/ppermute | solution.py:58
  92.5 4.4 %collective-permute-done.15 = f32[1,128]{1,0:T(1,128)S(1)} collective-permute-done((f32[1,128]{1,0:T(1,128)S(1)}, f32[1,128]{1,0:T(1,128)S(1)}, u32[]{:S(2)}, u32[]{:S(2)}) %collective-permute-start.15) | collective-permute-done | bytes 544 | tf_op jit(solution)/shard_map/ppermute | solution.py:58
  97.0 0.1 fusion
  97.0 1.3 %collective-permute-start.16 = (f16[96,1024]{1,0:T(8,128)(2,1)S(1)}, f16[96,1024]{1,0:T(8,128)(2,1)S(1)}, u32[]{:S(2)}, u32[]{:S(2)}) collective-permute-start(f16[96,1024]{1,0:T(8,128)(2,1)S(1)} %fusion), channel_id=1, source_target_pairs={{0,24},{2,10},{4,28},{6,14},{8,0},{10,18},{12,4},{14,22},{16,8},{1... | collective-permute-start | bytes 589832 | tf_op jit(solution)/shard_map/ppermute | solution.py:33
  98.3 2.5 %collective-permute-start.17 = (f32[1,128]{1,0:T(1,128)S(1)}, f32[1,128]{1,0:T(1,128)S(1)}, u32[]{:S(2)}, u32[]{:S(2)}) collective-permute-start(f32[1,128]{1,0:T(1,128)S(1)} %add.197), channel_id=1, source_target_pairs={{0,16},{4,20},{8,24},{12,28},{16,0},{20,4},{24,8},{28,12},{1,17},{... | collective-permute-start | bytes 1544 | tf_op jit(solution)/shard_map/ppermute | solution.py:58
  100.8 5.0 %collective-permute-done.17 = f32[1,128]{1,0:T(1,128)S(1)} collective-permute-done((f32[1,128]{1,0:T(1,128)S(1)}, f32[1,128]{1,0:T(1,128)S(1)}, u32[]{:S(2)}, u32[]{:S(2)}) %collective-permute-start.17) | collective-permute-done | bytes 544 | tf_op jit(solution)/shard_map/ppermute | solution.py:58
  105.9 0.1 collective-permute-start.20
  106.0 1.5 %collective-permute-start.18 = (f32[1,128]{1,0:T(1,128)S(1)}, f32[1,128]{1,0:T(1,128)S(1)}, u32[]{:S(2)}, u32[]{:S(2)}) collective-permute-start(f32[1,128]{1,0:T(1,128)S(1)} %add.201), channel_id=1, source_target_pairs={{0,32},{32,0},{64,96},{96,64},{1,33},{33,1},{65,97},{97,65},{2,34}... | collective-permute-start | bytes 1544 | tf_op jit(solution)/shard_map/ppermute | solution.py:58
  107.6 2.1 %collective-permute-done.18 = f32[1,128]{1,0:T(1,128)S(1)} collective-permute-done((f32[1,128]{1,0:T(1,128)S(1)}, f32[1,128]{1,0:T(1,128)S(1)}, u32[]{:S(2)}, u32[]{:S(2)}) %collective-permute-start.18) | collective-permute-done | bytes 544 | tf_op jit(solution)/shard_map/ppermute | solution.py:58
  109.7 3.0 %collective-permute-start.19 = (f32[1,128]{1,0:T(1,128)S(1)}, f32[1,128]{1,0:T(1,128)S(1)}, u32[]{:S(2)}, u32[]{:S(2)}) collective-permute-start(f32[1,128]{1,0:T(1,128)S(1)} %add.202), channel_id=1, source_target_pairs={{0,64},{32,96},{64,0},{96,32},{1,65},{33,97},{65,1},{97,33},{2,66}... | collective-permute-start | bytes 1544 | tf_op jit(solution)/shard_map/ppermute | solution.py:58
  112.6 2.4 %convert_reduce_fusion = f32[48,1024]{1,0:T(8,128)} fusion(f16[16,48,1024]{2,1,0:T(8,128)(2,1)} %all-to-all-done.1), kind=kLoop, calls=%fused_computation | loop fusion | flops 1523712 | bytes 1769472 | tf_op jit(solution)/shard_map/reduce_sum | solution.py:291
  115.1 1.7 %fusion.3 = f32[48,1024]{1,0:T(8,128)} fusion(f32[48,1024]{1,0:T(8,128)S(1)} %collective-permute-done.20, f32[384,1024]{1,0:T(8,128)} %copy-done, f32[96,1024]{1,0:T(8,128)S(1)} %convert_element_type.50, s32[]{:T(128)S(6)} %select_n.119, f16[96,1024]{1,0:T(8,128)(2,1)S(1)} %slice.34), kind=kLoop, calls=%fused_computation.13 | loop fusion | flops 196608 | bytes 884740 | tf_op jit(solution)/shard_map/add | solution.py:79
  (53 shorter events, 0.5 us)
Async XLA Ops:
  0.6 6.9 %copy-start.8 = (s32[192]{0:T(256)S(1)}, s32[192]{0:T(256)}, u32[]{:S(2)}) copy-start(s32[192]{0:T(256)} %param.9) | copy-start | bytes 2308
  5.2 12.4 %collective-permute-start = (f32[96,1024]{1,0:T(8,128)S(1)}, f32[96,1024]{1,0:T(8,128)S(1)}, u32[]{:S(2)}, u32[]{:S(2)}) collective-permute-start(f32[96,1024]{1,0:T(8,128)S(1)} %get-tuple-element.26), channel_id=1, source_target_pairs={{0,1},{1,0},{2,3},{3,2},{4,5},{5,4},{6,7},{7,6},{8,9},{9,8},{10,11... | collective-permute-start | bytes 1179656 | tf_op jit(solution)/shard_map/ppermute | solution.py:149
  17.9 1.5 %collective-permute-start.1 = (bf16[96,1024]{1,0:T(8,128)(2,1)S(1)}, bf16[96,1024]{1,0:T(8,128)(2,1)S(1)}, u32[]{:S(2)}, u32[]{:S(2)}) collective-permute-start(bf16[96,1024]{1,0:T(8,128)(2,1)S(1)} %multiply_convert_fusion), channel_id=1, source_target_pairs={{0,2},{2,0},{1,3},{3,1},{4,6},{6,4},{5,7},{7,5},{8,10},{10,8},{9,1... | collective-permute-start | bytes 589832 | tf_op jit(solution)/shard_map/ppermute | solution.py:263
  19.6 19.7 %copy-start.1 = (bf16[96,1152]{1,0:T(8,128)(2,1)}, bf16[96,1152]{1,0:T(8,128)(2,1)S(1)}, u32[]{:S(2)}) copy-start(bf16[96,1152]{1,0:T(8,128)(2,1)S(1)} %pad_maximum_fusion.1.own) | copy-start | bytes 663556
  21.0 35.2 %all-to-all-start = ((bf16[16,48,1024]{2,1,0:T(8,128)(2,1)}), bf16[16,48,1024]{2,1,0:T(8,128)(2,1)S(1)}, u32[]{:S(2)}, u32[]{:S(2)}) async-start(bf16[16,48,1024]{2,1,0:T(8,128)(2,1)} %broadcast_in_dim.29), calls=%async_computation | async-start | bytes 3145728 | tf_op jit(solution)/shard_map/all_to_all | solution.py:20
  28.4 10.8 %collective-permute-start.2 = (bf16[96,1152]{1,0:T(8,128)(2,1)S(1)}, bf16[96,1152]{1,0:T(8,128)(2,1)S(1)}, u32[]{:S(2)}, u32[]{:S(2)}) collective-permute-start(bf16[96,1152]{1,0:T(8,128)(2,1)S(1)} %pad_maximum_fusion.1.own), channel_id=1, source_target_pairs={{0,8},{2,26},{4,12},{6,30},{8,16},{10,2},{12,20},{14,6},{16,24},{1... | collective-permute-start | bytes 663560 | tf_op jit(solution)/shard_map/ppermute | solution.py:33
  39.3 17.6 %copy-start.2 = (bf16[96,1152]{1,0:T(8,128)(2,1)}, bf16[96,1152]{1,0:T(8,128)(2,1)S(1)}, u32[]{:S(2)}) copy-start(bf16[96,1152]{1,0:T(8,128)(2,1)S(1)} %collective-permute-done.2.two) | copy-start | bytes 663556
  39.3 13.4 %collective-permute-start.3 = (bf16[192,1152]{1,0:T(8,128)(2,1)S(1)}, bf16[192,1152]{1,0:T(8,128)(2,1)S(1)}, u32[]{:S(2)}, u32[]{:S(2)}) collective-permute-start(bf16[192,1152]{1,0:T(8,128)(2,1)S(1)} %pad_maximum_fusion), channel_id=1, source_target_pairs={{0,4},{2,30},{4,8},{6,2},{8,12},{10,6},{12,16},{14,10},{16,20},{18... | collective-permute-start | bytes 1327112 | tf_op jit(solution)/shard_map/ppermute | solution.py:33
  42.2 10.5 %collective-permute-start.4 = (bf16[48,1152]{1,0:T(8,128)(2,1)S(1)}, bf16[48,1152]{1,0:T(8,128)(2,1)S(1)}, u32[]{:S(2)}, u32[]{:S(2)}) collective-permute-start(bf16[48,1152]{1,0:T(8,128)(2,1)S(1)} %constant_dynamic-slice_fusion), channel_id=1, source_target_pairs={{0,8},{2,26},{4,12},{6,30},{8,16},{10,2},{12,20},{14,6},{16,24},{1... | collective-permute-start | bytes 331784 | tf_op jit(solution)/shard_map/ppermute | solution.py:33
  52.7 3.5 %copy-start.6 = (bf16[48,1152]{1,0:T(8,128)(2,1)}, bf16[48,1152]{1,0:T(8,128)(2,1)S(1)}, u32[]{:S(2)}) copy-start(bf16[48,1152]{1,0:T(8,128)(2,1)S(1)} %collective-permute-done.4.four) | copy-start | bytes 331780
  52.7 4.1 %copy-start.3 = (bf16[192,1152]{1,0:T(8,128)(2,1)}, bf16[192,1152]{1,0:T(8,128)(2,1)S(1)}, u32[]{:S(2)}) copy-start(bf16[192,1152]{1,0:T(8,128)(2,1)S(1)} %collective-permute-done.3.one_three) | copy-start | bytes 1327108
  52.7 3.5 %collective-permute-start.5 = (bf16[192,1152]{1,0:T(8,128)(2,1)S(1)}, bf16[192,1152]{1,0:T(8,128)(2,1)S(1)}, u32[]{:S(2)}, u32[]{:S(2)}) collective-permute-start(bf16[192,1152]{1,0:T(8,128)(2,1)S(1)} %collective-permute-done.3.one_three), channel_id=1, source_target_pairs={{0,2},{2,0},{1,3},{3,1},{4,6},{6,4},{5,7},{7,5},{8,10},{10,8},{9,1... | collective-permute-start | bytes 1327112 | tf_op jit(solution)/shard_map/ppermute | solution.py:47
  52.8 2.2 %collective-permute-start.6 = (bf16[96,1152]{1,0:T(8,128)(2,1)S(1)}, bf16[96,1152]{1,0:T(8,128)(2,1)S(1)}, u32[]{:S(2)}, u32[]{:S(2)}) collective-permute-start(bf16[96,1152]{1,0:T(8,128)(2,1)S(1)} %collective-permute-done.2.two), channel_id=1, source_target_pairs={{0,2},{2,0},{1,3},{3,1},{4,6},{6,4},{5,7},{7,5},{8,10},{10,8},{9,1... | collective-permute-start | bytes 663560 | tf_op jit(solution)/shard_map/ppermute | solution.py:43
  54.6 1.6 %collective-permute-start.7 = (bf16[48,1152]{1,0:T(8,128)(2,1)S(1)}, bf16[48,1152]{1,0:T(8,128)(2,1)S(1)}, u32[]{:S(2)}, u32[]{:S(2)}) collective-permute-start(bf16[48,1152]{1,0:T(8,128)(2,1)S(1)} %collective-permute-done.4.four), channel_id=1, source_target_pairs={{0,2},{2,0},{1,3},{3,1},{4,6},{6,4},{5,7},{7,5},{8,10},{10,8},{9,1... | collective-permute-start | bytes 331784 | tf_op jit(solution)/shard_map/ppermute | solution.py:48
  55.0 1.8 %copy-start.5 = (bf16[96,1152]{1,0:T(8,128)(2,1)}, bf16[96,1152]{1,0:T(8,128)(2,1)S(1)}, u32[]{:S(2)}) copy-start(bf16[96,1152]{1,0:T(8,128)(2,1)S(1)} %collective-permute-done.6.two_other) | copy-start | bytes 663556
  56.2 0.6 copy-start.7
  56.2 0.8 copy-start.4
  64.0 16.1 %collective-permute-start.10 = (f32[384,1024]{1,0:T(8,128)}, f32[384,1024]{1,0:T(8,128)}, u32[]{:S(2)}, u32[]{:S(2)}) collective-permute-start(f32[384,1024]{1,0:T(8,128)} %get-tuple-element.37), channel_id=1, source_target_pairs={{0,2},{2,0},{1,3},{3,1},{4,6},{6,4},{5,7},{7,5},{8,10},{10,8},{9,1... | collective-permute-start | bytes 4718600 | tf_op jit(solution)/shard_map/ppermute | solution.py:280
  64.3 5.1 %collective-permute-start.8 = (f32[1,128]{1,0:T(1,128)S(1)}, f32[1,128]{1,0:T(1,128)S(1)}, u32[]{:S(2)}, u32[]{:S(2)}) collective-permute-start(f32[1,128]{1,0:T(1,128)S(1)} %get-tuple-element.32), channel_id=1, source_target_pairs={{0,1},{1,0},{2,3},{3,2},{4,5},{5,4},{6,7},{7,6},{8,9},{9,8},{10,11... | collective-permute-start | bytes 1544 | tf_op jit(solution)/shard_map/ppermute | solution.py:58
  69.3 3.5 %collective-permute-start.9 = (f32[1,128]{1,0:T(1,128)S(1)}, f32[1,128]{1,0:T(1,128)S(1)}, u32[]{:S(2)}, u32[]{:S(2)}) collective-permute-start(f32[1,128]{1,0:T(1,128)S(1)} %add.192), channel_id=1, source_target_pairs={{0,128},{128,0},{1,129},{129,1},{2,130},{130,2},{3,131},{131,3},{4... | collective-permute-start | bytes 1544 | tf_op jit(solution)/shard_map/ppermute | solution.py:58
  72.9 7.2 %collective-permute-start.11 = (f32[1,128]{1,0:T(1,128)S(1)}, f32[1,128]{1,0:T(1,128)S(1)}, u32[]{:S(2)}, u32[]{:S(2)}) collective-permute-start(f32[1,128]{1,0:T(1,128)S(1)} %add.193), channel_id=1, source_target_pairs={{0,2},{2,0},{1,3},{3,1},{4,6},{6,4},{5,7},{7,5},{8,10},{10,8},{9,1... | collective-permute-start | bytes 1544 | tf_op jit(solution)/shard_map/ppermute | solution.py:58
  72.9 39.7 %all-to-all-start.1 = ((f16[16,48,1024]{2,1,0:T(8,128)(2,1)}), f16[16,48,1024]{2,1,0:T(8,128)(2,1)}, u32[]{:S(2)}, u32[]{:S(2)}) async-start(f16[16,48,1024]{2,1,0:T(8,128)(2,1)} %bitcast.13), calls=%async_computation.1 | async-start | bytes 3145728 | tf_op jit(solution)/shard_map/all_to_all | solution.py:20
  82.4 14.5 %copy-start = (f32[384,1024]{1,0:T(8,128)}, f32[384,1024]{1,0:T(8,128)S(1)}, u32[]{:S(2)}) copy-start(f32[384,1024]{1,0:T(8,128)S(1)} %get-tuple-element.54) | copy-start | bytes 4718596
  82.5 14.4 %collective-permute-start.12 = (f16[192,1024]{1,0:T(8,128)(2,1)S(1)}, f16[192,1024]{1,0:T(8,128)(2,1)S(1)}, u32[]{:S(2)}, u32[]{:S(2)}) collective-permute-start(f16[192,1024]{1,0:T(8,128)(2,1)S(1)} %slice.36), channel_id=1, source_target_pairs={{0,28},{2,6},{4,0},{6,10},{8,4},{10,14},{12,8},{14,18},{16,12},{18... | collective-permute-start | bytes 1179656 | tf_op jit(solution)/shard_map/ppermute | solution.py:33
  84.6 12.3 %collective-permute-start.13 = (f16[48,1024]{1,0:T(8,128)(2,1)S(1)}, f16[48,1024]{1,0:T(8,128)(2,1)S(1)}, u32[]{:S(2)}, u32[]{:S(2)}) collective-permute-start(f16[48,1024]{1,0:T(8,128)(2,1)S(1)} %slice.37), channel_id=1, source_target_pairs={{0,24},{2,10},{4,28},{6,14},{8,0},{10,18},{12,4},{14,22},{16,8},{1... | collective-permute-start | bytes 294920 | tf_op jit(solution)/shard_map/ppermute | solution.py:33
  88.4 4.0 %collective-permute-start.14 = (f32[1,128]{1,0:T(1,128)S(1)}, f32[1,128]{1,0:T(1,128)S(1)}, u32[]{:S(2)}, u32[]{:S(2)}) collective-permute-start(f32[1,128]{1,0:T(1,128)S(1)} %add.194), channel_id=1, source_target_pairs={{0,4},{4,0},{8,12},{12,8},{16,20},{20,16},{24,28},{28,24},{1,5},{5... | collective-permute-start | bytes 1544 | tf_op jit(solution)/shard_map/ppermute | solution.py:58
  92.5 4.4 %collective-permute-start.15 = (f32[1,128]{1,0:T(1,128)S(1)}, f32[1,128]{1,0:T(1,128)S(1)}, u32[]{:S(2)}, u32[]{:S(2)}) collective-permute-start(f32[1,128]{1,0:T(1,128)S(1)} %add.196), channel_id=1, source_target_pairs={{0,8},{4,12},{8,0},{12,4},{16,24},{20,28},{24,16},{28,20},{1,9},{5... | collective-permute-start | bytes 1544 | tf_op jit(solution)/shard_map/ppermute | solution.py:58
  97.0 8.8 %collective-permute-start.16 = (f16[96,1024]{1,0:T(8,128)(2,1)S(1)}, f16[96,1024]{1,0:T(8,128)(2,1)S(1)}, u32[]{:S(2)}, u32[]{:S(2)}) collective-permute-start(f16[96,1024]{1,0:T(8,128)(2,1)S(1)} %fusion), channel_id=1, source_target_pairs={{0,24},{2,10},{4,28},{6,14},{8,0},{10,18},{12,4},{14,22},{16,8},{1... | collective-permute-start | bytes 589832 | tf_op jit(solution)/shard_map/ppermute | solution.py:33
  98.3 7.5 %collective-permute-start.17 = (f32[1,128]{1,0:T(1,128)S(1)}, f32[1,128]{1,0:T(1,128)S(1)}, u32[]{:S(2)}, u32[]{:S(2)}) collective-permute-start(f32[1,128]{1,0:T(1,128)S(1)} %add.197), channel_id=1, source_target_pairs={{0,16},{4,20},{8,24},{12,28},{16,0},{20,4},{24,8},{28,12},{1,17},{... | collective-permute-start | bytes 1544 | tf_op jit(solution)/shard_map/ppermute | solution.py:58
  105.9 9.2 %collective-permute-start.20 = (f32[48,1024]{1,0:T(8,128)S(1)}, f32[48,1024]{1,0:T(8,128)S(1)}, u32[]{:S(2)}, u32[]{:S(2)}) collective-permute-start(f32[48,1024]{1,0:T(8,128)S(1)} %dynamic-slice_add_fusion), channel_id=1, source_target_pairs={{0,2},{2,0},{1,3},{3,1},{4,6},{6,4},{5,7},{7,5},{8,10},{10,8},{9,1... | collective-permute-start | bytes 589832 | tf_op jit(solution)/shard_map/ppermute | solution.py:76
  106.0 3.6 %collective-permute-start.18 = (f32[1,128]{1,0:T(1,128)S(1)}, f32[1,128]{1,0:T(1,128)S(1)}, u32[]{:S(2)}, u32[]{:S(2)}) collective-permute-start(f32[1,128]{1,0:T(1,128)S(1)} %add.201), channel_id=1, source_target_pairs={{0,32},{32,0},{64,96},{96,64},{1,33},{33,1},{65,97},{97,65},{2,34}... | collective-permute-start | bytes 1544 | tf_op jit(solution)/shard_map/ppermute | solution.py:58
  109.7 5.4 %collective-permute-start.19 = (f32[1,128]{1,0:T(1,128)S(1)}, f32[1,128]{1,0:T(1,128)S(1)}, u32[]{:S(2)}, u32[]{:S(2)}) collective-permute-start(f32[1,128]{1,0:T(1,128)S(1)} %add.202), channel_id=1, source_target_pairs={{0,64},{32,96},{64,0},{96,32},{1,65},{33,97},{65,1},{97,33},{2,66}... | collective-permute-start | bytes 1544 | tf_op jit(solution)/shard_map/ppermute | solution.py:58

commit v12 on v11

--- a/solution.py
+++ b/solution.py
@@ -74,7 +74,6 @@
     two = two.astype(F32)
     given = row_half(one_three[: 2 * half], 1 - section).astype(F32) + row_half(two, 1 - section)
     got = lax.ppermute(given, "section", SWAP)
-    loss = with_partner(with_partner(loss, "y", 1), "y", 2)
     mine = row_half(one_three[: 2 * half], section).astype(F32) + row_half(two, section)
     return kept[7 * half :] + mine + got, loss
 
@@ -182,13 +181,14 @@
             place += size
     for load in loads:
         load.start()
-    for load in loads:
-        load.wait()
+    needed = (loads[:1], loads[1:4], loads[4:5], loads[5:])
 
     total = jnp.zeros((1, count), F32)
     step = place // 4
     for k in range(4):
         start, stop = k * step, (k + 1) * step
+        for load in needed[k]:
+            load.wait()
         marks = rows[start:stop, width : width + 2].astype(F32)
         wanted = marks[:, 0:1] * LANES + marks[:, 1:2]
         dots = lax.dot_general(
@@ -278,17 +278,18 @@
         scale, bias, slides, pieces, reports_all, columns[None, :]
     )
     back = lax.ppermute(sent, "section", SWAP)
-    loss = with_partner(loss, "tensor", 1)
     report_part = report_part.astype(SENT).reshape(n_plane, quarter, width)
-    report_part, loss = tied(report_part, loss)
-    loss = with_partner(loss, "xl", 1)
-    report_part, loss, weight = tied(report_part, loss, weight)
+    report_part, weight = tied(report_part, weight)
     report_terms = exchanged(report_part, PLANE)
     loss = with_partner(loss, "section", 1)
     back, loss = tied(back, loss)
     kept = jnp.dot(weight, reports_all, preferred_element_type=F32) + back
     slide_grad, loss = summed_over_z(kept, section, loss)
+    report_terms, loss = tied(report_terms, loss)
     report_grad = report_terms.astype(F32).sum(axis=0)
+    loss, report_grad = tied(with_partner(loss, "tensor", 1), report_grad)
+    loss, slide_grad = tied(with_partner(loss, "xl", 1), slide_grad)
+    loss = with_partner(with_partner(loss, "y", 1), "y", 2)
     return (loss[0, :1] / total, slide_grad, report_grad)
 
 

time: 118 us -> 124 us (1.051)
  other arithmetic: 6.36 us -> 9.51 us
  waiting for transfers between devices: 51.4 us -> 54.1 us
    ppermute x8, waiting for transfers between devices: 21.3 us -> 24 us  [with_partner(): return value + lax.ppermute(value, axis, pairs)]
    another operation x0 -> x1, other arithmetic: none -> 2.24 us
    reduce_sum x1, other arithmetic: 2.44 us -> 1.01 us  [local(): report_grad = report_terms.astype(F32).sum(axis=0)]
  transfers between devices with their start and end apart: 23 -> 23, of which waited for: 11 -> 12; matrix products, arithmetic and copies ran while one was open for 6% -> 8% of each run, Pallas kernels for 0% -> 0%
where the time goes in v12:
time: 124 us
  waiting for transfers between devices  54.1 us (44%)
  starting transfers between devices  40.5 us (33%)
  Pallas kernels  12.2 us (10%)
  other arithmetic  9.51 us (8%)
  between operations  3.35 us (3%)
  local copies, waits for them, and re-layouts  2.5 us (2%)
  matrix products  1.96 us (2%)
    ppermute x8, waiting for transfers between devices, with_partner(): return value + lax.ppermute(value, axis, pairs)  24 us
    ppermute x6, waiting for transfers between devices, along_z(): return lax.ppermute(array, ('z', 'section'), pairs)  17.7 us
    all_to_all x2, starting transfers between devices, exchanged(): return lax.all_to_all(parts, axes, split_axis=0, concat_axis=0, tiled=True)  14.7 us
    ppermute x6, starting transfers between devices, along_z(): return lax.ppermute(array, ('z', 'section'), pairs)  13.7 us
    ppermute x1, waiting for transfers between devices, tower(): raw = own + lax.ppermute(sent, 'tensor', SWAP)  9.91 us
    ppermute x8, starting transfers between devices, with_partner(): return value + lax.ppermute(value, axis, pairs)  8.46 us
    pallas_call x1, Pallas kernels, scored(): pl.pallas_call(score_kernel, in_specs=[scalar] * 3 + [pl.BlockSpec(memory...  7.69 us
    pallas_call x1, Pallas kernels, tower(): pl.pallas_call(tower_kernel, in_specs=[pl.BlockSpec(memory_space=pltpu.SM...  4.54 us
  transfers between devices with their start and end apart: 23, of which 12 were waited for; matrix products, arithmetic and copies ran while one was open for 8% of the time, Pallas kernels for 0%

profile of v12, /device:TPU:4, one launch (start us, length us, event | category | flops | bytes accessed | tf_op | source)
XLA Modules:
  0.0 124.1 jit_solution(15407289773150710360)
XLA Ops:
  0.6 4.5 %tower.1 = (f32[96,1024]{1,0:T(8,128)S(1)}, f32[96,1024]{1,0:T(8,128)S(1)}) custom-call(s32[1]{0:T(128)} %bitcast.1.spot, bf16[192,1024]{1,0:T(8,128)(2,1)} %bitcast.16, bf16[1024,2048]{1,0:T(8,128)(2,1)} %bitcast.14, bf16[2048,1024]{1,0:T(8,128)(2,1)} %bitcast.15), custom_call_target="tpu_custom_call" | custom-call | tf_op jit(solution)/shard_map/tower/pallas_call | solution.py:131
  5.2 2.3 %collective-permute-start = (f32[96,1024]{1,0:T(8,128)S(1)}, f32[96,1024]{1,0:T(8,128)S(1)}, u32[]{:S(2)}, u32[]{:S(2)}) collective-permute-start(f32[96,1024]{1,0:T(8,128)S(1)} %get-tuple-element.29), channel_id=1, source_target_pairs={{0,1},{1,0},{2,3},{3,2},{4,5},{5,4},{6,7},{7,6},{8,9},{9,8},{10,11... | collective-permute-start | bytes 1179656 | tf_op jit(solution)/shard_map/ppermute | solution.py:148
  7.7 9.9 %collective-permute-done = f32[96,1024]{1,0:T(8,128)S(1)} collective-permute-done((f32[96,1024]{1,0:T(8,128)S(1)}, f32[96,1024]{1,0:T(8,128)S(1)}, u32[]{:S(2)}, u32[]{:S(2)}) %collective-permute-start) | collective-permute-done | bytes 393248 | tf_op jit(solution)/shard_map/ppermute | solution.py:148
  17.6 0.1 multiply_reduce_fusion
  17.8 0.1 multiply_convert_fusion
  17.9 0.1 collective-permute-start.1
  18.0 0.1 select_convert_fusion
  18.1 1.3 %collective-permute-done.1 = bf16[96,1024]{1,0:T(8,128)(2,1)S(1)} collective-permute-done((bf16[96,1024]{1,0:T(8,128)(2,1)S(1)}, bf16[96,1024]{1,0:T(8,128)(2,1)S(1)}, u32[]{:S(2)}, u32[]{:S(2)}) %collective-permute-start.1) | collective-permute-done | bytes 196640 | tf_op jit(solution)/shard_map/ppermute | solution.py:263
  19.4 0.1 broadcast_select_fusion
  19.6 1.4 %broadcast_in_dim.29 = bf16[16,48,1024]{2,1,0:T(8,128)(2,1)} broadcast(bf16[48,1024]{1,0:T(8,128)(2,1)S(1)} %dynamic-slice_select_fusion), dimensions={1,2} | broadcast | bytes 1671168 | tf_op jit(solution)/shard_map/broadcast_in_dim | solution.py:267
  21.0 7.5 %all-to-all-start = ((bf16[16,48,1024]{2,1,0:T(8,128)(2,1)}), bf16[16,48,1024]{2,1,0:T(8,128)(2,1)S(1)}, u32[]{:S(2)}, u32[]{:S(2)}) async-start(bf16[16,48,1024]{2,1,0:T(8,128)(2,1)} %broadcast_in_dim.29), calls=%async_computation | async-start | bytes 3145728 | tf_op jit(solution)/shard_map/all_to_all | solution.py:20
  28.4 3.3 %collective-permute-start.2 = (bf16[96,1152]{1,0:T(8,128)(2,1)S(1)}, bf16[96,1152]{1,0:T(8,128)(2,1)S(1)}, u32[]{:S(2)}, u32[]{:S(2)}) collective-permute-start(bf16[96,1152]{1,0:T(8,128)(2,1)S(1)} %pad_maximum_fusion.1.own), channel_id=1, source_target_pairs={{0,8},{2,26},{4,12},{6,30},{8,16},{10,2},{12,20},{14,6},{16,24},{1... | collective-permute-start | bytes 663560 | tf_op jit(solution)/shard_map/ppermute | solution.py:33
  31.7 7.6 %collective-permute-done.2.two = bf16[96,1152]{1,0:T(8,128)(2,1)S(1)} collective-permute-done((bf16[96,1152]{1,0:T(8,128)(2,1)S(1)}, bf16[96,1152]{1,0:T(8,128)(2,1)S(1)}, u32[]{:S(2)}, u32[]{:S(2)}) %collective-permute-start.2) | collective-permute-done | bytes 221216 | tf_op jit(solution)/shard_map/ppermute | solution.py:33
  39.3 2.8 %collective-permute-start.3 = (bf16[192,1152]{1,0:T(8,128)(2,1)S(1)}, bf16[192,1152]{1,0:T(8,128)(2,1)S(1)}, u32[]{:S(2)}, u32[]{:S(2)}) collective-permute-start(bf16[192,1152]{1,0:T(8,128)(2,1)S(1)} %pad_maximum_fusion), channel_id=1, source_target_pairs={{0,4},{2,30},{4,8},{6,2},{8,12},{10,6},{12,16},{14,10},{16,20},{18... | collective-permute-start | bytes 1327112 | tf_op jit(solution)/shard_map/ppermute | solution.py:33
  42.2 0.4 collective-permute-start.4
  42.6 10.1 %collective-permute-done.4.four = bf16[48,1152]{1,0:T(8,128)(2,1)S(1)} collective-permute-done((bf16[48,1152]{1,0:T(8,128)(2,1)S(1)}, bf16[48,1152]{1,0:T(8,128)(2,1)S(1)}, u32[]{:S(2)}, u32[]{:S(2)}) %collective-permute-start.4) | collective-permute-done | bytes 110624 | tf_op jit(solution)/shard_map/ppermute | solution.py:33
  52.8 0.5 collective-permute-start.6
  54.6 0.4 collective-permute-start.7
  55.0 1.2 collective-permute-done.7.four_other
  56.2 0.6 copy-done.8
  56.8 0.2 copy-done.5
  57.0 7.7 %scores.1 = (bf16[384,768]{1,0:T(8,128)(2,1)S(1)}, f32[384,1024]{1,0:T(8,128)S(1)}, f32[768,1024]{1,0:T(8,128)S(1)}, f32[1,128]{1,0:T(1,128)S(1)}) custom-call(s32[1]{0:T(128)} %bitcast.spot, f32[1]{0:T(128)S(6)} %copy.9.scale, f32[1]{0:T(128)S(6)} %copy.10.bias, bf16[96,1152]{1,0:T(8,128)(2,1)} %copy-done, bf16[192,1152]{1,0:T(8,128)(2,1)} %copy-done.4, ...), custom_call_target="tpu_custom_call" | custom-call | tf_op jit(solution)/shard_map/scores/pallas_call | solution.py:222
  64.7 0.2 collective-permute-start.8
  64.9 0.4 collective-permute-start.9
  65.3 1.5 %convert_element_type.45 = f16[768,1024]{1,0:T(8,128)(2,1)} convert(f32[768,1024]{1,0:T(8,128)S(1)} %get-tuple-element.34) | non-fusion elementwise | flops 786432 | bytes 4718592 | tf_op jit(solution)/shard_map/convert_element_type | solution.py:281
  66.8 2.0 %fusion.9 = f32[384,1024]{1,0:T(8,128)} fusion(bf16[384,768]{1,0:T(8,128)(2,1)S(1)} %get-tuple-element.37, bf16[768,1024]{1,0:T(8,128)(2,1)S(1)} %bitcast.12), kind=kOutput, calls=%fused_computation.42 | convolution fusion | flops 603979776 | bytes 3735552 | tf_op jit(solution)/shard_map/dot_general | solution.py:286
  68.8 7.2 %all-to-all-start.1 = ((f16[16,48,1024]{2,1,0:T(8,128)(2,1)}), f16[16,48,1024]{2,1,0:T(8,128)(2,1)S(1)}, u32[]{:S(2)}, u32[]{:S(2)}) async-start(f16[16,48,1024]{2,1,0:T(8,128)(2,1)} %bitcast.13), calls=%async_computation.1 | async-start | bytes 3145728 | tf_op jit(solution)/shard_map/all_to_all | solution.py:20
  76.0 2.2 %fusion.8 = (f16[384,1024]{1,0:T(8,128)(2,1)S(1)}, f32[384,1024]{1,0:T(8,128)S(1)}) fusion(f32[384,1024]{1,0:T(8,128)} %fusion.9, f32[384,1024]{1,0:T(8,128)} %collective-permute-done.8), kind=kLoop, calls=%fused_computation.41 | loop fusion | flops 786432 | bytes 5505024 | tf_op jit(solution)/shard_map/convert.1
  78.3 2.2 %collective-permute-start.10 = (f16[192,1024]{1,0:T(8,128)(2,1)S(1)}, f16[192,1024]{1,0:T(8,128)(2,1)S(1)}, u32[]{:S(2)}, u32[]{:S(2)}) collective-permute-start(f16[192,1024]{1,0:T(8,128)(2,1)S(1)} %slice.36), channel_id=1, source_target_pairs={{0,28},{2,6},{4,0},{6,10},{8,4},{10,14},{12,8},{14,18},{16,12},{18... | collective-permute-start | bytes 1179656 | tf_op jit(solution)/shard_map/ppermute | solution.py:33
  80.5 3.8 %collective-permute-start.11 = (f16[48,1024]{1,0:T(8,128)(2,1)S(1)}, f16[48,1024]{1,0:T(8,128)(2,1)S(1)}, u32[]{:S(2)}, u32[]{:S(2)}) collective-permute-start(f16[48,1024]{1,0:T(8,128)(2,1)S(1)} %slice.37), channel_id=1, source_target_pairs={{0,24},{2,10},{4,28},{6,14},{8,0},{10,18},{12,4},{14,22},{16,8},{1... | collective-permute-start | bytes 294920 | tf_op jit(solution)/shard_map/ppermute | solution.py:33
  84.3 4.0 %collective-permute-done.12 = f32[1,128]{1,0:T(1,128)S(1)} collective-permute-done((f32[1,128]{1,0:T(1,128)S(1)}, f32[1,128]{1,0:T(1,128)S(1)}, u32[]{:S(2)}, u32[]{:S(2)}) %collective-permute-start.12) | collective-permute-done | bytes 544 | tf_op jit(solution)/shard_map/ppermute | solution.py:58
  88.3 4.4 %collective-permute-done.13 = f32[1,128]{1,0:T(1,128)S(1)} collective-permute-done((f32[1,128]{1,0:T(1,128)S(1)}, f32[1,128]{1,0:T(1,128)S(1)}, u32[]{:S(2)}, u32[]{:S(2)}) %collective-permute-start.13) | collective-permute-done | bytes 544 | tf_op jit(solution)/shard_map/ppermute | solution.py:58
  92.8 0.7 fusion
  93.6 1.2 collective-permute-start.14
  94.8 2.4 %collective-permute-start.15 = (f32[1,128]{1,0:T(1,128)S(1)}, f32[1,128]{1,0:T(1,128)S(1)}, u32[]{:S(2)}, u32[]{:S(2)}) collective-permute-start(f32[1,128]{1,0:T(1,128)S(1)} %add.195), channel_id=1, source_target_pairs={{0,16},{4,20},{8,24},{12,28},{16,0},{20,4},{24,8},{28,12},{1,17},{... | collective-permute-start | bytes 1544 | tf_op jit(solution)/shard_map/ppermute | solution.py:58
  97.2 5.1 %collective-permute-done.15 = f32[1,128]{1,0:T(1,128)S(1)} collective-permute-done((f32[1,128]{1,0:T(1,128)S(1)}, f32[1,128]{1,0:T(1,128)S(1)}, u32[]{:S(2)}, u32[]{:S(2)}) %collective-permute-start.15) | collective-permute-done | bytes 544 | tf_op jit(solution)/shard_map/ppermute | solution.py:58
  102.3 1.0 convert_element_type.51
  103.3 0.7 dynamic-slice_add_fusion
  104.0 0.1 collective-permute-start.16
  104.2 1.0 convert_reduce_fusion
  105.2 4.0 %collective-permute-done.16 = f32[1,128]{1,0:T(1,128)S(1)} collective-permute-done((f32[1,128]{1,0:T(1,128)S(1)}, f32[1,128]{1,0:T(1,128)S(1)}, u32[]{:S(2)}, u32[]{:S(2)}) %collective-permute-start.16) | collective-permute-done | bytes 544 | tf_op jit(solution)/shard_map/ppermute | solution.py:58
  109.2 1.2 collective-permute-start.17
  110.3 2.4 %collective-permute-done.17 = f32[1,128]{1,0:T(1,128)S(1)} collective-permute-done((f32[1,128]{1,0:T(1,128)S(1)}, f32[1,128]{1,0:T(1,128)S(1)}, u32[]{:S(2)}, u32[]{:S(2)}) %collective-permute-start.17) | collective-permute-done | bytes 544 | tf_op jit(solution)/shard_map/ppermute | solution.py:58
  112.7 1.7 %fusion.3 = f32[48,1024]{1,0:T(8,128)} fusion(f32[48,1024]{1,0:T(8,128)} %collective-permute-done.18, f32[384,1024]{1,0:T(8,128)S(1)} %get-tuple-element.54, f32[96,1024]{1,0:T(8,128)S(1)} %convert_element_type.51, s32[]{:T(128)S(6)} %select_n.119, f16[96,1024]{1,0:T(8,128)(2,1)S(1)} %copy-done.3), kind=kLoop, calls=%fused_computation.12 | loop fusion | flops 196608 | bytes 884740 | tf_op jit(solution)/shard_map/add | solution.py:78
  114.4 1.5 %collective-permute-start.19 = (f32[1,128]{1,0:T(1,128)S(1)}, f32[1,128]{1,0:T(1,128)S(1)}, u32[]{:S(2)}, u32[]{:S(2)}) collective-permute-start(f32[1,128]{1,0:T(1,128)S(1)} %add.201), channel_id=1, source_target_pairs={{0,32},{32,0},{64,96},{96,64},{1,33},{33,1},{65,97},{97,65},{2,34}... | collective-permute-start | bytes 1544 | tf_op jit(solution)/shard_map/ppermute | solution.py:58
  115.8 2.1 %collective-permute-done.19 = f32[1,128]{1,0:T(1,128)S(1)} collective-permute-done((f32[1,128]{1,0:T(1,128)S(1)}, f32[1,128]{1,0:T(1,128)S(1)}, u32[]{:S(2)}, u32[]{:S(2)}) %collective-permute-start.19) | collective-permute-done | bytes 544 | tf_op jit(solution)/shard_map/ppermute | solution.py:58
  117.9 3.0 %collective-permute-start.20 = (f32[1,128]{1,0:T(1,128)S(1)}, f32[1,128]{1,0:T(1,128)S(1)}, u32[]{:S(2)}, u32[]{:S(2)}) collective-permute-start(f32[1,128]{1,0:T(1,128)S(1)} %add.207), channel_id=1, source_target_pairs={{0,64},{32,96},{64,0},{96,32},{1,65},{33,97},{65,1},{97,33},{2,66}... | collective-permute-start | bytes 1544 | tf_op jit(solution)/shard_map/ppermute | solution.py:58
  120.9 2.1 %collective-permute-done.20 = f32[1,128]{1,0:T(1,128)S(1)} collective-permute-done((f32[1,128]{1,0:T(1,128)S(1)}, f32[1,128]{1,0:T(1,128)S(1)}, u32[]{:S(2)}, u32[]{:S(2)}) %collective-permute-start.20) | collective-permute-done | bytes 544 | tf_op jit(solution)/shard_map/ppermute | solution.py:58
  (56 shorter events, 0.7 us)
Async XLA Ops:
  0.6 6.9 %copy-start.9 = (s32[192]{0:T(256)S(1)}, s32[192]{0:T(256)}, u32[]{:S(2)}) copy-start(s32[192]{0:T(256)} %param.9) | copy-start | bytes 2308
  5.2 12.4 %collective-permute-start = (f32[96,1024]{1,0:T(8,128)S(1)}, f32[96,1024]{1,0:T(8,128)S(1)}, u32[]{:S(2)}, u32[]{:S(2)}) collective-permute-start(f32[96,1024]{1,0:T(8,128)S(1)} %get-tuple-element.29), channel_id=1, source_target_pairs={{0,1},{1,0},{2,3},{3,2},{4,5},{5,4},{6,7},{7,6},{8,9},{9,8},{10,11... | collective-permute-start | bytes 1179656 | tf_op jit(solution)/shard_map/ppermute | solution.py:148
  17.9 1.5 %collective-permute-start.1 = (bf16[96,1024]{1,0:T(8,128)(2,1)S(1)}, bf16[96,1024]{1,0:T(8,128)(2,1)S(1)}, u32[]{:S(2)}, u32[]{:S(2)}) collective-permute-start(bf16[96,1024]{1,0:T(8,128)(2,1)S(1)} %multiply_convert_fusion), channel_id=1, source_target_pairs={{0,2},{2,0},{1,3},{3,1},{4,6},{6,4},{5,7},{7,5},{8,10},{10,8},{9,1... | collective-permute-start | bytes 589832 | tf_op jit(solution)/shard_map/ppermute | solution.py:263
  19.6 19.7 %copy-start = (bf16[96,1152]{1,0:T(8,128)(2,1)}, bf16[96,1152]{1,0:T(8,128)(2,1)S(1)}, u32[]{:S(2)}) copy-start(bf16[96,1152]{1,0:T(8,128)(2,1)S(1)} %pad_maximum_fusion.1.own) | copy-start | bytes 663556
  21.0 35.2 %all-to-all-start = ((bf16[16,48,1024]{2,1,0:T(8,128)(2,1)}), bf16[16,48,1024]{2,1,0:T(8,128)(2,1)S(1)}, u32[]{:S(2)}, u32[]{:S(2)}) async-start(bf16[16,48,1024]{2,1,0:T(8,128)(2,1)} %broadcast_in_dim.29), calls=%async_computation | async-start | bytes 3145728 | tf_op jit(solution)/shard_map/all_to_all | solution.py:20
  28.4 10.8 %collective-permute-start.2 = (bf16[96,1152]{1,0:T(8,128)(2,1)S(1)}, bf16[96,1152]{1,0:T(8,128)(2,1)S(1)}, u32[]{:S(2)}, u32[]{:S(2)}) collective-permute-start(bf16[96,1152]{1,0:T(8,128)(2,1)S(1)} %pad_maximum_fusion.1.own), channel_id=1, source_target_pairs={{0,8},{2,26},{4,12},{6,30},{8,16},{10,2},{12,20},{14,6},{16,24},{1... | collective-permute-start | bytes 663560 | tf_op jit(solution)/shard_map/ppermute | solution.py:33
  39.3 16.9 %copy-start.1 = (bf16[96,1152]{1,0:T(8,128)(2,1)}, bf16[96,1152]{1,0:T(8,128)(2,1)S(1)}, u32[]{:S(2)}) copy-start(bf16[96,1152]{1,0:T(8,128)(2,1)S(1)} %collective-permute-done.2.two) | copy-start | bytes 663556
  39.3 13.4 %collective-permute-start.3 = (bf16[192,1152]{1,0:T(8,128)(2,1)S(1)}, bf16[192,1152]{1,0:T(8,128)(2,1)S(1)}, u32[]{:S(2)}, u32[]{:S(2)}) collective-permute-start(bf16[192,1152]{1,0:T(8,128)(2,1)S(1)} %pad_maximum_fusion), channel_id=1, source_target_pairs={{0,4},{2,30},{4,8},{6,2},{8,12},{10,6},{12,16},{14,10},{16,20},{18... | collective-permute-start | bytes 1327112 | tf_op jit(solution)/shard_map/ppermute | solution.py:33
  42.2 10.5 %collective-permute-start.4 = (bf16[48,1152]{1,0:T(8,128)(2,1)S(1)}, bf16[48,1152]{1,0:T(8,128)(2,1)S(1)}, u32[]{:S(2)}, u32[]{:S(2)}) collective-permute-start(bf16[48,1152]{1,0:T(8,128)(2,1)S(1)} %constant_dynamic-slice_fusion), channel_id=1, source_target_pairs={{0,8},{2,26},{4,12},{6,30},{8,16},{10,2},{12,20},{14,6},{16,24},{1... | collective-permute-start | bytes 331784 | tf_op jit(solution)/shard_map/ppermute | solution.py:33
  52.7 4.3 %copy-start.7 = (bf16[48,1152]{1,0:T(8,128)(2,1)}, bf16[48,1152]{1,0:T(8,128)(2,1)S(1)}, u32[]{:S(2)}) copy-start(bf16[48,1152]{1,0:T(8,128)(2,1)S(1)} %collective-permute-done.4.four) | copy-start | bytes 331780
  52.7 3.5 %copy-start.4 = (bf16[192,1152]{1,0:T(8,128)(2,1)}, bf16[192,1152]{1,0:T(8,128)(2,1)S(1)}, u32[]{:S(2)}) copy-start(bf16[192,1152]{1,0:T(8,128)(2,1)S(1)} %collective-permute-done.3.one_three) | copy-start | bytes 1327108
  52.7 3.5 %collective-permute-start.5 = (bf16[192,1152]{1,0:T(8,128)(2,1)S(1)}, bf16[192,1152]{1,0:T(8,128)(2,1)S(1)}, u32[]{:S(2)}, u32[]{:S(2)}) collective-permute-start(bf16[192,1152]{1,0:T(8,128)(2,1)S(1)} %collective-permute-done.3.one_three), channel_id=1, source_target_pairs={{0,2},{2,0},{1,3},{3,1},{4,6},{6,4},{5,7},{7,5},{8,10},{10,8},{9,1... | collective-permute-start | bytes 1327112 | tf_op jit(solution)/shard_map/ppermute | solution.py:47
  52.8 2.2 %collective-permute-start.6 = (bf16[96,1152]{1,0:T(8,128)(2,1)S(1)}, bf16[96,1152]{1,0:T(8,128)(2,1)S(1)}, u32[]{:S(2)}, u32[]{:S(2)}) collective-permute-start(bf16[96,1152]{1,0:T(8,128)(2,1)S(1)} %collective-permute-done.2.two), channel_id=1, source_target_pairs={{0,2},{2,0},{1,3},{3,1},{4,6},{6,4},{5,7},{7,5},{8,10},{10,8},{9,1... | collective-permute-start | bytes 663560 | tf_op jit(solution)/shard_map/ppermute | solution.py:43
  54.6 1.6 %collective-permute-start.7 = (bf16[48,1152]{1,0:T(8,128)(2,1)S(1)}, bf16[48,1152]{1,0:T(8,128)(2,1)S(1)}, u32[]{:S(2)}, u32[]{:S(2)}) collective-permute-start(bf16[48,1152]{1,0:T(8,128)(2,1)S(1)} %collective-permute-done.4.four), channel_id=1, source_target_pairs={{0,2},{2,0},{1,3},{3,1},{4,6},{6,4},{5,7},{7,5},{8,10},{10,8},{9,1... | collective-permute-start | bytes 331784 | tf_op jit(solution)/shard_map/ppermute | solution.py:48
  55.0 2.0 %copy-start.6 = (bf16[96,1152]{1,0:T(8,128)(2,1)}, bf16[96,1152]{1,0:T(8,128)(2,1)S(1)}, u32[]{:S(2)}) copy-start(bf16[96,1152]{1,0:T(8,128)(2,1)S(1)} %collective-permute-done.6.two_other) | copy-start | bytes 663556
  56.2 0.6 copy-start.8
  56.2 0.8 copy-start.5
  64.7 11.3 %collective-permute-start.8 = (f32[384,1024]{1,0:T(8,128)S(1)}, f32[384,1024]{1,0:T(8,128)}, u32[]{:S(2)}, u32[]{:S(2)}) collective-permute-start(f32[384,1024]{1,0:T(8,128)S(1)} %get-tuple-element.38), channel_id=1, source_target_pairs={{0,2},{2,0},{1,3},{3,1},{4,6},{6,4},{5,7},{7,5},{8,10},{10,8},{9,1... | collective-permute-start | bytes 4718600 | tf_op jit(solution)/shard_map/ppermute | solution.py:280
  64.9 11.1 %collective-permute-start.9 = (f32[1,128]{1,0:T(1,128)S(1)}, f32[1,128]{1,0:T(1,128)S(1)}, u32[]{:S(2)}, u32[]{:S(2)}) collective-permute-start(f32[1,128]{1,0:T(1,128)S(1)} %get-tuple-element.39), channel_id=1, source_target_pairs={{0,2},{2,0},{1,3},{3,1},{4,6},{6,4},{5,7},{7,5},{8,10},{10,8},{9,1... | collective-permute-start | bytes 1544 | tf_op jit(solution)/shard_map/ppermute | solution.py:58
  68.8 35.2 %all-to-all-start.1 = ((f16[16,48,1024]{2,1,0:T(8,128)(2,1)}), f16[16,48,1024]{2,1,0:T(8,128)(2,1)S(1)}, u32[]{:S(2)}, u32[]{:S(2)}) async-start(f16[16,48,1024]{2,1,0:T(8,128)(2,1)} %bitcast.13), calls=%async_computation.1 | async-start | bytes 3145728 | tf_op jit(solution)/shard_map/all_to_all | solution.py:20
  78.3 14.4 %collective-permute-start.10 = (f16[192,1024]{1,0:T(8,128)(2,1)S(1)}, f16[192,1024]{1,0:T(8,128)(2,1)S(1)}, u32[]{:S(2)}, u32[]{:S(2)}) collective-permute-start(f16[192,1024]{1,0:T(8,128)(2,1)S(1)} %slice.36), channel_id=1, source_target_pairs={{0,28},{2,6},{4,0},{6,10},{8,4},{10,14},{12,8},{14,18},{16,12},{18... | collective-permute-start | bytes 1179656 | tf_op jit(solution)/shard_map/ppermute | solution.py:33
  80.5 12.3 %collective-permute-start.11 = (f16[48,1024]{1,0:T(8,128)(2,1)S(1)}, f16[48,1024]{1,0:T(8,128)(2,1)S(1)}, u32[]{:S(2)}, u32[]{:S(2)}) collective-permute-start(f16[48,1024]{1,0:T(8,128)(2,1)S(1)} %slice.37), channel_id=1, source_target_pairs={{0,24},{2,10},{4,28},{6,14},{8,0},{10,18},{12,4},{14,22},{16,8},{1... | collective-permute-start | bytes 294920 | tf_op jit(solution)/shard_map/ppermute | solution.py:33
  84.3 4.0 %collective-permute-start.12 = (f32[1,128]{1,0:T(1,128)S(1)}, f32[1,128]{1,0:T(1,128)S(1)}, u32[]{:S(2)}, u32[]{:S(2)}) collective-permute-start(f32[1,128]{1,0:T(1,128)S(1)} %add.192), channel_id=1, source_target_pairs={{0,4},{4,0},{8,12},{12,8},{16,20},{20,16},{24,28},{28,24},{1,5},{5... | collective-permute-start | bytes 1544 | tf_op jit(solution)/shard_map/ppermute | solution.py:58
  88.3 4.4 %collective-permute-start.13 = (f32[1,128]{1,0:T(1,128)S(1)}, f32[1,128]{1,0:T(1,128)S(1)}, u32[]{:S(2)}, u32[]{:S(2)}) collective-permute-start(f32[1,128]{1,0:T(1,128)S(1)} %add.194), channel_id=1, source_target_pairs={{0,8},{4,12},{8,0},{12,4},{16,24},{20,28},{24,16},{28,20},{1,9},{5... | collective-permute-start | bytes 1544 | tf_op jit(solution)/shard_map/ppermute | solution.py:58
  93.6 8.7 %collective-permute-start.14 = (f16[96,1024]{1,0:T(8,128)(2,1)}, f16[96,1024]{1,0:T(8,128)(2,1)}, u32[]{:S(2)}, u32[]{:S(2)}) collective-permute-start(f16[96,1024]{1,0:T(8,128)(2,1)} %fusion), channel_id=1, source_target_pairs={{0,24},{2,10},{4,28},{6,14},{8,0},{10,18},{12,4},{14,22},{16,8},{1... | collective-permute-start | bytes 589832 | tf_op jit(solution)/shard_map/ppermute | solution.py:33
  94.8 7.5 %collective-permute-start.15 = (f32[1,128]{1,0:T(1,128)S(1)}, f32[1,128]{1,0:T(1,128)S(1)}, u32[]{:S(2)}, u32[]{:S(2)}) collective-permute-start(f32[1,128]{1,0:T(1,128)S(1)} %add.195), channel_id=1, source_target_pairs={{0,16},{4,20},{8,24},{12,28},{16,0},{20,4},{24,8},{28,12},{1,17},{... | collective-permute-start | bytes 1544 | tf_op jit(solution)/shard_map/ppermute | solution.py:58
  97.2 6.8 %copy-start.2 = (f16[96,1024]{1,0:T(8,128)(2,1)}, f16[96,1024]{1,0:T(8,128)(2,1)S(1)}, u32[]{:S(2)}) copy-start(f16[96,1024]{1,0:T(8,128)(2,1)S(1)} %slice.33) | copy-start | bytes 589828
  104.0 8.7 %collective-permute-start.18 = (f32[48,1024]{1,0:T(8,128)}, f32[48,1024]{1,0:T(8,128)}, u32[]{:S(2)}, u32[]{:S(2)}) collective-permute-start(f32[48,1024]{1,0:T(8,128)} %dynamic-slice_add_fusion), channel_id=1, source_target_pairs={{0,2},{2,0},{1,3},{3,1},{4,6},{6,4},{5,7},{7,5},{8,10},{10,8},{9,1... | collective-permute-start | bytes 589832 | tf_op jit(solution)/shard_map/ppermute | solution.py:76
  104.0 8.7 %copy-start.3 = (f16[96,1024]{1,0:T(8,128)(2,1)S(1)}, f16[96,1024]{1,0:T(8,128)(2,1)}, u32[]{:S(2)}) copy-start(f16[96,1024]{1,0:T(8,128)(2,1)} %copy-done.2) | copy-start | bytes 589828
  104.0 5.1 %collective-permute-start.16 = (f32[1,128]{1,0:T(1,128)S(1)}, f32[1,128]{1,0:T(1,128)S(1)}, u32[]{:S(2)}, u32[]{:S(2)}) collective-permute-start(f32[1,128]{1,0:T(1,128)S(1)} %add.199), channel_id=1, source_target_pairs={{0,1},{1,0},{2,3},{3,2},{4,5},{5,4},{6,7},{7,6},{8,9},{9,8},{10,11... | collective-permute-start | bytes 1544 | tf_op jit(solution)/shard_map/ppermute | solution.py:58
  109.2 3.5 %collective-permute-start.17 = (f32[1,128]{1,0:T(1,128)S(1)}, f32[1,128]{1,0:T(1,128)S(1)}, u32[]{:S(2)}, u32[]{:S(2)}) collective-permute-start(f32[1,128]{1,0:T(1,128)S(1)} %add.200), channel_id=1, source_target_pairs={{0,128},{128,0},{1,129},{129,1},{2,130},{130,2},{3,131},{131,3},{4... | collective-permute-start | bytes 1544 | tf_op jit(solution)/shard_map/ppermute | solution.py:58
  114.4 3.5 %collective-permute-start.19 = (f32[1,128]{1,0:T(1,128)S(1)}, f32[1,128]{1,0:T(1,128)S(1)}, u32[]{:S(2)}, u32[]{:S(2)}) collective-permute-start(f32[1,128]{1,0:T(1,128)S(1)} %add.201), channel_id=1, source_target_pairs={{0,32},{32,0},{64,96},{96,64},{1,33},{33,1},{65,97},{97,65},{2,34}... | collective-permute-start | bytes 1544 | tf_op jit(solution)/shard_map/ppermute | solution.py:58
  117.9 5.0 %collective-permute-start.20 = (f32[1,128]{1,0:T(1,128)S(1)}, f32[1,128]{1,0:T(1,128)S(1)}, u32[]{:S(2)}, u32[]{:S(2)}) collective-permute-start(f32[1,128]{1,0:T(1,128)S(1)} %add.207), channel_id=1, source_target_pairs={{0,64},{32,96},{64,0},{96,32},{1,65},{33,97},{65,1},{97,33},{2,66}... | collective-permute-start | bytes 1544 | tf_op jit(solution)/shard_map/ppermute | solution.py:58

commit v13 on v11

--- a/solution.py
+++ b/solution.py
@@ -38,15 +38,16 @@
     return lax.dynamic_slice_in_dim(array, which * half, half, 0)
 
 
-def gathered_over_z(own, section, reports):
+def gathered_over_z(own, section):
     two = along_z(own, 2)
-    two_swapped = lax.ppermute(two, "section", SWAP)
-    one_three = along_z(jnp.concatenate([own, two], axis=0), 1)
+    one = along_z(own, 1)
+    one, two = tied(one, two)
+    three = along_z(two, 1)
     four = along_z(row_half(two, section), 2)
-    one_three, four = tied(one_three, four)
-    others = [lax.ppermute(one_three, "section", SWAP), two_swapped]
-    others.append(lax.ppermute(four, "section", SWAP))
-    return [one_three, two, four, *others], reports
+    early = [lax.ppermute(piece, "section", SWAP) for piece in (one, two)]
+    three, four = tied(three, four)
+    late = [lax.ppermute(piece, "section", SWAP) for piece in (three, four)]
+    return [one, three, two, four, early[0], late[0], early[1], late[1]]
 
 
 def tied(*arrays):
@@ -74,7 +75,6 @@
     two = two.astype(F32)
     given = row_half(one_three[: 2 * half], 1 - section).astype(F32) + row_half(two, 1 - section)
     got = lax.ppermute(given, "section", SWAP)
-    loss = with_partner(with_partner(loss, "y", 1), "y", 2)
     mine = row_half(one_three[: 2 * half], section).astype(F32) + row_half(two, section)
     return kept[7 * half :] + mine + got, loss
 
@@ -160,8 +160,8 @@
 
 
 def score_kernel(
-    spot, scale, bias, own, one_three, two, four, one_three_other, two_other, four_other,
-    reports, columns, kept, sent, report_part, loss, rows, weight, sems,
+    spot, scale, bias, own, one, three, two, four, one_other, three_other, two_other,
+    four_other, reports, columns, kept, sent, report_part, loss, rows, weight, sems,
 ):
     count, width = reports.shape
     scale_value, bias_value = scale[0], bias[0]
@@ -169,13 +169,13 @@
     quarter = own.shape[0] // 2
     place = 0
     groups = (
-        (one_three, two, four, section),
-        (one_three_other, two_other, four_other, 1 - section),
+        (one, three, two, four, section),
+        (one_other, three_other, two_other, four_other, 1 - section),
     )
     loads = []
     for group in groups:
-        start = pl.multiple_of(group[3] * quarter, 16)
-        for part in (*group[:3], own.at[pl.ds(start, quarter), :]):
+        start = pl.multiple_of(group[4] * quarter, 16)
+        for part in (*group[:4], own.at[pl.ds(start, quarter), :]):
             size = part.shape[0]
             held = rows.at[pl.ds(place, size), :]
             loads.append(pltpu.make_async_copy(part, held, sems.at[len(loads)]))
@@ -221,7 +221,7 @@
     whole = pl.BlockSpec(memory_space=pltpu.VMEM)
     return pl.pallas_call(
         score_kernel,
-        in_specs=[scalar] * 3 + [pl.BlockSpec(memory_space=pltpu.HBM)] * 7 + [whole] * 2,
+        in_specs=[scalar] * 3 + [pl.BlockSpec(memory_space=pltpu.HBM)] * 9 + [whole] * 2,
         out_specs=[whole, whole, whole, whole],
         out_shape=[
             jax.ShapeDtypeStruct((rows // 2, count), jnp.bfloat16),
@@ -232,7 +232,7 @@
         scratch_shapes=[
             pltpu.VMEM((rows, own.shape[1]), jnp.bfloat16),
             pltpu.VMEM((rows, count), jnp.bfloat16),
-            pltpu.SemaphoreType.DMA((8,)),
+            pltpu.SemaphoreType.DMA((10,)),
         ],
         compiler_params=pltpu.CompilerParams(vmem_limit_bytes=12 * 1024 * 1024),
         name="scores",
@@ -267,7 +267,7 @@
     repeated = jnp.broadcast_to(reports, (n_plane, *reports.shape))
     repeated, slides = tied(repeated, slides)
     reports_all = exchanged(repeated, PLANE).reshape(n_plane * quarter, -1)
-    pieces, reports_all = gathered_over_z(slides, section, reports_all)
+    pieces = gathered_over_z(slides, section)
 
     place = jnp.arange(n_plane * quarter, dtype=jnp.int32)
     member, row = place // quarter, place % quarter
@@ -288,7 +288,10 @@
     back, loss = tied(back, loss)
     kept = jnp.dot(weight, reports_all, preferred_element_type=F32) + back
     slide_grad, loss = summed_over_z(kept, section, loss)
+    report_terms, loss = tied(report_terms, loss)
     report_grad = report_terms.astype(F32).sum(axis=0)
+    loss, report_grad = tied(with_partner(loss, "y", 1), report_grad)
+    loss = with_partner(loss, "y", 2)
     return (loss[0, :1] / total, slide_grad, report_grad)
 
 

time: 118 us -> 119 us (level)
    ppermute x8, waiting for transfers between devices: 21.3 us -> 23.7 us  [with_partner(): return value + lax.ppermute(value, axis, pairs)]
    ppermute x6 -> x7, waiting for transfers between devices: 17.7 us -> 16.5 us  [along_z(): return lax.ppermute(array, ('z', 'section'), pairs)]
    ppermute x6 -> x7, starting transfers between devices: 13.8 us -> 13.4 us  [along_z(): return lax.ppermute(array, ('z', 'section'), pairs)]
  transfers between devices with their start and end apart: 23 -> 25, of which waited for: 11 -> 12; matrix products, arithmetic and copies ran while one was open for 6% -> 6% of each run, Pallas kernels for 0% -> 0%
where the time goes in v13:
time: 119 us
  waiting for transfers between devices  52.4 us (44%)
  starting transfers between devices  40.5 us (34%)
  Pallas kernels  11.7 us (10%)
  other arithmetic  6.32 us (5%)
  between operations  3.42 us (3%)
  local copies, waits for them, and re-layouts  2.41 us (2%)
  matrix products  2.19 us (2%)
    ppermute x8, waiting for transfers between devices, with_partner(): return value + lax.ppermute(value, axis, pairs)  23.7 us
    ppermute x7, waiting for transfers between devices, along_z(): return lax.ppermute(array, ('z', 'section'), pairs)  16.5 us
    all_to_all x2, starting transfers between devices, exchanged(): return lax.all_to_all(parts, axes, split_axis=0, concat_axis=0, tiled=True)  14.7 us
    ppermute x7, starting transfers between devices, along_z(): return lax.ppermute(array, ('z', 'section'), pairs)  13.4 us
    ppermute x1, waiting for transfers between devices, tower(): raw = own + lax.ppermute(sent, 'tensor', SWAP)  9.91 us
    ppermute x8, starting transfers between devices, with_partner(): return value + lax.ppermute(value, axis, pairs)  8.13 us
    pallas_call x1, Pallas kernels, scored(): pl.pallas_call(score_kernel, in_specs=[scalar] * 3 + [pl.BlockSpec(memory...  7.14 us
    pallas_call x1, Pallas kernels, tower(): pl.pallas_call(tower_kernel, in_specs=[pl.BlockSpec(memory_space=pltpu.SM...  4.54 us
  transfers between devices with their start and end apart: 25, of which 12 were waited for; matrix products, arithmetic and copies ran while one was open for 6% of the time, Pallas kernels for 0%

profile of v13, /device:TPU:4, one launch (start us, length us, event | category | flops | bytes accessed | tf_op | source)
XLA Modules:
  0.0 118.9 jit_solution(16932582977067535955)
XLA Ops:
  0.6 4.5 %tower.1 = (f32[96,1024]{1,0:T(8,128)S(1)}, f32[96,1024]{1,0:T(8,128)S(1)}) custom-call(s32[1]{0:T(128)} %bitcast.1.spot, bf16[192,1024]{1,0:T(8,128)(2,1)} %bitcast.16, bf16[1024,2048]{1,0:T(8,128)(2,1)} %bitcast.14, bf16[2048,1024]{1,0:T(8,128)(2,1)} %bitcast.15), custom_call_target="tpu_custom_call" | custom-call | tf_op jit(solution)/shard_map/tower/pallas_call | solution.py:132
  5.2 2.3 %collective-permute-start = (f32[96,1024]{1,0:T(8,128)S(1)}, f32[96,1024]{1,0:T(8,128)S(1)}, u32[]{:S(2)}, u32[]{:S(2)}) collective-permute-start(f32[96,1024]{1,0:T(8,128)S(1)} %get-tuple-element.32), channel_id=1, source_target_pairs={{0,1},{1,0},{2,3},{3,2},{4,5},{5,4},{6,7},{7,6},{8,9},{9,8},{10,11... | collective-permute-start | bytes 1179656 | tf_op jit(solution)/shard_map/ppermute | solution.py:149
  7.5 0.1 reshape.258
  7.6 0.1 reshape.259
  7.7 9.9 %collective-permute-done = f32[96,1024]{1,0:T(8,128)S(1)} collective-permute-done((f32[96,1024]{1,0:T(8,128)S(1)}, f32[96,1024]{1,0:T(8,128)S(1)}, u32[]{:S(2)}, u32[]{:S(2)}) %collective-permute-start) | collective-permute-done | bytes 393248 | tf_op jit(solution)/shard_map/ppermute | solution.py:149
  17.6 0.1 multiply_reduce_fusion
  17.8 0.1 multiply_convert_fusion
  17.9 0.1 collective-permute-start.1
  18.0 0.1 select_convert_fusion
  18.1 1.3 %collective-permute-done.1 = bf16[96,1024]{1,0:T(8,128)(2,1)S(1)} collective-permute-done((bf16[96,1024]{1,0:T(8,128)(2,1)S(1)}, bf16[96,1024]{1,0:T(8,128)(2,1)S(1)}, u32[]{:S(2)}, u32[]{:S(2)}) %collective-permute-start.1) | collective-permute-done | bytes 196640 | tf_op jit(solution)/shard_map/ppermute | solution.py:263
  19.4 0.1 broadcast_select_fusion
  19.6 1.4 %broadcast_in_dim.29 = bf16[16,48,1024]{2,1,0:T(8,128)(2,1)} broadcast(bf16[48,1024]{1,0:T(8,128)(2,1)S(1)} %dynamic-slice_select_fusion), dimensions={1,2} | broadcast | bytes 1671168 | tf_op jit(solution)/shard_map/broadcast_in_dim | solution.py:267
  21.0 7.5 %all-to-all-start = ((bf16[16,48,1024]{2,1,0:T(8,128)(2,1)}), bf16[16,48,1024]{2,1,0:T(8,128)(2,1)S(1)}, u32[]{:S(2)}, u32[]{:S(2)}) async-start(bf16[16,48,1024]{2,1,0:T(8,128)(2,1)} %broadcast_in_dim.29), calls=%async_computation | async-start | bytes 3145728 | tf_op jit(solution)/shard_map/all_to_all | solution.py:20
  28.4 1.9 %collective-permute-start.2 = (bf16[96,1152]{1,0:T(8,128)(2,1)S(1)}, bf16[96,1152]{1,0:T(8,128)(2,1)S(1)}, u32[]{:S(2)}, u32[]{:S(2)}) collective-permute-start(bf16[96,1152]{1,0:T(8,128)(2,1)S(1)} %pad_maximum_fusion.own), channel_id=1, source_target_pairs={{0,4},{2,30},{4,8},{6,2},{8,12},{10,6},{12,16},{14,10},{16,20},{18... | collective-permute-start | bytes 663560 | tf_op jit(solution)/shard_map/ppermute | solution.py:33
  30.3 3.3 %collective-permute-start.3 = (bf16[96,1152]{1,0:T(8,128)(2,1)S(1)}, bf16[96,1152]{1,0:T(8,128)(2,1)S(1)}, u32[]{:S(2)}, u32[]{:S(2)}) collective-permute-start(bf16[96,1152]{1,0:T(8,128)(2,1)S(1)} %pad_maximum_fusion.own), channel_id=1, source_target_pairs={{0,8},{2,26},{4,12},{6,30},{8,16},{10,2},{12,20},{14,6},{16,24},{1... | collective-permute-start | bytes 663560 | tf_op jit(solution)/shard_map/ppermute | solution.py:33
  33.6 4.6 %collective-permute-done.2.one = bf16[96,1152]{1,0:T(8,128)(2,1)S(1)} collective-permute-done((bf16[96,1152]{1,0:T(8,128)(2,1)S(1)}, bf16[96,1152]{1,0:T(8,128)(2,1)S(1)}, u32[]{:S(2)}, u32[]{:S(2)}) %collective-permute-start.2) | collective-permute-done | bytes 221216 | tf_op jit(solution)/shard_map/ppermute | solution.py:33
  38.2 4.4 %collective-permute-done.3.two = bf16[96,1152]{1,0:T(8,128)(2,1)S(1)} collective-permute-done((bf16[96,1152]{1,0:T(8,128)(2,1)S(1)}, bf16[96,1152]{1,0:T(8,128)(2,1)S(1)}, u32[]{:S(2)}, u32[]{:S(2)}) %collective-permute-start.3) | collective-permute-done | bytes 221216 | tf_op jit(solution)/shard_map/ppermute | solution.py:33
  42.6 1.8 %collective-permute-start.4 = (bf16[96,1152]{1,0:T(8,128)(2,1)S(1)}, bf16[96,1152]{1,0:T(8,128)(2,1)S(1)}, u32[]{:S(2)}, u32[]{:S(2)}) collective-permute-start(bf16[96,1152]{1,0:T(8,128)(2,1)S(1)} %collective-permute-done.3.two), channel_id=1, source_target_pairs={{0,4},{2,30},{4,8},{6,2},{8,12},{10,6},{12,16},{14,10},{16,20},{18... | collective-permute-start | bytes 663560 | tf_op jit(solution)/shard_map/ppermute | solution.py:33
  44.4 0.7 collective-permute-start.5
  45.1 0.5 collective-permute-start.8
  45.6 7.5 %collective-permute-done.5.four = bf16[48,1152]{1,0:T(8,128)(2,1)S(1)} collective-permute-done((bf16[48,1152]{1,0:T(8,128)(2,1)S(1)}, bf16[48,1152]{1,0:T(8,128)(2,1)S(1)}, u32[]{:S(2)}, u32[]{:S(2)}) %collective-permute-start.5) | collective-permute-done | bytes 110624 | tf_op jit(solution)/shard_map/ppermute | solution.py:33
  53.2 0.1 collective-permute-start.7
  54.6 0.7 collective-permute-start.9
  55.4 0.9 collective-permute-done.9.four_other
  56.3 0.6 copy-done.9
  57.0 7.1 %scores.1 = (bf16[384,768]{1,0:T(8,128)(2,1)S(1)}, f32[384,1024]{1,0:T(8,128)}, f32[768,1024]{1,0:T(8,128)S(1)}, f32[1,128]{1,0:T(1,128)S(1)}) custom-call(s32[1]{0:T(128)} %bitcast.spot, f32[1]{0:T(128)S(6)} %copy.9.scale, f32[1]{0:T(128)S(6)} %copy.10.bias, bf16[96,1152]{1,0:T(8,128)(2,1)} %copy-done.1, bf16[96,1152]{1,0:T(8,128)(2,1)} %copy-done.3, ...), custom_call_target="tpu_custom_call" | custom-call | tf_op jit(solution)/shard_map/scores/pallas_call | solution.py:222
  64.2 0.4 collective-permute-start.12
  64.6 0.2 collective-permute-start.10
  64.8 1.5 %convert_element_type.45 = f16[768,1024]{1,0:T(8,128)(2,1)} convert(f32[768,1024]{1,0:T(8,128)S(1)} %get-tuple-element.39) | non-fusion elementwise | flops 786432 | bytes 4718592 | tf_op jit(solution)/shard_map/convert_element_type | solution.py:282
  66.2 3.4 %collective-permute-done.10 = f32[1,128]{1,0:T(1,128)S(1)} collective-permute-done((f32[1,128]{1,0:T(1,128)S(1)}, f32[1,128]{1,0:T(1,128)S(1)}, u32[]{:S(2)}, u32[]{:S(2)}) %collective-permute-start.10) | collective-permute-done | bytes 544 | tf_op jit(solution)/shard_map/ppermute | solution.py:59
  69.7 1.2 collective-permute-start.11
  70.8 2.4 %collective-permute-done.11 = f32[1,128]{1,0:T(1,128)S(1)} collective-permute-done((f32[1,128]{1,0:T(1,128)S(1)}, f32[1,128]{1,0:T(1,128)S(1)}, u32[]{:S(2)}, u32[]{:S(2)}) %collective-permute-start.11) | collective-permute-done | bytes 544 | tf_op jit(solution)/shard_map/ppermute | solution.py:59
  73.2 7.2 %all-to-all-start.1 = ((f16[16,48,1024]{2,1,0:T(8,128)(2,1)}), f16[16,48,1024]{2,1,0:T(8,128)(2,1)}, u32[]{:S(2)}, u32[]{:S(2)}) async-start(f16[16,48,1024]{2,1,0:T(8,128)(2,1)} %bitcast.13), calls=%async_computation.1 | async-start | bytes 3145728 | tf_op jit(solution)/shard_map/all_to_all | solution.py:20
  80.5 2.2 %fusion.8 = (f16[384,1024]{1,0:T(8,128)(2,1)S(1)}, f32[384,1024]{1,0:T(8,128)S(1)}) fusion(f32[384,1024]{1,0:T(8,128)} %collective-permute-done.12, bf16[384,768]{1,0:T(8,128)(2,1)S(1)} %get-tuple-element.45, bf16[768,1024]{1,0:T(8,128)(2,1)S(1)} %bitcast.12), kind=kOutput, calls=%fused_computation.41 | convolution fusion | flops 604766208 | bytes 6094848 | tf_op jit(solution)/shard_map/dot_general | solution.py:289
  82.7 0.2 collective-permute-start.14
  82.9 3.5 %collective-permute-start.15 = (f16[48,1024]{1,0:T(8,128)(2,1)S(1)}, f16[48,1024]{1,0:T(8,128)(2,1)S(1)}, u32[]{:S(2)}, u32[]{:S(2)}) collective-permute-start(f16[48,1024]{1,0:T(8,128)(2,1)S(1)} %slice.37), channel_id=1, source_target_pairs={{0,24},{2,10},{4,28},{6,14},{8,0},{10,18},{12,4},{14,22},{16,8},{1... | collective-permute-start | bytes 294920 | tf_op jit(solution)/shard_map/ppermute | solution.py:33
  86.4 0.5 collective-permute-start.16
  86.9 5.8 %collective-permute-done.16 = f32[1,128]{1,0:T(1,128)S(1)} collective-permute-done((f32[1,128]{1,0:T(1,128)S(1)}, f32[1,128]{1,0:T(1,128)S(1)}, u32[]{:S(2)}, u32[]{:S(2)}) %collective-permute-start.16) | collective-permute-done | bytes 544 | tf_op jit(solution)/shard_map/ppermute | solution.py:59
  92.7 4.4 %collective-permute-done.17 = f32[1,128]{1,0:T(1,128)S(1)} collective-permute-done((f32[1,128]{1,0:T(1,128)S(1)}, f32[1,128]{1,0:T(1,128)S(1)}, u32[]{:S(2)}, u32[]{:S(2)}) %collective-permute-start.17) | collective-permute-done | bytes 544 | tf_op jit(solution)/shard_map/ppermute | solution.py:59
  97.3 2.1 %collective-permute-start.18 = (f16[96,1024]{1,0:T(8,128)(2,1)S(1)}, f16[96,1024]{1,0:T(8,128)(2,1)S(1)}, u32[]{:S(2)}, u32[]{:S(2)}) collective-permute-start(f16[96,1024]{1,0:T(8,128)(2,1)S(1)} %fusion), channel_id=1, source_target_pairs={{0,24},{2,10},{4,28},{6,14},{8,0},{10,18},{12,4},{14,22},{16,8},{1... | collective-permute-start | bytes 589832 | tf_op jit(solution)/shard_map/ppermute | solution.py:33
  99.4 2.0 %collective-permute-start.19 = (f32[1,128]{1,0:T(1,128)S(1)}, f32[1,128]{1,0:T(1,128)S(1)}, u32[]{:S(2)}, u32[]{:S(2)}) collective-permute-start(f32[1,128]{1,0:T(1,128)S(1)} %add.197), channel_id=1, source_target_pairs={{0,16},{4,20},{8,24},{12,28},{16,0},{20,4},{24,8},{28,12},{1,17},{... | collective-permute-start | bytes 1544 | tf_op jit(solution)/shard_map/ppermute | solution.py:59
  101.4 5.4 %collective-permute-done.19 = f32[1,128]{1,0:T(1,128)S(1)} collective-permute-done((f32[1,128]{1,0:T(1,128)S(1)}, f32[1,128]{1,0:T(1,128)S(1)}, u32[]{:S(2)}, u32[]{:S(2)}) %collective-permute-start.19) | collective-permute-done | bytes 544 | tf_op jit(solution)/shard_map/ppermute | solution.py:59
  106.9 0.1 collective-permute-start.22
  107.0 1.6 %collective-permute-start.20 = (f32[1,128]{1,0:T(1,128)S(1)}, f32[1,128]{1,0:T(1,128)S(1)}, u32[]{:S(2)}, u32[]{:S(2)}) collective-permute-start(f32[1,128]{1,0:T(1,128)S(1)} %add.201), channel_id=1, source_target_pairs={{0,32},{32,0},{64,96},{96,64},{1,33},{33,1},{65,97},{97,65},{2,34}... | collective-permute-start | bytes 1544 | tf_op jit(solution)/shard_map/ppermute | solution.py:59
  108.5 2.4 %convert_reduce_fusion = f32[48,1024]{1,0:T(8,128)} fusion(f16[16,48,1024]{2,1,0:T(8,128)(2,1)} %all-to-all-done.1), kind=kLoop, calls=%fused_computation | loop fusion | flops 1523712 | bytes 1769472 | tf_op jit(solution)/shard_map/reduce_sum | solution.py:292
  111.0 2.7 %collective-permute-start.21 = (f32[1,128]{1,0:T(1,128)S(1)}, f32[1,128]{1,0:T(1,128)S(1)}, u32[]{:S(2)}, u32[]{:S(2)}) collective-permute-start(f32[1,128]{1,0:T(1,128)S(1)} %add.202), channel_id=1, source_target_pairs={{0,64},{32,96},{64,0},{96,32},{1,65},{33,97},{65,1},{97,33},{2,66}... | collective-permute-start | bytes 1544 | tf_op jit(solution)/shard_map/ppermute | solution.py:59
  113.7 2.4 %collective-permute-done.21 = f32[1,128]{1,0:T(1,128)S(1)} collective-permute-done((f32[1,128]{1,0:T(1,128)S(1)}, f32[1,128]{1,0:T(1,128)S(1)}, u32[]{:S(2)}, u32[]{:S(2)}) %collective-permute-start.21) | collective-permute-done | bytes 544 | tf_op jit(solution)/shard_map/ppermute | solution.py:59
  116.1 1.7 %fusion.3 = f32[48,1024]{1,0:T(8,128)} fusion(f32[48,1024]{1,0:T(8,128)S(1)} %collective-permute-done.22, f32[384,1024]{1,0:T(8,128)} %copy-done, f32[96,1024]{1,0:T(8,128)S(1)} %convert_element_type.51, s32[]{:T(128)S(6)} %select_n.119, f16[96,1024]{1,0:T(8,128)(2,1)S(1)} %slice.34), kind=kLoop, calls=%fused_computation.12 | loop fusion | flops 196608 | bytes 884740 | tf_op jit(solution)/shard_map/add | solution.py:79
  (60 shorter events, 0.6 us)
Async XLA Ops:
  0.6 6.9 %copy-start.10 = (s32[192]{0:T(256)S(1)}, s32[192]{0:T(256)}, u32[]{:S(2)}) copy-start(s32[192]{0:T(256)} %param.9) | copy-start | bytes 2308
  5.2 12.4 %collective-permute-start = (f32[96,1024]{1,0:T(8,128)S(1)}, f32[96,1024]{1,0:T(8,128)S(1)}, u32[]{:S(2)}, u32[]{:S(2)}) collective-permute-start(f32[96,1024]{1,0:T(8,128)S(1)} %get-tuple-element.32), channel_id=1, source_target_pairs={{0,1},{1,0},{2,3},{3,2},{4,5},{5,4},{6,7},{7,6},{8,9},{9,8},{10,11... | collective-permute-start | bytes 1179656 | tf_op jit(solution)/shard_map/ppermute | solution.py:149
  17.9 1.5 %collective-permute-start.1 = (bf16[96,1024]{1,0:T(8,128)(2,1)S(1)}, bf16[96,1024]{1,0:T(8,128)(2,1)S(1)}, u32[]{:S(2)}, u32[]{:S(2)}) collective-permute-start(bf16[96,1024]{1,0:T(8,128)(2,1)S(1)} %multiply_convert_fusion), channel_id=1, source_target_pairs={{0,2},{2,0},{1,3},{3,1},{4,6},{6,4},{5,7},{7,5},{8,10},{10,8},{9,1... | collective-permute-start | bytes 589832 | tf_op jit(solution)/shard_map/ppermute | solution.py:263
  19.6 10.8 %copy-start.1 = (bf16[96,1152]{1,0:T(8,128)(2,1)}, bf16[96,1152]{1,0:T(8,128)(2,1)S(1)}, u32[]{:S(2)}) copy-start(bf16[96,1152]{1,0:T(8,128)(2,1)S(1)} %pad_maximum_fusion.own) | copy-start | bytes 663556
  21.0 35.3 %all-to-all-start = ((bf16[16,48,1024]{2,1,0:T(8,128)(2,1)}), bf16[16,48,1024]{2,1,0:T(8,128)(2,1)S(1)}, u32[]{:S(2)}, u32[]{:S(2)}) async-start(bf16[16,48,1024]{2,1,0:T(8,128)(2,1)} %broadcast_in_dim.29), calls=%async_computation | async-start | bytes 3145728 | tf_op jit(solution)/shard_map/all_to_all | solution.py:20
  28.4 9.8 %collective-permute-start.2 = (bf16[96,1152]{1,0:T(8,128)(2,1)S(1)}, bf16[96,1152]{1,0:T(8,128)(2,1)S(1)}, u32[]{:S(2)}, u32[]{:S(2)}) collective-permute-start(bf16[96,1152]{1,0:T(8,128)(2,1)S(1)} %pad_maximum_fusion.own), channel_id=1, source_target_pairs={{0,4},{2,30},{4,8},{6,2},{8,12},{10,6},{12,16},{14,10},{16,20},{18... | collective-permute-start | bytes 663560 | tf_op jit(solution)/shard_map/ppermute | solution.py:33
  30.3 12.2 %collective-permute-start.3 = (bf16[96,1152]{1,0:T(8,128)(2,1)S(1)}, bf16[96,1152]{1,0:T(8,128)(2,1)S(1)}, u32[]{:S(2)}, u32[]{:S(2)}) collective-permute-start(bf16[96,1152]{1,0:T(8,128)(2,1)S(1)} %pad_maximum_fusion.own), channel_id=1, source_target_pairs={{0,8},{2,26},{4,12},{6,30},{8,16},{10,2},{12,20},{14,6},{16,24},{1... | collective-permute-start | bytes 663560 | tf_op jit(solution)/shard_map/ppermute | solution.py:33
  38.2 18.7 %copy-start.3 = (bf16[96,1152]{1,0:T(8,128)(2,1)}, bf16[96,1152]{1,0:T(8,128)(2,1)S(1)}, u32[]{:S(2)}) copy-start(bf16[96,1152]{1,0:T(8,128)(2,1)S(1)} %collective-permute-done.2.one) | copy-start | bytes 663556
  42.6 14.4 %copy-start.2 = (bf16[96,1152]{1,0:T(8,128)(2,1)}, bf16[96,1152]{1,0:T(8,128)(2,1)S(1)}, u32[]{:S(2)}) copy-start(bf16[96,1152]{1,0:T(8,128)(2,1)S(1)} %collective-permute-done.3.two) | copy-start | bytes 663556
  42.6 10.6 %collective-permute-start.4 = (bf16[96,1152]{1,0:T(8,128)(2,1)S(1)}, bf16[96,1152]{1,0:T(8,128)(2,1)S(1)}, u32[]{:S(2)}, u32[]{:S(2)}) collective-permute-start(bf16[96,1152]{1,0:T(8,128)(2,1)S(1)} %collective-permute-done.3.two), channel_id=1, source_target_pairs={{0,4},{2,30},{4,8},{6,2},{8,12},{10,6},{12,16},{14,10},{16,20},{18... | collective-permute-start | bytes 663560 | tf_op jit(solution)/shard_map/ppermute | solution.py:33
  44.4 8.7 %collective-permute-start.5 = (bf16[48,1152]{1,0:T(8,128)(2,1)S(1)}, bf16[48,1152]{1,0:T(8,128)(2,1)S(1)}, u32[]{:S(2)}, u32[]{:S(2)}) collective-permute-start(bf16[48,1152]{1,0:T(8,128)(2,1)S(1)} %constant_dynamic-slice_fusion), channel_id=1, source_target_pairs={{0,8},{2,26},{4,12},{6,30},{8,16},{10,2},{12,20},{14,6},{16,24},{1... | collective-permute-start | bytes 331784 | tf_op jit(solution)/shard_map/ppermute | solution.py:33
  45.1 10.3 %collective-permute-start.8 = (bf16[96,1152]{1,0:T(8,128)(2,1)S(1)}, bf16[96,1152]{1,0:T(8,128)(2,1)S(1)}, u32[]{:S(2)}, u32[]{:S(2)}) collective-permute-start(bf16[96,1152]{1,0:T(8,128)(2,1)S(1)} %collective-permute-done.3.two), channel_id=1, source_target_pairs={{0,2},{2,0},{1,3},{3,1},{4,6},{6,4},{5,7},{7,5},{8,10},{10,8},{9,1... | collective-permute-start | bytes 663560 | tf_op jit(solution)/shard_map/ppermute | solution.py:47
  45.6 9.8 %collective-permute-start.6 = (bf16[96,1152]{1,0:T(8,128)(2,1)S(1)}, bf16[96,1152]{1,0:T(8,128)(2,1)S(1)}, u32[]{:S(2)}, u32[]{:S(2)}) collective-permute-start(bf16[96,1152]{1,0:T(8,128)(2,1)S(1)} %collective-permute-done.2.one), channel_id=1, source_target_pairs={{0,2},{2,0},{1,3},{3,1},{4,6},{6,4},{5,7},{7,5},{8,10},{10,8},{9,1... | collective-permute-start | bytes 663560 | tf_op jit(solution)/shard_map/ppermute | solution.py:47
  53.1 3.1 %copy-start.8 = (bf16[48,1152]{1,0:T(8,128)(2,1)}, bf16[48,1152]{1,0:T(8,128)(2,1)S(1)}, u32[]{:S(2)}) copy-start(bf16[48,1152]{1,0:T(8,128)(2,1)S(1)} %collective-permute-done.5.four) | copy-start | bytes 331780
  53.2 3.8 %copy-start.4 = (bf16[96,1152]{1,0:T(8,128)(2,1)}, bf16[96,1152]{1,0:T(8,128)(2,1)S(1)}, u32[]{:S(2)}) copy-start(bf16[96,1152]{1,0:T(8,128)(2,1)S(1)} %collective-permute-done.4.three) | copy-start | bytes 663556
  53.2 3.1 %collective-permute-start.7 = (bf16[96,1152]{1,0:T(8,128)(2,1)S(1)}, bf16[96,1152]{1,0:T(8,128)(2,1)S(1)}, u32[]{:S(2)}, u32[]{:S(2)}) collective-permute-start(bf16[96,1152]{1,0:T(8,128)(2,1)S(1)} %collective-permute-done.4.three), channel_id=1, source_target_pairs={{0,2},{2,0},{1,3},{3,1},{4,6},{6,4},{5,7},{7,5},{8,10},{10,8},{9,1... | collective-permute-start | bytes 663560 | tf_op jit(solution)/shard_map/ppermute | solution.py:49
  54.6 1.7 %collective-permute-start.9 = (bf16[48,1152]{1,0:T(8,128)(2,1)S(1)}, bf16[48,1152]{1,0:T(8,128)(2,1)S(1)}, u32[]{:S(2)}, u32[]{:S(2)}) collective-permute-start(bf16[48,1152]{1,0:T(8,128)(2,1)S(1)} %collective-permute-done.5.four), channel_id=1, source_target_pairs={{0,2},{2,0},{1,3},{3,1},{4,6},{6,4},{5,7},{7,5},{8,10},{10,8},{9,1... | collective-permute-start | bytes 331784 | tf_op jit(solution)/shard_map/ppermute | solution.py:49
  55.4 1.6 %copy-start.6 = (bf16[96,1152]{1,0:T(8,128)(2,1)}, bf16[96,1152]{1,0:T(8,128)(2,1)S(1)}, u32[]{:S(2)}) copy-start(bf16[96,1152]{1,0:T(8,128)(2,1)S(1)} %collective-permute-done.6.one_other) | copy-start | bytes 663556
  55.4 1.5 %copy-start.5 = (bf16[96,1152]{1,0:T(8,128)(2,1)}, bf16[96,1152]{1,0:T(8,128)(2,1)S(1)}, u32[]{:S(2)}) copy-start(bf16[96,1152]{1,0:T(8,128)(2,1)S(1)} %collective-permute-done.8.two_other) | copy-start | bytes 663556
  56.3 0.6 copy-start.9
  56.3 0.7 copy-start.7
  64.2 16.3 %collective-permute-start.12 = (f32[384,1024]{1,0:T(8,128)}, f32[384,1024]{1,0:T(8,128)}, u32[]{:S(2)}, u32[]{:S(2)}) collective-permute-start(f32[384,1024]{1,0:T(8,128)} %get-tuple-element.46), channel_id=1, source_target_pairs={{0,2},{2,0},{1,3},{3,1},{4,6},{6,4},{5,7},{7,5},{8,10},{10,8},{9,1... | collective-permute-start | bytes 4718600 | tf_op jit(solution)/shard_map/ppermute | solution.py:280
  64.6 5.0 %collective-permute-start.10 = (f32[1,128]{1,0:T(1,128)S(1)}, f32[1,128]{1,0:T(1,128)S(1)}, u32[]{:S(2)}, u32[]{:S(2)}) collective-permute-start(f32[1,128]{1,0:T(1,128)S(1)} %get-tuple-element.40), channel_id=1, source_target_pairs={{0,1},{1,0},{2,3},{3,2},{4,5},{5,4},{6,7},{7,6},{8,9},{9,8},{10,11... | collective-permute-start | bytes 1544 | tf_op jit(solution)/shard_map/ppermute | solution.py:59
  69.7 3.5 %collective-permute-start.11 = (f32[1,128]{1,0:T(1,128)S(1)}, f32[1,128]{1,0:T(1,128)S(1)}, u32[]{:S(2)}, u32[]{:S(2)}) collective-permute-start(f32[1,128]{1,0:T(1,128)S(1)} %add.192), channel_id=1, source_target_pairs={{0,128},{128,0},{1,129},{129,1},{2,130},{130,2},{3,131},{131,3},{4... | collective-permute-start | bytes 1544 | tf_op jit(solution)/shard_map/ppermute | solution.py:59
  73.2 7.2 %collective-permute-start.13 = (f32[1,128]{1,0:T(1,128)S(1)}, f32[1,128]{1,0:T(1,128)S(1)}, u32[]{:S(2)}, u32[]{:S(2)}) collective-permute-start(f32[1,128]{1,0:T(1,128)S(1)} %add.193), channel_id=1, source_target_pairs={{0,2},{2,0},{1,3},{3,1},{4,6},{6,4},{5,7},{7,5},{8,10},{10,8},{9,1... | collective-permute-start | bytes 1544 | tf_op jit(solution)/shard_map/ppermute | solution.py:59
  73.2 33.8 %all-to-all-start.1 = ((f16[16,48,1024]{2,1,0:T(8,128)(2,1)}), f16[16,48,1024]{2,1,0:T(8,128)(2,1)}, u32[]{:S(2)}, u32[]{:S(2)}) async-start(f16[16,48,1024]{2,1,0:T(8,128)(2,1)} %bitcast.13), calls=%async_computation.1 | async-start | bytes 3145728 | tf_op jit(solution)/shard_map/all_to_all | solution.py:20
  82.6 14.5 %copy-start = (f32[384,1024]{1,0:T(8,128)}, f32[384,1024]{1,0:T(8,128)S(1)}, u32[]{:S(2)}) copy-start(f32[384,1024]{1,0:T(8,128)S(1)} %get-tuple-element.66) | copy-start | bytes 4718596
  82.7 14.4 %collective-permute-start.14 = (f16[192,1024]{1,0:T(8,128)(2,1)S(1)}, f16[192,1024]{1,0:T(8,128)(2,1)S(1)}, u32[]{:S(2)}, u32[]{:S(2)}) collective-permute-start(f16[192,1024]{1,0:T(8,128)(2,1)S(1)} %slice.36), channel_id=1, source_target_pairs={{0,28},{2,6},{4,0},{6,10},{8,4},{10,14},{12,8},{14,18},{16,12},{18... | collective-permute-start | bytes 1179656 | tf_op jit(solution)/shard_map/ppermute | solution.py:33
  82.9 14.2 %collective-permute-start.15 = (f16[48,1024]{1,0:T(8,128)(2,1)S(1)}, f16[48,1024]{1,0:T(8,128)(2,1)S(1)}, u32[]{:S(2)}, u32[]{:S(2)}) collective-permute-start(f16[48,1024]{1,0:T(8,128)(2,1)S(1)} %slice.37), channel_id=1, source_target_pairs={{0,24},{2,10},{4,28},{6,14},{8,0},{10,18},{12,4},{14,22},{16,8},{1... | collective-permute-start | bytes 294920 | tf_op jit(solution)/shard_map/ppermute | solution.py:33
  86.4 6.3 %collective-permute-start.16 = (f32[1,128]{1,0:T(1,128)S(1)}, f32[1,128]{1,0:T(1,128)S(1)}, u32[]{:S(2)}, u32[]{:S(2)}) collective-permute-start(f32[1,128]{1,0:T(1,128)S(1)} %add.194), channel_id=1, source_target_pairs={{0,4},{4,0},{8,12},{12,8},{16,20},{20,16},{24,28},{28,24},{1,5},{5... | collective-permute-start | bytes 1544 | tf_op jit(solution)/shard_map/ppermute | solution.py:59
  92.7 4.4 %collective-permute-start.17 = (f32[1,128]{1,0:T(1,128)S(1)}, f32[1,128]{1,0:T(1,128)S(1)}, u32[]{:S(2)}, u32[]{:S(2)}) collective-permute-start(f32[1,128]{1,0:T(1,128)S(1)} %add.196), channel_id=1, source_target_pairs={{0,8},{4,12},{8,0},{12,4},{16,24},{20,28},{24,16},{28,20},{1,9},{5... | collective-permute-start | bytes 1544 | tf_op jit(solution)/shard_map/ppermute | solution.py:59
  97.3 9.5 %collective-permute-start.18 = (f16[96,1024]{1,0:T(8,128)(2,1)S(1)}, f16[96,1024]{1,0:T(8,128)(2,1)S(1)}, u32[]{:S(2)}, u32[]{:S(2)}) collective-permute-start(f16[96,1024]{1,0:T(8,128)(2,1)S(1)} %fusion), channel_id=1, source_target_pairs={{0,24},{2,10},{4,28},{6,14},{8,0},{10,18},{12,4},{14,22},{16,8},{1... | collective-permute-start | bytes 589832 | tf_op jit(solution)/shard_map/ppermute | solution.py:33
  99.4 7.4 %collective-permute-start.19 = (f32[1,128]{1,0:T(1,128)S(1)}, f32[1,128]{1,0:T(1,128)S(1)}, u32[]{:S(2)}, u32[]{:S(2)}) collective-permute-start(f32[1,128]{1,0:T(1,128)S(1)} %add.197), channel_id=1, source_target_pairs={{0,16},{4,20},{8,24},{12,28},{16,0},{20,4},{24,8},{28,12},{1,17},{... | collective-permute-start | bytes 1544 | tf_op jit(solution)/shard_map/ppermute | solution.py:59
  106.9 9.2 %collective-permute-start.22 = (f32[48,1024]{1,0:T(8,128)S(1)}, f32[48,1024]{1,0:T(8,128)S(1)}, u32[]{:S(2)}, u32[]{:S(2)}) collective-permute-start(f32[48,1024]{1,0:T(8,128)S(1)} %dynamic-slice_add_fusion), channel_id=1, source_target_pairs={{0,2},{2,0},{1,3},{3,1},{4,6},{6,4},{5,7},{7,5},{8,10},{10,8},{9,1... | collective-permute-start | bytes 589832 | tf_op jit(solution)/shard_map/ppermute | solution.py:77
  107.0 4.0 %collective-permute-start.20 = (f32[1,128]{1,0:T(1,128)S(1)}, f32[1,128]{1,0:T(1,128)S(1)}, u32[]{:S(2)}, u32[]{:S(2)}) collective-permute-start(f32[1,128]{1,0:T(1,128)S(1)} %add.201), channel_id=1, source_target_pairs={{0,32},{32,0},{64,96},{96,64},{1,33},{33,1},{65,97},{97,65},{2,34}... | collective-permute-start | bytes 1544 | tf_op jit(solution)/shard_map/ppermute | solution.py:59
  111.0 5.0 %collective-permute-start.21 = (f32[1,128]{1,0:T(1,128)S(1)}, f32[1,128]{1,0:T(1,128)S(1)}, u32[]{:S(2)}, u32[]{:S(2)}) collective-permute-start(f32[1,128]{1,0:T(1,128)S(1)} %add.202), channel_id=1, source_target_pairs={{0,64},{32,96},{64,0},{96,32},{1,65},{33,97},{65,1},{97,33},{2,66}... | collective-permute-start | bytes 1544 | tf_op jit(solution)/shard_map/ppermute | solution.py:59

commit v14 on v13

--- a/solution.py
+++ b/solution.py
@@ -57,6 +57,13 @@
 def with_partner(value, axis, bit):
     pairs = [(i, i ^ bit) for i in range(lax.axis_size(axis))]
     return value + lax.ppermute(value, axis, pairs)
+
+
+def with_other_three(value, axes):
+    first, second, third = (
+        lax.ppermute(value, axes, [(i, i ^ k) for i in range(4)]) for k in (1, 2, 3)
+    )
+    return (value + first) + (second + third)
 
 
 def summed_over_z(kept, section, loss):
@@ -278,10 +285,8 @@
         scale, bias, slides, pieces, reports_all, columns[None, :]
     )
     back = lax.ppermute(sent, "section", SWAP)
-    loss = with_partner(loss, "tensor", 1)
+    loss = with_other_three(loss, ("xl", "tensor"))
     report_part = report_part.astype(SENT).reshape(n_plane, quarter, width)
-    report_part, loss = tied(report_part, loss)
-    loss = with_partner(loss, "xl", 1)
     report_part, loss, weight = tied(report_part, loss, weight)
     report_terms = exchanged(report_part, PLANE)
     loss = with_partner(loss, "section", 1)
@@ -290,8 +295,7 @@
     slide_grad, loss = summed_over_z(kept, section, loss)
     report_terms, loss = tied(report_terms, loss)
     report_grad = report_terms.astype(F32).sum(axis=0)
-    loss, report_grad = tied(with_partner(loss, "y", 1), report_grad)
-    loss = with_partner(loss, "y", 2)
+    loss, report_grad = tied(with_other_three(loss, "y"), report_grad)
     return (loss[0, :1] / total, slide_grad, report_grad)
 
 

time: 119 us -> 118 us (level)
  waiting for transfers between devices: 52.4 us -> 47.5 us
  starting transfers between devices: 40.5 us -> 44 us
    ppermute x0 -> x6, starting transfers between devices: none -> 8.88 us  [with_other_three(): lax.ppermute(value, axes, [(i, i ^ k) for i in range(4)])]
    ppermute x8 -> x4, waiting for transfers between devices: 23.7 us -> 16.7 us  [with_partner(): return value + lax.ppermute(value, axis, pairs)]
    ppermute x8 -> x4, starting transfers between devices: 8.13 us -> 2.57 us  [with_partner(): return value + lax.ppermute(value, axis, pairs)]
    ppermute x0 -> x6, waiting for transfers between devices: none -> 2.2 us  [with_other_three(): lax.ppermute(value, axes, [(i, i ^ k) for i in range(4)])]
  transfers between devices with their start and end apart: 25 -> 27, of which waited for: 12 -> 12; matrix products, arithmetic and copies ran while one was open for 6% -> 6% of each run, Pallas kernels for 0% -> 0%
where the time goes in v14:
time: 118 us
  waiting for transfers between devices  47.5 us (40%)
  starting transfers between devices  44 us (37%)
  Pallas kernels  11.7 us (10%)
  other arithmetic  6.33 us (5%)
  between operations  3.41 us (3%)
  local copies, waits for them, and re-layouts  2.43 us (2%)
  matrix products  2.19 us (2%)
    ppermute x4, waiting for transfers between devices, with_partner(): return value + lax.ppermute(value, axis, pairs)  16.7 us
    ppermute x7, waiting for transfers between devices, along_z(): return lax.ppermute(array, ('z', 'section'), pairs)  16.5 us
    all_to_all x2, starting transfers between devices, exchanged(): return lax.all_to_all(parts, axes, split_axis=0, concat_axis=0, tiled=True)  14.7 us
    ppermute x7, starting transfers between devices, along_z(): return lax.ppermute(array, ('z', 'section'), pairs)  13.6 us
    ppermute x1, waiting for transfers between devices, tower(): raw = own + lax.ppermute(sent, 'tensor', SWAP)  9.91 us
    ppermute x6, starting transfers between devices, with_other_three(): lax.ppermute(value, axes, [(i, i ^ k) for i in range(4)])  8.88 us
    pallas_call x1, Pallas kernels, scored(): pl.pallas_call(score_kernel, in_specs=[scalar] * 3 + [pl.BlockSpec(memory...  7.14 us
    pallas_call x1, Pallas kernels, tower(): pl.pallas_call(tower_kernel, in_specs=[pl.BlockSpec(memory_space=pltpu.SM...  4.54 us
  transfers between devices with their start and end apart: 27, of which 12 were waited for; matrix products, arithmetic and copies ran while one was open for 6% of the time, Pallas kernels for 0%

profile of v14, /device:TPU:4, one launch (start us, length us, event | category | flops | bytes accessed | tf_op | source)
XLA Modules:
  0.0 117.6 jit_solution(6387035682359416908)
XLA Ops:
  0.6 4.5 %tower.1 = (f32[96,1024]{1,0:T(8,128)S(1)}, f32[96,1024]{1,0:T(8,128)S(1)}) custom-call(s32[1]{0:T(128)} %bitcast.1.spot, bf16[192,1024]{1,0:T(8,128)(2,1)} %bitcast.16, bf16[1024,2048]{1,0:T(8,128)(2,1)} %bitcast.14, bf16[2048,1024]{1,0:T(8,128)(2,1)} %bitcast.15), custom_call_target="tpu_custom_call" | custom-call | tf_op jit(solution)/shard_map/tower/pallas_call | solution.py:139
  5.2 2.3 %collective-permute-start = (f32[96,1024]{1,0:T(8,128)S(1)}, f32[96,1024]{1,0:T(8,128)S(1)}, u32[]{:S(2)}, u32[]{:S(2)}) collective-permute-start(f32[96,1024]{1,0:T(8,128)S(1)} %get-tuple-element.30), channel_id=1, source_target_pairs={{0,1},{1,0},{2,3},{3,2},{4,5},{5,4},{6,7},{7,6},{8,9},{9,8},{10,11... | collective-permute-start | bytes 1179656 | tf_op jit(solution)/shard_map/ppermute | solution.py:156
  7.7 9.9 %collective-permute-done = f32[96,1024]{1,0:T(8,128)S(1)} collective-permute-done((f32[96,1024]{1,0:T(8,128)S(1)}, f32[96,1024]{1,0:T(8,128)S(1)}, u32[]{:S(2)}, u32[]{:S(2)}) %collective-permute-start) | collective-permute-done | bytes 393248 | tf_op jit(solution)/shard_map/ppermute | solution.py:156
  17.6 0.1 multiply_reduce_fusion
  17.8 0.1 multiply_convert_fusion
  17.9 0.1 collective-permute-start.1
  18.0 0.1 select_convert_fusion
  18.1 1.3 %collective-permute-done.1 = bf16[96,1024]{1,0:T(8,128)(2,1)S(1)} collective-permute-done((bf16[96,1024]{1,0:T(8,128)(2,1)S(1)}, bf16[96,1024]{1,0:T(8,128)(2,1)S(1)}, u32[]{:S(2)}, u32[]{:S(2)}) %collective-permute-start.1) | collective-permute-done | bytes 196640 | tf_op jit(solution)/shard_map/ppermute | solution.py:270
  19.4 0.1 broadcast_select_fusion
  19.6 1.4 %broadcast_in_dim.29 = bf16[16,48,1024]{2,1,0:T(8,128)(2,1)} broadcast(bf16[48,1024]{1,0:T(8,128)(2,1)S(1)} %dynamic-slice_select_fusion), dimensions={1,2} | broadcast | bytes 1671168 | tf_op jit(solution)/shard_map/broadcast_in_dim | solution.py:274
  21.0 7.5 %all-to-all-start = ((bf16[16,48,1024]{2,1,0:T(8,128)(2,1)}), bf16[16,48,1024]{2,1,0:T(8,128)(2,1)S(1)}, u32[]{:S(2)}, u32[]{:S(2)}) async-start(bf16[16,48,1024]{2,1,0:T(8,128)(2,1)} %broadcast_in_dim.29), calls=%async_computation | async-start | bytes 3145728 | tf_op jit(solution)/shard_map/all_to_all | solution.py:20
  28.5 1.9 %collective-permute-start.2 = (bf16[96,1152]{1,0:T(8,128)(2,1)S(1)}, bf16[96,1152]{1,0:T(8,128)(2,1)S(1)}, u32[]{:S(2)}, u32[]{:S(2)}) collective-permute-start(bf16[96,1152]{1,0:T(8,128)(2,1)S(1)} %pad_maximum_fusion.own), channel_id=1, source_target_pairs={{0,4},{2,30},{4,8},{6,2},{8,12},{10,6},{12,16},{14,10},{16,20},{18... | collective-permute-start | bytes 663560 | tf_op jit(solution)/shard_map/ppermute | solution.py:33
  30.4 3.3 %collective-permute-start.3 = (bf16[96,1152]{1,0:T(8,128)(2,1)S(1)}, bf16[96,1152]{1,0:T(8,128)(2,1)S(1)}, u32[]{:S(2)}, u32[]{:S(2)}) collective-permute-start(bf16[96,1152]{1,0:T(8,128)(2,1)S(1)} %pad_maximum_fusion.own), channel_id=1, source_target_pairs={{0,8},{2,26},{4,12},{6,30},{8,16},{10,2},{12,20},{14,6},{16,24},{1... | collective-permute-start | bytes 663560 | tf_op jit(solution)/shard_map/ppermute | solution.py:33
  33.6 4.6 %collective-permute-done.2.one = bf16[96,1152]{1,0:T(8,128)(2,1)S(1)} collective-permute-done((bf16[96,1152]{1,0:T(8,128)(2,1)S(1)}, bf16[96,1152]{1,0:T(8,128)(2,1)S(1)}, u32[]{:S(2)}, u32[]{:S(2)}) %collective-permute-start.2) | collective-permute-done | bytes 221216 | tf_op jit(solution)/shard_map/ppermute | solution.py:33
  38.2 4.4 %collective-permute-done.3.two = bf16[96,1152]{1,0:T(8,128)(2,1)S(1)} collective-permute-done((bf16[96,1152]{1,0:T(8,128)(2,1)S(1)}, bf16[96,1152]{1,0:T(8,128)(2,1)S(1)}, u32[]{:S(2)}, u32[]{:S(2)}) %collective-permute-start.3) | collective-permute-done | bytes 221216 | tf_op jit(solution)/shard_map/ppermute | solution.py:33
  42.6 1.8 %collective-permute-start.4 = (bf16[96,1152]{1,0:T(8,128)(2,1)S(1)}, bf16[96,1152]{1,0:T(8,128)(2,1)S(1)}, u32[]{:S(2)}, u32[]{:S(2)}) collective-permute-start(bf16[96,1152]{1,0:T(8,128)(2,1)S(1)} %collective-permute-done.3.two), channel_id=1, source_target_pairs={{0,4},{2,30},{4,8},{6,2},{8,12},{10,6},{12,16},{14,10},{16,20},{18... | collective-permute-start | bytes 663560 | tf_op jit(solution)/shard_map/ppermute | solution.py:33
  44.4 0.7 collective-permute-start.5
  45.1 0.5 collective-permute-start.8
  45.6 7.5 %collective-permute-done.5.four = bf16[48,1152]{1,0:T(8,128)(2,1)S(1)} collective-permute-done((bf16[48,1152]{1,0:T(8,128)(2,1)S(1)}, bf16[48,1152]{1,0:T(8,128)(2,1)S(1)}, u32[]{:S(2)}, u32[]{:S(2)}) %collective-permute-start.5) | collective-permute-done | bytes 110624 | tf_op jit(solution)/shard_map/ppermute | solution.py:33
  53.2 0.1 collective-permute-start.7
  54.6 0.7 collective-permute-start.9
  55.4 0.9 collective-permute-done.9.four_other
  56.3 0.6 copy-done.9
  57.0 7.1 %scores.1 = (bf16[384,768]{1,0:T(8,128)(2,1)S(1)}, f32[384,1024]{1,0:T(8,128)}, f32[768,1024]{1,0:T(8,128)S(1)}, f32[1,128]{1,0:T(1,128)S(1)}) custom-call(s32[1]{0:T(128)} %bitcast.spot, f32[1]{0:T(128)S(6)} %copy.9.scale, f32[1]{0:T(128)S(6)} %copy.10.bias, bf16[96,1152]{1,0:T(8,128)(2,1)} %copy-done.1, bf16[96,1152]{1,0:T(8,128)(2,1)} %copy-done.3, ...), custom_call_target="tpu_custom_call" | custom-call | tf_op jit(solution)/shard_map/scores/pallas_call | solution.py:229
  64.2 0.4 collective-permute-start.13
  64.6 0.2 collective-permute-start.10
  64.8 2.5 %collective-permute-start.11 = (f32[1,128]{1,0:T(1,128)S(1)}, f32[1,128]{1,0:T(1,128)S(1)}, u32[]{:S(2)}, u32[]{:S(2)}) collective-permute-start(f32[1,128]{1,0:T(1,128)S(1)} %get-tuple-element.38), channel_id=1, source_target_pairs={{0,128},{1,129},{128,0},{129,1},{2,130},{3,131},{130,2},{131,3},{4... | collective-permute-start | bytes 1544 | tf_op jit(solution)/shard_map/ppermute | solution.py:64
  67.3 1.5 %collective-permute-start.12 = (f32[1,128]{1,0:T(1,128)S(1)}, f32[1,128]{1,0:T(1,128)S(1)}, u32[]{:S(2)}, u32[]{:S(2)}) collective-permute-start(f32[1,128]{1,0:T(1,128)S(1)} %get-tuple-element.38), channel_id=1, source_target_pairs={{0,129},{1,128},{128,1},{129,0},{2,131},{3,130},{130,3},{131,2},{4... | collective-permute-start | bytes 1544 | tf_op jit(solution)/shard_map/ppermute | solution.py:64
  68.7 1.5 %convert_element_type.45 = f16[768,1024]{1,0:T(8,128)(2,1)} convert(f32[768,1024]{1,0:T(8,128)S(1)} %get-tuple-element.37) | non-fusion elementwise | flops 786432 | bytes 4718592 | tf_op jit(solution)/shard_map/convert_element_type | solution.py:289
  70.2 0.6 collective-permute-done.12
  70.8 7.2 %all-to-all-start.1 = ((f16[16,48,1024]{2,1,0:T(8,128)(2,1)}), f16[16,48,1024]{2,1,0:T(8,128)(2,1)}, u32[]{:S(2)}, u32[]{:S(2)}) async-start(f16[16,48,1024]{2,1,0:T(8,128)(2,1)} %bitcast.13), calls=%async_computation.1 | async-start | bytes 3145728 | tf_op jit(solution)/shard_map/all_to_all | solution.py:20
  78.0 1.1 collective-permute-done.14
  79.2 2.2 %fusion.8 = (f16[384,1024]{1,0:T(8,128)(2,1)S(1)}, f32[384,1024]{1,0:T(8,128)S(1)}) fusion(f32[384,1024]{1,0:T(8,128)} %collective-permute-done.13, bf16[384,768]{1,0:T(8,128)(2,1)S(1)} %get-tuple-element.41, bf16[768,1024]{1,0:T(8,128)(2,1)S(1)} %bitcast.12), kind=kOutput, calls=%fused_computation.42 | convolution fusion | flops 604766208 | bytes 6094848 | tf_op jit(solution)/shard_map/dot_general | solution.py:294
  81.4 0.4 collective-permute-start.15
  81.8 3.3 %collective-permute-start.16 = (f16[48,1024]{1,0:T(8,128)(2,1)S(1)}, f16[48,1024]{1,0:T(8,128)(2,1)S(1)}, u32[]{:S(2)}, u32[]{:S(2)}) collective-permute-start(f16[48,1024]{1,0:T(8,128)(2,1)S(1)} %slice.37), channel_id=1, source_target_pairs={{0,24},{2,10},{4,28},{6,14},{8,0},{10,18},{12,4},{14,22},{16,8},{1... | collective-permute-start | bytes 294920 | tf_op jit(solution)/shard_map/ppermute | solution.py:33
  85.1 0.5 collective-permute-start.17
  85.6 5.7 %collective-permute-done.17 = f32[1,128]{1,0:T(1,128)S(1)} collective-permute-done((f32[1,128]{1,0:T(1,128)S(1)}, f32[1,128]{1,0:T(1,128)S(1)}, u32[]{:S(2)}, u32[]{:S(2)}) %collective-permute-start.17) | collective-permute-done | bytes 544 | tf_op jit(solution)/shard_map/ppermute | solution.py:59
  91.4 4.4 %collective-permute-done.18 = f32[1,128]{1,0:T(1,128)S(1)} collective-permute-done((f32[1,128]{1,0:T(1,128)S(1)}, f32[1,128]{1,0:T(1,128)S(1)}, u32[]{:S(2)}, u32[]{:S(2)}) %collective-permute-start.18) | collective-permute-done | bytes 544 | tf_op jit(solution)/shard_map/ppermute | solution.py:59
  96.0 2.3 %collective-permute-start.19 = (f16[96,1024]{1,0:T(8,128)(2,1)S(1)}, f16[96,1024]{1,0:T(8,128)(2,1)S(1)}, u32[]{:S(2)}, u32[]{:S(2)}) collective-permute-start(f16[96,1024]{1,0:T(8,128)(2,1)S(1)} %fusion), channel_id=1, source_target_pairs={{0,24},{2,10},{4,28},{6,14},{8,0},{10,18},{12,4},{14,22},{16,8},{1... | collective-permute-start | bytes 589832 | tf_op jit(solution)/shard_map/ppermute | solution.py:33
  98.3 2.0 %collective-permute-start.20 = (f32[1,128]{1,0:T(1,128)S(1)}, f32[1,128]{1,0:T(1,128)S(1)}, u32[]{:S(2)}, u32[]{:S(2)}) collective-permute-start(f32[1,128]{1,0:T(1,128)S(1)} %add.204), channel_id=1, source_target_pairs={{0,16},{4,20},{8,24},{12,28},{16,0},{20,4},{24,8},{28,12},{1,17},{... | collective-permute-start | bytes 1544 | tf_op jit(solution)/shard_map/ppermute | solution.py:59
  100.3 5.4 %collective-permute-done.20 = f32[1,128]{1,0:T(1,128)S(1)} collective-permute-done((f32[1,128]{1,0:T(1,128)S(1)}, f32[1,128]{1,0:T(1,128)S(1)}, u32[]{:S(2)}, u32[]{:S(2)}) %collective-permute-start.20) | collective-permute-done | bytes 544 | tf_op jit(solution)/shard_map/ppermute | solution.py:59
  105.7 1.6 %collective-permute-start.21 = (f32[1,128]{1,0:T(1,128)S(1)}, f32[1,128]{1,0:T(1,128)S(1)}, u32[]{:S(2)}, u32[]{:S(2)}) collective-permute-start(f32[1,128]{1,0:T(1,128)S(1)} %add.208), channel_id=1, source_target_pairs={{0,32},{32,0},{64,96},{96,64},{1,33},{33,1},{65,97},{97,65},{2,34}... | collective-permute-start | bytes 1544 | tf_op jit(solution)/shard_map/ppermute | solution.py:64
  107.3 2.7 %collective-permute-start.22 = (f32[1,128]{1,0:T(1,128)S(1)}, f32[1,128]{1,0:T(1,128)S(1)}, u32[]{:S(2)}, u32[]{:S(2)}) collective-permute-start(f32[1,128]{1,0:T(1,128)S(1)} %add.208), channel_id=1, source_target_pairs={{0,64},{32,96},{64,0},{96,32},{1,65},{33,97},{65,1},{97,33},{2,66}... | collective-permute-start | bytes 1544 | tf_op jit(solution)/shard_map/ppermute | solution.py:64
  110.0 0.6 collective-permute-start.23
  110.6 0.1 collective-permute-start.24
  110.7 2.4 %convert_reduce_fusion = f32[48,1024]{1,0:T(8,128)} fusion(f16[16,48,1024]{2,1,0:T(8,128)(2,1)} %all-to-all-done.1), kind=kLoop, calls=%fused_computation | loop fusion | flops 1523712 | bytes 1769472 | tf_op jit(solution)/shard_map/reduce_sum | solution.py:297
  113.1 1.6 %collective-permute-done.23 = f32[1,128]{1,0:T(1,128)S(1)} collective-permute-done((f32[1,128]{1,0:T(1,128)S(1)}, f32[1,128]{1,0:T(1,128)S(1)}, u32[]{:S(2)}, u32[]{:S(2)}) %collective-permute-start.23) | collective-permute-done | bytes 544 | tf_op jit(solution)/shard_map/ppermute | solution.py:64
  114.8 1.7 %fusion.3 = f32[48,1024]{1,0:T(8,128)} fusion(f32[48,1024]{1,0:T(8,128)S(1)} %collective-permute-done.24, f32[384,1024]{1,0:T(8,128)} %copy-done, f32[96,1024]{1,0:T(8,128)S(1)} %convert_element_type.51, s32[]{:T(128)S(6)} %select_n.119, f16[96,1024]{1,0:T(8,128)(2,1)S(1)} %slice.34), kind=kLoop, calls=%fused_computation.11 | loop fusion | flops 196608 | bytes 884740 | tf_op jit(solution)/shard_map/add | solution.py:86
  (62 shorter events, 0.8 us)
Async XLA Ops:
  0.6 6.9 %copy-start.10 = (s32[192]{0:T(256)S(1)}, s32[192]{0:T(256)}, u32[]{:S(2)}) copy-start(s32[192]{0:T(256)} %param.9) | copy-start | bytes 2308
  5.2 12.4 %collective-permute-start = (f32[96,1024]{1,0:T(8,128)S(1)}, f32[96,1024]{1,0:T(8,128)S(1)}, u32[]{:S(2)}, u32[]{:S(2)}) collective-permute-start(f32[96,1024]{1,0:T(8,128)S(1)} %get-tuple-element.30), channel_id=1, source_target_pairs={{0,1},{1,0},{2,3},{3,2},{4,5},{5,4},{6,7},{7,6},{8,9},{9,8},{10,11... | collective-permute-start | bytes 1179656 | tf_op jit(solution)/shard_map/ppermute | solution.py:156
  17.9 1.5 %collective-permute-start.1 = (bf16[96,1024]{1,0:T(8,128)(2,1)S(1)}, bf16[96,1024]{1,0:T(8,128)(2,1)S(1)}, u32[]{:S(2)}, u32[]{:S(2)}) collective-permute-start(bf16[96,1024]{1,0:T(8,128)(2,1)S(1)} %multiply_convert_fusion), channel_id=1, source_target_pairs={{0,2},{2,0},{1,3},{3,1},{4,6},{6,4},{5,7},{7,5},{8,10},{10,8},{9,1... | collective-permute-start | bytes 589832 | tf_op jit(solution)/shard_map/ppermute | solution.py:270
  19.6 10.8 %copy-start.1 = (bf16[96,1152]{1,0:T(8,128)(2,1)}, bf16[96,1152]{1,0:T(8,128)(2,1)S(1)}, u32[]{:S(2)}) copy-start(bf16[96,1152]{1,0:T(8,128)(2,1)S(1)} %pad_maximum_fusion.own) | copy-start | bytes 663556
  21.0 35.3 %all-to-all-start = ((bf16[16,48,1024]{2,1,0:T(8,128)(2,1)}), bf16[16,48,1024]{2,1,0:T(8,128)(2,1)S(1)}, u32[]{:S(2)}, u32[]{:S(2)}) async-start(bf16[16,48,1024]{2,1,0:T(8,128)(2,1)} %broadcast_in_dim.29), calls=%async_computation | async-start | bytes 3145728 | tf_op jit(solution)/shard_map/all_to_all | solution.py:20
  28.5 9.8 %collective-permute-start.2 = (bf16[96,1152]{1,0:T(8,128)(2,1)S(1)}, bf16[96,1152]{1,0:T(8,128)(2,1)S(1)}, u32[]{:S(2)}, u32[]{:S(2)}) collective-permute-start(bf16[96,1152]{1,0:T(8,128)(2,1)S(1)} %pad_maximum_fusion.own), channel_id=1, source_target_pairs={{0,4},{2,30},{4,8},{6,2},{8,12},{10,6},{12,16},{14,10},{16,20},{18... | collective-permute-start | bytes 663560 | tf_op jit(solution)/shard_map/ppermute | solution.py:33
  30.4 12.2 %collective-permute-start.3 = (bf16[96,1152]{1,0:T(8,128)(2,1)S(1)}, bf16[96,1152]{1,0:T(8,128)(2,1)S(1)}, u32[]{:S(2)}, u32[]{:S(2)}) collective-permute-start(bf16[96,1152]{1,0:T(8,128)(2,1)S(1)} %pad_maximum_fusion.own), channel_id=1, source_target_pairs={{0,8},{2,26},{4,12},{6,30},{8,16},{10,2},{12,20},{14,6},{16,24},{1... | collective-permute-start | bytes 663560 | tf_op jit(solution)/shard_map/ppermute | solution.py:33
  38.2 18.7 %copy-start.3 = (bf16[96,1152]{1,0:T(8,128)(2,1)}, bf16[96,1152]{1,0:T(8,128)(2,1)S(1)}, u32[]{:S(2)}) copy-start(bf16[96,1152]{1,0:T(8,128)(2,1)S(1)} %collective-permute-done.2.one) | copy-start | bytes 663556
  42.6 14.4 %copy-start.2 = (bf16[96,1152]{1,0:T(8,128)(2,1)}, bf16[96,1152]{1,0:T(8,128)(2,1)S(1)}, u32[]{:S(2)}) copy-start(bf16[96,1152]{1,0:T(8,128)(2,1)S(1)} %collective-permute-done.3.two) | copy-start | bytes 663556
  42.6 10.6 %collective-permute-start.4 = (bf16[96,1152]{1,0:T(8,128)(2,1)S(1)}, bf16[96,1152]{1,0:T(8,128)(2,1)S(1)}, u32[]{:S(2)}, u32[]{:S(2)}) collective-permute-start(bf16[96,1152]{1,0:T(8,128)(2,1)S(1)} %collective-permute-done.3.two), channel_id=1, source_target_pairs={{0,4},{2,30},{4,8},{6,2},{8,12},{10,6},{12,16},{14,10},{16,20},{18... | collective-permute-start | bytes 663560 | tf_op jit(solution)/shard_map/ppermute | solution.py:33
  44.4 8.7 %collective-permute-start.5 = (bf16[48,1152]{1,0:T(8,128)(2,1)S(1)}, bf16[48,1152]{1,0:T(8,128)(2,1)S(1)}, u32[]{:S(2)}, u32[]{:S(2)}) collective-permute-start(bf16[48,1152]{1,0:T(8,128)(2,1)S(1)} %constant_dynamic-slice_fusion), channel_id=1, source_target_pairs={{0,8},{2,26},{4,12},{6,30},{8,16},{10,2},{12,20},{14,6},{16,24},{1... | collective-permute-start | bytes 331784 | tf_op jit(solution)/shard_map/ppermute | solution.py:33
  45.1 10.3 %collective-permute-start.8 = (bf16[96,1152]{1,0:T(8,128)(2,1)S(1)}, bf16[96,1152]{1,0:T(8,128)(2,1)S(1)}, u32[]{:S(2)}, u32[]{:S(2)}) collective-permute-start(bf16[96,1152]{1,0:T(8,128)(2,1)S(1)} %collective-permute-done.3.two), channel_id=1, source_target_pairs={{0,2},{2,0},{1,3},{3,1},{4,6},{6,4},{5,7},{7,5},{8,10},{10,8},{9,1... | collective-permute-start | bytes 663560 | tf_op jit(solution)/shard_map/ppermute | solution.py:47
  45.6 9.8 %collective-permute-start.6 = (bf16[96,1152]{1,0:T(8,128)(2,1)S(1)}, bf16[96,1152]{1,0:T(8,128)(2,1)S(1)}, u32[]{:S(2)}, u32[]{:S(2)}) collective-permute-start(bf16[96,1152]{1,0:T(8,128)(2,1)S(1)} %collective-permute-done.2.one), channel_id=1, source_target_pairs={{0,2},{2,0},{1,3},{3,1},{4,6},{6,4},{5,7},{7,5},{8,10},{10,8},{9,1... | collective-permute-start | bytes 663560 | tf_op jit(solution)/shard_map/ppermute | solution.py:47
  53.2 3.1 %copy-start.8 = (bf16[48,1152]{1,0:T(8,128)(2,1)}, bf16[48,1152]{1,0:T(8,128)(2,1)S(1)}, u32[]{:S(2)}) copy-start(bf16[48,1152]{1,0:T(8,128)(2,1)S(1)} %collective-permute-done.5.four) | copy-start | bytes 331780
  53.2 3.8 %copy-start.4 = (bf16[96,1152]{1,0:T(8,128)(2,1)}, bf16[96,1152]{1,0:T(8,128)(2,1)S(1)}, u32[]{:S(2)}) copy-start(bf16[96,1152]{1,0:T(8,128)(2,1)S(1)} %collective-permute-done.4.three) | copy-start | bytes 663556
  53.2 3.1 %collective-permute-start.7 = (bf16[96,1152]{1,0:T(8,128)(2,1)S(1)}, bf16[96,1152]{1,0:T(8,128)(2,1)S(1)}, u32[]{:S(2)}, u32[]{:S(2)}) collective-permute-start(bf16[96,1152]{1,0:T(8,128)(2,1)S(1)} %collective-permute-done.4.three), channel_id=1, source_target_pairs={{0,2},{2,0},{1,3},{3,1},{4,6},{6,4},{5,7},{7,5},{8,10},{10,8},{9,1... | collective-permute-start | bytes 663560 | tf_op jit(solution)/shard_map/ppermute | solution.py:49
  54.6 1.7 %collective-permute-start.9 = (bf16[48,1152]{1,0:T(8,128)(2,1)S(1)}, bf16[48,1152]{1,0:T(8,128)(2,1)S(1)}, u32[]{:S(2)}, u32[]{:S(2)}) collective-permute-start(bf16[48,1152]{1,0:T(8,128)(2,1)S(1)} %collective-permute-done.5.four), channel_id=1, source_target_pairs={{0,2},{2,0},{1,3},{3,1},{4,6},{6,4},{5,7},{7,5},{8,10},{10,8},{9,1... | collective-permute-start | bytes 331784 | tf_op jit(solution)/shard_map/ppermute | solution.py:49
  55.4 1.6 %copy-start.6 = (bf16[96,1152]{1,0:T(8,128)(2,1)}, bf16[96,1152]{1,0:T(8,128)(2,1)S(1)}, u32[]{:S(2)}) copy-start(bf16[96,1152]{1,0:T(8,128)(2,1)S(1)} %collective-permute-done.6.one_other) | copy-start | bytes 663556
  55.4 1.5 %copy-start.5 = (bf16[96,1152]{1,0:T(8,128)(2,1)}, bf16[96,1152]{1,0:T(8,128)(2,1)S(1)}, u32[]{:S(2)}) copy-start(bf16[96,1152]{1,0:T(8,128)(2,1)S(1)} %collective-permute-done.8.two_other) | copy-start | bytes 663556
  56.3 0.6 copy-start.9
  56.3 0.7 copy-start.7
  64.2 15.0 %collective-permute-start.13 = (f32[384,1024]{1,0:T(8,128)}, f32[384,1024]{1,0:T(8,128)}, u32[]{:S(2)}, u32[]{:S(2)}) collective-permute-start(f32[384,1024]{1,0:T(8,128)} %get-tuple-element.42), channel_id=1, source_target_pairs={{0,2},{2,0},{1,3},{3,1},{4,6},{6,4},{5,7},{7,5},{8,10},{10,8},{9,1... | collective-permute-start | bytes 4718600 | tf_op jit(solution)/shard_map/ppermute | solution.py:287
  64.6 5.6 %collective-permute-start.10 = (f32[1,128]{1,0:T(1,128)S(1)}, f32[1,128]{1,0:T(1,128)S(1)}, u32[]{:S(2)}, u32[]{:S(2)}) collective-permute-start(f32[1,128]{1,0:T(1,128)S(1)} %get-tuple-element.38), channel_id=1, source_target_pairs={{0,1},{1,0},{128,129},{129,128},{2,3},{3,2},{130,131},{131,130},{4... | collective-permute-start | bytes 1544 | tf_op jit(solution)/shard_map/ppermute | solution.py:64
  64.8 5.4 %collective-permute-start.11 = (f32[1,128]{1,0:T(1,128)S(1)}, f32[1,128]{1,0:T(1,128)S(1)}, u32[]{:S(2)}, u32[]{:S(2)}) collective-permute-start(f32[1,128]{1,0:T(1,128)S(1)} %get-tuple-element.38), channel_id=1, source_target_pairs={{0,128},{1,129},{128,0},{129,1},{2,130},{3,131},{130,2},{131,3},{4... | collective-permute-start | bytes 1544 | tf_op jit(solution)/shard_map/ppermute | solution.py:64
  67.3 3.5 %collective-permute-start.12 = (f32[1,128]{1,0:T(1,128)S(1)}, f32[1,128]{1,0:T(1,128)S(1)}, u32[]{:S(2)}, u32[]{:S(2)}) collective-permute-start(f32[1,128]{1,0:T(1,128)S(1)} %get-tuple-element.38), channel_id=1, source_target_pairs={{0,129},{1,128},{128,1},{129,0},{2,131},{3,130},{130,3},{131,2},{4... | collective-permute-start | bytes 1544 | tf_op jit(solution)/shard_map/ppermute | solution.py:64
  70.8 34.9 %all-to-all-start.1 = ((f16[16,48,1024]{2,1,0:T(8,128)(2,1)}), f16[16,48,1024]{2,1,0:T(8,128)(2,1)}, u32[]{:S(2)}, u32[]{:S(2)}) async-start(f16[16,48,1024]{2,1,0:T(8,128)(2,1)} %bitcast.13), calls=%async_computation.1 | async-start | bytes 3145728 | tf_op jit(solution)/shard_map/all_to_all | solution.py:20
  78.0 1.1 collective-permute-start.14
  81.3 14.5 %copy-start = (f32[384,1024]{1,0:T(8,128)}, f32[384,1024]{1,0:T(8,128)S(1)}, u32[]{:S(2)}) copy-start(f32[384,1024]{1,0:T(8,128)S(1)} %get-tuple-element.56) | copy-start | bytes 4718596
  81.4 14.4 %collective-permute-start.15 = (f16[192,1024]{1,0:T(8,128)(2,1)S(1)}, f16[192,1024]{1,0:T(8,128)(2,1)S(1)}, u32[]{:S(2)}, u32[]{:S(2)}) collective-permute-start(f16[192,1024]{1,0:T(8,128)(2,1)S(1)} %slice.36), channel_id=1, source_target_pairs={{0,28},{2,6},{4,0},{6,10},{8,4},{10,14},{12,8},{14,18},{16,12},{18... | collective-permute-start | bytes 1179656 | tf_op jit(solution)/shard_map/ppermute | solution.py:33
  81.8 14.0 %collective-permute-start.16 = (f16[48,1024]{1,0:T(8,128)(2,1)S(1)}, f16[48,1024]{1,0:T(8,128)(2,1)S(1)}, u32[]{:S(2)}, u32[]{:S(2)}) collective-permute-start(f16[48,1024]{1,0:T(8,128)(2,1)S(1)} %slice.37), channel_id=1, source_target_pairs={{0,24},{2,10},{4,28},{6,14},{8,0},{10,18},{12,4},{14,22},{16,8},{1... | collective-permute-start | bytes 294920 | tf_op jit(solution)/shard_map/ppermute | solution.py:33
  85.1 6.3 %collective-permute-start.17 = (f32[1,128]{1,0:T(1,128)S(1)}, f32[1,128]{1,0:T(1,128)S(1)}, u32[]{:S(2)}, u32[]{:S(2)}) collective-permute-start(f32[1,128]{1,0:T(1,128)S(1)} %add.201), channel_id=1, source_target_pairs={{0,4},{4,0},{8,12},{12,8},{16,20},{20,16},{24,28},{28,24},{1,5},{5... | collective-permute-start | bytes 1544 | tf_op jit(solution)/shard_map/ppermute | solution.py:59
  91.4 4.4 %collective-permute-start.18 = (f32[1,128]{1,0:T(1,128)S(1)}, f32[1,128]{1,0:T(1,128)S(1)}, u32[]{:S(2)}, u32[]{:S(2)}) collective-permute-start(f32[1,128]{1,0:T(1,128)S(1)} %add.203), channel_id=1, source_target_pairs={{0,8},{4,12},{8,0},{12,4},{16,24},{20,28},{24,16},{28,20},{1,9},{5... | collective-permute-start | bytes 1544 | tf_op jit(solution)/shard_map/ppermute | solution.py:59
  96.0 9.8 %collective-permute-start.19 = (f16[96,1024]{1,0:T(8,128)(2,1)S(1)}, f16[96,1024]{1,0:T(8,128)(2,1)S(1)}, u32[]{:S(2)}, u32[]{:S(2)}) collective-permute-start(f16[96,1024]{1,0:T(8,128)(2,1)S(1)} %fusion), channel_id=1, source_target_pairs={{0,24},{2,10},{4,28},{6,14},{8,0},{10,18},{12,4},{14,22},{16,8},{1... | collective-permute-start | bytes 589832 | tf_op jit(solution)/shard_map/ppermute | solution.py:33
  98.3 7.4 %collective-permute-start.20 = (f32[1,128]{1,0:T(1,128)S(1)}, f32[1,128]{1,0:T(1,128)S(1)}, u32[]{:S(2)}, u32[]{:S(2)}) collective-permute-start(f32[1,128]{1,0:T(1,128)S(1)} %add.204), channel_id=1, source_target_pairs={{0,16},{4,20},{8,24},{12,28},{16,0},{20,4},{24,8},{28,12},{1,17},{... | collective-permute-start | bytes 1544 | tf_op jit(solution)/shard_map/ppermute | solution.py:59
  105.7 7.4 %collective-permute-start.21 = (f32[1,128]{1,0:T(1,128)S(1)}, f32[1,128]{1,0:T(1,128)S(1)}, u32[]{:S(2)}, u32[]{:S(2)}) collective-permute-start(f32[1,128]{1,0:T(1,128)S(1)} %add.208), channel_id=1, source_target_pairs={{0,32},{32,0},{64,96},{96,64},{1,33},{33,1},{65,97},{97,65},{2,34}... | collective-permute-start | bytes 1544 | tf_op jit(solution)/shard_map/ppermute | solution.py:64
  107.3 5.9 %collective-permute-start.22 = (f32[1,128]{1,0:T(1,128)S(1)}, f32[1,128]{1,0:T(1,128)S(1)}, u32[]{:S(2)}, u32[]{:S(2)}) collective-permute-start(f32[1,128]{1,0:T(1,128)S(1)} %add.208), channel_id=1, source_target_pairs={{0,64},{32,96},{64,0},{96,32},{1,65},{33,97},{65,1},{97,33},{2,66}... | collective-permute-start | bytes 1544 | tf_op jit(solution)/shard_map/ppermute | solution.py:64
  110.0 4.8 %collective-permute-start.23 = (f32[1,128]{1,0:T(1,128)S(1)}, f32[1,128]{1,0:T(1,128)S(1)}, u32[]{:S(2)}, u32[]{:S(2)}) collective-permute-start(f32[1,128]{1,0:T(1,128)S(1)} %add.208), channel_id=1, source_target_pairs={{0,96},{32,64},{64,32},{96,0},{1,97},{33,65},{65,33},{97,1},{2,98}... | collective-permute-start | bytes 1544 | tf_op jit(solution)/shard_map/ppermute | solution.py:64
  110.6 4.2 %collective-permute-start.24 = (f32[48,1024]{1,0:T(8,128)S(1)}, f32[48,1024]{1,0:T(8,128)S(1)}, u32[]{:S(2)}, u32[]{:S(2)}) collective-permute-start(f32[48,1024]{1,0:T(8,128)S(1)} %dynamic-slice_add_fusion), channel_id=1, source_target_pairs={{0,2},{2,0},{1,3},{3,1},{4,6},{6,4},{5,7},{7,5},{8,10},{10,8},{9,1... | collective-permute-start | bytes 589832 | tf_op jit(solution)/shard_map/ppermute | solution.py:84

commit v15 on v14

--- a/solution.py
+++ b/solution.py
@@ -61,7 +61,8 @@
 
 def with_other_three(value, axes):
     first, second, third = (
-        lax.ppermute(value, axes, [(i, i ^ k) for i in range(4)]) for k in (1, 2, 3)
+        lax.ppermute(value, axes, [(i, i ^ k) for i in range(lax.axis_size(axes))])
+        for k in (1, 2, 3)
     )
     return (value + first) + (second + third)
 
@@ -70,7 +71,7 @@
     half = kept.shape[0] // 8
     one_three = along_z(kept[: 4 * half].astype(SENT), -1)
     four = along_z(kept[6 * half : 7 * half].astype(SENT), -2)
-    loss = with_partner(with_partner(loss, "z", 1), "z", 2)
+    loss = with_other_three(loss, "z")
     one_three, four, loss = tied(one_three, four, loss)
     four = four.astype(F32)
     upper = kept[4 * half : 5 * half] + jnp.where(section == 0, four, 0.0)

time: 118 us -> 116 us (0.983)
  waiting for transfers between devices: 47.5 us -> 42.2 us
  starting transfers between devices: 44 us -> 47.2 us
    ppermute x4 -> x2, waiting for transfers between devices: 16.7 us -> 7.29 us  [with_partner(): return value + lax.ppermute(value, axis, pairs)]
    ppermute x6 -> x9, starting transfers between devices: 8.88 us -> 13.3 us  [with_other_three(): lax.ppermute(value, axes, [(i, i ^ k) for i in range(lax.axis_size(axes))])]
    ppermute x7, waiting for transfers between devices: 16.5 us -> 20 us  [along_z(): return lax.ppermute(array, ('z', 'section'), pairs)]
    ppermute x4 -> x2, starting transfers between devices: 2.57 us -> 1.24 us  [with_partner(): return value + lax.ppermute(value, axis, pairs)]
    ppermute x6 -> x9, waiting for transfers between devices: 2.2 us -> 2.77 us  [with_other_three(): lax.ppermute(value, axes, [(i, i ^ k) for i in range(lax.axis_size(axes))])]
  transfers between devices with their start and end apart: 27 -> 28, of which waited for: 12 -> 12; matrix products, arithmetic and copies ran while one was open for 6% -> 6% of each run, Pallas kernels for 0% -> 0%
where the time goes in v15:
time: 116 us; the launch traced here: 115 us
  starting transfers between devices  47.2 us (41%)
  waiting for transfers between devices  42.2 us (36%)
  Pallas kernels  11.7 us (10%)
  other arithmetic  6.32 us (5%)
  between operations  3.4 us (3%)
  local copies, waits for them, and re-layouts  2.42 us (2%)
  matrix products  2.19 us (2%)
    ppermute x7, waiting for transfers between devices, along_z(): return lax.ppermute(array, ('z', 'section'), pairs)  20 us
    all_to_all x2, starting transfers between devices, exchanged(): return lax.all_to_all(parts, axes, split_axis=0, concat_axis=0, tiled=True)  14.7 us
    ppermute x7, starting transfers between devices, along_z(): return lax.ppermute(array, ('z', 'section'), pairs)  13.8 us
    ppermute x9, starting transfers between devices, with_other_three(): lax.ppermute(value, axes, [(i, i ^ k) for i in range(lax.axis_size(axes))])  13.3 us
    ppermute x1, waiting for transfers between devices, tower(): raw = own + lax.ppermute(sent, 'tensor', SWAP)  9.91 us
    ppermute x2, waiting for transfers between devices, with_partner(): return value + lax.ppermute(value, axis, pairs)  7.29 us
    pallas_call x1, Pallas kernels, scored(): pl.pallas_call(score_kernel, in_specs=[scalar] * 3 + [pl.BlockSpec(memory...  7.13 us
    pallas_call x1, Pallas kernels, tower(): pl.pallas_call(tower_kernel, in_specs=[pl.BlockSpec(memory_space=pltpu.SM...  4.54 us
  transfers between devices with their start and end apart: 28, of which 12 were waited for; matrix products, arithmetic and copies ran while one was open for 6% of the time, Pallas kernels for 0%

profile of v15, /device:TPU:4, one launch (start us, length us, event | category | flops | bytes accessed | tf_op | source)
XLA Modules:
  0.0 115.5 jit_solution(4567586988131786072)
XLA Ops:
  0.6 4.5 %tower.1 = (f32[96,1024]{1,0:T(8,128)S(1)}, f32[96,1024]{1,0:T(8,128)S(1)}) custom-call(s32[1]{0:T(128)} %bitcast.1.spot, bf16[192,1024]{1,0:T(8,128)(2,1)} %bitcast.16, bf16[1024,2048]{1,0:T(8,128)(2,1)} %bitcast.14, bf16[2048,1024]{1,0:T(8,128)(2,1)} %bitcast.15), custom_call_target="tpu_custom_call" | custom-call | tf_op jit(solution)/shard_map/tower/pallas_call | solution.py:140
  5.2 2.3 %collective-permute-start = (f32[96,1024]{1,0:T(8,128)S(1)}, f32[96,1024]{1,0:T(8,128)S(1)}, u32[]{:S(2)}, u32[]{:S(2)}) collective-permute-start(f32[96,1024]{1,0:T(8,128)S(1)} %get-tuple-element.30), channel_id=1, source_target_pairs={{0,1},{1,0},{2,3},{3,2},{4,5},{5,4},{6,7},{7,6},{8,9},{9,8},{10,11... | collective-permute-start | bytes 1179656 | tf_op jit(solution)/shard_map/ppermute | solution.py:157
  7.7 9.9 %collective-permute-done = f32[96,1024]{1,0:T(8,128)S(1)} collective-permute-done((f32[96,1024]{1,0:T(8,128)S(1)}, f32[96,1024]{1,0:T(8,128)S(1)}, u32[]{:S(2)}, u32[]{:S(2)}) %collective-permute-start) | collective-permute-done | bytes 393248 | tf_op jit(solution)/shard_map/ppermute | solution.py:157
  17.6 0.1 multiply_reduce_fusion
  17.8 0.1 multiply_convert_fusion
  17.9 0.1 collective-permute-start.1
  18.1 1.3 %collective-permute-done.1 = bf16[96,1024]{1,0:T(8,128)(2,1)S(1)} collective-permute-done((bf16[96,1024]{1,0:T(8,128)(2,1)S(1)}, bf16[96,1024]{1,0:T(8,128)(2,1)S(1)}, u32[]{:S(2)}, u32[]{:S(2)}) %collective-permute-start.1) | collective-permute-done | bytes 196640 | tf_op jit(solution)/shard_map/ppermute | solution.py:271
  19.4 0.1 broadcast_select_fusion
  19.6 1.4 %broadcast_in_dim.29 = bf16[16,48,1024]{2,1,0:T(8,128)(2,1)} broadcast(bf16[48,1024]{1,0:T(8,128)(2,1)S(1)} %dynamic-slice_select_fusion), dimensions={1,2} | broadcast | bytes 1671168 | tf_op jit(solution)/shard_map/broadcast_in_dim | solution.py:275
  21.0 7.5 %all-to-all-start = ((bf16[16,48,1024]{2,1,0:T(8,128)(2,1)}), bf16[16,48,1024]{2,1,0:T(8,128)(2,1)S(1)}, u32[]{:S(2)}, u32[]{:S(2)}) async-start(bf16[16,48,1024]{2,1,0:T(8,128)(2,1)} %broadcast_in_dim.29), calls=%async_computation | async-start | bytes 3145728 | tf_op jit(solution)/shard_map/all_to_all | solution.py:20
  28.4 1.9 %collective-permute-start.2 = (bf16[96,1152]{1,0:T(8,128)(2,1)S(1)}, bf16[96,1152]{1,0:T(8,128)(2,1)S(1)}, u32[]{:S(2)}, u32[]{:S(2)}) collective-permute-start(bf16[96,1152]{1,0:T(8,128)(2,1)S(1)} %pad_maximum_fusion.own), channel_id=1, source_target_pairs={{0,4},{2,30},{4,8},{6,2},{8,12},{10,6},{12,16},{14,10},{16,20},{18... | collective-permute-start | bytes 663560 | tf_op jit(solution)/shard_map/ppermute | solution.py:33
  30.4 3.3 %collective-permute-start.3 = (bf16[96,1152]{1,0:T(8,128)(2,1)S(1)}, bf16[96,1152]{1,0:T(8,128)(2,1)S(1)}, u32[]{:S(2)}, u32[]{:S(2)}) collective-permute-start(bf16[96,1152]{1,0:T(8,128)(2,1)S(1)} %pad_maximum_fusion.own), channel_id=1, source_target_pairs={{0,8},{2,26},{4,12},{6,30},{8,16},{10,2},{12,20},{14,6},{16,24},{1... | collective-permute-start | bytes 663560 | tf_op jit(solution)/shard_map/ppermute | solution.py:33
  33.6 4.6 %collective-permute-done.2.one = bf16[96,1152]{1,0:T(8,128)(2,1)S(1)} collective-permute-done((bf16[96,1152]{1,0:T(8,128)(2,1)S(1)}, bf16[96,1152]{1,0:T(8,128)(2,1)S(1)}, u32[]{:S(2)}, u32[]{:S(2)}) %collective-permute-start.2) | collective-permute-done | bytes 221216 | tf_op jit(solution)/shard_map/ppermute | solution.py:33
  38.2 4.4 %collective-permute-done.3.two = bf16[96,1152]{1,0:T(8,128)(2,1)S(1)} collective-permute-done((bf16[96,1152]{1,0:T(8,128)(2,1)S(1)}, bf16[96,1152]{1,0:T(8,128)(2,1)S(1)}, u32[]{:S(2)}, u32[]{:S(2)}) %collective-permute-start.3) | collective-permute-done | bytes 221216 | tf_op jit(solution)/shard_map/ppermute | solution.py:33
  42.6 1.8 %collective-permute-start.4 = (bf16[96,1152]{1,0:T(8,128)(2,1)S(1)}, bf16[96,1152]{1,0:T(8,128)(2,1)S(1)}, u32[]{:S(2)}, u32[]{:S(2)}) collective-permute-start(bf16[96,1152]{1,0:T(8,128)(2,1)S(1)} %collective-permute-done.3.two), channel_id=1, source_target_pairs={{0,4},{2,30},{4,8},{6,2},{8,12},{10,6},{12,16},{14,10},{16,20},{18... | collective-permute-start | bytes 663560 | tf_op jit(solution)/shard_map/ppermute | solution.py:33
  44.4 0.7 collective-permute-start.5
  45.1 0.5 collective-permute-start.8
  45.6 7.5 %collective-permute-done.5.four = bf16[48,1152]{1,0:T(8,128)(2,1)S(1)} collective-permute-done((bf16[48,1152]{1,0:T(8,128)(2,1)S(1)}, bf16[48,1152]{1,0:T(8,128)(2,1)S(1)}, u32[]{:S(2)}, u32[]{:S(2)}) %collective-permute-start.5) | collective-permute-done | bytes 110624 | tf_op jit(solution)/shard_map/ppermute | solution.py:33
  54.6 0.7 collective-permute-start.9
  55.4 0.9 collective-permute-done.9.four_other
  56.3 0.6 copy-done.9
  57.0 7.1 %scores.1 = (bf16[384,768]{1,0:T(8,128)(2,1)S(1)}, f32[384,1024]{1,0:T(8,128)}, f32[768,1024]{1,0:T(8,128)S(1)}, f32[1,128]{1,0:T(1,128)S(1)}) custom-call(s32[1]{0:T(128)} %bitcast.spot, f32[1]{0:T(128)S(6)} %copy.9.scale, f32[1]{0:T(128)S(6)} %copy.10.bias, bf16[96,1152]{1,0:T(8,128)(2,1)} %copy-done.1, bf16[96,1152]{1,0:T(8,128)(2,1)} %copy-done.3, ...), custom_call_target="tpu_custom_call" | custom-call | tf_op jit(solution)/shard_map/scores/pallas_call | solution.py:230
  64.2 0.4 collective-permute-start.13
  64.6 0.2 collective-permute-start.10
  64.8 2.5 %collective-permute-start.11 = (f32[1,128]{1,0:T(1,128)S(1)}, f32[1,128]{1,0:T(1,128)S(1)}, u32[]{:S(2)}, u32[]{:S(2)}) collective-permute-start(f32[1,128]{1,0:T(1,128)S(1)} %get-tuple-element.38), channel_id=1, source_target_pairs={{0,128},{1,129},{128,0},{129,1},{2,130},{3,131},{130,2},{131,3},{4... | collective-permute-start | bytes 1544 | tf_op jit(solution)/shard_map/ppermute | solution.py:64
  67.2 1.5 %collective-permute-start.12 = (f32[1,128]{1,0:T(1,128)S(1)}, f32[1,128]{1,0:T(1,128)S(1)}, u32[]{:S(2)}, u32[]{:S(2)}) collective-permute-start(f32[1,128]{1,0:T(1,128)S(1)} %get-tuple-element.38), channel_id=1, source_target_pairs={{0,129},{1,128},{128,1},{129,0},{2,131},{3,130},{130,3},{131,2},{4... | collective-permute-start | bytes 1544 | tf_op jit(solution)/shard_map/ppermute | solution.py:64
  68.7 1.5 %convert_element_type.45 = f16[768,1024]{1,0:T(8,128)(2,1)} convert(f32[768,1024]{1,0:T(8,128)S(1)} %get-tuple-element.37) | non-fusion elementwise | flops 786432 | bytes 4718592 | tf_op jit(solution)/shard_map/convert_element_type | solution.py:290
  70.2 0.6 collective-permute-done.12
  70.8 7.2 %all-to-all-start.1 = ((f16[16,48,1024]{2,1,0:T(8,128)(2,1)}), f16[16,48,1024]{2,1,0:T(8,128)(2,1)}, u32[]{:S(2)}, u32[]{:S(2)}) async-start(f16[16,48,1024]{2,1,0:T(8,128)(2,1)} %bitcast.13), calls=%async_computation.1 | async-start | bytes 3145728 | tf_op jit(solution)/shard_map/all_to_all | solution.py:20
  78.0 1.1 collective-permute-done.14
  79.1 2.2 %fusion.8 = (f16[384,1024]{1,0:T(8,128)(2,1)S(1)}, f32[384,1024]{1,0:T(8,128)S(1)}) fusion(f32[384,1024]{1,0:T(8,128)} %collective-permute-done.13, bf16[384,768]{1,0:T(8,128)(2,1)S(1)} %get-tuple-element.41, bf16[768,1024]{1,0:T(8,128)(2,1)S(1)} %bitcast.12), kind=kOutput, calls=%fused_computation.43 | convolution fusion | flops 604766208 | bytes 6094848 | tf_op jit(solution)/shard_map/dot_general | solution.py:295
  81.4 0.4 collective-permute-start.15
  81.8 1.7 %collective-permute-start.17 = (f32[1,128]{1,0:T(1,128)S(1)}, f32[1,128]{1,0:T(1,128)S(1)}, u32[]{:S(2)}, u32[]{:S(2)}) collective-permute-start(f32[1,128]{1,0:T(1,128)S(1)} %add.204), channel_id=1, source_target_pairs={{0,4},{4,0},{8,12},{12,8},{16,20},{20,16},{24,28},{28,24},{1,5},{5... | collective-permute-start | bytes 1544 | tf_op jit(solution)/shard_map/ppermute | solution.py:64
  83.5 0.5 collective-permute-start.18
  84.0 2.2 %collective-permute-start.19 = (f32[1,128]{1,0:T(1,128)S(1)}, f32[1,128]{1,0:T(1,128)S(1)}, u32[]{:S(2)}, u32[]{:S(2)}) collective-permute-start(f32[1,128]{1,0:T(1,128)S(1)} %add.204), channel_id=1, source_target_pairs={{0,12},{4,8},{8,4},{12,0},{16,28},{20,24},{24,20},{28,16},{1,13},{... | collective-permute-start | bytes 1544 | tf_op jit(solution)/shard_map/ppermute | solution.py:64
  86.2 2.6 %collective-permute-start.16 = (f16[48,1024]{1,0:T(8,128)(2,1)S(1)}, f16[48,1024]{1,0:T(8,128)(2,1)S(1)}, u32[]{:S(2)}, u32[]{:S(2)}) collective-permute-start(f16[48,1024]{1,0:T(8,128)(2,1)S(1)} %slice.37), channel_id=1, source_target_pairs={{0,24},{2,10},{4,28},{6,14},{8,0},{10,18},{12,4},{14,22},{16,8},{1... | collective-permute-start | bytes 294920 | tf_op jit(solution)/shard_map/ppermute | solution.py:33
  88.8 0.6 collective-permute-done.17
  89.4 3.5 %collective-permute-done.16 = f16[48,1024]{1,0:T(8,128)(2,1)S(1)} collective-permute-done((f16[48,1024]{1,0:T(8,128)(2,1)S(1)}, f16[48,1024]{1,0:T(8,128)(2,1)S(1)}, u32[]{:S(2)}, u32[]{:S(2)}) %collective-permute-start.16) | collective-permute-done | bytes 98336 | tf_op jit(solution)/shard_map/ppermute | solution.py:33
  93.0 3.1 %collective-permute-start.20 = (f16[96,1024]{1,0:T(8,128)(2,1)S(1)}, f16[96,1024]{1,0:T(8,128)(2,1)S(1)}, u32[]{:S(2)}, u32[]{:S(2)}) collective-permute-start(f16[96,1024]{1,0:T(8,128)(2,1)S(1)} %fusion), channel_id=1, source_target_pairs={{0,24},{2,10},{4,28},{6,14},{8,0},{10,18},{12,4},{14,22},{16,8},{1... | collective-permute-start | bytes 589832 | tf_op jit(solution)/shard_map/ppermute | solution.py:33
  96.2 1.2 %collective-permute-start.21 = (f32[1,128]{1,0:T(1,128)S(1)}, f32[1,128]{1,0:T(1,128)S(1)}, u32[]{:S(2)}, u32[]{:S(2)}) collective-permute-start(f32[1,128]{1,0:T(1,128)S(1)} %add_add_fusion.1), channel_id=1, source_target_pairs={{0,16},{4,20},{8,24},{12,28},{16,0},{20,4},{24,8},{28,12},{1,17},{... | collective-permute-start | bytes 1544 | tf_op jit(solution)/shard_map/ppermute | solution.py:59
  97.4 6.2 %collective-permute-done.21 = f32[1,128]{1,0:T(1,128)S(1)} collective-permute-done((f32[1,128]{1,0:T(1,128)S(1)}, f32[1,128]{1,0:T(1,128)S(1)}, u32[]{:S(2)}, u32[]{:S(2)}) %collective-permute-start.21) | collective-permute-done | bytes 544 | tf_op jit(solution)/shard_map/ppermute | solution.py:59
  103.6 1.6 %collective-permute-start.22 = (f32[1,128]{1,0:T(1,128)S(1)}, f32[1,128]{1,0:T(1,128)S(1)}, u32[]{:S(2)}, u32[]{:S(2)}) collective-permute-start(f32[1,128]{1,0:T(1,128)S(1)} %add.212), channel_id=1, source_target_pairs={{0,32},{32,0},{64,96},{96,64},{1,33},{33,1},{65,97},{97,65},{2,34}... | collective-permute-start | bytes 1544 | tf_op jit(solution)/shard_map/ppermute | solution.py:64
  105.2 2.7 %collective-permute-start.23 = (f32[1,128]{1,0:T(1,128)S(1)}, f32[1,128]{1,0:T(1,128)S(1)}, u32[]{:S(2)}, u32[]{:S(2)}) collective-permute-start(f32[1,128]{1,0:T(1,128)S(1)} %add.212), channel_id=1, source_target_pairs={{0,64},{32,96},{64,0},{96,32},{1,65},{33,97},{65,1},{97,33},{2,66}... | collective-permute-start | bytes 1544 | tf_op jit(solution)/shard_map/ppermute | solution.py:64
  107.8 0.6 collective-permute-start.24
  108.5 0.1 collective-permute-start.25
  108.6 2.4 %convert_reduce_fusion = f32[48,1024]{1,0:T(8,128)} fusion(f16[16,48,1024]{2,1,0:T(8,128)(2,1)} %all-to-all-done.1), kind=kLoop, calls=%fused_computation | loop fusion | flops 1523712 | bytes 1769472 | tf_op jit(solution)/shard_map/reduce_sum | solution.py:298
  111.0 1.6 %collective-permute-done.24 = f32[1,128]{1,0:T(1,128)S(1)} collective-permute-done((f32[1,128]{1,0:T(1,128)S(1)}, f32[1,128]{1,0:T(1,128)S(1)}, u32[]{:S(2)}, u32[]{:S(2)}) %collective-permute-start.24) | collective-permute-done | bytes 544 | tf_op jit(solution)/shard_map/ppermute | solution.py:64
  112.7 1.7 %fusion.3 = f32[48,1024]{1,0:T(8,128)} fusion(f32[48,1024]{1,0:T(8,128)S(1)} %collective-permute-done.25, f32[384,1024]{1,0:T(8,128)} %copy-done, f32[96,1024]{1,0:T(8,128)S(1)} %convert_element_type.51, s32[]{:T(128)S(6)} %select_n.119, f16[96,1024]{1,0:T(8,128)(2,1)S(1)} %slice.34), kind=kLoop, calls=%fused_computation.11 | loop fusion | flops 196608 | bytes 884740 | tf_op jit(solution)/shard_map/add | solution.py:87
  (63 shorter events, 1.0 us)
Async XLA Ops:
  0.6 6.9 %copy-start.10 = (s32[192]{0:T(256)S(1)}, s32[192]{0:T(256)}, u32[]{:S(2)}) copy-start(s32[192]{0:T(256)} %param.9) | copy-start | bytes 2308
  5.2 12.4 %collective-permute-start = (f32[96,1024]{1,0:T(8,128)S(1)}, f32[96,1024]{1,0:T(8,128)S(1)}, u32[]{:S(2)}, u32[]{:S(2)}) collective-permute-start(f32[96,1024]{1,0:T(8,128)S(1)} %get-tuple-element.30), channel_id=1, source_target_pairs={{0,1},{1,0},{2,3},{3,2},{4,5},{5,4},{6,7},{7,6},{8,9},{9,8},{10,11... | collective-permute-start | bytes 1179656 | tf_op jit(solution)/shard_map/ppermute | solution.py:157
  17.9 1.5 %collective-permute-start.1 = (bf16[96,1024]{1,0:T(8,128)(2,1)S(1)}, bf16[96,1024]{1,0:T(8,128)(2,1)S(1)}, u32[]{:S(2)}, u32[]{:S(2)}) collective-permute-start(bf16[96,1024]{1,0:T(8,128)(2,1)S(1)} %multiply_convert_fusion), channel_id=1, source_target_pairs={{0,2},{2,0},{1,3},{3,1},{4,6},{6,4},{5,7},{7,5},{8,10},{10,8},{9,1... | collective-permute-start | bytes 589832 | tf_op jit(solution)/shard_map/ppermute | solution.py:271
  19.6 10.8 %copy-start.1 = (bf16[96,1152]{1,0:T(8,128)(2,1)}, bf16[96,1152]{1,0:T(8,128)(2,1)S(1)}, u32[]{:S(2)}) copy-start(bf16[96,1152]{1,0:T(8,128)(2,1)S(1)} %pad_maximum_fusion.own) | copy-start | bytes 663556
  21.0 35.3 %all-to-all-start = ((bf16[16,48,1024]{2,1,0:T(8,128)(2,1)}), bf16[16,48,1024]{2,1,0:T(8,128)(2,1)S(1)}, u32[]{:S(2)}, u32[]{:S(2)}) async-start(bf16[16,48,1024]{2,1,0:T(8,128)(2,1)} %broadcast_in_dim.29), calls=%async_computation | async-start | bytes 3145728 | tf_op jit(solution)/shard_map/all_to_all | solution.py:20
  28.4 9.8 %collective-permute-start.2 = (bf16[96,1152]{1,0:T(8,128)(2,1)S(1)}, bf16[96,1152]{1,0:T(8,128)(2,1)S(1)}, u32[]{:S(2)}, u32[]{:S(2)}) collective-permute-start(bf16[96,1152]{1,0:T(8,128)(2,1)S(1)} %pad_maximum_fusion.own), channel_id=1, source_target_pairs={{0,4},{2,30},{4,8},{6,2},{8,12},{10,6},{12,16},{14,10},{16,20},{18... | collective-permute-start | bytes 663560 | tf_op jit(solution)/shard_map/ppermute | solution.py:33
  30.4 12.2 %collective-permute-start.3 = (bf16[96,1152]{1,0:T(8,128)(2,1)S(1)}, bf16[96,1152]{1,0:T(8,128)(2,1)S(1)}, u32[]{:S(2)}, u32[]{:S(2)}) collective-permute-start(bf16[96,1152]{1,0:T(8,128)(2,1)S(1)} %pad_maximum_fusion.own), channel_id=1, source_target_pairs={{0,8},{2,26},{4,12},{6,30},{8,16},{10,2},{12,20},{14,6},{16,24},{1... | collective-permute-start | bytes 663560 | tf_op jit(solution)/shard_map/ppermute | solution.py:33
  38.2 18.7 %copy-start.3 = (bf16[96,1152]{1,0:T(8,128)(2,1)}, bf16[96,1152]{1,0:T(8,128)(2,1)S(1)}, u32[]{:S(2)}) copy-start(bf16[96,1152]{1,0:T(8,128)(2,1)S(1)} %collective-permute-done.2.one) | copy-start | bytes 663556
  42.6 14.4 %copy-start.2 = (bf16[96,1152]{1,0:T(8,128)(2,1)}, bf16[96,1152]{1,0:T(8,128)(2,1)S(1)}, u32[]{:S(2)}) copy-start(bf16[96,1152]{1,0:T(8,128)(2,1)S(1)} %collective-permute-done.3.two) | copy-start | bytes 663556
  42.6 10.6 %collective-permute-start.4 = (bf16[96,1152]{1,0:T(8,128)(2,1)S(1)}, bf16[96,1152]{1,0:T(8,128)(2,1)S(1)}, u32[]{:S(2)}, u32[]{:S(2)}) collective-permute-start(bf16[96,1152]{1,0:T(8,128)(2,1)S(1)} %collective-permute-done.3.two), channel_id=1, source_target_pairs={{0,4},{2,30},{4,8},{6,2},{8,12},{10,6},{12,16},{14,10},{16,20},{18... | collective-permute-start | bytes 663560 | tf_op jit(solution)/shard_map/ppermute | solution.py:33
  44.4 8.7 %collective-permute-start.5 = (bf16[48,1152]{1,0:T(8,128)(2,1)S(1)}, bf16[48,1152]{1,0:T(8,128)(2,1)S(1)}, u32[]{:S(2)}, u32[]{:S(2)}) collective-permute-start(bf16[48,1152]{1,0:T(8,128)(2,1)S(1)} %constant_dynamic-slice_fusion), channel_id=1, source_target_pairs={{0,8},{2,26},{4,12},{6,30},{8,16},{10,2},{12,20},{14,6},{16,24},{1... | collective-permute-start | bytes 331784 | tf_op jit(solution)/shard_map/ppermute | solution.py:33
  45.1 10.3 %collective-permute-start.8 = (bf16[96,1152]{1,0:T(8,128)(2,1)S(1)}, bf16[96,1152]{1,0:T(8,128)(2,1)S(1)}, u32[]{:S(2)}, u32[]{:S(2)}) collective-permute-start(bf16[96,1152]{1,0:T(8,128)(2,1)S(1)} %collective-permute-done.3.two), channel_id=1, source_target_pairs={{0,2},{2,0},{1,3},{3,1},{4,6},{6,4},{5,7},{7,5},{8,10},{10,8},{9,1... | collective-permute-start | bytes 663560 | tf_op jit(solution)/shard_map/ppermute | solution.py:47
  45.6 9.8 %collective-permute-start.6 = (bf16[96,1152]{1,0:T(8,128)(2,1)S(1)}, bf16[96,1152]{1,0:T(8,128)(2,1)S(1)}, u32[]{:S(2)}, u32[]{:S(2)}) collective-permute-start(bf16[96,1152]{1,0:T(8,128)(2,1)S(1)} %collective-permute-done.2.one), channel_id=1, source_target_pairs={{0,2},{2,0},{1,3},{3,1},{4,6},{6,4},{5,7},{7,5},{8,10},{10,8},{9,1... | collective-permute-start | bytes 663560 | tf_op jit(solution)/shard_map/ppermute | solution.py:47
  53.2 3.1 %copy-start.8 = (bf16[48,1152]{1,0:T(8,128)(2,1)}, bf16[48,1152]{1,0:T(8,128)(2,1)S(1)}, u32[]{:S(2)}) copy-start(bf16[48,1152]{1,0:T(8,128)(2,1)S(1)} %collective-permute-done.5.four) | copy-start | bytes 331780
  53.2 3.8 %copy-start.4 = (bf16[96,1152]{1,0:T(8,128)(2,1)}, bf16[96,1152]{1,0:T(8,128)(2,1)S(1)}, u32[]{:S(2)}) copy-start(bf16[96,1152]{1,0:T(8,128)(2,1)S(1)} %collective-permute-done.4.three) | copy-start | bytes 663556
  53.2 3.1 %collective-permute-start.7 = (bf16[96,1152]{1,0:T(8,128)(2,1)S(1)}, bf16[96,1152]{1,0:T(8,128)(2,1)S(1)}, u32[]{:S(2)}, u32[]{:S(2)}) collective-permute-start(bf16[96,1152]{1,0:T(8,128)(2,1)S(1)} %collective-permute-done.4.three), channel_id=1, source_target_pairs={{0,2},{2,0},{1,3},{3,1},{4,6},{6,4},{5,7},{7,5},{8,10},{10,8},{9,1... | collective-permute-start | bytes 663560 | tf_op jit(solution)/shard_map/ppermute | solution.py:49
  54.6 1.7 %collective-permute-start.9 = (bf16[48,1152]{1,0:T(8,128)(2,1)S(1)}, bf16[48,1152]{1,0:T(8,128)(2,1)S(1)}, u32[]{:S(2)}, u32[]{:S(2)}) collective-permute-start(bf16[48,1152]{1,0:T(8,128)(2,1)S(1)} %collective-permute-done.5.four), channel_id=1, source_target_pairs={{0,2},{2,0},{1,3},{3,1},{4,6},{6,4},{5,7},{7,5},{8,10},{10,8},{9,1... | collective-permute-start | bytes 331784 | tf_op jit(solution)/shard_map/ppermute | solution.py:49
  55.4 1.6 %copy-start.6 = (bf16[96,1152]{1,0:T(8,128)(2,1)}, bf16[96,1152]{1,0:T(8,128)(2,1)S(1)}, u32[]{:S(2)}) copy-start(bf16[96,1152]{1,0:T(8,128)(2,1)S(1)} %collective-permute-done.6.one_other) | copy-start | bytes 663556
  55.4 1.5 %copy-start.5 = (bf16[96,1152]{1,0:T(8,128)(2,1)}, bf16[96,1152]{1,0:T(8,128)(2,1)S(1)}, u32[]{:S(2)}) copy-start(bf16[96,1152]{1,0:T(8,128)(2,1)S(1)} %collective-permute-done.8.two_other) | copy-start | bytes 663556
  56.3 0.6 copy-start.9
  56.3 0.7 copy-start.7
  64.2 15.0 %collective-permute-start.13 = (f32[384,1024]{1,0:T(8,128)}, f32[384,1024]{1,0:T(8,128)}, u32[]{:S(2)}, u32[]{:S(2)}) collective-permute-start(f32[384,1024]{1,0:T(8,128)} %get-tuple-element.42), channel_id=1, source_target_pairs={{0,2},{2,0},{1,3},{3,1},{4,6},{6,4},{5,7},{7,5},{8,10},{10,8},{9,1... | collective-permute-start | bytes 4718600 | tf_op jit(solution)/shard_map/ppermute | solution.py:288
  64.6 5.6 %collective-permute-start.10 = (f32[1,128]{1,0:T(1,128)S(1)}, f32[1,128]{1,0:T(1,128)S(1)}, u32[]{:S(2)}, u32[]{:S(2)}) collective-permute-start(f32[1,128]{1,0:T(1,128)S(1)} %get-tuple-element.38), channel_id=1, source_target_pairs={{0,1},{1,0},{128,129},{129,128},{2,3},{3,2},{130,131},{131,130},{4... | collective-permute-start | bytes 1544 | tf_op jit(solution)/shard_map/ppermute | solution.py:64
  64.8 5.4 %collective-permute-start.11 = (f32[1,128]{1,0:T(1,128)S(1)}, f32[1,128]{1,0:T(1,128)S(1)}, u32[]{:S(2)}, u32[]{:S(2)}) collective-permute-start(f32[1,128]{1,0:T(1,128)S(1)} %get-tuple-element.38), channel_id=1, source_target_pairs={{0,128},{1,129},{128,0},{129,1},{2,130},{3,131},{130,2},{131,3},{4... | collective-permute-start | bytes 1544 | tf_op jit(solution)/shard_map/ppermute | solution.py:64
  67.2 3.5 %collective-permute-start.12 = (f32[1,128]{1,0:T(1,128)S(1)}, f32[1,128]{1,0:T(1,128)S(1)}, u32[]{:S(2)}, u32[]{:S(2)}) collective-permute-start(f32[1,128]{1,0:T(1,128)S(1)} %get-tuple-element.38), channel_id=1, source_target_pairs={{0,129},{1,128},{128,1},{129,0},{2,131},{3,130},{130,3},{131,2},{4... | collective-permute-start | bytes 1544 | tf_op jit(solution)/shard_map/ppermute | solution.py:64
  70.8 32.8 %all-to-all-start.1 = ((f16[16,48,1024]{2,1,0:T(8,128)(2,1)}), f16[16,48,1024]{2,1,0:T(8,128)(2,1)}, u32[]{:S(2)}, u32[]{:S(2)}) async-start(f16[16,48,1024]{2,1,0:T(8,128)(2,1)} %bitcast.13), calls=%async_computation.1 | async-start | bytes 3145728 | tf_op jit(solution)/shard_map/all_to_all | solution.py:20
  78.0 1.1 collective-permute-start.14
  81.3 11.6 %copy-start = (f32[384,1024]{1,0:T(8,128)}, f32[384,1024]{1,0:T(8,128)S(1)}, u32[]{:S(2)}) copy-start(f32[384,1024]{1,0:T(8,128)S(1)} %get-tuple-element.56) | copy-start | bytes 4718596
  81.4 11.5 %collective-permute-start.15 = (f16[192,1024]{1,0:T(8,128)(2,1)S(1)}, f16[192,1024]{1,0:T(8,128)(2,1)S(1)}, u32[]{:S(2)}, u32[]{:S(2)}) collective-permute-start(f16[192,1024]{1,0:T(8,128)(2,1)S(1)} %slice.36), channel_id=1, source_target_pairs={{0,28},{2,6},{4,0},{6,10},{8,4},{10,14},{12,8},{14,18},{16,12},{18... | collective-permute-start | bytes 1179656 | tf_op jit(solution)/shard_map/ppermute | solution.py:33
  81.8 7.5 %collective-permute-start.17 = (f32[1,128]{1,0:T(1,128)S(1)}, f32[1,128]{1,0:T(1,128)S(1)}, u32[]{:S(2)}, u32[]{:S(2)}) collective-permute-start(f32[1,128]{1,0:T(1,128)S(1)} %add.204), channel_id=1, source_target_pairs={{0,4},{4,0},{8,12},{12,8},{16,20},{20,16},{24,28},{28,24},{1,5},{5... | collective-permute-start | bytes 1544 | tf_op jit(solution)/shard_map/ppermute | solution.py:64
  83.5 5.8 %collective-permute-start.18 = (f32[1,128]{1,0:T(1,128)S(1)}, f32[1,128]{1,0:T(1,128)S(1)}, u32[]{:S(2)}, u32[]{:S(2)}) collective-permute-start(f32[1,128]{1,0:T(1,128)S(1)} %add.204), channel_id=1, source_target_pairs={{0,8},{4,12},{8,0},{12,4},{16,24},{20,28},{24,16},{28,20},{1,9},{5... | collective-permute-start | bytes 1544 | tf_op jit(solution)/shard_map/ppermute | solution.py:64
  84.0 5.3 %collective-permute-start.19 = (f32[1,128]{1,0:T(1,128)S(1)}, f32[1,128]{1,0:T(1,128)S(1)}, u32[]{:S(2)}, u32[]{:S(2)}) collective-permute-start(f32[1,128]{1,0:T(1,128)S(1)} %add.204), channel_id=1, source_target_pairs={{0,12},{4,8},{8,4},{12,0},{16,28},{20,24},{24,20},{28,16},{1,13},{... | collective-permute-start | bytes 1544 | tf_op jit(solution)/shard_map/ppermute | solution.py:64
  86.2 6.7 %collective-permute-start.16 = (f16[48,1024]{1,0:T(8,128)(2,1)S(1)}, f16[48,1024]{1,0:T(8,128)(2,1)S(1)}, u32[]{:S(2)}, u32[]{:S(2)}) collective-permute-start(f16[48,1024]{1,0:T(8,128)(2,1)S(1)} %slice.37), channel_id=1, source_target_pairs={{0,24},{2,10},{4,28},{6,14},{8,0},{10,18},{12,4},{14,22},{16,8},{1... | collective-permute-start | bytes 294920 | tf_op jit(solution)/shard_map/ppermute | solution.py:33
  93.0 10.6 %collective-permute-start.20 = (f16[96,1024]{1,0:T(8,128)(2,1)S(1)}, f16[96,1024]{1,0:T(8,128)(2,1)S(1)}, u32[]{:S(2)}, u32[]{:S(2)}) collective-permute-start(f16[96,1024]{1,0:T(8,128)(2,1)S(1)} %fusion), channel_id=1, source_target_pairs={{0,24},{2,10},{4,28},{6,14},{8,0},{10,18},{12,4},{14,22},{16,8},{1... | collective-permute-start | bytes 589832 | tf_op jit(solution)/shard_map/ppermute | solution.py:33
  96.2 7.4 %collective-permute-start.21 = (f32[1,128]{1,0:T(1,128)S(1)}, f32[1,128]{1,0:T(1,128)S(1)}, u32[]{:S(2)}, u32[]{:S(2)}) collective-permute-start(f32[1,128]{1,0:T(1,128)S(1)} %add_add_fusion.1), channel_id=1, source_target_pairs={{0,16},{4,20},{8,24},{12,28},{16,0},{20,4},{24,8},{28,12},{1,17},{... | collective-permute-start | bytes 1544 | tf_op jit(solution)/shard_map/ppermute | solution.py:59
  103.6 7.4 %collective-permute-start.22 = (f32[1,128]{1,0:T(1,128)S(1)}, f32[1,128]{1,0:T(1,128)S(1)}, u32[]{:S(2)}, u32[]{:S(2)}) collective-permute-start(f32[1,128]{1,0:T(1,128)S(1)} %add.212), channel_id=1, source_target_pairs={{0,32},{32,0},{64,96},{96,64},{1,33},{33,1},{65,97},{97,65},{2,34}... | collective-permute-start | bytes 1544 | tf_op jit(solution)/shard_map/ppermute | solution.py:64
  105.2 5.9 %collective-permute-start.23 = (f32[1,128]{1,0:T(1,128)S(1)}, f32[1,128]{1,0:T(1,128)S(1)}, u32[]{:S(2)}, u32[]{:S(2)}) collective-permute-start(f32[1,128]{1,0:T(1,128)S(1)} %add.212), channel_id=1, source_target_pairs={{0,64},{32,96},{64,0},{96,32},{1,65},{33,97},{65,1},{97,33},{2,66}... | collective-permute-start | bytes 1544 | tf_op jit(solution)/shard_map/ppermute | solution.py:64
  107.8 4.8 %collective-permute-start.24 = (f32[1,128]{1,0:T(1,128)S(1)}, f32[1,128]{1,0:T(1,128)S(1)}, u32[]{:S(2)}, u32[]{:S(2)}) collective-permute-start(f32[1,128]{1,0:T(1,128)S(1)} %add.212), channel_id=1, source_target_pairs={{0,96},{32,64},{64,32},{96,0},{1,97},{33,65},{65,33},{97,1},{2,98}... | collective-permute-start | bytes 1544 | tf_op jit(solution)/shard_map/ppermute | solution.py:64
  108.5 4.2 %collective-permute-start.25 = (f32[48,1024]{1,0:T(8,128)S(1)}, f32[48,1024]{1,0:T(8,128)S(1)}, u32[]{:S(2)}, u32[]{:S(2)}) collective-permute-start(f32[48,1024]{1,0:T(8,128)S(1)} %dynamic-slice_add_fusion), channel_id=1, source_target_pairs={{0,2},{2,0},{1,3},{3,1},{4,6},{6,4},{5,7},{7,5},{8,10},{10,8},{9,1... | collective-permute-start | bytes 589832 | tf_op jit(solution)/shard_map/ppermute | solution.py:85
